TPU v7x, 256 devices: a whole 4x4x8 slice. The times are simulated.
256 devices in a mesh: cuts: 2 (over z_hi), region: 128 (over y, x, z_lo, core).
Axes of the slice: x: 4, y: 4, z: 8 (z_hi: 2, z_lo: 4; z = z_hi * 4 + z_lo), core: 2. Of those that a mesh axis runs over, the one named last changes fastest.
Arguments:
- objects: float32 [2, 2, 32768, 1024], P('cuts', None, 'region'), may hold values from -4 to 4
- probes: bfloat16 [4, 2, 256, 256], replicated, may hold values from -4 to 4
- amplitudes: float32 [512, 256, 256], P('region'), may hold values from 0.2 to 2.5
- prop_phase: float32 [256, 256], replicated, may hold values from -3.140625 to 3.140625
- scan_rows: int32 [512], P('region'), may hold values from -128 to 128, as said below
- scan_cols: int32 [512], P('region'), may hold values from 0 to 768
- probe_choice: int32 [512], P('region'), may hold values from 0 to 3
Outputs:
- gradient: float32 [2, 2, 32768, 1024], P('cuts', None, 'region')
Inputs may be any that keep to these rules, and one draw needn't show every extreme that they name: `scan_rows`: in every region, half of the positions start between 64 and 128 rows above the band's first row, and the other half end between 64 and 128 rows below its last row.
All inputs are finite; a program needn't handle non-finite values.
Results may differ from a plain program's by a relative error of at most 0.039.
Values may be sent and summed in bfloat16 or wider, within the bound.
No kernel may reach another device: no remote copies, remote signals or barrier semaphores. Data moves between devices by JAX's collectives and lax.ppermute only.
A program may use at most 64 MiB of HBM per device.

v0:
```python
import jax
import jax.numpy as jnp
from jax import lax
from jax.sharding import PartitionSpec as P

modulus_floor = 0.25


def padded(block, sides, width):
    for axis, dim in sides:
        count = lax.axis_size(axis)
        forward = [(i, i + 1) for i in range(count - 1)]
        forward.append((count - 1, 0))
        backward = [(target, source) for source, target in forward]
        low = lax.ppermute(
            lax.slice_in_dim(block, block.shape[dim] - width, None, axis=dim), axis, forward
        )
        high = lax.ppermute(lax.slice_in_dim(block, 0, width, axis=dim), axis, backward)
        block = jnp.concatenate([low, block, high], axis=dim)
    return block


def from_behind(block, axis, distance):
    devices = range(lax.axis_size(axis))
    route = [(i - distance, i) for i in devices if i - distance in devices]
    return lax.ppermute(block, axis, route)


def widened(narrow):
    return lax.optimization_barrier(narrow).astype(jnp.float32)


def dft_tables(length, direction):
    indices = jnp.arange(length, dtype=jnp.int32)
    product = indices[:, None] * indices[None, :] % length
    angles = product.astype(jnp.float32) * (2.0 * jnp.pi / length)
    scaling = 1.0 / jnp.sqrt(jnp.float32(length))
    table = jnp.stack([jnp.cos(angles) * scaling, direction * jnp.sin(angles) * scaling]).astype(
        jnp.bfloat16
    )
    real_table = table[0]
    imag_table = table[1]
    negated = -imag_table
    left_block = jnp.stack([jnp.stack([real_table, negated]), jnp.stack([imag_table, real_table])])
    right_block = jnp.stack([jnp.stack([real_table, imag_table]), jnp.stack([negated, real_table])])
    return (left_block, right_block)


def transform(input_field, block_tables):
    left_block, right_block = block_tables
    middle = jnp.einsum(
        "dcjk,nckl->ndjl",
        left_block,
        input_field.astype(jnp.bfloat16),
        preferred_element_type=jnp.float32,
    ).astype(jnp.bfloat16)
    return jnp.einsum("nckl,cdlm->ndkm", middle, right_block, preferred_element_type=jnp.float32)


def multiply_complex(left_field, right_field):
    real_part = (
        left_field[..., 0, :, :] * right_field[..., 0, :, :]
        - left_field[..., 1, :, :] * right_field[..., 1, :, :]
    )
    imag_part = (
        left_field[..., 0, :, :] * right_field[..., 1, :, :]
        + left_field[..., 1, :, :] * right_field[..., 0, :, :]
    )
    return jnp.stack([real_part, imag_part], axis=-3)


def multiply_conjugate(left_field, right_field):
    real_part = (
        left_field[..., 0, :, :] * right_field[..., 0, :, :]
        + left_field[..., 1, :, :] * right_field[..., 1, :, :]
    )
    imag_part = (
        left_field[..., 0, :, :] * right_field[..., 1, :, :]
        - left_field[..., 1, :, :] * right_field[..., 0, :, :]
    )
    return jnp.stack([real_part, imag_part], axis=-3)


def propagate_adjoint(input_field, optics):
    propagator, forward_table, inverse_table = optics
    return transform(
        multiply_conjugate(propagator, transform(input_field, forward_table)), inverse_table
    )


def forward_slices(incoming, patch_set, measured, optics, last_cut):
    current = incoming
    stored = [current]
    exit_field = multiply_complex(widened(current), patch_set[:, 0])
    far_field = transform(exit_field, optics[1])
    modulus = jnp.sqrt(far_field[:, 0] * far_field[:, 0] + far_field[:, 1] * far_field[:, 1])
    factor = 1.0 - measured / jnp.maximum(modulus, modulus_floor)
    detected = far_field * factor[:, None]
    onward = multiply_complex(optics[0], far_field)
    chosen = jnp.where(last_cut, detected, onward)
    current = transform(chosen, optics[2]).astype(jnp.bfloat16)
    return (jnp.stack(stored, axis=1), current)


def adjoint_slices(seed_wave, stored_set, patch_set, optics):
    local_count = patch_set.shape[1]
    current = seed_wave
    pieces = [None] * local_count
    for slice_index in reversed(range(local_count)):
        arriving = widened(current)
        pieces[slice_index] = multiply_conjugate(widened(stored_set[:, slice_index]), arriving)
        backward = multiply_conjugate(patch_set[:, slice_index], arriving)
        current = propagate_adjoint(backward, optics).astype(jnp.bfloat16)
    return (jnp.stack(pieces, axis=1), current)


def cut_patches(extended, top_rows, left_cols, rim_depth, patch_side):
    zero_index = jnp.zeros((), jnp.int32)

    def window(top_row, left_col):
        return lax.dynamic_slice(
            extended,
            (zero_index, zero_index, top_row + rim_depth, left_col),
            (extended.shape[0], 2, patch_side, patch_side),
        )

    return jax.vmap(window)(top_rows, left_cols)


def add_patches(gradient, pieces, top_rows, left_cols, rim_depth):
    zero_index = jnp.zeros((), jnp.int32)

    def deposit(position, running):
        corner = (zero_index, zero_index, top_rows[position] + rim_depth, left_cols[position])
        existing = lax.dynamic_slice(running, corner, pieces.shape[1:])
        return lax.dynamic_update_slice(running, existing + pieces[position], corner)

    return lax.fori_loop(0, pieces.shape[0], deposit, gradient)


def select_probes(probes, probe_choice):
    mode_ids = jnp.arange(probes.shape[0], dtype=jnp.int32)
    picked = probe_choice[:, None] == mode_ids[None, :]
    return jnp.sum(
        jnp.where(picked[:, :, None, None, None], probes[None], jnp.zeros((), probes.dtype)), axis=1
    )


def shards(objects, probes, amplitudes, prop_phase, scan_rows, scan_cols, probe_choice):
    patch_side = probes.shape[-1]
    rim_depth = patch_side // 2
    band_rows = objects.shape[2]
    optics = (
        jnp.stack([jnp.cos(prop_phase), jnp.sin(prop_phase)]),
        dft_tables(patch_side, -1.0),
        dft_tables(patch_side, 1.0),
    )
    cut_index = lax.axis_index("cuts")
    cut_count = lax.axis_size("cuts")
    first_cut = cut_index == 0
    last_cut = cut_index == cut_count - 1
    extended = padded(objects, (("region", 2),), rim_depth)
    patches = cut_patches(extended, scan_rows, scan_cols, rim_depth, patch_side)
    illumination = select_probes(probes, probe_choice)

    def run_forward(wave_in, patch_set, measured):
        return forward_slices(wave_in, patch_set, measured, optics, last_cut)

    def blank_forward(wave_in, patch_set, measured):
        return (jnp.zeros(patch_set.shape, jnp.bfloat16), jnp.zeros_like(wave_in))

    def run_adjoint(arriving, stored_set, patch_set):
        return adjoint_slices(arriving, stored_set, patch_set, optics)

    def blank_adjoint(arriving, stored_set, patch_set):
        return (jnp.zeros(patch_set.shape, jnp.float32), jnp.zeros_like(arriving))

    incoming = illumination
    stored_all = jnp.zeros(patches.shape, jnp.bfloat16)
    outgoing = jnp.zeros(illumination.shape, jnp.bfloat16)
    for section_index in range(cut_count):
        active = cut_index == section_index
        stored_now, outgoing = lax.cond(
            active, run_forward, blank_forward, incoming, patches, amplitudes
        )
        stored_all = jnp.where(active, stored_now, stored_all)
        if section_index < cut_count - 1:
            passed = from_behind(outgoing, "cuts", 1)
            incoming = jnp.where(first_cut, illumination, passed)
    arriving = outgoing
    pieces = jnp.zeros(patches.shape, jnp.float32)
    for section_index in reversed(range(cut_count)):
        active = cut_index == section_index
        pieces_now, backward = lax.cond(
            active, run_adjoint, blank_adjoint, arriving, stored_all, patches
        )
        pieces = jnp.where(active, pieces_now, pieces)
        if section_index > 0:
            arriving = from_behind(backward, "cuts", -1)
    gradient_ext = add_patches(
        jnp.zeros(extended.shape, jnp.float32), pieces, scan_rows, scan_cols, rim_depth
    )
    rim_pair = jnp.stack(
        [gradient_ext[:, :, :rim_depth], gradient_ext[:, :, band_rows + rim_depth :]]
    )
    received = padded(rim_pair.astype(jnp.bfloat16), (("region", 0),), 1).astype(rim_pair.dtype)
    interior = gradient_ext[:, :, rim_depth : band_rows + rim_depth]
    interior = interior.at[:, :, :rim_depth].add(received[0])
    interior = interior.at[:, :, band_rows - rim_depth :].add(received[3])
    return interior


def solution(mesh):
    return jax.shard_map(
        shards,
        mesh=mesh,
        in_specs=(
            P("cuts", None, "region", None),
            P(),
            P("region", None, None),
            P(),
            P("region"),
            P("region"),
            P("region"),
        ),
        out_specs=P("cuts", None, "region", None),
        check_vma=False,
    )
```

profile of v0, /device:TPU:1, one launch (start us, length us, event | category | flops | bytes accessed | tf_op | source)
XLA Modules:
  0.0 252.4 jit_solution(4936341434827090286)
XLA Ops:
  0.0 3.1 %fusion.97 = (f32[1,2,128,1024]{3,2,1,0:T(8,128)}, f32[1,2,128,1024]{3,2,1,0:T(8,128)}) fusion(f32[1,2,256,1024]{3,2,1,0:T(8,128)} %param.21), kind=kLoop, calls=%fused_computation.151 | loop fusion | bytes 4194304 | tf_op jit(solution)/shard_map/slice | solution.py:16
  3.2 3.0 %collective-permute-start = (f32[1,2,128,1024]{3,2,1,0:T(8,128)}, f32[1,2,128,1024]{3,2,1,0:T(8,128)}, u32[]{:S(2)}, u32[]{:S(2)}) collective-permute-start(f32[1,2,128,1024]{3,2,1,0:T(8,128)} %get-tuple-element.388), channel_id=1, source_target_pairs={{0,1},{1,2},{2,3},{3,4},{4,5},{5,6},{6,7},{7,8},{8,9},{9,10},{10,1... | collective-permute-start | bytes 3145736 | tf_op jit(solution)/shard_map/ppermute | solution.py:15
  21.7 10.6 %collective-permute-done.1 = f32[1,2,128,1024]{3,2,1,0:T(8,128)} collective-permute-done((f32[1,2,128,1024]{3,2,1,0:T(8,128)}, f32[1,2,128,1024]{3,2,1,0:T(8,128)}, u32[]{:S(2)}, u32[]{:S(2)}) %collective-permute-start.1) | collective-permute-done | bytes 1048608 | tf_op jit(solution)/shard_map/ppermute | solution.py:18
  32.3 4.0 %pad_maximum_fusion = f32[1,2,512,1024]{3,2,1,0:T(8,128)} fusion(f32[1,2,128,1024]{3,2,1,0:T(8,128)} %collective-permute-done.1, f32[1,2,256,1024]{3,2,1,0:T(8,128)S(1)} %copy-done.3, f32[1,2,128,1024]{3,2,1,0:T(8,128)} %collective-permute-done), kind=kLoop, calls=%fused_computation.90 | loop fusion | flops 2097152 | bytes 8388608 | tf_op jit(solution)/shard_map/concatenate | solution.py:19
  36.3 13.6 %while.21 = (s32[]{:T(128)}, f32[1,2,512,1024]{3,2,1,0:T(8,128)}, s32[4,4]{1,0:T(4,128)S(1)}, f32[4,1,2,256,256]{4,3,2,1,0:T(8,128)S(1)}) while((s32[]{:T(128)}, f32[1,2,512,1024]{3,2,1,0:T(8,128)}, s32[4,4]{1,0:T(4,128)S(1)}, f32[4,1,2,256,256]{4,3,2,1,0:T(8,128)S(1)}) %tuple.130), condition=%wide.while_cond.2.clone, body=%wide.while_body.2.sunk.clone | while | flops 2 | bytes 1048701 | solution.py:121
  36.9 2.7 %bitcast_dynamic-update-slice_fusion.3 = f32[4,1,2,256,256]{4,3,2,1,0:T(8,128)S(1)} fusion(f32[4,1,2,256,256]{4,3,2,1,0:T(8,128)S(1)} %get-tuple-element.503, s32[]{:T(128)S(6)} %copy.76, f32[1,2,512,1024]{3,2,1,0:T(8,128)} %get-tuple-element.505, s32[]{:T(128)} %bitcast.320, s32[]{:T(128)} %bitcast.321), kind=kLoop, calls=%fused_computation.88.clone.1.clone | loop fusion | bytes 1048588 | tf_op jit(solution)/shard_map/vmap()/gather
  40.3 2.7 %bitcast_dynamic-update-slice_fusion.3 = f32[4,1,2,256,256]{4,3,2,1,0:T(8,128)S(1)} fusion(f32[4,1,2,256,256]{4,3,2,1,0:T(8,128)S(1)} %get-tuple-element.503, s32[]{:T(128)S(6)} %copy.76, f32[1,2,512,1024]{3,2,1,0:T(8,128)} %get-tuple-element.505, s32[]{:T(128)} %bitcast.320, s32[]{:T(128)} %bitcast.321), kind=kLoop, calls=%fused_computation.88.clone.1.clone | loop fusion | bytes 1048588 | tf_op jit(solution)/shard_map/vmap()/gather
  43.7 2.7 %bitcast_dynamic-update-slice_fusion.3 = f32[4,1,2,256,256]{4,3,2,1,0:T(8,128)S(1)} fusion(f32[4,1,2,256,256]{4,3,2,1,0:T(8,128)S(1)} %get-tuple-element.503, s32[]{:T(128)S(6)} %copy.76, f32[1,2,512,1024]{3,2,1,0:T(8,128)} %get-tuple-element.505, s32[]{:T(128)} %bitcast.320, s32[]{:T(128)} %bitcast.321), kind=kLoop, calls=%fused_computation.88.clone.1.clone | loop fusion | bytes 1048588 | tf_op jit(solution)/shard_map/vmap()/gather
  47.1 2.7 %bitcast_dynamic-update-slice_fusion.3 = f32[4,1,2,256,256]{4,3,2,1,0:T(8,128)S(1)} fusion(f32[4,1,2,256,256]{4,3,2,1,0:T(8,128)S(1)} %get-tuple-element.503, s32[]{:T(128)S(6)} %copy.76, f32[1,2,512,1024]{3,2,1,0:T(8,128)} %get-tuple-element.505, s32[]{:T(128)} %bitcast.320, s32[]{:T(128)} %bitcast.321), kind=kLoop, calls=%fused_computation.88.clone.1.clone | loop fusion | bytes 1048588 | tf_op jit(solution)/shard_map/vmap()/gather
  49.8 16.2 %conditional.4 = (bf16[4,1,2,256,256]{4,3,2,0,1:T(8,128)(2,1)}, bf16[4,2,256,256]{3,2,1,0:T(8,128)(2,1)}) conditional(s32[]{:T(128)} %convert_element_type.194, () %tuple.67, (bf16[4,2,256,256]{3,2,1,0:T(8,128)(2,1)S(1)}, pred[]{:T(512)}, f32[4,1,2,256,256]{4,3,2,1,0:T(8,128)S(1)}, bf16[2,2,256,256]{3,2,1,0:T(8,128)(2,1)}, ...), branch_computations={%region_1.2_spmd, %region_2.3_spmd} | conditional | flops 2160590848 | bytes 41418824 | solution.py:183
  52.6 4.1 %convolution_bitcast_fusion = f32[4,2,256,256]{3,2,1,0:T(8,128)} fusion(bf16[4,1,256,256]{3,2,1,0:T(8,128)(2,1)} %get-tuple-element.367, bf16[4,1,256,256]{3,2,1,0:T(8,128)(2,1)} %get-tuple-element.366, bf16[2,2,256,256]{3,2,1,0:T(8,128)(2,1)} %get-tuple-element.228, bf16[2,2,256,256]{3,2,1,0:T(8,128)(2,1)} %get-tuple-element.321), kind=kOutput, calls=%fused_computation.5 | convolution fusion | flops 1076363264 | bytes 4194304 | tf_op jit(solution)/shard_map/cond/branch_1_fun/nckl,cdlm->ndkm/dot_general | solution.py:57
  56.8 3.0 %multiply_subtract_fusion = (bf16[4,1,256,256]{3,2,1,0:T(8,128)(2,1)}, bf16[4,1,256,256]{3,2,1,0:T(8,128)(2,1)}) fusion(f32[4,2,256,256]{3,2,1,0:T(8,128)} %convolution_bitcast_fusion, f32[256,256]{1,0:T(8,128)S(1)} %bitcast.328, f32[256,256]{1,0:T(8,128)} %bitcast.331), kind=kLoop, calls=%fused_computation.16 | loop fusion | flops 2097152 | bytes 3670016 | tf_op jit(solution)/shard_map/cond/branch_1_fun/sub | solution.py:62
  61.2 4.8 %fusion.3 = bf16[4,2,256,256]{3,2,1,0:T(8,128)(2,1)} fusion(bf16[4,1,256,256]{3,2,1,0:T(8,128)(2,1)} %get-tuple-element.369, bf16[4,1,256,256]{3,2,1,0:T(8,128)(2,1)} %get-tuple-element.368, f32[4,2,256,256]{3,2,1,0:T(8,128)} %convolution_bitcast_fusion, f32[4,256,256]{2,1,0:T(8,128)} %fusion.10, pred[]{:T(512)} %get-tuple-element.226, ...), kind=kOutput, calls=%fused_computation.8 | convolution fusion | flops 1077936128 | bytes 6291457 | tf_op jit(solution)/shard_map/cond/branch_1_fun/nckl,cdlm->ndkm/dot_general | solution.py:57
  68.3 18.0 %collective-permute-done.2 = bf16[4,2,256,256]{3,2,1,0:T(8,128)(2,1)} collective-permute-done((bf16[4,2,256,256]{3,2,1,0:T(8,128)(2,1)}, bf16[4,2,256,256]{3,2,1,0:T(8,128)(2,1)}, u32[]{:S(2)}, u32[]{:S(2)}) %collective-permute-start.2) | collective-permute-done | bytes 1048608 | tf_op jit(solution)/shard_map/ppermute | solution.py:26
  92.8 53.7 %collective-permute-done.3 = bf16[4,2,256,256]{3,2,1,0:T(8,128)(2,1)S(1)} collective-permute-done((bf16[4,2,256,256]{3,2,1,0:T(8,128)(2,1)}, bf16[4,2,256,256]{3,2,1,0:T(8,128)(2,1)S(1)}, u32[]{:S(2)}, u32[]{:S(2)}) %collective-permute-start.3) | collective-permute-done | bytes 1048608 | tf_op jit(solution)/shard_map/ppermute | solution.py:26
  146.5 4.5 %conditional.7 = (f32[4,1,2,256,256]{4,3,2,0,1:T(8,128)}) conditional(s32[]{:T(128)} %convert_element_type.194, () %tuple.65, (bf16[4,1,2,256,256]{4,3,2,1,0:T(8,128)(2,1)S(1)}, bf16[4,2,256,256]{3,2,1,0:T(8,128)(2,1)S(1)}) %tuple.72), branch_computations={%region_7.8_spmd, %region_8.9_spmd} | conditional | flops 3145728 | bytes 20971556 | solution.py:194
  156.0 48.7 %while.20 = (s32[]{:T(128)}, f32[1,2,512,1024]{3,2,1,0:T(8,128)}, s32[4]{0:T(128)S(1)}, s32[4]{0:T(128)S(1)}, f32[4,1,2,256,256]{4,3,2,1,0:T(8,128)S(1)}, /*index=5*/s32[1]{0:T(128)}, s32[1]{0:T(128)}) while((s32[]{:T(128)}, f32[1,2,512,1024]{3,2,1,0:T(8,128)}, s32[4]{0:T(128)S(1)}, s32[4]{0:T(128)S(1)}, ...), condition=%wide.region_10.11_spmd.clone, body=%wide.region_9.10_spmd.sunk.clone | while | flops 131081 | bytes 2621645 | solution.py:138
  161.8 6.3 %dynamic_update_slice.12 = f32[1,2,512,1024]{3,2,1,0:T(8,128)} dynamic-update-slice(f32[1,2,512,1024]{3,2,1,0:T(8,128)} %get-tuple-element.528, f32[1,2,256,256]{3,2,1,0:T(8,128)S(1)} %bitcast_add_fusion.3, s32[]{:T(128)} %constant.174.clone.1..sunk.1, s32[]{:T(128)} %constant.174.clone.1..sunk.1, s32[]{:T(128)S(6)} %select_n.242, s32[]{:T(128)S(6)} %select_n.243) | dynamic-update-slice | bytes 1048580 | tf_op jit(solution)/shard_map/while/body/eval_jaxpr/dynamic_update_slice | solution.py:136
  173.8 6.0 %dynamic_update_slice.12 = f32[1,2,512,1024]{3,2,1,0:T(8,128)} dynamic-update-slice(f32[1,2,512,1024]{3,2,1,0:T(8,128)} %get-tuple-element.528, f32[1,2,256,256]{3,2,1,0:T(8,128)S(1)} %bitcast_add_fusion.3, s32[]{:T(128)} %constant.174.clone.1..sunk.1, s32[]{:T(128)} %constant.174.clone.1..sunk.1, s32[]{:T(128)S(6)} %select_n.242, s32[]{:T(128)S(6)} %select_n.243) | dynamic-update-slice | bytes 1048580 | tf_op jit(solution)/shard_map/while/body/eval_jaxpr/dynamic_update_slice | solution.py:136
  185.6 6.8 %dynamic_update_slice.12 = f32[1,2,512,1024]{3,2,1,0:T(8,128)} dynamic-update-slice(f32[1,2,512,1024]{3,2,1,0:T(8,128)} %get-tuple-element.528, f32[1,2,256,256]{3,2,1,0:T(8,128)S(1)} %bitcast_add_fusion.3, s32[]{:T(128)} %constant.174.clone.1..sunk.1, s32[]{:T(128)} %constant.174.clone.1..sunk.1, s32[]{:T(128)S(6)} %select_n.242, s32[]{:T(128)S(6)} %select_n.243) | dynamic-update-slice | bytes 1048580 | tf_op jit(solution)/shard_map/while/body/eval_jaxpr/dynamic_update_slice | solution.py:136
  198.2 6.5 %dynamic_update_slice.12 = f32[1,2,512,1024]{3,2,1,0:T(8,128)} dynamic-update-slice(f32[1,2,512,1024]{3,2,1,0:T(8,128)} %get-tuple-element.528, f32[1,2,256,256]{3,2,1,0:T(8,128)S(1)} %bitcast_add_fusion.3, s32[]{:T(128)} %constant.174.clone.1..sunk.1, s32[]{:T(128)} %constant.174.clone.1..sunk.1, s32[]{:T(128)S(6)} %select_n.242, s32[]{:T(128)S(6)} %select_n.243) | dynamic-update-slice | bytes 1048580 | tf_op jit(solution)/shard_map/while/body/eval_jaxpr/dynamic_update_slice | solution.py:136
  206.4 5.1 %collective-permute-start.5 = (bf16[1,1,2,128,1024]{4,3,2,1,0:T(8,128)(2,1)S(1)}, bf16[1,1,2,128,1024]{4,3,2,1,0:T(8,128)(2,1)S(1)}, u32[]{:S(2)}, u32[]{:S(2)}) collective-permute-start(bf16[1,1,2,128,1024]{4,3,2,1,0:T(8,128)(2,1)S(1)} %bitcast.335), channel_id=1, source_target_pairs={{1,0},{2,1},{3,2},{4,3},{5,4},{6,5},{7,6},{8,7},{9,8},{10,9},{11,1... | collective-permute-start | bytes 1572872 | tf_op jit(solution)/shard_map/ppermute | solution.py:18
  211.5 29.0 %collective-permute-start.4 = (bf16[1,1,2,128,1024]{4,3,2,1,0:T(8,128)(2,1)S(1)}, bf16[1,1,2,128,1024]{4,3,2,1,0:T(8,128)(2,1)S(1)}, u32[]{:S(2)}, u32[]{:S(2)}) collective-permute-start(bf16[1,1,2,128,1024]{4,3,2,1,0:T(8,128)(2,1)S(1)} %bitcast.334), channel_id=1, source_target_pairs={{0,1},{1,2},{2,3},{3,4},{4,5},{5,6},{6,7},{7,8},{8,9},{9,10},{10,1... | collective-permute-start | bytes 1572872 | tf_op jit(solution)/shard_map/ppermute | solution.py:15
  242.5 4.8 %collective-permute-done.5 = bf16[1,1,2,128,1024]{4,3,2,1,0:T(8,128)(2,1)S(1)} collective-permute-done((bf16[1,1,2,128,1024]{4,3,2,1,0:T(8,128)(2,1)S(1)}, bf16[1,1,2,128,1024]{4,3,2,1,0:T(8,128)(2,1)S(1)}, u32[]{:S(2)}, u32[]{:S(2)}) %collective-permute-start.5) | collective-permute-done | bytes 524320 | tf_op jit(solution)/shard_map/ppermute | solution.py:18
  (94 shorter events, 61.6 us)
Async XLA Ops:
  0.0 14.3 %copy-start.15 = (s32[4]{0:T(128)S(1)}, s32[4]{0:T(128)}, u32[]{:S(2)}) copy-start(s32[4]{0:T(128)} %param.26) | copy-start | bytes 52
  0.0 14.4 %copy-start.14 = (s32[4]{0:T(128)S(1)}, s32[4]{0:T(128)}, u32[]{:S(2)}) copy-start(s32[4]{0:T(128)} %param.25) | copy-start | bytes 52
  3.2 18.5 %collective-permute-start = (f32[1,2,128,1024]{3,2,1,0:T(8,128)}, f32[1,2,128,1024]{3,2,1,0:T(8,128)}, u32[]{:S(2)}, u32[]{:S(2)}) collective-permute-start(f32[1,2,128,1024]{3,2,1,0:T(8,128)} %get-tuple-element.388), channel_id=1, source_target_pairs={{0,1},{1,2},{2,3},{3,4},{4,5},{5,6},{6,7},{7,8},{8,9},{9,10},{10,1... | collective-permute-start | bytes 3145736 | tf_op jit(solution)/shard_map/ppermute | solution.py:15
  6.2 26.1 %collective-permute-start.1 = (f32[1,2,128,1024]{3,2,1,0:T(8,128)}, f32[1,2,128,1024]{3,2,1,0:T(8,128)}, u32[]{:S(2)}, u32[]{:S(2)}) collective-permute-start(f32[1,2,128,1024]{3,2,1,0:T(8,128)} %get-tuple-element.389), channel_id=1, source_target_pairs={{1,0},{2,1},{3,2},{4,3},{5,4},{6,5},{7,6},{8,7},{9,8},{10,9},{11,1... | collective-permute-start | bytes 3145736 | tf_op jit(solution)/shard_map/ppermute | solution.py:18
  14.5 3.1 %copy-start.16 = (s32[4]{0:T(128)S(1)}, s32[4]{0:T(128)}, u32[]{:S(2)}) copy-start(s32[4]{0:T(128)} %param.27) | copy-start | bytes 52
  14.6 3.2 %copy-start.13 = (f32[256,256]{1,0:T(8,128)S(1)}, f32[256,256]{1,0:T(8,128)}, u32[]{:S(2)}) copy-start(f32[256,256]{1,0:T(8,128)} %param.24) | copy-start | bytes 786436
  17.6 14.7 %copy-start.3 = (f32[1,2,256,1024]{3,2,1,0:T(8,128)S(1)}, f32[1,2,256,1024]{3,2,1,0:T(8,128)}, u32[]{:S(2)}) copy-start(f32[1,2,256,1024]{3,2,1,0:T(8,128)} %param.21) | copy-start | bytes 6291460
  56.8 3.0 %copy-start = (f32[4,2,256,256]{3,2,1,0:T(8,128)S(1)}, f32[4,2,256,256]{3,2,1,0:T(8,128)}, u32[]{:S(2)}) copy-start(f32[4,2,256,256]{3,2,1,0:T(8,128)} %convolution_bitcast_fusion) | copy-start | bytes 6291460 | tf_op jit(solution)/shard_map/cond
  56.8 3.0 %copy-start.9 = (f32[4,256,256]{2,1,0:T(8,128)S(1)}, f32[4,256,256]{2,1,0:T(8,128)}, u32[]{:S(2)}) copy-start(f32[4,256,256]{2,1,0:T(8,128)} %get-tuple-element.230) | copy-start | bytes 3145732 | tf_op jit(solution)/shard_map/cond
  66.1 20.3 %collective-permute-start.2 = (bf16[4,2,256,256]{3,2,1,0:T(8,128)(2,1)}, bf16[4,2,256,256]{3,2,1,0:T(8,128)(2,1)}, u32[]{:S(2)}, u32[]{:S(2)}) collective-permute-start(bf16[4,2,256,256]{3,2,1,0:T(8,128)(2,1)} %get-tuple-element.271), channel_id=1, source_target_pairs={{0,128},{1,129},{2,130},{3,131},{4,132},{5,133},{6,134},{7,135},{8... | collective-permute-start | bytes 3145736 | tf_op jit(solution)/shard_map/ppermute | solution.py:26
  87.4 1.0 copy-start.7
  88.4 1.9 copy-start.8
  91.5 55.0 %copy-start.2 = (f32[4,1,2,256,256]{4,3,2,0,1:T(8,128)}, f32[4,1,2,256,256]{4,3,2,0,1:T(8,128)S(1)}, u32[]{:S(2)}) copy-start(f32[4,1,2,256,256]{4,3,2,0,1:T(8,128)S(1)} %get-tuple-element.276) | copy-start | bytes 6291460
  91.5 55.0 %collective-permute-start.3 = (bf16[4,2,256,256]{3,2,1,0:T(8,128)(2,1)}, bf16[4,2,256,256]{3,2,1,0:T(8,128)(2,1)S(1)}, u32[]{:S(2)}, u32[]{:S(2)}) collective-permute-start(bf16[4,2,256,256]{3,2,1,0:T(8,128)(2,1)} %get-tuple-element.275), channel_id=1, source_target_pairs={{128,0},{129,1},{130,2},{131,3},{132,4},{133,5},{134,6},{135,7},{1... | collective-permute-start | bytes 3145736 | tf_op jit(solution)/shard_map/ppermute | solution.py:26
  146.5 1.0 copy-start.11
  206.4 41.0 %collective-permute-start.5 = (bf16[1,1,2,128,1024]{4,3,2,1,0:T(8,128)(2,1)S(1)}, bf16[1,1,2,128,1024]{4,3,2,1,0:T(8,128)(2,1)S(1)}, u32[]{:S(2)}, u32[]{:S(2)}) collective-permute-start(bf16[1,1,2,128,1024]{4,3,2,1,0:T(8,128)(2,1)S(1)} %bitcast.335), channel_id=1, source_target_pairs={{1,0},{2,1},{3,2},{4,3},{5,4},{6,5},{7,6},{8,7},{9,8},{10,9},{11,1... | collective-permute-start | bytes 1572872 | tf_op jit(solution)/shard_map/ppermute | solution.py:18
  211.5 35.8 %collective-permute-start.4 = (bf16[1,1,2,128,1024]{4,3,2,1,0:T(8,128)(2,1)S(1)}, bf16[1,1,2,128,1024]{4,3,2,1,0:T(8,128)(2,1)S(1)}, u32[]{:S(2)}, u32[]{:S(2)}) collective-permute-start(bf16[1,1,2,128,1024]{4,3,2,1,0:T(8,128)(2,1)S(1)} %bitcast.334), channel_id=1, source_target_pairs={{0,1},{1,2},{2,3},{3,4},{4,5},{5,6},{6,7},{7,8},{8,9},{9,10},{10,1... | collective-permute-start | bytes 1572872 | tf_op jit(solution)/shard_map/ppermute | solution.py:15
  248.7 1.3 copy-start.4
where the time goes:
time: 254 us; the launch traced here: 252 us
  waiting for transfers between devices  87.1 us (34%)
  local copies, waits for them, and re-layouts  61.4 us (24%)
  starting transfers between devices  41 us (16%)
  other arithmetic  40.5 us (16%)
  loops' own time  13.3 us (5%)
  matrix products  8.93 us (4%)
    ppermute x2, waiting for transfers between devices, from_behind(): return lax.ppermute(block, axis, route)  71.6 us
    ppermute x2, starting transfers between devices, padded(): lax.ppermute(lax.slice_in_dim(block, block.shape[dim] - width, None, axis...  32.1 us
    dynamic_update_slice x4, local copies, waits for them, and re-layouts, deposit(): lax.dynamic_update_slice(running, existing + pieces[position], corner)  25.5 us
    ppermute x2, waiting for transfers between devices, padded(): lax.ppermute(lax.slice_in_dim(block, 0, width, axis=dim), axis, backward)  15.4 us
    gather x12, local copies, waits for them, and re-layouts  13.5 us
    another operation x1, loops' own time, add_patches(): return lax.fori_loop(0, pieces.shape[0], deposit, gradient)  13 us
    dot_general x2, matrix products, transform(): jnp.einsum('nckl,cdlm->ndkm', middle, right_block, preferred_element_type...  8.93 us
    add x4, other arithmetic, deposit(): existing + pieces[position]  5.49 us
  transfers between devices with their start and end apart: 6, of which 4 were waited for; matrix products, arithmetic and copies ran while one was open for 7% of the time, Pallas kernels for 0%

commit v1 on v0

v1 whole, which is shorter than its diff:
```python
import functools

import jax
import jax.numpy as jnp
import ml_dtypes
import numpy as np
from jax import lax
from jax.experimental import pallas as pl
from jax.experimental.pallas import tpu as pltpu
from jax.sharding import PartitionSpec as P

modulus_floor = 0.25
AXES = ("cuts", "region")
BF = jnp.bfloat16
F32 = jnp.float32
SIDE = 256
HALF = 128
BAND = 256
COLS = 1024
EXT = BAND + 2 * HALF
WIDE = SIDE + 128
VM = pl.BlockSpec(memory_space=pltpu.VMEM)
SM = pl.BlockSpec(memory_space=pltpu.SMEM)


def routes(regions):
    at = lambda c, r: c * regions + r % regions
    both = [(c, r) for c in range(2) for r in range(regions)]
    return {
        "mate": [(at(c, r), at(1 - c, r)) for c, r in both],
        "next": [(at(c, r), at(c, r + 1)) for c, r in both],
        "prev": [(at(c, r), at(c, r - 1)) for c, r in both],
        "solo": [(at(c, r), at(c, r - 1 if c == 0 else r + 1)) for c, r in both],
        "relay": [(at(c, r), at(c, r + 1 if c == 0 else r - 1)) for c, r in both],
    }


def dft_blocks():
    index = np.arange(SIDE)
    angles = (index[:, None] * index[None, :] % SIDE) * (2.0 * np.pi / SIDE)
    real = np.cos(angles) / np.sqrt(SIDE)
    imag = -np.sin(angles) / np.sqrt(SIDE)
    first = np.block([[real, -imag], [imag, real]]).astype(ml_dtypes.bfloat16)
    second = np.block([[real, imag], [-imag, real]]).astype(ml_dtypes.bfloat16)
    return first, second


def places(rows):
    up = [rows[i] < 0 for i in range(4)]
    first = lambda a, b: jnp.where(a, 0, jnp.where(b, 1, 2))
    last = lambda a, b: jnp.where(a, 3, jnp.where(b, 2, 1))
    no = [jnp.logical_not(u) for u in up]
    return first(up[0], up[1]), last(up[3], up[2]), first(no[0], no[1]), last(no[3], no[2])


def column_split(left):
    base = jnp.minimum(lax.shift_right_logical(left, 7), (COLS - WIDE) // 128) * 128
    return pl.multiple_of(base, 128), left - base


def row_split(top, most):
    base = jnp.minimum(lax.shift_right_logical(top, 3), most // 8) * 8
    return pl.multiple_of(base, 8), top - base


def cut_window(load, top, left, count, total):
    row_base, row_shift = row_split(top, total - count - 8)
    col_base, col_shift = column_split(left)
    block = load(pl.ds(row_base, count + 8), pl.ds(col_base, WIDE))
    block = pltpu.roll(block, lax.rem(count + 8 - row_shift, count + 8), 0)[:count]
    return pltpu.roll(block, lax.rem(WIDE - col_shift, WIDE), 1)[:, :SIDE]


def put_window(total_ref, channel, top, left, block):
    count = block.shape[0]
    row_base, row_shift = row_split(top, EXT - count - 8)
    col_base, col_shift = column_split(left)
    block = jnp.concatenate([block, jnp.zeros((count, WIDE - SIDE), F32)], axis=1)
    block = pltpu.roll(block, col_shift, 1)
    block = jnp.concatenate([block, jnp.zeros((8, WIDE), F32)], axis=0)
    block = pltpu.roll(block, row_shift, 0)
    where = (channel, pl.ds(row_base, count + 8), pl.ds(col_base, WIDE))
    total_ref[where] = total_ref[where] + block


def inband_kernel(rows, cols, objects, inband, low, high):
    cut = lax.axis_index("cuts")
    u0, u1, l0, l1 = places(rows)
    other_up = cut == 1
    for slot, (place, up) in enumerate(
        [(jnp.where(other_up, u1, l1), other_up), (u0, None), (l0, None)]
    ):
        offset = jnp.where(up, HALF, 0) if slot == 0 else (HALF if slot == 1 else 0)
        for channel in range(2):
            inband[slot, channel] = cut_window(
                lambda r, c: objects[0, channel, r, c], rows[place] + offset, cols[place], HALF, BAND
            ).astype(BF)
    for channel in range(2):
        low[channel] = objects[0, channel, :HALF].astype(BF)
        high[channel] = objects[0, channel, HALF:].astype(BF)


def outer_kernel(rows, cols, objects, above, below, half0, half1, half2, windows, ext):
    cut = lax.axis_index("cuts")
    u0, u1, l0, l1 = places(rows)
    other_up = cut == 1
    for channel in range(2):
        ext[channel, :HALF] = above[channel].astype(F32)
        ext[channel, HALF : HALF + BAND] = objects[0, channel]
        ext[channel, HALF + BAND :] = below[channel].astype(F32)
    other = jnp.where(other_up, u1, l1)
    solo = jnp.where(other_up, l1, u1)
    for channel in range(2):
        load = lambda r, c: ext[channel, r, c]
        top = rows[other] + jnp.where(other_up, HALF, 2 * HALF)
        half0[channel] = cut_window(load, top, cols[other], HALF, EXT).astype(BF)
        for slot, place in enumerate((solo, u0, l0)):
            window = cut_window(load, rows[place] + HALF, cols[place], SIDE, EXT).astype(BF)
            windows[slot, channel] = window
            if slot == 1:
                half1[channel] = window[:HALF]
            if slot == 2:
                half2[channel] = window[HALF:]


def transform(fields, left, right):
    count = len(fields)
    stacked = jnp.concatenate(
        [jnp.concatenate([f[part].astype(BF) for f in fields], axis=1) for part in range(2)], axis=0
    )
    middle = jnp.dot(left, stacked, preferred_element_type=F32).astype(BF)
    spans = [slice(SIDE * k, SIDE * (k + 1)) for k in range(count)]
    middle = jnp.concatenate(
        [jnp.concatenate([middle[:SIDE, s], middle[SIDE:, s]], axis=1) for s in spans], axis=0
    )
    result = jnp.dot(middle, right, preferred_element_type=F32)
    return [(result[s, :SIDE], result[s, SIDE:]) for s in spans]


def times(a, b):
    return a[0] * b[0] - a[1] * b[1], a[0] * b[1] + a[1] * b[0]


def conj_times(a, b):
    return a[0] * b[0] + a[1] * b[1], a[0] * b[1] - a[1] * b[0]


def wide(pair):
    return pair[0].astype(F32), pair[1].astype(F32)


def chain(incoming, patches, measured, wave, first, second, store):
    spots = range(len(incoming))
    propagator = (wave[0], wave[1])
    fields = [times(wide(incoming[k]()), patches[k](0)) for k in spots]
    fields = [times(propagator, f) for f in transform(fields, first, second)]
    psi = [(f[0].astype(BF), f[1].astype(BF)) for f in transform(fields, second, first)]
    fields = [times(wide(psi[k]), patches[k](1)) for k in spots]
    detected = []
    for k, (real, imag) in enumerate(transform(fields, first, second)):
        modulus = jnp.sqrt(real * real + imag * imag)
        factor = 1.0 - measured[k]() / jnp.maximum(modulus, modulus_floor)
        detected.append((real * factor, imag * factor))
    arriving = [(f[0].astype(BF), f[1].astype(BF)) for f in transform(detected, second, first)]
    arriving = [wide(f) for f in arriving]
    for k in spots:
        store(k, 1, conj_times(wide(psi[k]), arriving[k]))
    fields = [conj_times(patches[k](1), arriving[k]) for k in spots]
    fields = [conj_times(propagator, f) for f in transform(fields, first, second)]
    for k, (real, imag) in enumerate(transform(fields, second, first)):
        arrived = real.astype(BF).astype(F32), imag.astype(BF).astype(F32)
        store(k, 0, conj_times(wide(incoming[k]()), arrived))


def fill_patches(held, own, inband, outer, cut, start):
    for channel in range(2):
        held[cut, channel] = own[channel]
        held[1 - cut, channel, pl.ds(start, HALF)] = outer[channel]
        held[1 - cut, channel, pl.ds(HALF - start, HALF)] = inband[channel]


def patch_of(held):
    return lambda which: wide((held[which, 0], held[which, 1]))


def probe_of(probes, choice):
    return lambda: (probes[choice, 0], probes[choice, 1])


def solo_kernel(
    rows, picks, windows, inband, outer, probes, amplitudes, wave, first, second,
    sent_outer, sent_inband, kept, edge, held, made,
):
    cut = lax.axis_index("cuts")
    u0, u1, l0, l1 = places(rows)
    place = jnp.where(cut == 0, u1, l1)
    start = pl.multiple_of(jnp.where(cut == 0, 0, HALF), HALF)
    fill_patches(held, windows.at[0], inband.at[0], outer, cut, start)

    def store(k, which, value):
        made[which, 0], made[which, 1] = value

    chain(
        [probe_of(probes, picks[place])], [patch_of(held)], [lambda: amplitudes[place]],
        wave, first[...], second[...], store,
    )
    for channel in range(2):
        sent_outer[channel] = made[1 - cut, channel, pl.ds(start, HALF)].astype(BF)
        sent_inband[channel] = made[1 - cut, channel, pl.ds(HALF - start, HALF)].astype(BF)
        kept[channel] = made[cut, channel]
        edge[channel] = made[cut, channel, pl.ds(start, HALF)].astype(BF)


def shared_kernel(
    rows, picks, windows, inband, outer1, outer2, probes, amplitudes, wave, first, second,
    kept, edge_up, edge_low, held, made,
):
    cut = lax.axis_index("cuts")
    u0, u1, l0, l1 = places(rows)
    fill_patches(held.at[0], windows.at[1], inband.at[1], outer1, cut, 0)
    fill_patches(held.at[1], windows.at[2], inband.at[2], outer2, cut, HALF)

    def store(k, which, value):
        made[k, which, 0], made[k, which, 1] = value

    chain(
        [probe_of(probes, picks[u0]), probe_of(probes, picks[l0])],
        [patch_of(held.at[0]), patch_of(held.at[1])],
        [lambda: amplitudes[u0], lambda: amplitudes[l0]],
        wave, first[...], second[...], store,
    )
    for channel in range(2):
        for k in range(2):
            kept[k, channel] = made[k, cut, channel]
        edge_up[channel] = made[0, cut, channel, :HALF].astype(BF)
        edge_low[channel] = made[1, cut, channel, HALF:].astype(BF)


def gather_kernel(
    rows, cols, after, before, solo, shared, from_outer, from_inband,
    edge_solo, edge_relay, edge_up, edge_low, output, total,
):
    cut = lax.axis_index("cuts")
    u0, u1, l0, l1 = places(rows)
    after_rows = [after[i] for i in range(4)]
    before_rows = [before[i] for i in range(4)]
    next_u0, next_u1, _, _ = places(after_rows)
    _, _, last_l0, last_l1 = places(before_rows)
    total[...] = jnp.zeros_like(total)
    own = jnp.where(cut == 0, u1, l1)
    other = jnp.where(cut == 0, l1, u1)
    start = jnp.where(cut == 0, HALF, 0)
    next_top = lambda place: after[place] + HALF + BAND
    last_top = lambda place: before[place]
    solo_top = jnp.where(cut == 0, next_top(next_u1), last_top(last_l1))
    solo_left = jnp.where(cut == 0, after[4 + next_u1], before[4 + last_l1])
    relay_top = jnp.where(cut == 0, last_top(last_l1), next_top(next_u1))
    relay_left = jnp.where(cut == 0, before[4 + last_l1], after[4 + next_u1])
    for channel in range(2):
        put = functools.partial(put_window, total, channel)
        put(rows[own] + HALF, cols[own], solo[channel])
        put(rows[u0] + HALF, cols[u0], shared[0, channel])
        put(rows[l0] + HALF, cols[l0], shared[1, channel])
        put(rows[other] + HALF + start, cols[other], from_outer[channel].astype(F32))
        put(rows[other] + 2 * HALF - start, cols[other], from_inband[channel].astype(F32))
        put(solo_top, solo_left, edge_solo[channel].astype(F32))
        put(relay_top, relay_left, edge_relay[channel].astype(F32))
        put(next_top(next_u0), after[4 + next_u0], edge_up[channel].astype(F32))
        put(last_top(last_l0), before[4 + last_l0], edge_low[channel].astype(F32))
        output[0, channel] = total[channel, HALF : HALF + BAND]


def call(kernel, name, inputs, outputs, scratch=(), flops=0):
    scalars = [x for x in inputs if x.dtype == jnp.int32]
    moved = sum(x.size * x.dtype.itemsize for x in list(inputs) + list(outputs))
    return pl.pallas_call(
        kernel,
        name=name,
        out_shape=outputs,
        in_specs=[SM] * len(scalars) + [VM] * (len(inputs) - len(scalars)),
        out_specs=[VM] * len(outputs),
        scratch_shapes=list(scratch),
        cost_estimate=pl.CostEstimate(flops=flops, bytes_accessed=moved, transcendentals=0),
        compiler_params=pltpu.CompilerParams(vmem_limit_bytes=40 << 20),
    )(*inputs)


def arr(*shape, dtype=BF):
    return jax.ShapeDtypeStruct(shape, dtype)


def shards(objects, probes, amplitudes, prop_phase, scan_rows, scan_cols, probe_choice):
    route = routes(lax.axis_size("region"))
    move = lambda x, way: lax.ppermute(x, AXES, route[way])
    first, second = (jnp.asarray(t) for t in dft_blocks())
    wave = jnp.stack([jnp.cos(prop_phase), jnp.sin(prop_phase)])
    half = arr(2, HALF, SIDE)
    product = 2 * 2 * 512 * 512 * 256

    inband, low, high = call(
        inband_kernel, "inband", [scan_rows, scan_cols, objects],
        [arr(3, 2, HALF, SIDE), arr(2, HALF, COLS), arr(2, HALF, COLS)],
    )
    mate_inband = move(inband, "mate")
    above = move(high, "next")
    below = move(low, "prev")
    scan = jnp.concatenate([scan_rows, scan_cols])
    before = move(scan, "next")
    after = move(scan, "prev")
    half0, half1, half2, windows = call(
        outer_kernel, "outer", [scan_rows, scan_cols, objects, above, below],
        [half, half, half, arr(3, 2, SIDE, SIDE)],
        [pltpu.VMEM((2, EXT, COLS), F32)],
    )
    mate0 = move(half0, "mate")
    mate1 = move(half1, "mate")
    mate2 = move(half2, "mate")
    sent_outer, sent_inband, solo, edge = call(
        solo_kernel, "solo",
        [scan_rows, probe_choice, windows, mate_inband, mate0, probes, amplitudes, wave, first, second],
        [half, half, arr(2, SIDE, SIDE, dtype=F32), half],
        [pltpu.VMEM((2, 2, SIDE, SIDE), BF), pltpu.VMEM((2, 2, SIDE, SIDE), F32)],
        flops=6 * product,
    )
    from_outer = move(sent_outer, "mate")
    from_inband = move(sent_inband, "mate")
    edge_solo = move(edge, "solo")
    shared, up, down = call(
        shared_kernel, "shared",
        [scan_rows, probe_choice, windows, mate_inband, mate1, mate2, probes, amplitudes, wave, first, second],
        [arr(2, 2, SIDE, SIDE, dtype=F32), half, half],
        [pltpu.VMEM((2, 2, 2, SIDE, SIDE), BF), pltpu.VMEM((2, 2, 2, SIDE, SIDE), F32)],
        flops=12 * product,
    )
    edge_up = move(up, "prev")
    edge_low = move(down, "next")
    edge_relay = move(from_outer, "relay")
    (gradient,) = call(
        gather_kernel, "gather",
        [scan_rows, scan_cols, after, before, solo, shared, from_outer, from_inband,
         edge_solo, edge_relay, edge_up, edge_low],
        [arr(1, 2, BAND, COLS, dtype=F32)],
        [pltpu.VMEM((2, EXT, COLS), F32)],
    )
    return gradient


def solution(mesh):
    return jax.shard_map(
        shards,
        mesh=mesh,
        in_specs=(
            P("cuts", None, "region", None),
            P(),
            P("region", None, None),
            P(),
            P("region"),
            P("region"),
            P("region"),
        ),
        out_specs=P("cuts", None, "region", None),
        check_vma=False,
    )
```

time: 254 us -> 91.1 us (0.36)
  the two profiles are of different devices: /device:TPU:1 before, /device:TPU:8 now
where the time goes in v1:
time: 91.1 us; the launch traced here: 90.8 us
  starting transfers between devices  52.3 us (57%)
  Pallas kernels  18.9 us (21%)
  waiting for transfers between devices  15.5 us (17%)
  local copies, waits for them, and re-layouts  3.88 us (4%)
    ppermute x14, starting transfers between devices, shards(): move = lambda x, way: lax.ppermute(x, AXES, route[way])  52.3 us
    pallas_call x5, Pallas kernels, call(): pl.pallas_call(kernel, name=name, out_shape=outputs, in_specs=[SM] * len(...  18.9 us
    ppermute x14, waiting for transfers between devices, shards(): move = lambda x, way: lax.ppermute(x, AXES, route[way])  15.5 us
    unnamed x20, local copies, waits for them, and re-layouts  2.93 us
  transfers between devices with their start and end apart: 14, of which 5 were waited for; matrix products, arithmetic and copies ran while one was open for 1% of the time, Pallas kernels for 14%

profile of v1, /device:TPU:8, one launch (start us, length us, event | category | flops | bytes accessed | tf_op | source)
XLA Modules:
  0.0 90.8 jit_solution(9125337759259036098)
XLA Ops:
  0.0 1.6 %copy-done = f32[1,2,256,1024]{3,2,1,0:T(8,128)S(1)} copy-done((f32[1,2,256,1024]{3,2,1,0:T(8,128)S(1)}, f32[1,2,256,1024]{3,2,1,0:T(8,128)}, u32[]{:S(2)}) %copy-start) | copy-done | bytes 2097176
  1.6 0.7 copy-done.1
  2.2 0.7 copy-done.2
  2.9 1.2 %inband.1 = (bf16[3,2,128,256]{3,2,1,0:T(8,128)(2,1)S(1)}, bf16[2,128,1024]{2,1,0:T(8,128)(2,1)S(1)}, bf16[2,128,1024]{2,1,0:T(8,128)(2,1)S(1)}) custom-call(s32[4]{0:T(128)S(1)} %copy-done.1, s32[4]{0:T(128)S(1)} %copy-done.2, f32[1,2,256,1024]{3,2,1,0:T(8,128)S(1)} %copy-done), custom_call_target="tpu_custom_call" | custom-call | bytes 3538976 | tf_op jit(solution)/shard_map/inband/pallas_call | solution.py:276
  4.2 6.5 %collective-permute-start.3 = (bf16[2,128,1024]{2,1,0:T(8,128)(2,1)S(1)}, bf16[2,128,1024]{2,1,0:T(8,128)(2,1)S(1)}, u32[]{:S(2)}, u32[]{:S(2)}) collective-permute-start(bf16[2,128,1024]{2,1,0:T(8,128)(2,1)S(1)} %get-tuple-element.20), channel_id=1, source_target_pairs={{0,127},{1,0},{2,1},{3,2},{4,3},{5,4},{6,5},{7,6},{8,7},{9,8},{10,... | collective-permute-start | bytes 1572872 | tf_op jit(solution)/shard_map/ppermute | solution.py:294
  10.7 7.2 %collective-permute-start.4 = (bf16[3,2,128,256]{3,2,1,0:T(8,128)(2,1)S(1)}, bf16[3,2,128,256]{3,2,1,0:T(8,128)(2,1)S(1)}, u32[]{:S(2)}, u32[]{:S(2)}) collective-permute-start(bf16[3,2,128,256]{3,2,1,0:T(8,128)(2,1)S(1)} %get-tuple-element.22), channel_id=1, source_target_pairs={{0,128},{1,129},{2,130},{3,131},{4,132},{5,133},{6,134},{7,135},{8... | collective-permute-start | bytes 1179656 | tf_op jit(solution)/shard_map/ppermute | solution.py:294
  18.1 6.5 %collective-permute-start = (s32[8]{0:T(128)S(1)}, s32[8]{0:T(128)S(1)}, u32[]{:S(2)}, u32[]{:S(2)}) collective-permute-start(s32[8]{0:T(128)S(1)} %pad_add_fusion), channel_id=1, source_target_pairs={{0,127},{1,0},{2,1},{3,2},{4,3},{5,4},{6,5},{7,6},{8,7},{9,8},{10,... | collective-permute-start | bytes 104 | tf_op jit(solution)/shard_map/ppermute | solution.py:294
  24.6 0.6 collective-permute-done.3.below
  25.3 2.1 %outer.1 = (bf16[2,128,256]{2,1,0:T(8,128)(2,1)S(1)}, bf16[2,128,256]{2,1,0:T(8,128)(2,1)S(1)}, bf16[2,128,256]{2,1,0:T(8,128)(2,1)S(1)}, bf16[3,2,256,256]{3,2,1,0:T(8,128)(2,1)S(1)}) custom-call(s32[4]{0:T(128)S(1)} %copy-done.1, s32[4]{0:T(128)S(1)} %copy-done.2, f32[1,2,256,1024]{3,2,1,0:T(8,128)S(1)} %copy-done, ...), custom_call_target="tpu_custom_call" | custom-call | bytes 4325408 | tf_op jit(solution)/shard_map/outer/pallas_call | solution.py:276
  27.4 9.9 %collective-permute-start.5 = (bf16[2,128,256]{2,1,0:T(8,128)(2,1)S(1)}, bf16[2,128,256]{2,1,0:T(8,128)(2,1)S(1)}, u32[]{:S(2)}, u32[]{:S(2)}) collective-permute-start(bf16[2,128,256]{2,1,0:T(8,128)(2,1)S(1)} %get-tuple-element.23), channel_id=1, source_target_pairs={{0,128},{1,129},{2,130},{3,131},{4,132},{5,133},{6,134},{7,135},{8... | collective-permute-start | bytes 393224 | tf_op jit(solution)/shard_map/ppermute | solution.py:294
  37.3 0.9 %cosine_bitcast_fusion = (f32[1,256,256]{2,1,0:T(8,128)S(1)}, f32[1,256,256]{2,1,0:T(8,128)S(1)}) fusion(f32[256,256]{1,0:T(8,128)S(1)} %copy-done.9), kind=kLoop, calls=%fused_computation.2 | loop fusion | bytes 786432 | tf_op jit(solution)/shard_map/stack | solution.py:296
  38.3 0.1 collective-permute-start.6
  38.4 5.9 %collective-permute-start.7 = (bf16[2,128,256]{2,1,0:T(8,128)(2,1)S(1)}, bf16[2,128,256]{2,1,0:T(8,128)(2,1)S(1)}, u32[]{:S(2)}, u32[]{:S(2)}) collective-permute-start(bf16[2,128,256]{2,1,0:T(8,128)(2,1)S(1)} %get-tuple-element.26), channel_id=1, source_target_pairs={{0,128},{1,129},{2,130},{3,131},{4,132},{5,133},{6,134},{7,135},{8... | collective-permute-start | bytes 393224 | tf_op jit(solution)/shard_map/ppermute | solution.py:294
  44.3 4.7 %collective-permute-done.5.outer = bf16[2,128,256]{2,1,0:T(8,128)(2,1)S(1)} collective-permute-done((bf16[2,128,256]{2,1,0:T(8,128)(2,1)S(1)}, bf16[2,128,256]{2,1,0:T(8,128)(2,1)S(1)}, u32[]{:S(2)}, u32[]{:S(2)}) %collective-permute-start.5) | collective-permute-done | bytes 131104 | tf_op jit(solution)/shard_map/ppermute | solution.py:294
  49.1 4.8 %solo.1 = (bf16[2,128,256]{2,1,0:T(8,128)(2,1)S(1)}, bf16[2,128,256]{2,1,0:T(8,128)(2,1)S(1)}, f32[2,256,256]{2,1,0:T(8,128)S(1)}, bf16[2,128,256]{2,1,0:T(8,128)(2,1)S(1)}) custom-call(s32[4]{0:T(128)S(1)} %copy-done.1, s32[4]{0:T(128)S(1)} %copy-done.6, bf16[3,2,256,256]{3,2,1,0:T(8,128)(2,1)S(1)} %get-tuple-element.21.windows, ...), custom_call_target="tpu_custom_call" | custom-call | flops 1610612736 | bytes 5898272 | tf_op jit(solution)/shard_map/solo/pallas_call | solution.py:276
  53.9 5.7 %collective-permute-start.8 = (bf16[2,128,256]{2,1,0:T(8,128)(2,1)S(1)}, bf16[2,128,256]{2,1,0:T(8,128)(2,1)S(1)}, u32[]{:S(2)}, u32[]{:S(2)}) collective-permute-start(bf16[2,128,256]{2,1,0:T(8,128)(2,1)S(1)} %get-tuple-element.28), channel_id=1, source_target_pairs={{0,128},{1,129},{2,130},{3,131},{4,132},{5,133},{6,134},{7,135},{8... | collective-permute-start | bytes 393224 | tf_op jit(solution)/shard_map/ppermute | solution.py:294
  59.6 2.2 %collective-permute-start.9 = (bf16[2,128,256]{2,1,0:T(8,128)(2,1)S(1)}, bf16[2,128,256]{2,1,0:T(8,128)(2,1)S(1)}, u32[]{:S(2)}, u32[]{:S(2)}) collective-permute-start(bf16[2,128,256]{2,1,0:T(8,128)(2,1)S(1)} %get-tuple-element.29), channel_id=1, source_target_pairs={{0,128},{1,129},{2,130},{3,131},{4,132},{5,133},{6,134},{7,135},{8... | collective-permute-start | bytes 393224 | tf_op jit(solution)/shard_map/ppermute | solution.py:294
  61.8 7.4 %collective-permute-start.10 = (bf16[2,128,256]{2,1,0:T(8,128)(2,1)S(1)}, bf16[2,128,256]{2,1,0:T(8,128)(2,1)S(1)}, u32[]{:S(2)}, u32[]{:S(2)}) collective-permute-start(bf16[2,128,256]{2,1,0:T(8,128)(2,1)S(1)} %get-tuple-element.30), channel_id=1, source_target_pairs={{0,127},{1,0},{2,1},{3,2},{4,3},{5,4},{6,5},{7,6},{8,7},{9,8},{10,... | collective-permute-start | bytes 393224 | tf_op jit(solution)/shard_map/ppermute | solution.py:294
  69.2 5.5 %shared.1 = (f32[2,2,256,256]{3,2,1,0:T(8,128)S(1)}, bf16[2,128,256]{2,1,0:T(8,128)(2,1)S(1)}, bf16[2,128,256]{2,1,0:T(8,128)(2,1)S(1)}) custom-call(s32[4]{0:T(128)S(1)} %copy-done.1, s32[4]{0:T(128)S(1)} %copy-done.6, bf16[3,2,256,256]{3,2,1,0:T(8,128)(2,1)S(1)} %get-tuple-element.21.windows, bf16[3,2,128,256]{3,2,1,0:T(8,128)(2,1)S(1)} %collective-permute-done.4.inband, ...), custom_call_target="tpu_custom_call" | custom-call | flops 3221225472 | bytes 6422560 | tf_op jit(solution)/shard_map/shared/pallas_call | solution.py:276
  74.8 0.5 collective-permute-start.13
  75.4 3.3 %collective-permute-done.12.edge_up = bf16[2,128,256]{2,1,0:T(8,128)(2,1)S(1)} collective-permute-done((bf16[2,128,256]{2,1,0:T(8,128)(2,1)S(1)}, bf16[2,128,256]{2,1,0:T(8,128)(2,1)S(1)}, u32[]{:S(2)}, u32[]{:S(2)}) %collective-permute-start.12) | collective-permute-done | bytes 131104 | tf_op jit(solution)/shard_map/ppermute | solution.py:294
  78.7 5.4 %collective-permute-done.13.edge_low = bf16[2,128,256]{2,1,0:T(8,128)(2,1)S(1)} collective-permute-done((bf16[2,128,256]{2,1,0:T(8,128)(2,1)S(1)}, bf16[2,128,256]{2,1,0:T(8,128)(2,1)S(1)}, u32[]{:S(2)}, u32[]{:S(2)}) %collective-permute-start.13) | collective-permute-done | bytes 131104 | tf_op jit(solution)/shard_map/ppermute | solution.py:294
  84.1 1.4 %collective-permute-done.11.edge_relay = bf16[2,128,256]{2,1,0:T(8,128)(2,1)S(1)} collective-permute-done((bf16[2,128,256]{2,1,0:T(8,128)(2,1)S(1)}, bf16[2,128,256]{2,1,0:T(8,128)(2,1)S(1)}, u32[]{:S(2)}, u32[]{:S(2)}) %collective-permute-start.11) | collective-permute-done | bytes 131104 | tf_op jit(solution)/shard_map/ppermute | solution.py:294
  85.5 5.3 %gather.1 = f32[1,2,256,1024]{3,2,1,0:T(8,128)} custom-call(s32[4]{0:T(128)S(1)} %copy-done.1, s32[4]{0:T(128)S(1)} %copy-done.3, s32[8]{0:T(128)S(1)} %collective-permute-done.after, s32[8]{0:T(128)S(1)} %collective-permute-done.1.before, f32[2,256,256]{2,1,0:T(8,128)S(1)} %get-tuple-element.24.solo, f32[2,2,256,256]{3,2,1,0:T(8,128)S(1)} %get-tuple-element.27.shared, ...), custom_call_target="tpu_custom_call" | custom-call | bytes 4456544 | tf_op jit(solution)/shard_map/gather/pallas_call | solution.py:276
  (32 shorter events, 0.5 us)
Async XLA Ops:
  0.0 1.6 %copy-start = (f32[1,2,256,1024]{3,2,1,0:T(8,128)S(1)}, f32[1,2,256,1024]{3,2,1,0:T(8,128)}, u32[]{:S(2)}) copy-start(f32[1,2,256,1024]{3,2,1,0:T(8,128)} %objects.3) | copy-start | bytes 6291460
  1.6 0.7 copy-start.1
  2.2 0.7 copy-start.2
  4.1 33.2 %copy-start.9 = (f32[256,256]{1,0:T(8,128)S(1)}, f32[256,256]{1,0:T(8,128)}, u32[]{:S(2)}) copy-start(f32[256,256]{1,0:T(8,128)} %param.12) | copy-start | bytes 786436
  4.1 20.6 %collective-permute-start.2 = (bf16[2,128,1024]{2,1,0:T(8,128)(2,1)S(1)}, bf16[2,128,1024]{2,1,0:T(8,128)(2,1)S(1)}, u32[]{:S(2)}, u32[]{:S(2)}) collective-permute-start(bf16[2,128,1024]{2,1,0:T(8,128)(2,1)S(1)} %get-tuple-element.19), channel_id=1, source_target_pairs={{0,1},{1,2},{2,3},{3,4},{4,5},{5,6},{6,7},{7,8},{8,9},{9,10},{10,1... | collective-permute-start | bytes 1572872 | tf_op jit(solution)/shard_map/ppermute | solution.py:294
  4.2 21.1 %collective-permute-start.3 = (bf16[2,128,1024]{2,1,0:T(8,128)(2,1)S(1)}, bf16[2,128,1024]{2,1,0:T(8,128)(2,1)S(1)}, u32[]{:S(2)}, u32[]{:S(2)}) collective-permute-start(bf16[2,128,1024]{2,1,0:T(8,128)(2,1)S(1)} %get-tuple-element.20), channel_id=1, source_target_pairs={{0,127},{1,0},{2,1},{3,2},{4,3},{5,4},{6,5},{7,6},{8,7},{9,8},{10,... | collective-permute-start | bytes 1572872 | tf_op jit(solution)/shard_map/ppermute | solution.py:294
  10.7 27.7 %collective-permute-start.4 = (bf16[3,2,128,256]{3,2,1,0:T(8,128)(2,1)S(1)}, bf16[3,2,128,256]{3,2,1,0:T(8,128)(2,1)S(1)}, u32[]{:S(2)}, u32[]{:S(2)}) collective-permute-start(bf16[3,2,128,256]{3,2,1,0:T(8,128)(2,1)S(1)} %get-tuple-element.22), channel_id=1, source_target_pairs={{0,128},{1,129},{2,130},{3,131},{4,132},{5,133},{6,134},{7,135},{8... | collective-permute-start | bytes 1179656 | tf_op jit(solution)/shard_map/ppermute | solution.py:294
  18.0 31.1 %copy-start.4 = (bf16[4,2,256,256]{3,2,1,0:T(8,128)(2,1)S(1)}, bf16[4,2,256,256]{3,2,1,0:T(8,128)(2,1)}, u32[]{:S(2)}) copy-start(bf16[4,2,256,256]{3,2,1,0:T(8,128)(2,1)} %probes.3) | copy-start | bytes 3145732
  18.0 31.1 %copy-start.5 = (f32[4,256,256]{2,1,0:T(8,128)S(1)}, f32[4,256,256]{2,1,0:T(8,128)}, u32[]{:S(2)}) copy-start(f32[4,256,256]{2,1,0:T(8,128)} %amplitudes.3) | copy-start | bytes 3145732
  18.0 31.1 %copy-start.6 = (s32[4]{0:T(128)S(1)}, s32[4]{0:T(128)}, u32[]{:S(2)}) copy-start(s32[4]{0:T(128)} %picks.3) | copy-start | bytes 52
  18.0 31.1 %copy-start.7 = (bf16[512,512]{1,0:T(8,128)(2,1)S(1)}, bf16[512,512]{1,0:T(8,128)(2,1)}, u32[]{:S(2)}) copy-start(bf16[512,512]{1,0:T(8,128)(2,1)} %constant.5.clone.second) | copy-start | bytes 1572868
  18.0 31.1 %copy-start.8 = (bf16[512,512]{1,0:T(8,128)(2,1)S(1)}, bf16[512,512]{1,0:T(8,128)(2,1)}, u32[]{:S(2)}) copy-start(bf16[512,512]{1,0:T(8,128)(2,1)} %constant.4.clone.first) | copy-start | bytes 1572868
  18.0 56.7 %collective-permute-start.1 = (s32[8]{0:T(128)S(1)}, s32[8]{0:T(128)S(1)}, u32[]{:S(2)}, u32[]{:S(2)}) collective-permute-start(s32[8]{0:T(128)S(1)} %pad_add_fusion), channel_id=1, source_target_pairs={{0,1},{1,2},{2,3},{3,4},{4,5},{5,6},{6,7},{7,8},{8,9},{9,10},{10,1... | collective-permute-start | bytes 104 | tf_op jit(solution)/shard_map/ppermute | solution.py:294
  18.1 56.7 %collective-permute-start = (s32[8]{0:T(128)S(1)}, s32[8]{0:T(128)S(1)}, u32[]{:S(2)}, u32[]{:S(2)}) collective-permute-start(s32[8]{0:T(128)S(1)} %pad_add_fusion), channel_id=1, source_target_pairs={{0,127},{1,0},{2,1},{3,2},{4,3},{5,4},{6,5},{7,6},{8,7},{9,8},{10,... | collective-permute-start | bytes 104 | tf_op jit(solution)/shard_map/ppermute | solution.py:294
  27.4 21.6 %collective-permute-start.5 = (bf16[2,128,256]{2,1,0:T(8,128)(2,1)S(1)}, bf16[2,128,256]{2,1,0:T(8,128)(2,1)S(1)}, u32[]{:S(2)}, u32[]{:S(2)}) collective-permute-start(bf16[2,128,256]{2,1,0:T(8,128)(2,1)S(1)} %get-tuple-element.23), channel_id=1, source_target_pairs={{0,128},{1,129},{2,130},{3,131},{4,132},{5,133},{6,134},{7,135},{8... | collective-permute-start | bytes 393224 | tf_op jit(solution)/shard_map/ppermute | solution.py:294
  38.3 21.3 %collective-permute-start.6 = (bf16[2,128,256]{2,1,0:T(8,128)(2,1)S(1)}, bf16[2,128,256]{2,1,0:T(8,128)(2,1)S(1)}, u32[]{:S(2)}, u32[]{:S(2)}) collective-permute-start(bf16[2,128,256]{2,1,0:T(8,128)(2,1)S(1)} %get-tuple-element.25), channel_id=1, source_target_pairs={{0,128},{1,129},{2,130},{3,131},{4,132},{5,133},{6,134},{7,135},{8... | collective-permute-start | bytes 393224 | tf_op jit(solution)/shard_map/ppermute | solution.py:294
  38.4 23.3 %collective-permute-start.7 = (bf16[2,128,256]{2,1,0:T(8,128)(2,1)S(1)}, bf16[2,128,256]{2,1,0:T(8,128)(2,1)S(1)}, u32[]{:S(2)}, u32[]{:S(2)}) collective-permute-start(bf16[2,128,256]{2,1,0:T(8,128)(2,1)S(1)} %get-tuple-element.26), channel_id=1, source_target_pairs={{0,128},{1,129},{2,130},{3,131},{4,132},{5,133},{6,134},{7,135},{8... | collective-permute-start | bytes 393224 | tf_op jit(solution)/shard_map/ppermute | solution.py:294
  53.9 21.4 %collective-permute-start.8 = (bf16[2,128,256]{2,1,0:T(8,128)(2,1)S(1)}, bf16[2,128,256]{2,1,0:T(8,128)(2,1)S(1)}, u32[]{:S(2)}, u32[]{:S(2)}) collective-permute-start(bf16[2,128,256]{2,1,0:T(8,128)(2,1)S(1)} %get-tuple-element.28), channel_id=1, source_target_pairs={{0,128},{1,129},{2,130},{3,131},{4,132},{5,133},{6,134},{7,135},{8... | collective-permute-start | bytes 393224 | tf_op jit(solution)/shard_map/ppermute | solution.py:294
  59.6 15.8 %collective-permute-start.9 = (bf16[2,128,256]{2,1,0:T(8,128)(2,1)S(1)}, bf16[2,128,256]{2,1,0:T(8,128)(2,1)S(1)}, u32[]{:S(2)}, u32[]{:S(2)}) collective-permute-start(bf16[2,128,256]{2,1,0:T(8,128)(2,1)S(1)} %get-tuple-element.29), channel_id=1, source_target_pairs={{0,128},{1,129},{2,130},{3,131},{4,132},{5,133},{6,134},{7,135},{8... | collective-permute-start | bytes 393224 | tf_op jit(solution)/shard_map/ppermute | solution.py:294
  61.8 23.7 %copy-start.3 = (s32[4]{0:T(128)S(1)}, s32[4]{0:T(128)}, u32[]{:S(2)}) copy-start(s32[4]{0:T(128)} %cols.5) | copy-start | bytes 52
  61.8 13.6 %collective-permute-start.10 = (bf16[2,128,256]{2,1,0:T(8,128)(2,1)S(1)}, bf16[2,128,256]{2,1,0:T(8,128)(2,1)S(1)}, u32[]{:S(2)}, u32[]{:S(2)}) collective-permute-start(bf16[2,128,256]{2,1,0:T(8,128)(2,1)S(1)} %get-tuple-element.30), channel_id=1, source_target_pairs={{0,127},{1,0},{2,1},{3,2},{4,3},{5,4},{6,5},{7,6},{8,7},{9,8},{10,... | collective-permute-start | bytes 393224 | tf_op jit(solution)/shard_map/ppermute | solution.py:294
  74.7 4.0 %collective-permute-start.12 = (bf16[2,128,256]{2,1,0:T(8,128)(2,1)S(1)}, bf16[2,128,256]{2,1,0:T(8,128)(2,1)S(1)}, u32[]{:S(2)}, u32[]{:S(2)}) collective-permute-start(bf16[2,128,256]{2,1,0:T(8,128)(2,1)S(1)} %get-tuple-element.31), channel_id=1, source_target_pairs={{0,127},{1,0},{2,1},{3,2},{4,3},{5,4},{6,5},{7,6},{8,7},{9,8},{10,... | collective-permute-start | bytes 393224 | tf_op jit(solution)/shard_map/ppermute | solution.py:294
  74.8 9.3 %collective-permute-start.13 = (bf16[2,128,256]{2,1,0:T(8,128)(2,1)S(1)}, bf16[2,128,256]{2,1,0:T(8,128)(2,1)S(1)}, u32[]{:S(2)}, u32[]{:S(2)}) collective-permute-start(bf16[2,128,256]{2,1,0:T(8,128)(2,1)S(1)} %get-tuple-element.32), channel_id=1, source_target_pairs={{0,1},{1,2},{2,3},{3,4},{4,5},{5,6},{6,7},{7,8},{8,9},{9,10},{10,1... | collective-permute-start | bytes 393224 | tf_op jit(solution)/shard_map/ppermute | solution.py:294
  75.3 10.2 %collective-permute-start.11 = (bf16[2,128,256]{2,1,0:T(8,128)(2,1)S(1)}, bf16[2,128,256]{2,1,0:T(8,128)(2,1)S(1)}, u32[]{:S(2)}, u32[]{:S(2)}) collective-permute-start(bf16[2,128,256]{2,1,0:T(8,128)(2,1)S(1)} %collective-permute-done.8.from_outer), channel_id=1, source_target_pairs={{0,1},{1,2},{2,3},{3,4},{4,5},{5,6},{6,7},{7,8},{8,9},{9,10},{10,1... | collective-permute-start | bytes 393224 | tf_op jit(solution)/shard_map/ppermute | solution.py:294

commit v2 on v1

--- a/solution.py
+++ b/solution.py
@@ -21,6 +21,7 @@
 WIDE = SIDE + 128
 VM = pl.BlockSpec(memory_space=pltpu.VMEM)
 SM = pl.BlockSpec(memory_space=pltpu.SMEM)
+HB = pl.BlockSpec(memory_space=pltpu.HBM)
 
 
 def routes(regions):
@@ -30,8 +31,6 @@
         "mate": [(at(c, r), at(1 - c, r)) for c, r in both],
         "next": [(at(c, r), at(c, r + 1)) for c, r in both],
         "prev": [(at(c, r), at(c, r - 1)) for c, r in both],
-        "solo": [(at(c, r), at(c, r - 1 if c == 0 else r + 1)) for c, r in both],
-        "relay": [(at(c, r), at(c, r + 1 if c == 0 else r - 1)) for c, r in both],
     }
 
 
@@ -83,24 +82,34 @@
     total_ref[where] = total_ref[where] + block
 
 
-def inband_kernel(rows, cols, objects, inband, low, high):
-    cut = lax.axis_index("cuts")
+def inband_kernel(rows_in, cols_in, objects_in, inband, low, high, rows, cols, objects, sems):
+    cut = lax.axis_index("cuts")
+    copies = [
+        pltpu.make_async_copy(rows_in, rows, sems.at[0]),
+        pltpu.make_async_copy(cols_in, cols, sems.at[1]),
+        pltpu.make_async_copy(objects_in.at[0, 0], objects.at[0], sems.at[2]),
+        pltpu.make_async_copy(objects_in.at[0, 1], objects.at[1], sems.at[3]),
+    ]
+    for copy in copies:
+        copy.start()
+    copies[0].wait()
+    copies[1].wait()
     u0, u1, l0, l1 = places(rows)
     other_up = cut == 1
-    for slot, (place, up) in enumerate(
-        [(jnp.where(other_up, u1, l1), other_up), (u0, None), (l0, None)]
-    ):
-        offset = jnp.where(up, HALF, 0) if slot == 0 else (HALF if slot == 1 else 0)
-        for channel in range(2):
+    spots = [
+        (jnp.where(other_up, u1, l1), jnp.where(other_up, HALF, 0)), (u0, HALF), (l0, 0)
+    ]
+    for channel in range(2):
+        copies[2 + channel].wait()
+        low[channel] = objects[channel, :HALF].astype(BF)
+        high[channel] = objects[channel, HALF:].astype(BF)
+        for slot, (place, offset) in enumerate(spots):
             inband[slot, channel] = cut_window(
-                lambda r, c: objects[0, channel, r, c], rows[place] + offset, cols[place], HALF, BAND
+                lambda r, c: objects[channel, r, c], rows[place] + offset, cols[place], HALF, BAND
             ).astype(BF)
-    for channel in range(2):
-        low[channel] = objects[0, channel, :HALF].astype(BF)
-        high[channel] = objects[0, channel, HALF:].astype(BF)
-
-
-def outer_kernel(rows, cols, objects, above, below, half0, half1, half2, windows, ext):
+
+
+def outer_kernel(rows, cols, objects, above, below, half0, half12, windows, ext):
     cut = lax.axis_index("cuts")
     u0, u1, l0, l1 = places(rows)
     other_up = cut == 1
@@ -118,9 +127,9 @@
             window = cut_window(load, rows[place] + HALF, cols[place], SIDE, EXT).astype(BF)
             windows[slot, channel] = window
             if slot == 1:
-                half1[channel] = window[:HALF]
+                half12[0, channel] = window[:HALF]
             if slot == 2:
-                half2[channel] = window[HALF:]
+                half12[1, channel] = window[HALF:]
 
 
 def transform(fields, left, right):
@@ -212,13 +221,13 @@
 
 
 def shared_kernel(
-    rows, picks, windows, inband, outer1, outer2, probes, amplitudes, wave, first, second,
+    rows, picks, windows, inband, outer, probes, amplitudes, wave, first, second,
     kept, edge_up, edge_low, held, made,
 ):
     cut = lax.axis_index("cuts")
     u0, u1, l0, l1 = places(rows)
-    fill_patches(held.at[0], windows.at[1], inband.at[1], outer1, cut, 0)
-    fill_patches(held.at[1], windows.at[2], inband.at[2], outer2, cut, HALF)
+    fill_patches(held.at[0], windows.at[1], inband.at[1], outer.at[0], cut, 0)
+    fill_patches(held.at[1], windows.at[2], inband.at[2], outer.at[1], cut, HALF)
 
     def store(k, which, value):
         made[k, which, 0], made[k, which, 1] = value
@@ -236,52 +245,75 @@
         edge_low[channel] = made[1, cut, channel, HALF:].astype(BF)
 
 
-def gather_kernel(
-    rows, cols, after, before, solo, shared, from_outer, from_inband,
-    edge_solo, edge_relay, edge_up, edge_low, output, total,
-):
-    cut = lax.axis_index("cuts")
-    u0, u1, l0, l1 = places(rows)
-    after_rows = [after[i] for i in range(4)]
-    before_rows = [before[i] for i in range(4)]
-    next_u0, next_u1, _, _ = places(after_rows)
-    _, _, last_l0, last_l1 = places(before_rows)
-    total[...] = jnp.zeros_like(total)
+def edges_kernel(solo, up, low, relay, to_prev, to_next):
+    cut = lax.axis_index("cuts")
+    to_prev[0] = up[...]
+    to_next[0] = low[...]
+
+    @pl.when(cut == 0)
+    def _():
+        to_prev[1] = solo[...]
+        to_next[1] = relay[...]
+
+    @pl.when(cut == 1)
+    def _():
+        to_prev[1] = relay[...]
+        to_next[1] = solo[...]
+
+
+def own_kernel(rows, cols, solo, shared, from_inband, total):
+    cut = lax.axis_index("cuts")
+    u0, u1, l0, l1 = places(rows)
     own = jnp.where(cut == 0, u1, l1)
     other = jnp.where(cut == 0, l1, u1)
     start = jnp.where(cut == 0, HALF, 0)
-    next_top = lambda place: after[place] + HALF + BAND
-    last_top = lambda place: before[place]
-    solo_top = jnp.where(cut == 0, next_top(next_u1), last_top(last_l1))
-    solo_left = jnp.where(cut == 0, after[4 + next_u1], before[4 + last_l1])
-    relay_top = jnp.where(cut == 0, last_top(last_l1), next_top(next_u1))
-    relay_left = jnp.where(cut == 0, before[4 + last_l1], after[4 + next_u1])
+    total[...] = jnp.zeros_like(total)
     for channel in range(2):
         put = functools.partial(put_window, total, channel)
         put(rows[own] + HALF, cols[own], solo[channel])
         put(rows[u0] + HALF, cols[u0], shared[0, channel])
         put(rows[l0] + HALF, cols[l0], shared[1, channel])
+        put(rows[other] + 2 * HALF - start, cols[other], from_inband[channel].astype(F32))
+
+
+def rest_kernel(rows, cols, after, before, given, from_outer, from_next, from_prev, total, output, sems):
+    cut = lax.axis_index("cuts")
+    u0, u1, l0, l1 = places(rows)
+    next_spots = places([after[i] for i in range(4)])[:2]
+    prev_spots = places([before[i] for i in range(4)])[2:]
+    other = jnp.where(cut == 0, l1, u1)
+    start = jnp.where(cut == 0, HALF, 0)
+    copies = []
+    for channel in range(2):
+        put = functools.partial(put_window, total, channel)
         put(rows[other] + HALF + start, cols[other], from_outer[channel].astype(F32))
-        put(rows[other] + 2 * HALF - start, cols[other], from_inband[channel].astype(F32))
-        put(solo_top, solo_left, edge_solo[channel].astype(F32))
-        put(relay_top, relay_left, edge_relay[channel].astype(F32))
-        put(next_top(next_u0), after[4 + next_u0], edge_up[channel].astype(F32))
-        put(last_top(last_l0), before[4 + last_l0], edge_low[channel].astype(F32))
-        output[0, channel] = total[channel, HALF : HALF + BAND]
-
-
-def call(kernel, name, inputs, outputs, scratch=(), flops=0):
+        for k in range(2):
+            spot = next_spots[k]
+            put(after[spot] + HALF + BAND, after[4 + spot], from_next[k, channel].astype(F32))
+            spot = prev_spots[k]
+            put(before[spot], before[4 + spot], from_prev[k, channel].astype(F32))
+        copies.append(
+            pltpu.make_async_copy(
+                total.at[channel, pl.ds(HALF, BAND)], output.at[0, channel], sems.at[channel]
+            )
+        )
+        copies[channel].start()
+    for copy in copies:
+        copy.wait()
+
+
+def call(kernel, name, inputs, outputs, scratch=(), in_specs=None, out_specs=None, aliases={}, vmem=40, flops=1):
     scalars = [x for x in inputs if x.dtype == jnp.int32]
-    moved = sum(x.size * x.dtype.itemsize for x in list(inputs) + list(outputs))
     return pl.pallas_call(
         kernel,
         name=name,
         out_shape=outputs,
-        in_specs=[SM] * len(scalars) + [VM] * (len(inputs) - len(scalars)),
-        out_specs=[VM] * len(outputs),
+        in_specs=in_specs or [SM] * len(scalars) + [VM] * (len(inputs) - len(scalars)),
+        out_specs=out_specs or [VM] * len(outputs),
         scratch_shapes=list(scratch),
-        cost_estimate=pl.CostEstimate(flops=flops, bytes_accessed=moved, transcendentals=0),
-        compiler_params=pltpu.CompilerParams(vmem_limit_bytes=40 << 20),
+        input_output_aliases=aliases,
+        cost_estimate=pl.CostEstimate(flops=flops, bytes_accessed=1, transcendentals=0),
+        compiler_params=pltpu.CompilerParams(vmem_limit_bytes=vmem << 20),
     )(*inputs)
 
 
@@ -295,52 +327,58 @@
     first, second = (jnp.asarray(t) for t in dft_blocks())
     wave = jnp.stack([jnp.cos(prop_phase), jnp.sin(prop_phase)])
     half = arr(2, HALF, SIDE)
-    product = 2 * 2 * 512 * 512 * 256
 
     inband, low, high = call(
         inband_kernel, "inband", [scan_rows, scan_cols, objects],
         [arr(3, 2, HALF, SIDE), arr(2, HALF, COLS), arr(2, HALF, COLS)],
-    )
-    mate_inband = move(inband, "mate")
+        [pltpu.SMEM((4,), jnp.int32), pltpu.SMEM((4,), jnp.int32), pltpu.VMEM((2, BAND, COLS), F32),
+         pltpu.SemaphoreType.DMA((4,))],
+        in_specs=[HB] * 3, vmem=56,
+    )
     above = move(high, "next")
     below = move(low, "prev")
-    scan = jnp.concatenate([scan_rows, scan_cols])
+    mate_inband = move(inband, "mate")
+    half0, half12, windows = call(
+        outer_kernel, "outer", [scan_rows, scan_cols, objects, above, below],
+        [half, arr(2, 2, HALF, SIDE), arr(3, 2, SIDE, SIDE)],
+        [pltpu.VMEM((2, EXT, COLS), F32)],
+    )
+    mate0 = move(half0, "mate")
+    mate12 = move(half12, "mate")
+    scan, half0 = lax.optimization_barrier((jnp.concatenate([scan_rows, scan_cols]), half0))
     before = move(scan, "next")
     after = move(scan, "prev")
-    half0, half1, half2, windows = call(
-        outer_kernel, "outer", [scan_rows, scan_cols, objects, above, below],
-        [half, half, half, arr(3, 2, SIDE, SIDE)],
-        [pltpu.VMEM((2, EXT, COLS), F32)],
-    )
-    mate0 = move(half0, "mate")
-    mate1 = move(half1, "mate")
-    mate2 = move(half2, "mate")
+    mate0, before, after = lax.optimization_barrier((mate0, before, after))
     sent_outer, sent_inband, solo, edge = call(
         solo_kernel, "solo",
         [scan_rows, probe_choice, windows, mate_inband, mate0, probes, amplitudes, wave, first, second],
         [half, half, arr(2, SIDE, SIDE, dtype=F32), half],
         [pltpu.VMEM((2, 2, SIDE, SIDE), BF), pltpu.VMEM((2, 2, SIDE, SIDE), F32)],
-        flops=6 * product,
     )
     from_outer = move(sent_outer, "mate")
     from_inband = move(sent_inband, "mate")
-    edge_solo = move(edge, "solo")
     shared, up, down = call(
         shared_kernel, "shared",
-        [scan_rows, probe_choice, windows, mate_inband, mate1, mate2, probes, amplitudes, wave, first, second],
+        [scan_rows, probe_choice, windows, mate_inband, mate12, probes, amplitudes, wave, first, second],
         [arr(2, 2, SIDE, SIDE, dtype=F32), half, half],
         [pltpu.VMEM((2, 2, 2, SIDE, SIDE), BF), pltpu.VMEM((2, 2, 2, SIDE, SIDE), F32)],
-        flops=12 * product,
-    )
-    edge_up = move(up, "prev")
-    edge_low = move(down, "next")
-    edge_relay = move(from_outer, "relay")
-    (gradient,) = call(
-        gather_kernel, "gather",
-        [scan_rows, scan_cols, after, before, solo, shared, from_outer, from_inband,
-         edge_solo, edge_relay, edge_up, edge_low],
-        [arr(1, 2, BAND, COLS, dtype=F32)],
-        [pltpu.VMEM((2, EXT, COLS), F32)],
+    )
+    to_prev, to_next = call(
+        edges_kernel, "edges", [edge, up, down, from_outer], [arr(2, 2, HALF, SIDE)] * 2
+    )
+    from_next = move(to_prev, "prev")
+    from_prev = move(to_next, "next")
+    (total,) = call(
+        own_kernel, "own", [scan_rows, scan_cols, solo, shared, from_inband],
+        [arr(2, EXT, COLS, dtype=F32)], flops=10**11,
+    )
+    _, gradient = call(
+        rest_kernel, "rest",
+        [scan_rows, scan_cols, after, before, total, from_outer, from_next, from_prev],
+        [arr(2, EXT, COLS, dtype=F32), arr(1, 2, BAND, COLS, dtype=F32)],
+        [pltpu.SemaphoreType.DMA((2,))],
+        out_specs=[VM, HB],
+        aliases={4: 0},
     )
     return gradient
 

time: 91.1 us -> 92.1 us (1.011); the launches traced: 90.8 us -> 90.7 us
  starting transfers between devices: 52.3 us -> 38.3 us
  waiting for transfers between devices: 15.5 us -> 27.7 us
  Pallas kernels: 18.9 us -> 21 us
    ppermute x14 -> x11, starting transfers between devices: 52.3 us -> 38.3 us  [shards(): move = lambda x, way: lax.ppermute(x, AXES, route[way])]
    ppermute x14 -> x11, waiting for transfers between devices: 15.5 us -> 27.7 us  [shards(): move = lambda x, way: lax.ppermute(x, AXES, route[way])]
    pallas_call x5 -> x7, Pallas kernels: 18.9 us -> 21 us  [call(): pl.pallas_call(kernel, name=name, out_shape=outputs, in_specs=in_specs or...]
    unnamed x20 -> x16, local copies, waits for them, and re-layouts: 2.93 us -> 1.33 us
  transfers between devices with their start and end apart: 14 -> 11, of which waited for: 5 -> 6; matrix products, arithmetic and copies ran while one was open for 1% -> 2% of each run, Pallas kernels for 14% -> 17%
where the time goes in v2:
time: 92.1 us; the launch traced here: 90.7 us
  starting transfers between devices  38.3 us (42%)
  waiting for transfers between devices  27.7 us (30%)
  Pallas kernels  21 us (23%)
  local copies, waits for them, and re-layouts  3.19 us (3%)
    ppermute x11, starting transfers between devices, shards(): move = lambda x, way: lax.ppermute(x, AXES, route[way])  38.3 us
    ppermute x11, waiting for transfers between devices, shards(): move = lambda x, way: lax.ppermute(x, AXES, route[way])  27.7 us
    pallas_call x7, Pallas kernels, call(): pl.pallas_call(kernel, name=name, out_shape=outputs, in_specs=in_specs or...  21 us
    another operation x1, local copies, waits for them, and re-layouts, shards(): wave = jnp.stack([jnp.cos(prop_phase), jnp.sin(prop_phase)])  1.85 us
  transfers between devices with their start and end apart: 11, of which 6 were waited for; matrix products, arithmetic and copies ran while one was open for 2% of the time, Pallas kernels for 17%

profile of v2, /device:TPU:8, one launch (start us, length us, event | category | flops | bytes accessed | tf_op | source)
XLA Modules:
  0.0 90.7 jit_solution(15606246328200094923)
XLA Ops:
  0.0 3.2 %inband.1 = (bf16[3,2,128,256]{3,2,1,0:T(8,128)(2,1)}, bf16[2,128,1024]{2,1,0:T(8,128)(2,1)}, bf16[2,128,1024]{2,1,0:T(8,128)(2,1)}) custom-call(s32[4]{0:T(128)} %rows.9, s32[4]{0:T(128)} %cols.5, f32[1,2,256,1024]{3,2,1,0:T(8,128)} %objects.1), custom_call_target="tpu_custom_call" | custom-call | flops 1 | bytes 1 | tf_op jit(solution)/shard_map/inband/pallas_call | solution.py:307
  3.3 0.1 collective-permute-start
  3.3 6.5 %collective-permute-start.1 = (bf16[2,128,1024]{2,1,0:T(8,128)(2,1)}, bf16[2,128,1024]{2,1,0:T(8,128)(2,1)S(1)}, u32[]{:S(2)}, u32[]{:S(2)}) collective-permute-start(bf16[2,128,1024]{2,1,0:T(8,128)(2,1)} %get-tuple-element.26), channel_id=1, source_target_pairs={{0,127},{1,0},{2,1},{3,2},{4,3},{5,4},{6,5},{7,6},{8,7},{9,8},{10,... | collective-permute-start | bytes 1572872 | tf_op jit(solution)/shard_map/ppermute | solution.py:326
  9.9 7.2 %collective-permute-start.5 = (bf16[3,2,128,256]{3,2,1,0:T(8,128)(2,1)}, bf16[3,2,128,256]{3,2,1,0:T(8,128)(2,1)S(1)}, u32[]{:S(2)}, u32[]{:S(2)}) collective-permute-start(bf16[3,2,128,256]{3,2,1,0:T(8,128)(2,1)} %get-tuple-element.32), channel_id=1, source_target_pairs={{0,128},{1,129},{2,130},{3,131},{4,132},{5,133},{6,134},{7,135},{8... | collective-permute-start | bytes 1179656 | tf_op jit(solution)/shard_map/ppermute | solution.py:326
  17.1 1.9 %cosine_bitcast_fusion = (f32[1,256,256]{2,1,0:T(8,128)S(1)}, f32[1,256,256]{2,1,0:T(8,128)S(1)}) fusion(f32[256,256]{1,0:T(8,128)} %param.12), kind=kLoop, calls=%fused_computation.2 | loop fusion | bytes 786432 | tf_op jit(solution)/shard_map/stack | solution.py:328
  18.9 5.0 %collective-permute-done.above = bf16[2,128,1024]{2,1,0:T(8,128)(2,1)S(1)} collective-permute-done((bf16[2,128,1024]{2,1,0:T(8,128)(2,1)}, bf16[2,128,1024]{2,1,0:T(8,128)(2,1)S(1)}, u32[]{:S(2)}, u32[]{:S(2)}) %collective-permute-start) | collective-permute-done | bytes 524320 | tf_op jit(solution)/shard_map/ppermute | solution.py:326
  23.9 0.9 collective-permute-done.1.below
  24.8 0.7 copy-done.5
  25.4 0.7 copy-done.6
  26.1 2.1 %outer.1 = (bf16[2,128,256]{2,1,0:T(8,128)(2,1)S(1)}, bf16[2,2,128,256]{3,2,1,0:T(8,128)(2,1)S(1)}, bf16[3,2,256,256]{3,2,1,0:T(8,128)(2,1)S(1)}) custom-call(s32[4]{0:T(128)S(1)} %copy-done.5, s32[4]{0:T(128)S(1)} %copy-done.6, f32[1,2,256,1024]{3,2,1,0:T(8,128)S(1)} %copy-done, bf16[2,128,1024]{2,1,0:T(8,128)(2,1)S(1)} %collective-permute-done.above, ...), custom_call_target="tpu_custom_call" | custom-call | flops 1 | bytes 1 | tf_op jit(solution)/shard_map/outer/pallas_call | solution.py:307
  28.2 9.8 %collective-permute-start.2 = (bf16[2,128,256]{2,1,0:T(8,128)(2,1)S(1)}, bf16[2,128,256]{2,1,0:T(8,128)(2,1)S(1)}, u32[]{:S(2)}, u32[]{:S(2)}) collective-permute-start(bf16[2,128,256]{2,1,0:T(8,128)(2,1)S(1)} %get-tuple-element.27), channel_id=1, source_target_pairs={{0,128},{1,129},{2,130},{3,131},{4,132},{5,133},{6,134},{7,135},{8... | collective-permute-start | bytes 393224 | tf_op jit(solution)/shard_map/ppermute | solution.py:326
  38.0 0.1 collective-permute-start.6
  38.2 2.3 %collective-permute-start.4 = (s32[8]{0:T(128)S(1)}, s32[8]{0:T(128)S(1)}, u32[]{:S(2)}, u32[]{:S(2)}) collective-permute-start(s32[8]{0:T(128)S(1)} %pad_add_fusion), channel_id=1, source_target_pairs={{0,127},{1,0},{2,1},{3,2},{4,3},{5,4},{6,5},{7,6},{8,7},{9,8},{10,... | collective-permute-start | bytes 104 | tf_op jit(solution)/shard_map/ppermute | solution.py:326
  40.5 14.0 %collective-permute-done.4.after = s32[8]{0:T(128)S(1)} collective-permute-done((s32[8]{0:T(128)S(1)}, s32[8]{0:T(128)S(1)}, u32[]{:S(2)}, u32[]{:S(2)}) %collective-permute-start.4) | collective-permute-done | bytes 64 | tf_op jit(solution)/shard_map/ppermute | solution.py:326
  54.6 4.8 %solo.1 = (bf16[2,128,256]{2,1,0:T(8,128)(2,1)S(1)}, bf16[2,128,256]{2,1,0:T(8,128)(2,1)S(1)}, f32[2,256,256]{2,1,0:T(8,128)S(1)}, bf16[2,128,256]{2,1,0:T(8,128)(2,1)S(1)}) custom-call(s32[4]{0:T(128)S(1)} %copy-done.5, s32[4]{0:T(128)S(1)} %copy-done.7, bf16[3,2,256,256]{3,2,1,0:T(8,128)(2,1)S(1)} %get-tuple-element.31.windows, ...), custom_call_target="tpu_custom_call" | custom-call | flops 1 | bytes 1 | tf_op jit(solution)/shard_map/solo/pallas_call | solution.py:307
  59.4 10.0 %collective-permute-start.8 = (bf16[2,128,256]{2,1,0:T(8,128)(2,1)S(1)}, bf16[2,128,256]{2,1,0:T(8,128)(2,1)S(1)}, u32[]{:S(2)}, u32[]{:S(2)}) collective-permute-start(bf16[2,128,256]{2,1,0:T(8,128)(2,1)S(1)} %get-tuple-element.38), channel_id=1, source_target_pairs={{0,128},{1,129},{2,130},{3,131},{4,132},{5,133},{6,134},{7,135},{8... | collective-permute-start | bytes 393224 | tf_op jit(solution)/shard_map/ppermute | solution.py:326
  69.4 0.3 collective-permute-start.7
  69.7 5.5 %shared.1 = (f32[2,2,256,256]{3,2,1,0:T(8,128)S(1)}, bf16[2,128,256]{2,1,0:T(8,128)(2,1)S(1)}, bf16[2,128,256]{2,1,0:T(8,128)(2,1)S(1)}) custom-call(s32[4]{0:T(128)S(1)} %copy-done.5, s32[4]{0:T(128)S(1)} %copy-done.7, bf16[3,2,256,256]{3,2,1,0:T(8,128)(2,1)S(1)} %get-tuple-element.31.windows, bf16[3,2,128,256]{3,2,1,0:T(8,128)(2,1)S(1)} %collective-permute-done.5.inband, ...), custom_call_target="tpu_custom_call" | custom-call | flops 1 | bytes 1 | tf_op jit(solution)/shard_map/shared/pallas_call | solution.py:307
  75.3 2.1 %collective-permute-start.9 = (bf16[2,2,128,256]{3,2,1,0:T(8,128)(2,1)S(1)}, bf16[2,2,128,256]{3,2,1,0:T(8,128)(2,1)S(1)}, u32[]{:S(2)}, u32[]{:S(2)}) collective-permute-start(bf16[2,2,128,256]{3,2,1,0:T(8,128)(2,1)S(1)} %get-tuple-element.42), channel_id=1, source_target_pairs={{0,127},{1,0},{2,1},{3,2},{4,3},{5,4},{6,5},{7,6},{8,7},{9,8},{10,... | collective-permute-start | bytes 786440 | tf_op jit(solution)/shard_map/ppermute | solution.py:326
  77.3 1.1 %collective-permute-done.7.from_inband = bf16[2,128,256]{2,1,0:T(8,128)(2,1)S(1)} collective-permute-done((bf16[2,128,256]{2,1,0:T(8,128)(2,1)S(1)}, bf16[2,128,256]{2,1,0:T(8,128)(2,1)S(1)}, u32[]{:S(2)}, u32[]{:S(2)}) %collective-permute-start.7) | collective-permute-done | bytes 131104 | tf_op jit(solution)/shard_map/ppermute | solution.py:326
  78.4 2.7 %own.1.given = f32[2,512,1024]{2,1,0:T(8,128)S(1)} custom-call(s32[4]{0:T(128)S(1)} %copy-done.5, s32[4]{0:T(128)S(1)} %copy-done.6, f32[2,256,256]{2,1,0:T(8,128)S(1)} %get-tuple-element.34.solo, f32[2,2,256,256]{3,2,1,0:T(8,128)S(1)} %get-tuple-element.36.shared, bf16[2,128,256]{2,1,0:T(8,128)(2,1)S(1)} %collective-permute-done.7.from_inband), custom_call_target="tpu_custom_call" | custom-call | flops 99999997952 | bytes 1 | tf_op jit(solution)/shard_map/own/pallas_call | solution.py:307
  81.1 0.8 collective-permute-done.9.from_next
  81.9 6.1 %collective-permute-done.10.from_prev = bf16[2,2,128,256]{3,2,1,0:T(8,128)(2,1)S(1)} collective-permute-done((bf16[2,2,128,256]{3,2,1,0:T(8,128)(2,1)S(1)}, bf16[2,2,128,256]{3,2,1,0:T(8,128)(2,1)S(1)}, u32[]{:S(2)}, u32[]{:S(2)}) %collective-permute-start.10) | collective-permute-done | bytes 262176 | tf_op jit(solution)/shard_map/ppermute | solution.py:326
  87.9 2.6 %rest.1 = (f32[2,512,1024]{2,1,0:T(8,128)S(1)}, f32[1,2,256,1024]{3,2,1,0:T(8,128)}) custom-call(s32[4]{0:T(128)S(1)} %copy-done.5, s32[4]{0:T(128)S(1)} %copy-done.6, s32[8]{0:T(128)S(1)} %collective-permute-done.4.after, s32[8]{0:T(128)S(1)} %collective-permute-done.3.before, f32[2,512,1024]{2,1,0:T(8,128)S(1)} %own.1.given, ...), custom_call_target="tpu_custom_call", output_to_operand_aliasing={{0}: (4, {})} | custom-call | flops 1 | bytes 1 | tf_op jit(solution)/shard_map/rest/pallas_call | solution.py:307
  (24 shorter events, 0.2 us)
Async XLA Ops:
  0.0 54.5 %copy-start.3 = (bf16[512,512]{1,0:T(8,128)(2,1)S(1)}, bf16[512,512]{1,0:T(8,128)(2,1)}, u32[]{:S(2)}) copy-start(bf16[512,512]{1,0:T(8,128)(2,1)} %constant.5.clone.second) | copy-start | bytes 1572868
  0.0 24.8 %copy-start = (f32[1,2,256,1024]{3,2,1,0:T(8,128)S(1)}, f32[1,2,256,1024]{3,2,1,0:T(8,128)}, u32[]{:S(2)}) copy-start(f32[1,2,256,1024]{3,2,1,0:T(8,128)} %objects.1) | copy-start | bytes 6291460
  0.0 54.5 %copy-start.4 = (bf16[512,512]{1,0:T(8,128)(2,1)S(1)}, bf16[512,512]{1,0:T(8,128)(2,1)}, u32[]{:S(2)}) copy-start(bf16[512,512]{1,0:T(8,128)(2,1)} %constant.4.clone.first) | copy-start | bytes 1572868
  0.0 54.5 %copy-start.2 = (f32[4,256,256]{2,1,0:T(8,128)S(1)}, f32[4,256,256]{2,1,0:T(8,128)}, u32[]{:S(2)}) copy-start(f32[4,256,256]{2,1,0:T(8,128)} %amplitudes.3) | copy-start | bytes 3145732
  0.0 54.5 %copy-start.1 = (bf16[4,2,256,256]{3,2,1,0:T(8,128)(2,1)S(1)}, bf16[4,2,256,256]{3,2,1,0:T(8,128)(2,1)}, u32[]{:S(2)}) copy-start(bf16[4,2,256,256]{3,2,1,0:T(8,128)(2,1)} %probes.3) | copy-start | bytes 3145732
  3.3 20.7 %collective-permute-start = (bf16[2,128,1024]{2,1,0:T(8,128)(2,1)}, bf16[2,128,1024]{2,1,0:T(8,128)(2,1)S(1)}, u32[]{:S(2)}, u32[]{:S(2)}) collective-permute-start(bf16[2,128,1024]{2,1,0:T(8,128)(2,1)} %get-tuple-element.25), channel_id=1, source_target_pairs={{0,1},{1,2},{2,3},{3,4},{4,5},{5,6},{6,7},{7,8},{8,9},{9,10},{10,1... | collective-permute-start | bytes 1572872 | tf_op jit(solution)/shard_map/ppermute | solution.py:326
  3.3 21.4 %collective-permute-start.1 = (bf16[2,128,1024]{2,1,0:T(8,128)(2,1)}, bf16[2,128,1024]{2,1,0:T(8,128)(2,1)S(1)}, u32[]{:S(2)}, u32[]{:S(2)}) collective-permute-start(bf16[2,128,1024]{2,1,0:T(8,128)(2,1)} %get-tuple-element.26), channel_id=1, source_target_pairs={{0,127},{1,0},{2,1},{3,2},{4,3},{5,4},{6,5},{7,6},{8,7},{9,8},{10,... | collective-permute-start | bytes 1572872 | tf_op jit(solution)/shard_map/ppermute | solution.py:326
  9.9 44.6 %collective-permute-start.5 = (bf16[3,2,128,256]{3,2,1,0:T(8,128)(2,1)}, bf16[3,2,128,256]{3,2,1,0:T(8,128)(2,1)S(1)}, u32[]{:S(2)}, u32[]{:S(2)}) collective-permute-start(bf16[3,2,128,256]{3,2,1,0:T(8,128)(2,1)} %get-tuple-element.32), channel_id=1, source_target_pairs={{0,128},{1,129},{2,130},{3,131},{4,132},{5,133},{6,134},{7,135},{8... | collective-permute-start | bytes 1179656 | tf_op jit(solution)/shard_map/ppermute | solution.py:326
  24.8 0.7 copy-start.5
  25.4 0.7 copy-start.6
  26.1 28.5 %copy-start.7 = (s32[4]{0:T(128)S(1)}, s32[4]{0:T(128)}, u32[]{:S(2)}) copy-start(s32[4]{0:T(128)} %picks.3) | copy-start | bytes 52
  28.2 26.3 %collective-permute-start.2 = (bf16[2,128,256]{2,1,0:T(8,128)(2,1)S(1)}, bf16[2,128,256]{2,1,0:T(8,128)(2,1)S(1)}, u32[]{:S(2)}, u32[]{:S(2)}) collective-permute-start(bf16[2,128,256]{2,1,0:T(8,128)(2,1)S(1)} %get-tuple-element.27), channel_id=1, source_target_pairs={{0,128},{1,129},{2,130},{3,131},{4,132},{5,133},{6,134},{7,135},{8... | collective-permute-start | bytes 393224 | tf_op jit(solution)/shard_map/ppermute | solution.py:326
  38.0 31.7 %collective-permute-start.6 = (bf16[2,2,128,256]{3,2,1,0:T(8,128)(2,1)S(1)}, bf16[2,2,128,256]{3,2,1,0:T(8,128)(2,1)S(1)}, u32[]{:S(2)}, u32[]{:S(2)}) collective-permute-start(bf16[2,2,128,256]{3,2,1,0:T(8,128)(2,1)S(1)} %get-tuple-element.35), channel_id=1, source_target_pairs={{0,128},{1,129},{2,130},{3,131},{4,132},{5,133},{6,134},{7,135},{8... | collective-permute-start | bytes 786440 | tf_op jit(solution)/shard_map/ppermute | solution.py:326
  38.2 16.3 %collective-permute-start.4 = (s32[8]{0:T(128)S(1)}, s32[8]{0:T(128)S(1)}, u32[]{:S(2)}, u32[]{:S(2)}) collective-permute-start(s32[8]{0:T(128)S(1)} %pad_add_fusion), channel_id=1, source_target_pairs={{0,127},{1,0},{2,1},{3,2},{4,3},{5,4},{6,5},{7,6},{8,7},{9,8},{10,... | collective-permute-start | bytes 104 | tf_op jit(solution)/shard_map/ppermute | solution.py:326
  40.5 14.0 %collective-permute-start.3 = (s32[8]{0:T(128)S(1)}, s32[8]{0:T(128)S(1)}, u32[]{:S(2)}, u32[]{:S(2)}) collective-permute-start(s32[8]{0:T(128)S(1)} %pad_add_fusion), channel_id=1, source_target_pairs={{0,1},{1,2},{2,3},{3,4},{4,5},{5,6},{6,7},{7,8},{8,9},{9,10},{10,1... | collective-permute-start | bytes 104 | tf_op jit(solution)/shard_map/ppermute | solution.py:326
  59.4 15.8 %collective-permute-start.8 = (bf16[2,128,256]{2,1,0:T(8,128)(2,1)S(1)}, bf16[2,128,256]{2,1,0:T(8,128)(2,1)S(1)}, u32[]{:S(2)}, u32[]{:S(2)}) collective-permute-start(bf16[2,128,256]{2,1,0:T(8,128)(2,1)S(1)} %get-tuple-element.38), channel_id=1, source_target_pairs={{0,128},{1,129},{2,130},{3,131},{4,132},{5,133},{6,134},{7,135},{8... | collective-permute-start | bytes 393224 | tf_op jit(solution)/shard_map/ppermute | solution.py:326
  69.4 9.0 %collective-permute-start.7 = (bf16[2,128,256]{2,1,0:T(8,128)(2,1)S(1)}, bf16[2,128,256]{2,1,0:T(8,128)(2,1)S(1)}, u32[]{:S(2)}, u32[]{:S(2)}) collective-permute-start(bf16[2,128,256]{2,1,0:T(8,128)(2,1)S(1)} %get-tuple-element.37), channel_id=1, source_target_pairs={{0,128},{1,129},{2,130},{3,131},{4,132},{5,133},{6,134},{7,135},{8... | collective-permute-start | bytes 393224 | tf_op jit(solution)/shard_map/ppermute | solution.py:326
  75.3 6.6 %collective-permute-start.9 = (bf16[2,2,128,256]{3,2,1,0:T(8,128)(2,1)S(1)}, bf16[2,2,128,256]{3,2,1,0:T(8,128)(2,1)S(1)}, u32[]{:S(2)}, u32[]{:S(2)}) collective-permute-start(bf16[2,2,128,256]{3,2,1,0:T(8,128)(2,1)S(1)} %get-tuple-element.42), channel_id=1, source_target_pairs={{0,127},{1,0},{2,1},{3,2},{4,3},{5,4},{6,5},{7,6},{8,7},{9,8},{10,... | collective-permute-start | bytes 786440 | tf_op jit(solution)/shard_map/ppermute | solution.py:326
  77.3 10.6 %collective-permute-start.10 = (bf16[2,2,128,256]{3,2,1,0:T(8,128)(2,1)S(1)}, bf16[2,2,128,256]{3,2,1,0:T(8,128)(2,1)S(1)}, u32[]{:S(2)}, u32[]{:S(2)}) collective-permute-start(bf16[2,2,128,256]{3,2,1,0:T(8,128)(2,1)S(1)} %get-tuple-element.43), channel_id=1, source_target_pairs={{0,1},{1,2},{2,3},{3,4},{4,5},{5,6},{6,7},{7,8},{8,9},{9,10},{10,1... | collective-permute-start | bytes 786440 | tf_op jit(solution)/shard_map/ppermute | solution.py:326

commit v3 on v2

--- a/solution.py
+++ b/solution.py
@@ -18,6 +18,7 @@
 BAND = 256
 COLS = 1024
 EXT = BAND + 2 * HALF
+EDGE = 2 * HALF * COLS // 128
 WIDE = SIDE + 128
 VM = pl.BlockSpec(memory_space=pltpu.VMEM)
 SM = pl.BlockSpec(memory_space=pltpu.SMEM)
@@ -31,6 +32,8 @@
         "mate": [(at(c, r), at(1 - c, r)) for c, r in both],
         "next": [(at(c, r), at(c, r + 1)) for c, r in both],
         "prev": [(at(c, r), at(c, r - 1)) for c, r in both],
+        "early": [(at(c, r), at(c, r - 1 if c == 0 else r + 1)) for c, r in both],
+        "late": [(at(c, r), at(c, r + 1 if c == 0 else r - 1)) for c, r in both],
     }
 
 
@@ -82,7 +85,19 @@
     total_ref[where] = total_ref[where] + block
 
 
-def inband_kernel(rows_in, cols_in, objects_in, inband, low, high, rows, cols, objects, sems):
+def tagged(rows, cols, spots):
+    line = lax.broadcasted_iota(jnp.int32, (16, 128), 0)
+    lane = lax.broadcasted_iota(jnp.int32, (16, 128), 1)
+    tile = jnp.zeros((16, 128), jnp.int32)
+    for k, spot in enumerate(spots):
+        left = cols[spot]
+        parts = (rows[spot] + HALF, lax.shift_right_logical(left, 3), jnp.bitwise_and(left, 7))
+        for n, part in enumerate(parts):
+            tile = jnp.where((line == k) & (lane == n), part, tile)
+    return tile.astype(F32).astype(BF)
+
+
+def inband_kernel(rows_in, cols_in, objects_in, inband, early, late, objects, rows, cols, sems):
     cut = lax.axis_index("cuts")
     copies = [
         pltpu.make_async_copy(rows_in, rows, sems.at[0]),
@@ -95,34 +110,56 @@
     copies[0].wait()
     copies[1].wait()
     u0, u1, l0, l1 = places(rows)
-    other_up = cut == 1
-    spots = [
-        (jnp.where(other_up, u1, l1), jnp.where(other_up, HALF, 0)), (u0, HALF), (l0, 0)
-    ]
+    up = cut == 0
+    early[EDGE:] = tagged(rows, cols, (jnp.where(up, u0, l0), jnp.where(up, u1, l1)))
+    late[EDGE:] = tagged(rows, cols, (jnp.where(up, l0, u0), jnp.where(up, l1, u1)))
+    start = pl.multiple_of(jnp.where(up, 0, HALF), HALF)
+    spots = [(jnp.where(up, l1, u1), jnp.where(up, 0, HALF)), (u0, HALF), (l0, 0)]
     for channel in range(2):
         copies[2 + channel].wait()
-        low[channel] = objects[channel, :HALF].astype(BF)
-        high[channel] = objects[channel, HALF:].astype(BF)
+        for k in range(COLS // 128):
+            where = pl.ds((channel * (COLS // 128) + k) * HALF, HALF)
+            lanes = slice(128 * k, 128 * (k + 1))
+            early[where] = objects[channel, pl.ds(start, HALF), lanes].astype(BF)
+            late[where] = objects[channel, pl.ds(HALF - start, HALF), lanes].astype(BF)
         for slot, (place, offset) in enumerate(spots):
             inband[slot, channel] = cut_window(
                 lambda r, c: objects[channel, r, c], rows[place] + offset, cols[place], HALF, BAND
             ).astype(BF)
 
 
-def outer_kernel(rows, cols, objects, above, below, half0, half12, windows, ext):
-    cut = lax.axis_index("cuts")
-    u0, u1, l0, l1 = places(rows)
-    other_up = cut == 1
-    for channel in range(2):
-        ext[channel, :HALF] = above[channel].astype(F32)
-        ext[channel, HALF : HALF + BAND] = objects[0, channel]
-        ext[channel, HALF + BAND :] = below[channel].astype(F32)
-    other = jnp.where(other_up, u1, l1)
-    solo = jnp.where(other_up, l1, u1)
-    for channel in range(2):
+def spread(target, channel, start, edge):
+    for k in range(COLS // 128):
+        target[channel, pl.ds(start, HALF), 128 * k : 128 * (k + 1)] = edge[
+            pl.ds((channel * (COLS // 128) + k) * HALF, HALF)
+        ].astype(F32)
+
+
+def first_kernel(rows, cols, objects, early, half0, near):
+    cut = lax.axis_index("cuts")
+    u0, u1, l0, l1 = places(rows)
+    other = jnp.where(cut == 0, l1, u1)
+    start = pl.multiple_of(jnp.where(cut == 0, HALF, 0), HALF)
+    top = rows[other] + jnp.where(cut == 0, 0, HALF)
+    for channel in range(2):
+        spread(near, channel, start, early)
+        near[channel, pl.ds(HALF - start, HALF)] = objects[channel, pl.ds(start, HALF)]
+        half0[channel] = cut_window(
+            lambda r, c: near[channel, r, c], top, cols[other], HALF, BAND
+        ).astype(BF)
+
+
+def outer_kernel(rows, cols, objects, early, late, half12, windows, ext):
+    cut = lax.axis_index("cuts")
+    u0, u1, l0, l1 = places(rows)
+    solo = jnp.where(cut == 0, u1, l1)
+    far = HALF + BAND
+    start = pl.multiple_of(jnp.where(cut == 0, far, 0), HALF)
+    for channel in range(2):
+        spread(ext, channel, start, early)
+        spread(ext, channel, far - start, late)
+        ext[channel, HALF:far] = objects[channel]
         load = lambda r, c: ext[channel, r, c]
-        top = rows[other] + jnp.where(other_up, HALF, 2 * HALF)
-        half0[channel] = cut_window(load, top, cols[other], HALF, EXT).astype(BF)
         for slot, place in enumerate((solo, u0, l0)):
             window = cut_window(load, rows[place] + HALF, cols[place], SIDE, EXT).astype(BF)
             windows[slot, channel] = window
@@ -130,6 +167,18 @@
                 half12[0, channel] = window[:HALF]
             if slot == 2:
                 half12[1, channel] = window[HALF:]
+
+
+def decode_kernel(early, late, spots):
+    line = lax.broadcasted_iota(jnp.int32, (16, 128), 0)
+    lane = lax.broadcasted_iota(jnp.int32, (16, 128), 1)
+    for n, edge in enumerate((early, late)):
+        tile = edge[EDGE:].astype(F32)
+        left = jnp.where(lane == 1, tile * 8.0, jnp.where(lane == 2, tile, 0.0))
+        top = jnp.where(lane == 0, tile, 0.0)
+        for k in range(2):
+            for m, part in enumerate((top, left)):
+                spots[4 * n + 2 * k + m] = jnp.sum(jnp.where(line == k, part, 0.0)).astype(jnp.int32)
 
 
 def transform(fields, left, right):
@@ -276,22 +325,22 @@
         put(rows[other] + 2 * HALF - start, cols[other], from_inband[channel].astype(F32))
 
 
-def rest_kernel(rows, cols, after, before, given, from_outer, from_next, from_prev, total, output, sems):
-    cut = lax.axis_index("cuts")
-    u0, u1, l0, l1 = places(rows)
-    next_spots = places([after[i] for i in range(4)])[:2]
-    prev_spots = places([before[i] for i in range(4)])[2:]
+def rest_kernel(rows, cols, spots, given, from_outer, from_next, from_prev, total, output, sems):
+    cut = lax.axis_index("cuts")
+    u0, u1, l0, l1 = places(rows)
     other = jnp.where(cut == 0, l1, u1)
     start = jnp.where(cut == 0, HALF, 0)
+    after = jnp.where(cut == 0, 0, 4)
+    before = 4 - after
     copies = []
     for channel in range(2):
         put = functools.partial(put_window, total, channel)
         put(rows[other] + HALF + start, cols[other], from_outer[channel].astype(F32))
         for k in range(2):
-            spot = next_spots[k]
-            put(after[spot] + HALF + BAND, after[4 + spot], from_next[k, channel].astype(F32))
-            spot = prev_spots[k]
-            put(before[spot], before[4 + spot], from_prev[k, channel].astype(F32))
+            top, left = spots[after + 2 * k] + BAND, spots[after + 2 * k + 1]
+            put(top, left, from_next[k, channel].astype(F32))
+            top, left = spots[before + 2 * k] - HALF, spots[before + 2 * k + 1]
+            put(top, left, from_prev[k, channel].astype(F32))
         copies.append(
             pltpu.make_async_copy(
                 total.at[channel, pl.ds(HALF, BAND)], output.at[0, channel], sems.at[channel]
@@ -328,30 +377,34 @@
     wave = jnp.stack([jnp.cos(prop_phase), jnp.sin(prop_phase)])
     half = arr(2, HALF, SIDE)
 
-    inband, low, high = call(
-        inband_kernel, "inband", [scan_rows, scan_cols, objects],
-        [arr(3, 2, HALF, SIDE), arr(2, HALF, COLS), arr(2, HALF, COLS)],
-        [pltpu.SMEM((4,), jnp.int32), pltpu.SMEM((4,), jnp.int32), pltpu.VMEM((2, BAND, COLS), F32),
-         pltpu.SemaphoreType.DMA((4,))],
-        in_specs=[HB] * 3, vmem=56,
-    )
-    above = move(high, "next")
-    below = move(low, "prev")
+    inband, early, late, band, rows, cols = call(
+        inband_kernel, "inband",
+        [pltpu.with_memory_space_constraint(x, pltpu.HBM) for x in (scan_rows, scan_cols, objects)],
+        [arr(3, 2, HALF, SIDE), arr(EDGE + 16, 128), arr(EDGE + 16, 128),
+         arr(2, BAND, COLS, dtype=F32), arr(4, dtype=jnp.int32), arr(4, dtype=jnp.int32)],
+        [pltpu.SemaphoreType.DMA((4,))],
+        in_specs=[HB] * 3, out_specs=[VM] * 4 + [SM] * 2, vmem=50,
+    )
+    early = move(early, "early")
+    late = move(late, "late")
     mate_inband = move(inband, "mate")
-    half0, half12, windows = call(
-        outer_kernel, "outer", [scan_rows, scan_cols, objects, above, below],
-        [half, arr(2, 2, HALF, SIDE), arr(3, 2, SIDE, SIDE)],
+    (half0,) = call(
+        first_kernel, "first", [rows, cols, band, early], [half],
+        [pltpu.VMEM((2, BAND, COLS), F32)],
+    )
+    mate0 = move(half0, "mate")
+    half12, windows = call(
+        outer_kernel, "outer", [rows, cols, band, early, late],
+        [arr(2, 2, HALF, SIDE), arr(3, 2, SIDE, SIDE)],
         [pltpu.VMEM((2, EXT, COLS), F32)],
     )
-    mate0 = move(half0, "mate")
     mate12 = move(half12, "mate")
-    scan, half0 = lax.optimization_barrier((jnp.concatenate([scan_rows, scan_cols]), half0))
-    before = move(scan, "next")
-    after = move(scan, "prev")
-    mate0, before, after = lax.optimization_barrier((mate0, before, after))
+    (spots,) = call(
+        decode_kernel, "decode", [early, late], [arr(8, dtype=jnp.int32)], out_specs=[SM]
+    )
     sent_outer, sent_inband, solo, edge = call(
         solo_kernel, "solo",
-        [scan_rows, probe_choice, windows, mate_inband, mate0, probes, amplitudes, wave, first, second],
+        [rows, probe_choice, windows, mate_inband, mate0, probes, amplitudes, wave, first, second],
         [half, half, arr(2, SIDE, SIDE, dtype=F32), half],
         [pltpu.VMEM((2, 2, SIDE, SIDE), BF), pltpu.VMEM((2, 2, SIDE, SIDE), F32)],
     )
@@ -359,7 +412,7 @@
     from_inband = move(sent_inband, "mate")
     shared, up, down = call(
         shared_kernel, "shared",
-        [scan_rows, probe_choice, windows, mate_inband, mate12, probes, amplitudes, wave, first, second],
+        [rows, probe_choice, windows, mate_inband, mate12, probes, amplitudes, wave, first, second],
         [arr(2, 2, SIDE, SIDE, dtype=F32), half, half],
         [pltpu.VMEM((2, 2, 2, SIDE, SIDE), BF), pltpu.VMEM((2, 2, 2, SIDE, SIDE), F32)],
     )
@@ -369,16 +422,16 @@
     from_next = move(to_prev, "prev")
     from_prev = move(to_next, "next")
     (total,) = call(
-        own_kernel, "own", [scan_rows, scan_cols, solo, shared, from_inband],
+        own_kernel, "own", [rows, cols, solo, shared, from_inband],
         [arr(2, EXT, COLS, dtype=F32)], flops=10**11,
     )
     _, gradient = call(
         rest_kernel, "rest",
-        [scan_rows, scan_cols, after, before, total, from_outer, from_next, from_prev],
+        [rows, cols, spots, total, from_outer, from_next, from_prev],
         [arr(2, EXT, COLS, dtype=F32), arr(1, 2, BAND, COLS, dtype=F32)],
         [pltpu.SemaphoreType.DMA((2,))],
         out_specs=[VM, HB],
-        aliases={4: 0},
+        aliases={3: 0},
     )
     return gradient
 

time: 92.1 us -> 86.7 us (0.941); the launches traced: 90.7 us -> 86.4 us
  waiting for transfers between devices: 27.7 us -> 25.3 us
  local copies, waits for them, and re-layouts: 3.19 us -> 1 us
    ppermute x11 -> x9, waiting for transfers between devices: 27.7 us -> 25.3 us  [shards(): move = lambda x, way: lax.ppermute(x, AXES, route[way])]
    unnamed x16 -> x12, local copies, waits for them, and re-layouts: 1.33 us -> 0.04 us
    pallas_call x7 -> x9, Pallas kernels: 21 us -> 21.8 us  [call(): pl.pallas_call(kernel, name=name, out_shape=outputs, in_specs=in_specs or...]
    ppermute x11 -> x9, starting transfers between devices: 38.3 us -> 37.8 us  [shards(): move = lambda x, way: lax.ppermute(x, AXES, route[way])]
  transfers between devices with their start and end apart: 11 -> 9, of which waited for: 6 -> 5; matrix products, arithmetic and copies ran while one was open for 2% -> 1% of each run, Pallas kernels for 17% -> 20%
where the time goes in v3:
time: 86.7 us; the launch traced here: 86.4 us
  starting transfers between devices  37.8 us (44%)
  waiting for transfers between devices  25.3 us (29%)
  Pallas kernels  21.8 us (25%)
  local copies, waits for them, and re-layouts  1 us (1%)
    ppermute x9, starting transfers between devices, shards(): move = lambda x, way: lax.ppermute(x, AXES, route[way])  37.8 us
    ppermute x9, waiting for transfers between devices, shards(): move = lambda x, way: lax.ppermute(x, AXES, route[way])  25.3 us
    pallas_call x9, Pallas kernels, call(): pl.pallas_call(kernel, name=name, out_shape=outputs, in_specs=in_specs or...  21.8 us
  transfers between devices with their start and end apart: 9, of which 5 were waited for; matrix products, arithmetic and copies ran while one was open for 1% of the time, Pallas kernels for 20%

profile of v3, /device:TPU:8, one launch (start us, length us, event | category | flops | bytes accessed | tf_op | source)
XLA Modules:
  0.0 86.4 jit_solution(12297949867883211107)
XLA Ops:
  0.0 2.4 %inband.1 = (bf16[3,2,128,256]{3,2,1,0:T(8,128)(2,1)S(1)}, bf16[2064,128]{1,0:T(8,128)(2,1)S(1)}, bf16[2064,128]{1,0:T(8,128)(2,1)S(1)}, f32[2,256,1024]{2,1,0:T...) custom-call(s32[4]{0:T(128)} %rows_in.1, s32[4]{0:T(128)} %cols_in.1, f32[1,2,256,1024]{3,2,1,0:T(8,128)} %objects_in.1), custom_call_target="tpu_custom_call" | custom-call | flops 1 | bytes 1 | tf_op jit(solution)/shard_map/inband/pallas_call | solution.py:356
  2.4 6.2 %collective-permute-start = (bf16[2064,128]{1,0:T(8,128)(2,1)S(1)}, bf16[2064,128]{1,0:T(8,128)(2,1)S(1)}, u32[]{:S(2)}, u32[]{:S(2)}) collective-permute-start(bf16[2064,128]{1,0:T(8,128)(2,1)S(1)} %get-tuple-element.25), channel_id=1, source_target_pairs={{0,127},{1,0},{2,1},{3,2},{4,3},{5,4},{6,5},{7,6},{8,7},{9,8},{10,... | collective-permute-start | bytes 1585160 | tf_op jit(solution)/shard_map/ppermute | solution.py:375
  8.6 7.6 %collective-permute-start.2 = (bf16[3,2,128,256]{3,2,1,0:T(8,128)(2,1)S(1)}, bf16[3,2,128,256]{3,2,1,0:T(8,128)(2,1)S(1)}, u32[]{:S(2)}, u32[]{:S(2)}) collective-permute-start(bf16[3,2,128,256]{3,2,1,0:T(8,128)(2,1)S(1)} %get-tuple-element.29), channel_id=1, source_target_pairs={{0,128},{1,129},{2,130},{3,131},{4,132},{5,133},{6,134},{7,135},{8... | collective-permute-start | bytes 1179656 | tf_op jit(solution)/shard_map/ppermute | solution.py:375
  16.2 8.5 %collective-permute-done.early = bf16[2064,128]{1,0:T(8,128)(2,1)S(1)} collective-permute-done((bf16[2064,128]{1,0:T(8,128)(2,1)S(1)}, bf16[2064,128]{1,0:T(8,128)(2,1)S(1)}, u32[]{:S(2)}, u32[]{:S(2)}) %collective-permute-start) | collective-permute-done | bytes 528416 | tf_op jit(solution)/shard_map/ppermute | solution.py:375
  24.7 0.9 %first.3 = bf16[2,128,256]{2,1,0:T(8,128)(2,1)S(1)} custom-call(s32[4]{0:T(128)S(1)} %get-tuple-element.23.rows, s32[4]{0:T(128)S(1)} %get-tuple-element.24.cols, f32[2,256,1024]{2,1,0:T(8,128)S(1)} %get-tuple-element.27.objects, bf16[2064,128]{1,0:T(8,128)(2,1)S(1)} %collective-permute-done.early), custom_call_target="tpu_custom_call" | custom-call | flops 1 | bytes 1 | tf_op jit(solution)/shard_map/first/pallas_call | solution.py:356
  25.6 0.0 copy-start.2
  25.6 0.0 copy-start.3
  25.7 17.3 %collective-permute-start.3 = (bf16[2,128,256]{2,1,0:T(8,128)(2,1)S(1)}, bf16[2,128,256]{2,1,0:T(8,128)(2,1)S(1)}, u32[]{:S(2)}, u32[]{:S(2)}) collective-permute-start(bf16[2,128,256]{2,1,0:T(8,128)(2,1)S(1)} %first.3), channel_id=1, source_target_pairs={{0,128},{1,129},{2,130},{3,131},{4,132},{5,133},{6,134},{7,135},{8... | collective-permute-start | bytes 393224 | tf_op jit(solution)/shard_map/ppermute | solution.py:375
  43.0 2.0 %outer.1 = (bf16[2,2,128,256]{3,2,1,0:T(8,128)(2,1)S(1)}, bf16[3,2,256,256]{3,2,1,0:T(8,128)(2,1)S(1)}) custom-call(s32[4]{0:T(128)S(1)} %get-tuple-element.23.rows, s32[4]{0:T(128)S(1)} %get-tuple-element.24.cols, f32[2,256,1024]{2,1,0:T(8,128)S(1)} %get-tuple-element.27.objects, bf16[2064,128]{1,0:T(8,128)(2,1)S(1)} %collective-permute-done.early, ...), custom_call_target="tpu_custom_call" | custom-call | flops 1 | bytes 1 | tf_op jit(solution)/shard_map/outer/pallas_call | solution.py:356
  45.0 0.1 collective-permute-start.4
  45.1 1.0 %cosine_bitcast_fusion = (f32[1,256,256]{2,1,0:T(8,128)S(1)}, f32[1,256,256]{2,1,0:T(8,128)S(1)}) fusion(f32[256,256]{1,0:T(8,128)S(1)} %copy-done.5), kind=kLoop, calls=%fused_computation.2 | loop fusion | bytes 786432 | tf_op jit(solution)/shard_map/stack | solution.py:377
  46.2 9.4 %collective-permute-done.3.outer = bf16[2,128,256]{2,1,0:T(8,128)(2,1)S(1)} collective-permute-done((bf16[2,128,256]{2,1,0:T(8,128)(2,1)S(1)}, bf16[2,128,256]{2,1,0:T(8,128)(2,1)S(1)}, u32[]{:S(2)}, u32[]{:S(2)}) %collective-permute-start.3) | collective-permute-done | bytes 131104 | tf_op jit(solution)/shard_map/ppermute | solution.py:375
  55.6 4.9 %solo.1 = (bf16[2,128,256]{2,1,0:T(8,128)(2,1)S(1)}, bf16[2,128,256]{2,1,0:T(8,128)(2,1)S(1)}, f32[2,256,256]{2,1,0:T(8,128)S(1)}, bf16[2,128,256]{2,1,0:T(8,128)(2,1)S(1)}) custom-call(s32[4]{0:T(128)S(1)} %get-tuple-element.23.rows, s32[4]{0:T(128)S(1)} %copy-done.4, bf16[3,2,256,256]{3,2,1,0:T(8,128)(2,1)S(1)} %get-tuple-element.28.windows, ...), custom_call_target="tpu_custom_call" | custom-call | flops 1 | bytes 1 | tf_op jit(solution)/shard_map/solo/pallas_call | solution.py:356
  60.4 4.5 %collective-permute-start.6 = (bf16[2,128,256]{2,1,0:T(8,128)(2,1)S(1)}, bf16[2,128,256]{2,1,0:T(8,128)(2,1)S(1)}, u32[]{:S(2)}, u32[]{:S(2)}) collective-permute-start(bf16[2,128,256]{2,1,0:T(8,128)(2,1)S(1)} %get-tuple-element.34), channel_id=1, source_target_pairs={{0,128},{1,129},{2,130},{3,131},{4,132},{5,133},{6,134},{7,135},{8... | collective-permute-start | bytes 393224 | tf_op jit(solution)/shard_map/ppermute | solution.py:375
  64.9 1.5 %collective-permute-start.5 = (bf16[2,128,256]{2,1,0:T(8,128)(2,1)S(1)}, bf16[2,128,256]{2,1,0:T(8,128)(2,1)S(1)}, u32[]{:S(2)}, u32[]{:S(2)}) collective-permute-start(bf16[2,128,256]{2,1,0:T(8,128)(2,1)S(1)} %get-tuple-element.33), channel_id=1, source_target_pairs={{0,128},{1,129},{2,130},{3,131},{4,132},{5,133},{6,134},{7,135},{8... | collective-permute-start | bytes 393224 | tf_op jit(solution)/shard_map/ppermute | solution.py:375
  66.5 0.7 decode.1.spots
  67.2 5.6 %shared.1 = (f32[2,2,256,256]{3,2,1,0:T(8,128)S(1)}, bf16[2,128,256]{2,1,0:T(8,128)(2,1)S(1)}, bf16[2,128,256]{2,1,0:T(8,128)(2,1)S(1)}) custom-call(s32[4]{0:T(128)S(1)} %get-tuple-element.23.rows, s32[4]{0:T(128)S(1)} %copy-done.4, bf16[3,2,256,256]{3,2,1,0:T(8,128)(2,1)S(1)} %get-tuple-element.28.windows, ...), custom_call_target="tpu_custom_call" | custom-call | flops 1 | bytes 1 | tf_op jit(solution)/shard_map/shared/pallas_call | solution.py:356
  72.8 0.1 collective-permute-start.7
  72.9 0.5 collective-permute-start.8
  73.4 0.5 collective-permute-done.5.from_inband
  73.9 2.7 %own.1.given = f32[2,512,1024]{2,1,0:T(8,128)S(1)} custom-call(s32[4]{0:T(128)S(1)} %get-tuple-element.23.rows, s32[4]{0:T(128)S(1)} %get-tuple-element.24.cols, f32[2,256,256]{2,1,0:T(8,128)S(1)} %get-tuple-element.30.solo, f32[2,2,256,256]{3,2,1,0:T(8,128)S(1)} %get-tuple-element.32.shared, bf16[2,128,256]{2,1,0:T(8,128)(2,1)S(1)} %collective-permute-done.5.from_inband), custom_call_target="tpu_custom_call" | custom-call | flops 99999997952 | bytes 1 | tf_op jit(solution)/shard_map/own/pallas_call | solution.py:356
  76.6 2.8 %collective-permute-done.7.from_next = bf16[2,2,128,256]{3,2,1,0:T(8,128)(2,1)S(1)} collective-permute-done((bf16[2,2,128,256]{3,2,1,0:T(8,128)(2,1)S(1)}, bf16[2,2,128,256]{3,2,1,0:T(8,128)(2,1)S(1)}, u32[]{:S(2)}, u32[]{:S(2)}) %collective-permute-start.7) | collective-permute-done | bytes 262176 | tf_op jit(solution)/shard_map/ppermute | solution.py:375
  79.4 4.2 %collective-permute-done.8.from_prev = bf16[2,2,128,256]{3,2,1,0:T(8,128)(2,1)S(1)} collective-permute-done((bf16[2,2,128,256]{3,2,1,0:T(8,128)(2,1)S(1)}, bf16[2,2,128,256]{3,2,1,0:T(8,128)(2,1)S(1)}, u32[]{:S(2)}, u32[]{:S(2)}) %collective-permute-start.8) | collective-permute-done | bytes 262176 | tf_op jit(solution)/shard_map/ppermute | solution.py:375
  83.6 2.6 %rest.1 = (f32[2,512,1024]{2,1,0:T(8,128)S(1)}, f32[1,2,256,1024]{3,2,1,0:T(8,128)}) custom-call(s32[4]{0:T(128)S(1)} %get-tuple-element.23.rows, s32[4]{0:T(128)S(1)} %get-tuple-element.24.cols, s32[8]{0:T(128)S(1)} %decode.1.spots, f32[2,512,1024]{2,1,0:T(8,128)S(1)} %own.1.given, ...), custom_call_target="tpu_custom_call", output_to_operand_aliasing={{0}: (3, {})} | custom-call | flops 1 | bytes 1 | tf_op jit(solution)/shard_map/rest/pallas_call | solution.py:356
  (17 shorter events, 0.1 us)
Async XLA Ops:
  2.4 22.3 %collective-permute-start = (bf16[2064,128]{1,0:T(8,128)(2,1)S(1)}, bf16[2064,128]{1,0:T(8,128)(2,1)S(1)}, u32[]{:S(2)}, u32[]{:S(2)}) collective-permute-start(bf16[2064,128]{1,0:T(8,128)(2,1)S(1)} %get-tuple-element.25), channel_id=1, source_target_pairs={{0,127},{1,0},{2,1},{3,2},{4,3},{5,4},{6,5},{7,6},{8,7},{9,8},{10,... | collective-permute-start | bytes 1585160 | tf_op jit(solution)/shard_map/ppermute | solution.py:375
  8.6 34.4 %collective-permute-start.1 = (bf16[2064,128]{1,0:T(8,128)(2,1)S(1)}, bf16[2064,128]{1,0:T(8,128)(2,1)S(1)}, u32[]{:S(2)}, u32[]{:S(2)}) collective-permute-start(bf16[2064,128]{1,0:T(8,128)(2,1)S(1)} %get-tuple-element.26), channel_id=1, source_target_pairs={{0,1},{1,2},{2,3},{3,4},{4,5},{5,6},{6,7},{7,8},{8,9},{9,10},{10,1... | collective-permute-start | bytes 1585160 | tf_op jit(solution)/shard_map/ppermute | solution.py:375
  8.6 37.5 %collective-permute-start.2 = (bf16[3,2,128,256]{3,2,1,0:T(8,128)(2,1)S(1)}, bf16[3,2,128,256]{3,2,1,0:T(8,128)(2,1)S(1)}, u32[]{:S(2)}, u32[]{:S(2)}) collective-permute-start(bf16[3,2,128,256]{3,2,1,0:T(8,128)(2,1)S(1)} %get-tuple-element.29), channel_id=1, source_target_pairs={{0,128},{1,129},{2,130},{3,131},{4,132},{5,133},{6,134},{7,135},{8... | collective-permute-start | bytes 1179656 | tf_op jit(solution)/shard_map/ppermute | solution.py:375
  24.7 20.5 %copy-start.5 = (f32[256,256]{1,0:T(8,128)S(1)}, f32[256,256]{1,0:T(8,128)}, u32[]{:S(2)}) copy-start(f32[256,256]{1,0:T(8,128)} %param.12) | copy-start | bytes 786436
  25.6 29.9 %copy-start = (bf16[4,2,256,256]{3,2,1,0:T(8,128)(2,1)S(1)}, bf16[4,2,256,256]{3,2,1,0:T(8,128)(2,1)}, u32[]{:S(2)}) copy-start(bf16[4,2,256,256]{3,2,1,0:T(8,128)(2,1)} %probes.3) | copy-start | bytes 3145732
  25.6 29.9 %copy-start.1 = (f32[4,256,256]{2,1,0:T(8,128)S(1)}, f32[4,256,256]{2,1,0:T(8,128)}, u32[]{:S(2)}) copy-start(f32[4,256,256]{2,1,0:T(8,128)} %amplitudes.3) | copy-start | bytes 3145732
  25.6 29.9 %copy-start.2 = (bf16[512,512]{1,0:T(8,128)(2,1)S(1)}, bf16[512,512]{1,0:T(8,128)(2,1)}, u32[]{:S(2)}) copy-start(bf16[512,512]{1,0:T(8,128)(2,1)} %constant.5.clone.second) | copy-start | bytes 1572868
  25.6 29.9 %copy-start.3 = (bf16[512,512]{1,0:T(8,128)(2,1)S(1)}, bf16[512,512]{1,0:T(8,128)(2,1)}, u32[]{:S(2)}) copy-start(bf16[512,512]{1,0:T(8,128)(2,1)} %constant.4.clone.first) | copy-start | bytes 1572868
  25.7 29.9 %copy-start.4 = (s32[4]{0:T(128)S(1)}, s32[4]{0:T(128)}, u32[]{:S(2)}) copy-start(s32[4]{0:T(128)} %picks.3) | copy-start | bytes 52
  25.7 29.9 %collective-permute-start.3 = (bf16[2,128,256]{2,1,0:T(8,128)(2,1)S(1)}, bf16[2,128,256]{2,1,0:T(8,128)(2,1)S(1)}, u32[]{:S(2)}, u32[]{:S(2)}) collective-permute-start(bf16[2,128,256]{2,1,0:T(8,128)(2,1)S(1)} %first.3), channel_id=1, source_target_pairs={{0,128},{1,129},{2,130},{3,131},{4,132},{5,133},{6,134},{7,135},{8... | collective-permute-start | bytes 393224 | tf_op jit(solution)/shard_map/ppermute | solution.py:375
  45.0 22.2 %collective-permute-start.4 = (bf16[2,2,128,256]{3,2,1,0:T(8,128)(2,1)S(1)}, bf16[2,2,128,256]{3,2,1,0:T(8,128)(2,1)S(1)}, u32[]{:S(2)}, u32[]{:S(2)}) collective-permute-start(bf16[2,2,128,256]{3,2,1,0:T(8,128)(2,1)S(1)} %get-tuple-element.31), channel_id=1, source_target_pairs={{0,128},{1,129},{2,130},{3,131},{4,132},{5,133},{6,134},{7,135},{8... | collective-permute-start | bytes 786440 | tf_op jit(solution)/shard_map/ppermute | solution.py:375
  60.4 12.3 %collective-permute-start.6 = (bf16[2,128,256]{2,1,0:T(8,128)(2,1)S(1)}, bf16[2,128,256]{2,1,0:T(8,128)(2,1)S(1)}, u32[]{:S(2)}, u32[]{:S(2)}) collective-permute-start(bf16[2,128,256]{2,1,0:T(8,128)(2,1)S(1)} %get-tuple-element.34), channel_id=1, source_target_pairs={{0,128},{1,129},{2,130},{3,131},{4,132},{5,133},{6,134},{7,135},{8... | collective-permute-start | bytes 393224 | tf_op jit(solution)/shard_map/ppermute | solution.py:375
  64.9 9.0 %collective-permute-start.5 = (bf16[2,128,256]{2,1,0:T(8,128)(2,1)S(1)}, bf16[2,128,256]{2,1,0:T(8,128)(2,1)S(1)}, u32[]{:S(2)}, u32[]{:S(2)}) collective-permute-start(bf16[2,128,256]{2,1,0:T(8,128)(2,1)S(1)} %get-tuple-element.33), channel_id=1, source_target_pairs={{0,128},{1,129},{2,130},{3,131},{4,132},{5,133},{6,134},{7,135},{8... | collective-permute-start | bytes 393224 | tf_op jit(solution)/shard_map/ppermute | solution.py:375
  72.8 6.6 %collective-permute-start.7 = (bf16[2,2,128,256]{3,2,1,0:T(8,128)(2,1)S(1)}, bf16[2,2,128,256]{3,2,1,0:T(8,128)(2,1)S(1)}, u32[]{:S(2)}, u32[]{:S(2)}) collective-permute-start(bf16[2,2,128,256]{3,2,1,0:T(8,128)(2,1)S(1)} %get-tuple-element.38), channel_id=1, source_target_pairs={{0,127},{1,0},{2,1},{3,2},{4,3},{5,4},{6,5},{7,6},{8,7},{9,8},{10,... | collective-permute-start | bytes 786440 | tf_op jit(solution)/shard_map/ppermute | solution.py:375
  72.9 10.7 %collective-permute-start.8 = (bf16[2,2,128,256]{3,2,1,0:T(8,128)(2,1)S(1)}, bf16[2,2,128,256]{3,2,1,0:T(8,128)(2,1)S(1)}, u32[]{:S(2)}, u32[]{:S(2)}) collective-permute-start(bf16[2,2,128,256]{3,2,1,0:T(8,128)(2,1)S(1)} %get-tuple-element.39), channel_id=1, source_target_pairs={{0,1},{1,2},{2,3},{3,4},{4,5},{5,6},{6,7},{7,8},{8,9},{9,10},{10,1... | collective-permute-start | bytes 786440 | tf_op jit(solution)/shard_map/ppermute | solution.py:375

commit v4 on v3

v4 whole, which is shorter than its diff:
```python
import functools

import jax
import jax.numpy as jnp
import ml_dtypes
import numpy as np
from jax import lax
from jax.experimental import pallas as pl
from jax.experimental.pallas import tpu as pltpu
from jax.sharding import PartitionSpec as P

modulus_floor = 0.25
AXES = ("cuts", "region")
BF = jnp.bfloat16
F32 = jnp.float32
SIDE = 256
HALF = 128
BAND = 256
COLS = 1024
EXT = BAND + 2 * HALF
EDGE = 2 * HALF * COLS // 128
WIDE = SIDE + 128
VM = pl.BlockSpec(memory_space=pltpu.VMEM)
SM = pl.BlockSpec(memory_space=pltpu.SMEM)
HB = pl.BlockSpec(memory_space=pltpu.HBM)


def routes(regions):
    at = lambda c, r: c * regions + r % regions
    both = [(c, r) for c in range(2) for r in range(regions)]
    return {
        "mate": [(at(c, r), at(1 - c, r)) for c, r in both],
        "early": [(at(c, r), at(c, r - 1 if c == 0 else r + 1)) for c, r in both],
        "late": [(at(c, r), at(c, r + 1 if c == 0 else r - 1)) for c, r in both],
    }


def dft_blocks():
    index = np.arange(SIDE)
    angles = (index[:, None] * index[None, :] % SIDE) * (2.0 * np.pi / SIDE)
    real = np.cos(angles) / np.sqrt(SIDE)
    imag = -np.sin(angles) / np.sqrt(SIDE)
    first = np.block([[real, -imag], [imag, real]]).astype(ml_dtypes.bfloat16)
    second = np.block([[real, imag], [-imag, real]]).astype(ml_dtypes.bfloat16)
    return first, second


def places(rows):
    up = [rows[i] < 0 for i in range(4)]
    first = lambda a, b: jnp.where(a, 0, jnp.where(b, 1, 2))
    last = lambda a, b: jnp.where(a, 3, jnp.where(b, 2, 1))
    no = [jnp.logical_not(u) for u in up]
    return first(up[0], up[1]), last(up[3], up[2]), first(no[0], no[1]), last(no[3], no[2])


def column_split(left):
    base = jnp.minimum(lax.shift_right_logical(left, 7), (COLS - WIDE) // 128) * 128
    return pl.multiple_of(base, 128), left - base


def row_split(top, most):
    base = jnp.minimum(lax.shift_right_logical(top, 3), most // 8) * 8
    return pl.multiple_of(base, 8), top - base


def cut_window(load, top, left, count, total):
    row_base, row_shift = row_split(top, total - count - 8)
    col_base, col_shift = column_split(left)
    block = load(pl.ds(row_base, count + 8), pl.ds(col_base, WIDE))
    block = pltpu.roll(block, lax.rem(count + 8 - row_shift, count + 8), 0)[:count]
    return pltpu.roll(block, lax.rem(WIDE - col_shift, WIDE), 1)[:, :SIDE]


def put_window(total_ref, channel, top, left, block):
    count = block.shape[0]
    row_base, row_shift = row_split(top, EXT - count - 8)
    col_base, col_shift = column_split(left)
    block = jnp.concatenate([block, jnp.zeros((count, WIDE - SIDE), F32)], axis=1)
    block = pltpu.roll(block, col_shift, 1)
    block = jnp.concatenate([block, jnp.zeros((8, WIDE), F32)], axis=0)
    block = pltpu.roll(block, row_shift, 0)
    where = (channel, pl.ds(row_base, count + 8), pl.ds(col_base, WIDE))
    total_ref[where] = total_ref[where] + block


def tagged(rows, cols, spots):
    line = lax.broadcasted_iota(jnp.int32, (16, 128), 0)
    lane = lax.broadcasted_iota(jnp.int32, (16, 128), 1)
    tile = jnp.zeros((16, 128), jnp.int32)
    for k, spot in enumerate(spots):
        left = cols[spot]
        parts = (rows[spot] + HALF, lax.shift_right_logical(left, 3), jnp.bitwise_and(left, 7))
        for n, part in enumerate(parts):
            tile = jnp.where((line == k) & (lane == n), part, tile)
    return tile.astype(F32).astype(BF)


def edge_kernel(rows_in, cols_in, objects_in, early, late, objects, rows, cols, sems):
    cut = lax.axis_index("cuts")
    copies = [
        pltpu.make_async_copy(rows_in, rows, sems.at[0]),
        pltpu.make_async_copy(cols_in, cols, sems.at[1]),
        pltpu.make_async_copy(objects_in.at[0, 0], objects.at[0], sems.at[2]),
        pltpu.make_async_copy(objects_in.at[0, 1], objects.at[1], sems.at[3]),
    ]
    for copy in copies:
        copy.start()
    copies[0].wait()
    copies[1].wait()
    u0, u1, l0, l1 = places(rows)
    up = cut == 0
    early[EDGE:] = tagged(rows, cols, (jnp.where(up, u0, l0), jnp.where(up, u1, l1)))
    late[EDGE:] = tagged(rows, cols, (jnp.where(up, l0, u0), jnp.where(up, l1, u1)))
    start = pl.multiple_of(jnp.where(up, 0, HALF), HALF)
    for channel in range(2):
        copies[2 + channel].wait()
        for k in range(COLS // 128):
            where = pl.ds((channel * (COLS // 128) + k) * HALF, HALF)
            lanes = slice(128 * k, 128 * (k + 1))
            early[where] = objects[channel, pl.ds(start, HALF), lanes].astype(BF)
            late[where] = objects[channel, pl.ds(HALF - start, HALF), lanes].astype(BF)


def cut_pair(rows, cols, objects, edge, lower, spots, outputs, near):
    start = pl.multiple_of(jnp.where(lower, BAND, 0), HALF)
    own = pl.multiple_of(jnp.where(lower, 0, HALF), HALF)
    for channel in range(2):
        for k in range(COLS // 128):
            near[channel, pl.ds(start, HALF), 128 * k : 128 * (k + 1)] = edge[
                pl.ds((channel * (COLS // 128) + k) * HALF, HALF)
            ].astype(F32)
        near[channel, pl.ds(own, BAND)] = objects[channel]
        for spot, output in zip(spots, outputs):
            output[channel] = cut_window(
                lambda r, c: near[channel, r, c], rows[spot] + own, cols[spot], SIDE, BAND + HALF
            ).astype(BF)


def mate_kernel(rows, cols, objects, early, window0, window1, near):
    lower = lax.axis_index("cuts") == 0
    u0, u1, l0, l1 = places(rows)
    spots = jnp.where(lower, l0, u0), jnp.where(lower, l1, u1)
    cut_pair(rows, cols, objects, early, lower, spots, (window0, window1), near)


def own_windows_kernel(rows, cols, objects, early, late, window0, window1, spots, near):
    lower = lax.axis_index("cuts") == 1
    u0, u1, l0, l1 = places(rows)
    mine = jnp.where(lower, l0, u0), jnp.where(lower, l1, u1)
    cut_pair(rows, cols, objects, late, lower, mine, (window0, window1), near)
    decode(early, late, spots)


def decode(early, late, spots):
    line = lax.broadcasted_iota(jnp.int32, (16, 128), 0)
    lane = lax.broadcasted_iota(jnp.int32, (16, 128), 1)
    for n, edge in enumerate((early, late)):
        tile = edge[EDGE:].astype(F32)
        left = jnp.where(lane == 1, tile * 8.0, jnp.where(lane == 2, tile, 0.0))
        top = jnp.where(lane == 0, tile, 0.0)
        for k in range(2):
            for m, part in enumerate((top, left)):
                spots[4 * n + 2 * k + m] = jnp.sum(jnp.where(line == k, part, 0.0)).astype(jnp.int32)


def transform(fields, left, right):
    count = len(fields)
    stacked = jnp.concatenate(
        [jnp.concatenate([f[part].astype(BF) for f in fields], axis=1) for part in range(2)], axis=0
    )
    middle = jnp.dot(left, stacked, preferred_element_type=F32).astype(BF)
    spans = [slice(SIDE * k, SIDE * (k + 1)) for k in range(count)]
    middle = jnp.concatenate(
        [jnp.concatenate([middle[:SIDE, s], middle[SIDE:, s]], axis=1) for s in spans], axis=0
    )
    result = jnp.dot(middle, right, preferred_element_type=F32)
    return [(result[s, :SIDE], result[s, SIDE:]) for s in spans]


def times(a, b):
    return a[0] * b[0] - a[1] * b[1], a[0] * b[1] + a[1] * b[0]


def conj_times(a, b):
    return a[0] * b[0] + a[1] * b[1], a[0] * b[1] - a[1] * b[0]


def wide(pair):
    return pair[0].astype(F32), pair[1].astype(F32)


def chain(incoming, patches, measured, wave, first, second, store):
    spots = range(len(incoming))
    propagator = (wave[0], wave[1])
    fields = [times(wide(incoming[k]()), patches[k](0)) for k in spots]
    fields = [times(propagator, f) for f in transform(fields, first, second)]
    psi = [(f[0].astype(BF), f[1].astype(BF)) for f in transform(fields, second, first)]
    fields = [times(wide(psi[k]), patches[k](1)) for k in spots]
    detected = []
    for k, (real, imag) in enumerate(transform(fields, first, second)):
        modulus = jnp.sqrt(real * real + imag * imag)
        factor = 1.0 - measured[k]() / jnp.maximum(modulus, modulus_floor)
        detected.append((real * factor, imag * factor))
    arriving = [(f[0].astype(BF), f[1].astype(BF)) for f in transform(detected, second, first)]
    arriving = [wide(f) for f in arriving]
    for k in spots:
        store(k, 1, conj_times(wide(psi[k]), arriving[k]))
    fields = [conj_times(patches[k](1), arriving[k]) for k in spots]
    fields = [conj_times(propagator, f) for f in transform(fields, first, second)]
    for k, (real, imag) in enumerate(transform(fields, second, first)):
        arrived = real.astype(BF).astype(F32), imag.astype(BF).astype(F32)
        store(k, 0, conj_times(wide(incoming[k]()), arrived))


def solo_kernel(
    number, rows, picks, own, mate, probes, amplitudes, wave, first, second, *refs
):
    if number == 0:
        sent_outer, sent_inband, kept, edge, held, made = refs
        edges = edge
    else:
        before, sent_outer, sent_inband, kept, both, held, made = refs
        both[0] = before[...]
        edges = both.at[1]
    cut = lax.axis_index("cuts")
    spots = places(rows)
    place = jnp.where(cut == 0, spots[number], spots[2 + number])
    start = pl.multiple_of(jnp.where(cut == 0, 0, HALF), HALF)
    held[cut] = own[...]
    held[1 - cut] = mate[...]

    def store(k, which, value):
        made[which, 0], made[which, 1] = value

    chain(
        [lambda: (probes[picks[place], 0], probes[picks[place], 1])],
        [lambda which: wide((held[which, 0], held[which, 1]))],
        [lambda: amplitudes[place]],
        wave, first[...], second[...], store,
    )
    for channel in range(2):
        sent_outer[channel] = made[1 - cut, channel, pl.ds(start, HALF)].astype(BF)
        sent_inband[channel] = made[1 - cut, channel, pl.ds(HALF - start, HALF)].astype(BF)
        kept[channel] = made[cut, channel]
        edges[channel] = made[cut, channel, pl.ds(start, HALF)].astype(BF)


def put_mate(put, rows, cols, number, outer, inband, channel):
    upper = lax.axis_index("cuts") == 1
    spots = places(rows)
    spot = jnp.where(upper, spots[number], spots[2 + number])
    start = jnp.where(upper, 0, HALF)
    put(rows[spot] + HALF + start, cols[spot], outer[channel].astype(F32))
    put(rows[spot] + 2 * HALF - start, cols[spot], inband[channel].astype(F32))


def own_kernel(rows, cols, kept0, kept1, outer, inband, total):
    cut = lax.axis_index("cuts")
    places_here = places(rows)
    total[...] = jnp.zeros_like(total)
    for channel in range(2):
        put = functools.partial(put_window, total, channel)
        for number, kept in enumerate((kept0, kept1)):
            spot = jnp.where(cut == 0, places_here[number], places_here[2 + number])
            put(rows[spot] + HALF, cols[spot], kept[channel])
        put_mate(put, rows, cols, 0, outer, inband, channel)


def rest_kernel(
    rows, cols, spots, given, outer, inband, edges, relay0, relay1, total, output, sems
):
    cut = lax.axis_index("cuts")
    shift = jnp.where(cut == 0, BAND, -HALF)
    copies = []
    for channel in range(2):
        put = functools.partial(put_window, total, channel)
        put_mate(put, rows, cols, 1, outer, inband, channel)
        for number, relay in enumerate((relay0, relay1)):
            k = 2 * number
            put(spots[k] + shift, spots[k + 1], edges[number, channel].astype(F32))
            put(spots[4 + k] + BAND - HALF - shift, spots[5 + k], relay[channel].astype(F32))
        copies.append(
            pltpu.make_async_copy(
                total.at[channel, pl.ds(HALF, BAND)], output.at[0, channel], sems.at[channel]
            )
        )
        copies[channel].start()
    for copy in copies:
        copy.wait()


def call(kernel, name, inputs, outputs, scratch=(), in_specs=None, out_specs=None, aliases={}, vmem=40, flops=1):
    scalars = [x for x in inputs if x.dtype == jnp.int32]
    return pl.pallas_call(
        kernel,
        name=name,
        out_shape=outputs,
        in_specs=in_specs or [SM] * len(scalars) + [VM] * (len(inputs) - len(scalars)),
        out_specs=out_specs or [VM] * len(outputs),
        scratch_shapes=list(scratch),
        input_output_aliases=aliases,
        cost_estimate=pl.CostEstimate(flops=flops, bytes_accessed=1, transcendentals=0),
        compiler_params=pltpu.CompilerParams(vmem_limit_bytes=vmem << 20),
    )(*inputs)


def arr(*shape, dtype=BF):
    return jax.ShapeDtypeStruct(shape, dtype)


def shards(objects, probes, amplitudes, prop_phase, scan_rows, scan_cols, probe_choice):
    route = routes(lax.axis_size("region"))
    move = lambda x, way: lax.ppermute(x, AXES, route[way])
    first, second = (jnp.asarray(t) for t in dft_blocks())
    wave = jnp.stack([jnp.cos(prop_phase), jnp.sin(prop_phase)])
    half = arr(2, HALF, SIDE)

    full = arr(2, SIDE, SIDE)
    near = pltpu.VMEM((2, BAND + HALF, COLS), F32)
    early, late, band, rows, cols = call(
        edge_kernel, "edge",
        [pltpu.with_memory_space_constraint(x, pltpu.HBM) for x in (scan_rows, scan_cols, objects)],
        [arr(EDGE + 16, 128), arr(EDGE + 16, 128),
         arr(2, BAND, COLS, dtype=F32), arr(4, dtype=jnp.int32), arr(4, dtype=jnp.int32)],
        [pltpu.SemaphoreType.DMA((4,))],
        in_specs=[HB] * 3, out_specs=[VM] * 3 + [SM] * 2, vmem=50,
    )
    early = move(early, "early")
    late = move(late, "late")
    sent = call(mate_kernel, "mate", [rows, cols, band, early], [full, full], [near])
    mates = [move(x, "mate") for x in sent]
    own0, own1, spots = call(
        own_windows_kernel, "windows", [rows, cols, band, early, late],
        [full, full, arr(8, dtype=jnp.int32)], [near], out_specs=[VM, VM, SM],
    )
    optics = [probes, amplitudes, wave, first, second]
    work = [pltpu.VMEM((2, 2, SIDE, SIDE), BF), pltpu.VMEM((2, 2, SIDE, SIDE), F32)]
    wide_full = arr(2, SIDE, SIDE, dtype=F32)
    outer0, inband0, kept0, edge0 = call(
        functools.partial(solo_kernel, 0), "solo0", [rows, probe_choice, own0, mates[0]] + optics,
        [half, half, wide_full, half], work,
    )
    outer0 = move(outer0, "mate")
    inband0 = move(inband0, "mate")
    outer1, inband1, kept1, edges = call(
        functools.partial(solo_kernel, 1), "solo1",
        [rows, probe_choice, own1, mates[1]] + optics + [edge0],
        [half, half, wide_full, arr(2, 2, HALF, SIDE)], work, flops=10**11,
    )
    outer1 = move(outer1, "mate")
    inband1 = move(inband1, "mate")
    edges = move(edges, "early")
    relay0 = move(outer0, "late")
    (total,) = call(
        own_kernel, "own", [rows, cols, kept0, kept1, outer0, inband0],
        [arr(2, EXT, COLS, dtype=F32)], flops=10**11,
    )
    total, outer1 = lax.optimization_barrier((total, outer1))
    relay1 = move(outer1, "late")
    _, gradient = call(
        rest_kernel, "rest",
        [rows, cols, spots, total, outer1, inband1, edges, relay0, relay1],
        [arr(2, EXT, COLS, dtype=F32), arr(1, 2, BAND, COLS, dtype=F32)],
        [pltpu.SemaphoreType.DMA((2,))],
        out_specs=[VM, HB],
        aliases={3: 0},
    )
    return gradient


def solution(mesh):
    return jax.shard_map(
        shards,
        mesh=mesh,
        in_specs=(
            P("cuts", None, "region", None),
            P(),
            P("region", None, None),
            P(),
            P("region"),
            P("region"),
            P("region"),
        ),
        out_specs=P("cuts", None, "region", None),
        check_vma=False,
    )
```

time: 86.7 us -> 89.1 us (1.028)
  waiting for transfers between devices: 25.3 us -> 35.8 us
  starting transfers between devices: 37.8 us -> 31 us
  Pallas kernels: 21.8 us -> 20.9 us
    ppermute x9 -> x11, waiting for transfers between devices: 25.3 us -> 35.8 us  [shards(): move = lambda x, way: lax.ppermute(x, AXES, route[way])]
    ppermute x9 -> x11, starting transfers between devices: 37.8 us -> 31 us  [shards(): move = lambda x, way: lax.ppermute(x, AXES, route[way])]
    pallas_call x9 -> x7, Pallas kernels: 21.8 us -> 20.9 us  [call(): pl.pallas_call(kernel, name=name, out_shape=outputs, in_specs=in_specs or...]
  transfers between devices with their start and end apart: 9 -> 11, of which waited for: 5 -> 7; matrix products, arithmetic and copies ran while one was open for 1% -> 1% of each run, Pallas kernels for 20% -> 18%
where the time goes in v4:
time: 89.1 us; the launch traced here: 89 us
  waiting for transfers between devices  35.8 us (40%)
  starting transfers between devices  31 us (35%)
  Pallas kernels  20.9 us (23%)
  local copies, waits for them, and re-layouts  0.98 us (1%)
    ppermute x11, waiting for transfers between devices, shards(): move = lambda x, way: lax.ppermute(x, AXES, route[way])  35.8 us
    ppermute x11, starting transfers between devices, shards(): move = lambda x, way: lax.ppermute(x, AXES, route[way])  31 us
    pallas_call x7, Pallas kernels, call(): pl.pallas_call(kernel, name=name, out_shape=outputs, in_specs=in_specs or...  20.9 us
  transfers between devices with their start and end apart: 11, of which 7 were waited for; matrix products, arithmetic and copies ran while one was open for 1% of the time, Pallas kernels for 18%

profile of v4, /device:TPU:8, one launch (start us, length us, event | category | flops | bytes accessed | tf_op | source)
XLA Modules:
  0.0 89.0 jit_solution(17430781266048073928)
XLA Ops:
  0.0 2.2 %edge.1 = (bf16[2064,128]{1,0:T(8,128)(2,1)S(1)}, bf16[2064,128]{1,0:T(8,128)(2,1)S(1)}, f32[2,256,1024]{2,1,0:T(8,128)S(1)}, s32[4]{0:T(128)S(1)}, s32[4]{0:T(128)S(1)}) custom-call(s32[4]{0:T(128)} %rows_in.1, s32[4]{0:T(128)} %cols_in.1, f32[1,2,256,1024]{3,2,1,0:T(8,128)} %objects_in.1), custom_call_target="tpu_custom_call" | custom-call | flops 1 | bytes 1 | tf_op jit(solution)/shard_map/edge/pallas_call | solution.py:294
  2.2 6.2 %collective-permute-start = (bf16[2064,128]{1,0:T(8,128)(2,1)S(1)}, bf16[2064,128]{1,0:T(8,128)(2,1)S(1)}, u32[]{:S(2)}, u32[]{:S(2)}) collective-permute-start(bf16[2064,128]{1,0:T(8,128)(2,1)S(1)} %get-tuple-element.29), channel_id=1, source_target_pairs={{0,127},{1,0},{2,1},{3,2},{4,3},{5,4},{6,5},{7,6},{8,7},{9,8},{10,... | collective-permute-start | bytes 1585160 | tf_op jit(solution)/shard_map/ppermute | solution.py:313
  8.5 7.7 %collective-permute-done.early = bf16[2064,128]{1,0:T(8,128)(2,1)S(1)} collective-permute-done((bf16[2064,128]{1,0:T(8,128)(2,1)S(1)}, bf16[2064,128]{1,0:T(8,128)(2,1)S(1)}, u32[]{:S(2)}, u32[]{:S(2)}) %collective-permute-start) | collective-permute-done | bytes 528416 | tf_op jit(solution)/shard_map/ppermute | solution.py:313
  16.2 1.6 %mate.1 = (bf16[2,256,256]{2,1,0:T(8,128)(2,1)S(1)}, bf16[2,256,256]{2,1,0:T(8,128)(2,1)S(1)}) custom-call(s32[4]{0:T(128)S(1)} %get-tuple-element.26.rows, s32[4]{0:T(128)S(1)} %get-tuple-element.27.cols, f32[2,256,1024]{2,1,0:T(8,128)S(1)} %get-tuple-element.28.objects, bf16[2064,128]{1,0:T(8,128)(2,1)S(1)} %collective-permute-done.early), custom_call_target="tpu_custom_call" | custom-call | flops 1 | bytes 1 | tf_op jit(solution)/shard_map/mate/pallas_call | solution.py:294
  17.8 12.4 %collective-permute-start.2 = (bf16[2,256,256]{2,1,0:T(8,128)(2,1)S(1)}, bf16[2,256,256]{2,1,0:T(8,128)(2,1)S(1)}, u32[]{:S(2)}, u32[]{:S(2)}) collective-permute-start(bf16[2,256,256]{2,1,0:T(8,128)(2,1)S(1)} %get-tuple-element.33), channel_id=1, source_target_pairs={{0,128},{1,129},{2,130},{3,131},{4,132},{5,133},{6,134},{7,135},{8... | collective-permute-start | bytes 786440 | tf_op jit(solution)/shard_map/ppermute | solution.py:313
  30.3 0.1 collective-permute-start.3
  30.4 0.9 %cosine_bitcast_fusion = (f32[1,256,256]{2,1,0:T(8,128)S(1)}, f32[1,256,256]{2,1,0:T(8,128)S(1)}) fusion(f32[256,256]{1,0:T(8,128)S(1)} %copy-done.5), kind=kLoop, calls=%fused_computation.2 | loop fusion | bytes 786432 | tf_op jit(solution)/shard_map/stack | solution.py:315
  31.4 2.2 %windows.1 = (bf16[2,256,256]{2,1,0:T(8,128)(2,1)S(1)}, bf16[2,256,256]{2,1,0:T(8,128)(2,1)S(1)}, s32[8]{0:T(128)S(1)}) custom-call(s32[4]{0:T(128)S(1)} %get-tuple-element.26.rows, s32[4]{0:T(128)S(1)} %get-tuple-element.27.cols, f32[2,256,1024]{2,1,0:T(8,128)S(1)} %get-tuple-element.28.objects, bf16[2064,128]{1,0:T(8,128)(2,1)S(1)} %collective-permute-done.early, ...), custom_call_target="tpu_custom_call" | custom-call | flops 1 | bytes 1 | tf_op jit(solution)/shard_map/windows/pallas_call | solution.py:294
  33.7 12.3 %collective-permute-done.2.mate = bf16[2,256,256]{2,1,0:T(8,128)(2,1)S(1)} collective-permute-done((bf16[2,256,256]{2,1,0:T(8,128)(2,1)S(1)}, bf16[2,256,256]{2,1,0:T(8,128)(2,1)S(1)}, u32[]{:S(2)}, u32[]{:S(2)}) %collective-permute-start.2) | collective-permute-done | bytes 262176 | tf_op jit(solution)/shard_map/ppermute | solution.py:313
  46.0 4.8 %solo0.1 = (bf16[2,128,256]{2,1,0:T(8,128)(2,1)S(1)}, bf16[2,128,256]{2,1,0:T(8,128)(2,1)S(1)}, f32[2,256,256]{2,1,0:T(8,128)S(1)}, bf16[2,128,256]{2,1,0:T(8,128)(2,1)S(1)}) custom-call(s32[4]{0:T(128)S(1)} %get-tuple-element.26.rows, s32[4]{0:T(128)S(1)} %copy-done.4, bf16[2,256,256]{2,1,0:T(8,128)(2,1)S(1)} %get-tuple-element.32.own, ...), custom_call_target="tpu_custom_call" | custom-call | flops 1 | bytes 1 | tf_op jit(solution)/shard_map/solo0/pallas_call | solution.py:294
  50.8 5.3 %collective-permute-start.4 = (bf16[2,128,256]{2,1,0:T(8,128)(2,1)S(1)}, bf16[2,128,256]{2,1,0:T(8,128)(2,1)S(1)}, u32[]{:S(2)}, u32[]{:S(2)}) collective-permute-start(bf16[2,128,256]{2,1,0:T(8,128)(2,1)S(1)} %get-tuple-element.39), channel_id=1, source_target_pairs={{0,128},{1,129},{2,130},{3,131},{4,132},{5,133},{6,134},{7,135},{8... | collective-permute-start | bytes 393224 | tf_op jit(solution)/shard_map/ppermute | solution.py:313
  56.1 0.7 collective-permute-start.5
  56.8 4.9 %solo1.1 = (bf16[2,128,256]{2,1,0:T(8,128)(2,1)S(1)}, bf16[2,128,256]{2,1,0:T(8,128)(2,1)S(1)}, f32[2,256,256]{2,1,0:T(8,128)S(1)}, bf16[2,2,128,256]{3,2,1,0:T(8,128)(2,1)S(1)}) custom-call(s32[4]{0:T(128)S(1)} %get-tuple-element.26.rows, s32[4]{0:T(128)S(1)} %copy-done.4, bf16[2,256,256]{2,1,0:T(8,128)(2,1)S(1)} %get-tuple-element.35.own, ...), custom_call_target="tpu_custom_call" | custom-call | flops 99999997952 | bytes 1 | tf_op jit(solution)/shard_map/solo1/pallas_call | solution.py:294
  61.7 5.3 %collective-permute-start.6 = (bf16[2,128,256]{2,1,0:T(8,128)(2,1)S(1)}, bf16[2,128,256]{2,1,0:T(8,128)(2,1)S(1)}, u32[]{:S(2)}, u32[]{:S(2)}) collective-permute-start(bf16[2,128,256]{2,1,0:T(8,128)(2,1)S(1)} %get-tuple-element.41), channel_id=1, source_target_pairs={{0,128},{1,129},{2,130},{3,131},{4,132},{5,133},{6,134},{7,135},{8... | collective-permute-start | bytes 393224 | tf_op jit(solution)/shard_map/ppermute | solution.py:313
  67.0 0.7 collective-permute-start.7
  67.7 2.4 %collective-permute-done.4.outer = bf16[2,128,256]{2,1,0:T(8,128)(2,1)S(1)} collective-permute-done((bf16[2,128,256]{2,1,0:T(8,128)(2,1)S(1)}, bf16[2,128,256]{2,1,0:T(8,128)(2,1)S(1)}, u32[]{:S(2)}, u32[]{:S(2)}) %collective-permute-start.4) | collective-permute-done | bytes 131104 | tf_op jit(solution)/shard_map/ppermute | solution.py:313
  70.2 2.8 %collective-permute-done.5.inband = bf16[2,128,256]{2,1,0:T(8,128)(2,1)S(1)} collective-permute-done((bf16[2,128,256]{2,1,0:T(8,128)(2,1)S(1)}, bf16[2,128,256]{2,1,0:T(8,128)(2,1)S(1)}, u32[]{:S(2)}, u32[]{:S(2)}) %collective-permute-start.5) | collective-permute-done | bytes 131104 | tf_op jit(solution)/shard_map/ppermute | solution.py:313
  73.0 2.3 %own.1.given = f32[2,512,1024]{2,1,0:T(8,128)S(1)} custom-call(s32[4]{0:T(128)S(1)} %get-tuple-element.26.rows, s32[4]{0:T(128)S(1)} %get-tuple-element.27.cols, f32[2,256,256]{2,1,0:T(8,128)S(1)} %get-tuple-element.34.kept0, f32[2,256,256]{2,1,0:T(8,128)S(1)} %get-tuple-element.38.kept1, bf16[2,128,256]{2,1,0:T(8,128)(2,1)S(1)} %collective-permute-done.4.outer, ...), custom_call_target="tpu_custom_call" | custom-call | flops 99999997952 | bytes 1 | tf_op jit(solution)/shard_map/own/pallas_call | solution.py:294
  75.3 0.1 collective-permute-start.9
  75.4 0.1 collective-permute-start.10
  75.5 0.4 collective-permute-done.7.inband
  75.9 8.7 %collective-permute-done.9.relay0 = bf16[2,128,256]{2,1,0:T(8,128)(2,1)S(1)} collective-permute-done((bf16[2,128,256]{2,1,0:T(8,128)(2,1)S(1)}, bf16[2,128,256]{2,1,0:T(8,128)(2,1)S(1)}, u32[]{:S(2)}, u32[]{:S(2)}) %collective-permute-start.9) | collective-permute-done | bytes 131104 | tf_op jit(solution)/shard_map/ppermute | solution.py:313
  84.6 1.4 %collective-permute-done.10.relay1 = bf16[2,128,256]{2,1,0:T(8,128)(2,1)S(1)} collective-permute-done((bf16[2,128,256]{2,1,0:T(8,128)(2,1)S(1)}, bf16[2,128,256]{2,1,0:T(8,128)(2,1)S(1)}, u32[]{:S(2)}, u32[]{:S(2)}) %collective-permute-start.10) | collective-permute-done | bytes 131104 | tf_op jit(solution)/shard_map/ppermute | solution.py:313
  86.0 2.8 %rest.1 = (f32[2,512,1024]{2,1,0:T(8,128)S(1)}, f32[1,2,256,1024]{3,2,1,0:T(8,128)}) custom-call(s32[4]{0:T(128)S(1)} %get-tuple-element.26.rows, s32[4]{0:T(128)S(1)} %get-tuple-element.27.cols, s32[8]{0:T(128)S(1)} %get-tuple-element.31.spots, f32[2,512,1024]{2,1,0:T(8,128)S(1)} %own.1.given, ...), custom_call_target="tpu_custom_call", output_to_operand_aliasing={{0}: (3, {})} | custom-call | flops 1 | bytes 1 | tf_op jit(solution)/shard_map/rest/pallas_call | solution.py:294
  (19 shorter events, 0.1 us)
Async XLA Ops:
  0.0 30.4 %copy-start.5 = (f32[256,256]{1,0:T(8,128)S(1)}, f32[256,256]{1,0:T(8,128)}, u32[]{:S(2)}) copy-start(f32[256,256]{1,0:T(8,128)} %param.12) | copy-start | bytes 786436
  2.2 14.0 %collective-permute-start = (bf16[2064,128]{1,0:T(8,128)(2,1)S(1)}, bf16[2064,128]{1,0:T(8,128)(2,1)S(1)}, u32[]{:S(2)}, u32[]{:S(2)}) collective-permute-start(bf16[2064,128]{1,0:T(8,128)(2,1)S(1)} %get-tuple-element.29), channel_id=1, source_target_pairs={{0,127},{1,0},{2,1},{3,2},{4,3},{5,4},{6,5},{7,6},{8,7},{9,8},{10,... | collective-permute-start | bytes 1585160 | tf_op jit(solution)/shard_map/ppermute | solution.py:313
  8.5 23.0 %collective-permute-start.1 = (bf16[2064,128]{1,0:T(8,128)(2,1)S(1)}, bf16[2064,128]{1,0:T(8,128)(2,1)S(1)}, u32[]{:S(2)}, u32[]{:S(2)}) collective-permute-start(bf16[2064,128]{1,0:T(8,128)(2,1)S(1)} %get-tuple-element.30), channel_id=1, source_target_pairs={{0,1},{1,2},{2,3},{3,4},{4,5},{5,6},{6,7},{7,8},{8,9},{9,10},{10,1... | collective-permute-start | bytes 1585160 | tf_op jit(solution)/shard_map/ppermute | solution.py:313
  17.8 28.1 %collective-permute-start.2 = (bf16[2,256,256]{2,1,0:T(8,128)(2,1)S(1)}, bf16[2,256,256]{2,1,0:T(8,128)(2,1)S(1)}, u32[]{:S(2)}, u32[]{:S(2)}) collective-permute-start(bf16[2,256,256]{2,1,0:T(8,128)(2,1)S(1)} %get-tuple-element.33), channel_id=1, source_target_pairs={{0,128},{1,129},{2,130},{3,131},{4,132},{5,133},{6,134},{7,135},{8... | collective-permute-start | bytes 786440 | tf_op jit(solution)/shard_map/ppermute | solution.py:313
  30.3 26.6 %collective-permute-start.3 = (bf16[2,256,256]{2,1,0:T(8,128)(2,1)S(1)}, bf16[2,256,256]{2,1,0:T(8,128)(2,1)S(1)}, u32[]{:S(2)}, u32[]{:S(2)}) collective-permute-start(bf16[2,256,256]{2,1,0:T(8,128)(2,1)S(1)} %get-tuple-element.36), channel_id=1, source_target_pairs={{0,128},{1,129},{2,130},{3,131},{4,132},{5,133},{6,134},{7,135},{8... | collective-permute-start | bytes 786440 | tf_op jit(solution)/shard_map/ppermute | solution.py:313
  31.3 14.6 %copy-start = (bf16[4,2,256,256]{3,2,1,0:T(8,128)(2,1)S(1)}, bf16[4,2,256,256]{3,2,1,0:T(8,128)(2,1)}, u32[]{:S(2)}) copy-start(bf16[4,2,256,256]{3,2,1,0:T(8,128)(2,1)} %probes.3) | copy-start | bytes 3145732
  31.3 14.6 %copy-start.1 = (f32[4,256,256]{2,1,0:T(8,128)S(1)}, f32[4,256,256]{2,1,0:T(8,128)}, u32[]{:S(2)}) copy-start(f32[4,256,256]{2,1,0:T(8,128)} %amplitudes.3) | copy-start | bytes 3145732
  31.3 14.6 %copy-start.2 = (bf16[512,512]{1,0:T(8,128)(2,1)S(1)}, bf16[512,512]{1,0:T(8,128)(2,1)}, u32[]{:S(2)}) copy-start(bf16[512,512]{1,0:T(8,128)(2,1)} %constant.5.clone.second) | copy-start | bytes 1572868
  31.4 14.6 %copy-start.3 = (bf16[512,512]{1,0:T(8,128)(2,1)S(1)}, bf16[512,512]{1,0:T(8,128)(2,1)}, u32[]{:S(2)}) copy-start(bf16[512,512]{1,0:T(8,128)(2,1)} %constant.4.clone.first) | copy-start | bytes 1572868
  31.4 14.6 %copy-start.4 = (s32[4]{0:T(128)S(1)}, s32[4]{0:T(128)}, u32[]{:S(2)}) copy-start(s32[4]{0:T(128)} %picks.3) | copy-start | bytes 52
  50.8 19.3 %collective-permute-start.4 = (bf16[2,128,256]{2,1,0:T(8,128)(2,1)S(1)}, bf16[2,128,256]{2,1,0:T(8,128)(2,1)S(1)}, u32[]{:S(2)}, u32[]{:S(2)}) collective-permute-start(bf16[2,128,256]{2,1,0:T(8,128)(2,1)S(1)} %get-tuple-element.39), channel_id=1, source_target_pairs={{0,128},{1,129},{2,130},{3,131},{4,132},{5,133},{6,134},{7,135},{8... | collective-permute-start | bytes 393224 | tf_op jit(solution)/shard_map/ppermute | solution.py:313
  56.1 16.9 %collective-permute-start.5 = (bf16[2,128,256]{2,1,0:T(8,128)(2,1)S(1)}, bf16[2,128,256]{2,1,0:T(8,128)(2,1)S(1)}, u32[]{:S(2)}, u32[]{:S(2)}) collective-permute-start(bf16[2,128,256]{2,1,0:T(8,128)(2,1)S(1)} %get-tuple-element.40), channel_id=1, source_target_pairs={{0,128},{1,129},{2,130},{3,131},{4,132},{5,133},{6,134},{7,135},{8... | collective-permute-start | bytes 393224 | tf_op jit(solution)/shard_map/ppermute | solution.py:313
  61.7 13.6 %collective-permute-start.6 = (bf16[2,128,256]{2,1,0:T(8,128)(2,1)S(1)}, bf16[2,128,256]{2,1,0:T(8,128)(2,1)S(1)}, u32[]{:S(2)}, u32[]{:S(2)}) collective-permute-start(bf16[2,128,256]{2,1,0:T(8,128)(2,1)S(1)} %get-tuple-element.41), channel_id=1, source_target_pairs={{0,128},{1,129},{2,130},{3,131},{4,132},{5,133},{6,134},{7,135},{8... | collective-permute-start | bytes 393224 | tf_op jit(solution)/shard_map/ppermute | solution.py:313
  67.0 8.9 %collective-permute-start.7 = (bf16[2,128,256]{2,1,0:T(8,128)(2,1)S(1)}, bf16[2,128,256]{2,1,0:T(8,128)(2,1)S(1)}, u32[]{:S(2)}, u32[]{:S(2)}) collective-permute-start(bf16[2,128,256]{2,1,0:T(8,128)(2,1)S(1)} %get-tuple-element.44), channel_id=1, source_target_pairs={{0,128},{1,129},{2,130},{3,131},{4,132},{5,133},{6,134},{7,135},{8... | collective-permute-start | bytes 393224 | tf_op jit(solution)/shard_map/ppermute | solution.py:313
  67.7 18.3 %collective-permute-start.8 = (bf16[2,2,128,256]{3,2,1,0:T(8,128)(2,1)S(1)}, bf16[2,2,128,256]{3,2,1,0:T(8,128)(2,1)S(1)}, u32[]{:S(2)}, u32[]{:S(2)}) collective-permute-start(bf16[2,2,128,256]{3,2,1,0:T(8,128)(2,1)S(1)} %get-tuple-element.45), channel_id=1, source_target_pairs={{0,127},{1,0},{2,1},{3,2},{4,3},{5,4},{6,5},{7,6},{8,7},{9,8},{10,... | collective-permute-start | bytes 786440 | tf_op jit(solution)/shard_map/ppermute | solution.py:313
  75.3 9.3 %collective-permute-start.9 = (bf16[2,128,256]{2,1,0:T(8,128)(2,1)S(1)}, bf16[2,128,256]{2,1,0:T(8,128)(2,1)S(1)}, u32[]{:S(2)}, u32[]{:S(2)}) collective-permute-start(bf16[2,128,256]{2,1,0:T(8,128)(2,1)S(1)} %collective-permute-done.4.outer), channel_id=1, source_target_pairs={{0,1},{1,2},{2,3},{3,4},{4,5},{5,6},{6,7},{7,8},{8,9},{9,10},{10,1... | collective-permute-start | bytes 393224 | tf_op jit(solution)/shard_map/ppermute | solution.py:313
  75.4 10.6 %collective-permute-start.10 = (bf16[2,128,256]{2,1,0:T(8,128)(2,1)S(1)}, bf16[2,128,256]{2,1,0:T(8,128)(2,1)S(1)}, u32[]{:S(2)}, u32[]{:S(2)}) collective-permute-start(bf16[2,128,256]{2,1,0:T(8,128)(2,1)S(1)} %collective-permute-done.6.outer), channel_id=1, source_target_pairs={{0,1},{1,2},{2,3},{3,4},{4,5},{5,6},{6,7},{7,8},{8,9},{9,10},{10,1... | collective-permute-start | bytes 393224 | tf_op jit(solution)/shard_map/ppermute | solution.py:313

commit v5 on v4

--- a/solution.py
+++ b/solution.py
@@ -30,6 +30,7 @@
     both = [(c, r) for c in range(2) for r in range(regions)]
     return {
         "mate": [(at(c, r), at(1 - c, r)) for c, r in both],
+        "direct": [(at(c, r), at(1 - c, r - 1 if c == 0 else r + 1)) for c, r in both],
         "early": [(at(c, r), at(c, r - 1 if c == 0 else r + 1)) for c, r in both],
         "late": [(at(c, r), at(c, r + 1 if c == 0 else r - 1)) for c, r in both],
     }
@@ -238,20 +239,22 @@
         [lambda: amplitudes[place]],
         wave, first[...], second[...], store,
     )
+    depth = sent_inband.shape[1]
+    inner = pl.multiple_of(jnp.where(cut == 0, SIDE - depth, 0), 64)
     for channel in range(2):
         sent_outer[channel] = made[1 - cut, channel, pl.ds(start, HALF)].astype(BF)
-        sent_inband[channel] = made[1 - cut, channel, pl.ds(HALF - start, HALF)].astype(BF)
+        sent_inband[channel] = made[1 - cut, channel, pl.ds(inner, depth)].astype(BF)
         kept[channel] = made[cut, channel]
         edges[channel] = made[cut, channel, pl.ds(start, HALF)].astype(BF)
 
 
-def put_mate(put, rows, cols, number, outer, inband, channel):
+def put_inband(put, rows, cols, number, inband, channel):
     upper = lax.axis_index("cuts") == 1
     spots = places(rows)
     spot = jnp.where(upper, spots[number], spots[2 + number])
-    start = jnp.where(upper, 0, HALF)
-    put(rows[spot] + HALF + start, cols[spot], outer[channel].astype(F32))
-    put(rows[spot] + 2 * HALF - start, cols[spot], inband[channel].astype(F32))
+    skip = jnp.where(upper, SIDE - inband.shape[1], 0)
+    put(rows[spot] + HALF + skip, cols[spot], inband[channel].astype(F32))
+    return rows[spot] + HALF + jnp.where(upper, 0, HALF), cols[spot]
 
 
 def own_kernel(rows, cols, kept0, kept1, outer, inband, total):
@@ -263,18 +266,19 @@
         for number, kept in enumerate((kept0, kept1)):
             spot = jnp.where(cut == 0, places_here[number], places_here[2 + number])
             put(rows[spot] + HALF, cols[spot], kept[channel])
-        put_mate(put, rows, cols, 0, outer, inband, channel)
+        top, left = put_inband(put, rows, cols, 0, inband, channel)
+        put(top, left, outer[channel].astype(F32))
 
 
 def rest_kernel(
-    rows, cols, spots, given, outer, inband, edges, relay0, relay1, total, output, sems
+    rows, cols, spots, given, inband, edges, relay0, relay1, total, output, sems
 ):
     cut = lax.axis_index("cuts")
     shift = jnp.where(cut == 0, BAND, -HALF)
     copies = []
     for channel in range(2):
         put = functools.partial(put_window, total, channel)
-        put_mate(put, rows, cols, 1, outer, inband, channel)
+        put_inband(put, rows, cols, 1, inband, channel)
         for number, relay in enumerate((relay0, relay1)):
             k = 2 * number
             put(spots[k] + shift, spots[k + 1], edges[number, channel].astype(F32))
@@ -328,6 +332,7 @@
     early = move(early, "early")
     late = move(late, "late")
     sent = call(mate_kernel, "mate", [rows, cols, band, early], [full, full], [near])
+    *sent, late = lax.optimization_barrier((*sent, late))
     mates = [move(x, "mate") for x in sent]
     own0, own1, spots = call(
         own_windows_kernel, "windows", [rows, cols, band, early, late],
@@ -345,9 +350,9 @@
     outer1, inband1, kept1, edges = call(
         functools.partial(solo_kernel, 1), "solo1",
         [rows, probe_choice, own1, mates[1]] + optics + [edge0],
-        [half, half, wide_full, arr(2, 2, HALF, SIDE)], work, flops=10**11,
-    )
-    outer1 = move(outer1, "mate")
+        [half, arr(2, HALF + 64, SIDE), wide_full, arr(2, 2, HALF, SIDE)], work, flops=10**11,
+    )
+    relay1 = move(outer1, "direct")
     inband1 = move(inband1, "mate")
     edges = move(edges, "early")
     relay0 = move(outer0, "late")
@@ -355,11 +360,9 @@
         own_kernel, "own", [rows, cols, kept0, kept1, outer0, inband0],
         [arr(2, EXT, COLS, dtype=F32)], flops=10**11,
     )
-    total, outer1 = lax.optimization_barrier((total, outer1))
-    relay1 = move(outer1, "late")
     _, gradient = call(
         rest_kernel, "rest",
-        [rows, cols, spots, total, outer1, inband1, edges, relay0, relay1],
+        [rows, cols, spots, total, inband1, edges, relay0, relay1],
         [arr(2, EXT, COLS, dtype=F32), arr(1, 2, BAND, COLS, dtype=F32)],
         [pltpu.SemaphoreType.DMA((2,))],
         out_specs=[VM, HB],

time: 89.1 us -> 83.5 us (0.937); the launches traced: 89 us -> 81.9 us
  waiting for transfers between devices: 35.8 us -> 30.3 us
  starting transfers between devices: 31 us -> 29.4 us
    ppermute x11 -> x10, waiting for transfers between devices: 35.8 us -> 30.3 us  [shards(): move = lambda x, way: lax.ppermute(x, AXES, route[way])]
    ppermute x11 -> x10, starting transfers between devices: 31 us -> 29.4 us  [shards(): move = lambda x, way: lax.ppermute(x, AXES, route[way])]
  transfers between devices with their start and end apart: 11 -> 10, of which waited for: 7 -> 6; matrix products, arithmetic and copies ran while one was open for 1% -> 1% of each run, Pallas kernels for 18% -> 19%
where the time goes in v5:
time: 83.5 us; the launch traced here: 81.9 us
  waiting for transfers between devices  30.3 us (36%)
  starting transfers between devices  29.4 us (35%)
  Pallas kernels  20.9 us (25%)
  local copies, waits for them, and re-layouts  0.98 us (1%)
    ppermute x10, waiting for transfers between devices, shards(): move = lambda x, way: lax.ppermute(x, AXES, route[way])  30.3 us
    ppermute x10, starting transfers between devices, shards(): move = lambda x, way: lax.ppermute(x, AXES, route[way])  29.4 us
    pallas_call x7, Pallas kernels, call(): pl.pallas_call(kernel, name=name, out_shape=outputs, in_specs=in_specs or...  20.9 us
  transfers between devices with their start and end apart: 10, of which 6 were waited for; matrix products, arithmetic and copies ran while one was open for 1% of the time, Pallas kernels for 19%

profile of v5, /device:TPU:8, one launch (start us, length us, event | category | flops | bytes accessed | tf_op | source)
XLA Modules:
  0.0 81.9 jit_solution(17019874951591428611)
XLA Ops:
  0.0 2.2 %edge.1 = (bf16[2064,128]{1,0:T(8,128)(2,1)S(1)}, bf16[2064,128]{1,0:T(8,128)(2,1)S(1)}, f32[2,256,1024]{2,1,0:T(8,128)S(1)}, s32[4]{0:T(128)S(1)}, s32[4]{0:T(128)S(1)}) custom-call(s32[4]{0:T(128)} %rows_in.1, s32[4]{0:T(128)} %cols_in.1, f32[1,2,256,1024]{3,2,1,0:T(8,128)} %objects_in.1), custom_call_target="tpu_custom_call" | custom-call | flops 1 | bytes 1 | tf_op jit(solution)/shard_map/edge/pallas_call | solution.py:298
  2.2 6.2 %collective-permute-start = (bf16[2064,128]{1,0:T(8,128)(2,1)S(1)}, bf16[2064,128]{1,0:T(8,128)(2,1)S(1)}, u32[]{:S(2)}, u32[]{:S(2)}) collective-permute-start(bf16[2064,128]{1,0:T(8,128)(2,1)S(1)} %get-tuple-element.30), channel_id=1, source_target_pairs={{0,127},{1,0},{2,1},{3,2},{4,3},{5,4},{6,5},{7,6},{8,7},{9,8},{10,... | collective-permute-start | bytes 1585160 | tf_op jit(solution)/shard_map/ppermute | solution.py:317
  8.5 7.7 %collective-permute-done.early = bf16[2064,128]{1,0:T(8,128)(2,1)S(1)} collective-permute-done((bf16[2064,128]{1,0:T(8,128)(2,1)S(1)}, bf16[2064,128]{1,0:T(8,128)(2,1)S(1)}, u32[]{:S(2)}, u32[]{:S(2)}) %collective-permute-start) | collective-permute-done | bytes 528416 | tf_op jit(solution)/shard_map/ppermute | solution.py:317
  16.2 1.6 %mate.1 = (bf16[2,256,256]{2,1,0:T(8,128)(2,1)S(1)}, bf16[2,256,256]{2,1,0:T(8,128)(2,1)S(1)}) custom-call(s32[4]{0:T(128)S(1)} %get-tuple-element.27.rows, s32[4]{0:T(128)S(1)} %get-tuple-element.28.cols, f32[2,256,1024]{2,1,0:T(8,128)S(1)} %get-tuple-element.29.objects, bf16[2064,128]{1,0:T(8,128)(2,1)S(1)} %collective-permute-done.early), custom_call_target="tpu_custom_call" | custom-call | flops 1 | bytes 1 | tf_op jit(solution)/shard_map/mate/pallas_call | solution.py:298
  17.8 4.1 %collective-permute-done.1.late = bf16[2064,128]{1,0:T(8,128)(2,1)S(1)} collective-permute-done((bf16[2064,128]{1,0:T(8,128)(2,1)S(1)}, bf16[2064,128]{1,0:T(8,128)(2,1)S(1)}, u32[]{:S(2)}, u32[]{:S(2)}) %collective-permute-start.1) | collective-permute-done | bytes 528416 | tf_op jit(solution)/shard_map/ppermute | solution.py:317
  21.9 7.9 %collective-permute-start.2 = (bf16[2,256,256]{2,1,0:T(8,128)(2,1)S(1)}, bf16[2,256,256]{2,1,0:T(8,128)(2,1)S(1)}, u32[]{:S(2)}, u32[]{:S(2)}) collective-permute-start(bf16[2,256,256]{2,1,0:T(8,128)(2,1)S(1)} %get-tuple-element.37), channel_id=1, source_target_pairs={{0,128},{1,129},{2,130},{3,131},{4,132},{5,133},{6,134},{7,135},{8... | collective-permute-start | bytes 786440 | tf_op jit(solution)/shard_map/ppermute | solution.py:317
  29.8 0.1 collective-permute-start.3
  29.9 0.9 %cosine_bitcast_fusion = (f32[1,256,256]{2,1,0:T(8,128)S(1)}, f32[1,256,256]{2,1,0:T(8,128)S(1)}) fusion(f32[256,256]{1,0:T(8,128)S(1)} %copy-done.5), kind=kLoop, calls=%fused_computation.2 | loop fusion | bytes 786432 | tf_op jit(solution)/shard_map/stack | solution.py:319
  30.9 0.0 copy-start.2
  30.9 0.0 copy-start.3
  31.0 2.2 %windows.1 = (bf16[2,256,256]{2,1,0:T(8,128)(2,1)S(1)}, bf16[2,256,256]{2,1,0:T(8,128)(2,1)S(1)}, s32[8]{0:T(128)S(1)}) custom-call(s32[4]{0:T(128)S(1)} %get-tuple-element.27.rows, s32[4]{0:T(128)S(1)} %get-tuple-element.28.cols, f32[2,256,1024]{2,1,0:T(8,128)S(1)} %get-tuple-element.29.objects, bf16[2064,128]{1,0:T(8,128)(2,1)S(1)} %collective-permute-done.early, ...), custom_call_target="tpu_custom_call" | custom-call | flops 1 | bytes 1 | tf_op jit(solution)/shard_map/windows/pallas_call | solution.py:298
  33.2 8.1 %collective-permute-done.2.mate = bf16[2,256,256]{2,1,0:T(8,128)(2,1)S(1)} collective-permute-done((bf16[2,256,256]{2,1,0:T(8,128)(2,1)S(1)}, bf16[2,256,256]{2,1,0:T(8,128)(2,1)S(1)}, u32[]{:S(2)}, u32[]{:S(2)}) %collective-permute-start.2) | collective-permute-done | bytes 262176 | tf_op jit(solution)/shard_map/ppermute | solution.py:317
  41.4 4.8 %solo0.1 = (bf16[2,128,256]{2,1,0:T(8,128)(2,1)S(1)}, bf16[2,128,256]{2,1,0:T(8,128)(2,1)S(1)}, f32[2,256,256]{2,1,0:T(8,128)S(1)}, bf16[2,128,256]{2,1,0:T(8,128)(2,1)S(1)}) custom-call(s32[4]{0:T(128)S(1)} %get-tuple-element.27.rows, s32[4]{0:T(128)S(1)} %copy-done.4, bf16[2,256,256]{2,1,0:T(8,128)(2,1)S(1)} %get-tuple-element.36.own, ...), custom_call_target="tpu_custom_call" | custom-call | flops 1 | bytes 1 | tf_op jit(solution)/shard_map/solo0/pallas_call | solution.py:298
  46.2 5.9 %collective-permute-start.4 = (bf16[2,128,256]{2,1,0:T(8,128)(2,1)S(1)}, bf16[2,128,256]{2,1,0:T(8,128)(2,1)S(1)}, u32[]{:S(2)}, u32[]{:S(2)}) collective-permute-start(bf16[2,128,256]{2,1,0:T(8,128)(2,1)S(1)} %get-tuple-element.43), channel_id=1, source_target_pairs={{0,128},{1,129},{2,130},{3,131},{4,132},{5,133},{6,134},{7,135},{8... | collective-permute-start | bytes 393224 | tf_op jit(solution)/shard_map/ppermute | solution.py:317
  52.1 0.3 collective-permute-start.5
  52.4 4.9 %solo1.1 = (bf16[2,128,256]{2,1,0:T(8,128)(2,1)S(1)}, bf16[2,192,256]{2,1,0:T(8,128)(2,1)S(1)}, f32[2,256,256]{2,1,0:T(8,128)S(1)}, bf16[2,2,128,256]{3,2,1,0:T(8,128)(2,1)S(1)}) custom-call(s32[4]{0:T(128)S(1)} %get-tuple-element.27.rows, s32[4]{0:T(128)S(1)} %copy-done.4, bf16[2,256,256]{2,1,0:T(8,128)(2,1)S(1)} %get-tuple-element.39.own, ...), custom_call_target="tpu_custom_call" | custom-call | flops 99999997952 | bytes 1 | tf_op jit(solution)/shard_map/solo1/pallas_call | solution.py:298
  57.2 4.5 %collective-permute-start.9 = (bf16[2,128,256]{2,1,0:T(8,128)(2,1)S(1)}, bf16[2,128,256]{2,1,0:T(8,128)(2,1)S(1)}, u32[]{:S(2)}, u32[]{:S(2)}) collective-permute-start(bf16[2,128,256]{2,1,0:T(8,128)(2,1)S(1)} %get-tuple-element.47), channel_id=1, source_target_pairs={{0,255},{1,128},{2,129},{3,130},{4,131},{5,132},{6,133},{7,134},{8... | collective-permute-start | bytes 393224 | tf_op jit(solution)/shard_map/ppermute | solution.py:317
  61.8 1.3 %collective-permute-start.6 = (bf16[2,192,256]{2,1,0:T(8,128)(2,1)S(1)}, bf16[2,192,256]{2,1,0:T(8,128)(2,1)S(1)}, u32[]{:S(2)}, u32[]{:S(2)}) collective-permute-start(bf16[2,192,256]{2,1,0:T(8,128)(2,1)S(1)} %get-tuple-element.45), channel_id=1, source_target_pairs={{0,128},{1,129},{2,130},{3,131},{4,132},{5,133},{6,134},{7,135},{8... | collective-permute-start | bytes 589832 | tf_op jit(solution)/shard_map/ppermute | solution.py:317
  63.1 3.2 %collective-permute-start.7 = (bf16[2,2,128,256]{3,2,1,0:T(8,128)(2,1)S(1)}, bf16[2,2,128,256]{3,2,1,0:T(8,128)(2,1)S(1)}, u32[]{:S(2)}, u32[]{:S(2)}) collective-permute-start(bf16[2,2,128,256]{3,2,1,0:T(8,128)(2,1)S(1)} %get-tuple-element.46), channel_id=1, source_target_pairs={{0,127},{1,0},{2,1},{3,2},{4,3},{5,4},{6,5},{7,6},{8,7},{9,8},{10,... | collective-permute-start | bytes 786440 | tf_op jit(solution)/shard_map/ppermute | solution.py:317
  66.3 2.3 %own.1.given = f32[2,512,1024]{2,1,0:T(8,128)S(1)} custom-call(s32[4]{0:T(128)S(1)} %get-tuple-element.27.rows, s32[4]{0:T(128)S(1)} %get-tuple-element.28.cols, f32[2,256,256]{2,1,0:T(8,128)S(1)} %get-tuple-element.38.kept0, f32[2,256,256]{2,1,0:T(8,128)S(1)} %get-tuple-element.42.kept1, bf16[2,128,256]{2,1,0:T(8,128)(2,1)S(1)} %collective-permute-done.4.outer, ...), custom_call_target="tpu_custom_call" | custom-call | flops 99999997952 | bytes 1 | tf_op jit(solution)/shard_map/own/pallas_call | solution.py:298
  68.6 5.8 %collective-permute-done.9.relay1 = bf16[2,128,256]{2,1,0:T(8,128)(2,1)S(1)} collective-permute-done((bf16[2,128,256]{2,1,0:T(8,128)(2,1)S(1)}, bf16[2,128,256]{2,1,0:T(8,128)(2,1)S(1)}, u32[]{:S(2)}, u32[]{:S(2)}) %collective-permute-start.9) | collective-permute-done | bytes 131104 | tf_op jit(solution)/shard_map/ppermute | solution.py:317
  74.4 1.6 %collective-permute-done.6.inband = bf16[2,192,256]{2,1,0:T(8,128)(2,1)S(1)} collective-permute-done((bf16[2,192,256]{2,1,0:T(8,128)(2,1)S(1)}, bf16[2,192,256]{2,1,0:T(8,128)(2,1)S(1)}, u32[]{:S(2)}, u32[]{:S(2)}) %collective-permute-start.6) | collective-permute-done | bytes 196640 | tf_op jit(solution)/shard_map/ppermute | solution.py:317
  76.1 2.9 %collective-permute-done.8.relay0 = bf16[2,128,256]{2,1,0:T(8,128)(2,1)S(1)} collective-permute-done((bf16[2,128,256]{2,1,0:T(8,128)(2,1)S(1)}, bf16[2,128,256]{2,1,0:T(8,128)(2,1)S(1)}, u32[]{:S(2)}, u32[]{:S(2)}) %collective-permute-start.8) | collective-permute-done | bytes 131104 | tf_op jit(solution)/shard_map/ppermute | solution.py:317
  79.0 2.8 %rest.1 = (f32[2,512,1024]{2,1,0:T(8,128)S(1)}, f32[1,2,256,1024]{3,2,1,0:T(8,128)}) custom-call(s32[4]{0:T(128)S(1)} %get-tuple-element.27.rows, s32[4]{0:T(128)S(1)} %get-tuple-element.28.cols, s32[8]{0:T(128)S(1)} %get-tuple-element.35.spots, f32[2,512,1024]{2,1,0:T(8,128)S(1)} %own.1.given, ...), custom_call_target="tpu_custom_call", output_to_operand_aliasing={{0}: (3, {})} | custom-call | flops 1 | bytes 1 | tf_op jit(solution)/shard_map/rest/pallas_call | solution.py:298
  (17 shorter events, 0.1 us)
Async XLA Ops:
  0.0 29.9 %copy-start.5 = (f32[256,256]{1,0:T(8,128)S(1)}, f32[256,256]{1,0:T(8,128)}, u32[]{:S(2)}) copy-start(f32[256,256]{1,0:T(8,128)} %param.12) | copy-start | bytes 786436
  2.2 14.0 %collective-permute-start = (bf16[2064,128]{1,0:T(8,128)(2,1)S(1)}, bf16[2064,128]{1,0:T(8,128)(2,1)S(1)}, u32[]{:S(2)}, u32[]{:S(2)}) collective-permute-start(bf16[2064,128]{1,0:T(8,128)(2,1)S(1)} %get-tuple-element.30), channel_id=1, source_target_pairs={{0,127},{1,0},{2,1},{3,2},{4,3},{5,4},{6,5},{7,6},{8,7},{9,8},{10,... | collective-permute-start | bytes 1585160 | tf_op jit(solution)/shard_map/ppermute | solution.py:317
  8.5 13.5 %collective-permute-start.1 = (bf16[2064,128]{1,0:T(8,128)(2,1)S(1)}, bf16[2064,128]{1,0:T(8,128)(2,1)S(1)}, u32[]{:S(2)}, u32[]{:S(2)}) collective-permute-start(bf16[2064,128]{1,0:T(8,128)(2,1)S(1)} %get-tuple-element.33), channel_id=1, source_target_pairs={{0,1},{1,2},{2,3},{3,4},{4,5},{5,6},{6,7},{7,8},{8,9},{9,10},{10,1... | collective-permute-start | bytes 1585160 | tf_op jit(solution)/shard_map/ppermute | solution.py:317
  21.9 19.4 %collective-permute-start.2 = (bf16[2,256,256]{2,1,0:T(8,128)(2,1)S(1)}, bf16[2,256,256]{2,1,0:T(8,128)(2,1)S(1)}, u32[]{:S(2)}, u32[]{:S(2)}) collective-permute-start(bf16[2,256,256]{2,1,0:T(8,128)(2,1)S(1)} %get-tuple-element.37), channel_id=1, source_target_pairs={{0,128},{1,129},{2,130},{3,131},{4,132},{5,133},{6,134},{7,135},{8... | collective-permute-start | bytes 786440 | tf_op jit(solution)/shard_map/ppermute | solution.py:317
  29.8 22.5 %collective-permute-start.3 = (bf16[2,256,256]{2,1,0:T(8,128)(2,1)S(1)}, bf16[2,256,256]{2,1,0:T(8,128)(2,1)S(1)}, u32[]{:S(2)}, u32[]{:S(2)}) collective-permute-start(bf16[2,256,256]{2,1,0:T(8,128)(2,1)S(1)} %get-tuple-element.40), channel_id=1, source_target_pairs={{0,128},{1,129},{2,130},{3,131},{4,132},{5,133},{6,134},{7,135},{8... | collective-permute-start | bytes 786440 | tf_op jit(solution)/shard_map/ppermute | solution.py:317
  30.9 10.5 %copy-start = (bf16[4,2,256,256]{3,2,1,0:T(8,128)(2,1)S(1)}, bf16[4,2,256,256]{3,2,1,0:T(8,128)(2,1)}, u32[]{:S(2)}) copy-start(bf16[4,2,256,256]{3,2,1,0:T(8,128)(2,1)} %probes.3) | copy-start | bytes 3145732
  30.9 10.4 %copy-start.1 = (f32[4,256,256]{2,1,0:T(8,128)S(1)}, f32[4,256,256]{2,1,0:T(8,128)}, u32[]{:S(2)}) copy-start(f32[4,256,256]{2,1,0:T(8,128)} %amplitudes.3) | copy-start | bytes 3145732
  30.9 10.4 %copy-start.2 = (bf16[512,512]{1,0:T(8,128)(2,1)S(1)}, bf16[512,512]{1,0:T(8,128)(2,1)}, u32[]{:S(2)}) copy-start(bf16[512,512]{1,0:T(8,128)(2,1)} %constant.5.clone.second) | copy-start | bytes 1572868
  30.9 10.4 %copy-start.3 = (bf16[512,512]{1,0:T(8,128)(2,1)S(1)}, bf16[512,512]{1,0:T(8,128)(2,1)}, u32[]{:S(2)}) copy-start(bf16[512,512]{1,0:T(8,128)(2,1)} %constant.4.clone.first) | copy-start | bytes 1572868
  31.0 10.4 %copy-start.4 = (s32[4]{0:T(128)S(1)}, s32[4]{0:T(128)}, u32[]{:S(2)}) copy-start(s32[4]{0:T(128)} %picks.3) | copy-start | bytes 52
  46.2 20.0 %collective-permute-start.4 = (bf16[2,128,256]{2,1,0:T(8,128)(2,1)S(1)}, bf16[2,128,256]{2,1,0:T(8,128)(2,1)S(1)}, u32[]{:S(2)}, u32[]{:S(2)}) collective-permute-start(bf16[2,128,256]{2,1,0:T(8,128)(2,1)S(1)} %get-tuple-element.43), channel_id=1, source_target_pairs={{0,128},{1,129},{2,130},{3,131},{4,132},{5,133},{6,134},{7,135},{8... | collective-permute-start | bytes 393224 | tf_op jit(solution)/shard_map/ppermute | solution.py:317
  52.1 14.2 %collective-permute-start.5 = (bf16[2,128,256]{2,1,0:T(8,128)(2,1)S(1)}, bf16[2,128,256]{2,1,0:T(8,128)(2,1)S(1)}, u32[]{:S(2)}, u32[]{:S(2)}) collective-permute-start(bf16[2,128,256]{2,1,0:T(8,128)(2,1)S(1)} %get-tuple-element.44), channel_id=1, source_target_pairs={{0,128},{1,129},{2,130},{3,131},{4,132},{5,133},{6,134},{7,135},{8... | collective-permute-start | bytes 393224 | tf_op jit(solution)/shard_map/ppermute | solution.py:317
  57.2 17.2 %collective-permute-start.9 = (bf16[2,128,256]{2,1,0:T(8,128)(2,1)S(1)}, bf16[2,128,256]{2,1,0:T(8,128)(2,1)S(1)}, u32[]{:S(2)}, u32[]{:S(2)}) collective-permute-start(bf16[2,128,256]{2,1,0:T(8,128)(2,1)S(1)} %get-tuple-element.47), channel_id=1, source_target_pairs={{0,255},{1,128},{2,129},{3,130},{4,131},{5,132},{6,133},{7,134},{8... | collective-permute-start | bytes 393224 | tf_op jit(solution)/shard_map/ppermute | solution.py:317
  61.8 14.3 %collective-permute-start.6 = (bf16[2,192,256]{2,1,0:T(8,128)(2,1)S(1)}, bf16[2,192,256]{2,1,0:T(8,128)(2,1)S(1)}, u32[]{:S(2)}, u32[]{:S(2)}) collective-permute-start(bf16[2,192,256]{2,1,0:T(8,128)(2,1)S(1)} %get-tuple-element.45), channel_id=1, source_target_pairs={{0,128},{1,129},{2,130},{3,131},{4,132},{5,133},{6,134},{7,135},{8... | collective-permute-start | bytes 589832 | tf_op jit(solution)/shard_map/ppermute | solution.py:317
  63.1 15.9 %collective-permute-start.7 = (bf16[2,2,128,256]{3,2,1,0:T(8,128)(2,1)S(1)}, bf16[2,2,128,256]{3,2,1,0:T(8,128)(2,1)S(1)}, u32[]{:S(2)}, u32[]{:S(2)}) collective-permute-start(bf16[2,2,128,256]{3,2,1,0:T(8,128)(2,1)S(1)} %get-tuple-element.46), channel_id=1, source_target_pairs={{0,127},{1,0},{2,1},{3,2},{4,3},{5,4},{6,5},{7,6},{8,7},{9,8},{10,... | collective-permute-start | bytes 786440 | tf_op jit(solution)/shard_map/ppermute | solution.py:317
  66.3 12.7 %collective-permute-start.8 = (bf16[2,128,256]{2,1,0:T(8,128)(2,1)S(1)}, bf16[2,128,256]{2,1,0:T(8,128)(2,1)S(1)}, u32[]{:S(2)}, u32[]{:S(2)}) collective-permute-start(bf16[2,128,256]{2,1,0:T(8,128)(2,1)S(1)} %collective-permute-done.4.outer), channel_id=1, source_target_pairs={{0,1},{1,2},{2,3},{3,4},{4,5},{5,6},{6,7},{7,8},{8,9},{9,10},{10,1... | collective-permute-start | bytes 393224 | tf_op jit(solution)/shard_map/ppermute | solution.py:317

commit v6 on v5

--- a/solution.py
+++ b/solution.py
@@ -217,8 +217,8 @@
     number, rows, picks, own, mate, probes, amplitudes, wave, first, second, *refs
 ):
     if number == 0:
-        sent_outer, sent_inband, kept, edge, held, made = refs
-        edges = edge
+        sent, kept, edges, held, made = refs
+        sent_outer, sent_inband = sent.at[0], sent.at[1]
     else:
         before, sent_outer, sent_inband, kept, both, held, made = refs
         both[0] = before[...]
@@ -257,7 +257,7 @@
     return rows[spot] + HALF + jnp.where(upper, 0, HALF), cols[spot]
 
 
-def own_kernel(rows, cols, kept0, kept1, outer, inband, total):
+def own_kernel(rows, cols, kept0, kept1, back, total):
     cut = lax.axis_index("cuts")
     places_here = places(rows)
     total[...] = jnp.zeros_like(total)
@@ -266,8 +266,8 @@
         for number, kept in enumerate((kept0, kept1)):
             spot = jnp.where(cut == 0, places_here[number], places_here[2 + number])
             put(rows[spot] + HALF, cols[spot], kept[channel])
-        top, left = put_inband(put, rows, cols, 0, inband, channel)
-        put(top, left, outer[channel].astype(F32))
+        top, left = put_inband(put, rows, cols, 0, back.at[1], channel)
+        put(top, left, back[0, channel].astype(F32))
 
 
 def rest_kernel(
@@ -332,8 +332,9 @@
     early = move(early, "early")
     late = move(late, "late")
     sent = call(mate_kernel, "mate", [rows, cols, band, early], [full, full], [near])
-    *sent, late = lax.optimization_barrier((*sent, late))
-    mates = [move(x, "mate") for x in sent]
+    sent0, sent1, late = lax.optimization_barrier((*sent, late))
+    mate0 = move(sent0, "mate")
+    mate1 = move(sent1, "mate")
     own0, own1, spots = call(
         own_windows_kernel, "windows", [rows, cols, band, early, late],
         [full, full, arr(8, dtype=jnp.int32)], [near], out_specs=[VM, VM, SM],
@@ -341,23 +342,23 @@
     optics = [probes, amplitudes, wave, first, second]
     work = [pltpu.VMEM((2, 2, SIDE, SIDE), BF), pltpu.VMEM((2, 2, SIDE, SIDE), F32)]
     wide_full = arr(2, SIDE, SIDE, dtype=F32)
-    outer0, inband0, kept0, edge0 = call(
-        functools.partial(solo_kernel, 0), "solo0", [rows, probe_choice, own0, mates[0]] + optics,
-        [half, half, wide_full, half], work,
-    )
-    outer0 = move(outer0, "mate")
-    inband0 = move(inband0, "mate")
+    back0, kept0, edge0 = call(
+        functools.partial(solo_kernel, 0), "solo0", [rows, probe_choice, own0, mate0] + optics,
+        [arr(2, 2, HALF, SIDE), wide_full, half], work,
+    )
+    back0 = move(back0, "mate")
     outer1, inband1, kept1, edges = call(
         functools.partial(solo_kernel, 1), "solo1",
-        [rows, probe_choice, own1, mates[1]] + optics + [edge0],
+        [rows, probe_choice, own1, mate1] + optics + [edge0],
         [half, arr(2, HALF + 64, SIDE), wide_full, arr(2, 2, HALF, SIDE)], work, flops=10**11,
     )
+    inband1 = move(inband1, "mate")
+    outer1, back0 = lax.optimization_barrier((outer1, back0))
     relay1 = move(outer1, "direct")
-    inband1 = move(inband1, "mate")
     edges = move(edges, "early")
-    relay0 = move(outer0, "late")
+    relay0 = move(back0[0], "late")
     (total,) = call(
-        own_kernel, "own", [rows, cols, kept0, kept1, outer0, inband0],
+        own_kernel, "own", [rows, cols, kept0, kept1, back0],
         [arr(2, EXT, COLS, dtype=F32)], flops=10**11,
     )
     _, gradient = call(

time: 83.5 us -> 84 us (level); the launches traced: 81.9 us -> 83.9 us
  waiting for transfers between devices: 30.3 us -> 32.6 us
    ppermute x10 -> x9, waiting for transfers between devices: 30.3 us -> 32.6 us  [shards(): move = lambda x, way: lax.ppermute(x, AXES, route[way])]
    ppermute x10 -> x9, starting transfers between devices: 29.4 us -> 29.1 us  [shards(): move = lambda x, way: lax.ppermute(x, AXES, route[way])]
  transfers between devices with their start and end apart: 10 -> 9, of which waited for: 6 -> 5; matrix products, arithmetic and copies ran while one was open for 1% -> 1% of each run, Pallas kernels for 19% -> 19%
where the time goes in v6:
time: 84 us; the launch traced here: 83.9 us
  waiting for transfers between devices  32.6 us (39%)
  starting transfers between devices  29.1 us (35%)
  Pallas kernels  20.8 us (25%)
  local copies, waits for them, and re-layouts  0.99 us (1%)
    ppermute x9, waiting for transfers between devices, shards(): move = lambda x, way: lax.ppermute(x, AXES, route[way])  32.6 us
    ppermute x9, starting transfers between devices, shards(): move = lambda x, way: lax.ppermute(x, AXES, route[way])  29.1 us
    pallas_call x7, Pallas kernels, call(): pl.pallas_call(kernel, name=name, out_shape=outputs, in_specs=in_specs or...  20.8 us
  transfers between devices with their start and end apart: 9, of which 5 were waited for; matrix products, arithmetic and copies ran while one was open for 1% of the time, Pallas kernels for 19%

profile of v6, /device:TPU:8, one launch (start us, length us, event | category | flops | bytes accessed | tf_op | source)
XLA Modules:
  0.0 83.9 jit_solution(14705839426872317632)
XLA Ops:
  0.0 2.2 %edge.1 = (bf16[2064,128]{1,0:T(8,128)(2,1)S(1)}, bf16[2064,128]{1,0:T(8,128)(2,1)S(1)}, f32[2,256,1024]{2,1,0:T(8,128)S(1)}, s32[4]{0:T(128)S(1)}, s32[4]{0:T(128)S(1)}) custom-call(s32[4]{0:T(128)} %rows_in.1, s32[4]{0:T(128)} %cols_in.1, f32[1,2,256,1024]{3,2,1,0:T(8,128)} %objects_in.1), custom_call_target="tpu_custom_call" | custom-call | flops 1 | bytes 1 | tf_op jit(solution)/shard_map/edge/pallas_call | solution.py:298
  2.2 6.2 %collective-permute-start = (bf16[2064,128]{1,0:T(8,128)(2,1)S(1)}, bf16[2064,128]{1,0:T(8,128)(2,1)S(1)}, u32[]{:S(2)}, u32[]{:S(2)}) collective-permute-start(bf16[2064,128]{1,0:T(8,128)(2,1)S(1)} %get-tuple-element.31), channel_id=1, source_target_pairs={{0,127},{1,0},{2,1},{3,2},{4,3},{5,4},{6,5},{7,6},{8,7},{9,8},{10,... | collective-permute-start | bytes 1585160 | tf_op jit(solution)/shard_map/ppermute | solution.py:317
  8.5 7.7 %collective-permute-done.early = bf16[2064,128]{1,0:T(8,128)(2,1)S(1)} collective-permute-done((bf16[2064,128]{1,0:T(8,128)(2,1)S(1)}, bf16[2064,128]{1,0:T(8,128)(2,1)S(1)}, u32[]{:S(2)}, u32[]{:S(2)}) %collective-permute-start) | collective-permute-done | bytes 528416 | tf_op jit(solution)/shard_map/ppermute | solution.py:317
  16.2 1.6 %mate.1 = (bf16[2,256,256]{2,1,0:T(8,128)(2,1)S(1)}, bf16[2,256,256]{2,1,0:T(8,128)(2,1)S(1)}) custom-call(s32[4]{0:T(128)S(1)} %get-tuple-element.28.rows, s32[4]{0:T(128)S(1)} %get-tuple-element.29.cols, f32[2,256,1024]{2,1,0:T(8,128)S(1)} %get-tuple-element.30.objects, bf16[2064,128]{1,0:T(8,128)(2,1)S(1)} %collective-permute-done.early), custom_call_target="tpu_custom_call" | custom-call | flops 1 | bytes 1 | tf_op jit(solution)/shard_map/mate/pallas_call | solution.py:298
  17.8 4.1 %collective-permute-done.1.late = bf16[2064,128]{1,0:T(8,128)(2,1)S(1)} collective-permute-done((bf16[2064,128]{1,0:T(8,128)(2,1)S(1)}, bf16[2064,128]{1,0:T(8,128)(2,1)S(1)}, u32[]{:S(2)}, u32[]{:S(2)}) %collective-permute-start.1) | collective-permute-done | bytes 528416 | tf_op jit(solution)/shard_map/ppermute | solution.py:317
  21.9 7.9 %collective-permute-start.2 = (bf16[2,256,256]{2,1,0:T(8,128)(2,1)S(1)}, bf16[2,256,256]{2,1,0:T(8,128)(2,1)S(1)}, u32[]{:S(2)}, u32[]{:S(2)}) collective-permute-start(bf16[2,256,256]{2,1,0:T(8,128)(2,1)S(1)} %get-tuple-element.38), channel_id=1, source_target_pairs={{0,128},{1,129},{2,130},{3,131},{4,132},{5,133},{6,134},{7,135},{8... | collective-permute-start | bytes 786440 | tf_op jit(solution)/shard_map/ppermute | solution.py:317
  29.8 0.1 collective-permute-start.3
  29.9 0.9 %cosine_bitcast_fusion = (f32[1,256,256]{2,1,0:T(8,128)S(1)}, f32[1,256,256]{2,1,0:T(8,128)S(1)}) fusion(f32[256,256]{1,0:T(8,128)S(1)} %copy-done.5), kind=kLoop, calls=%fused_computation.2 | loop fusion | bytes 786432 | tf_op jit(solution)/shard_map/stack | solution.py:319
  30.9 0.0 copy-start
  30.9 0.0 copy-start.2
  30.9 0.0 copy-start.3
  31.0 2.2 %windows.1 = (bf16[2,256,256]{2,1,0:T(8,128)(2,1)S(1)}, bf16[2,256,256]{2,1,0:T(8,128)(2,1)S(1)}, s32[8]{0:T(128)S(1)}) custom-call(s32[4]{0:T(128)S(1)} %get-tuple-element.28.rows, s32[4]{0:T(128)S(1)} %get-tuple-element.29.cols, f32[2,256,1024]{2,1,0:T(8,128)S(1)} %get-tuple-element.30.objects, bf16[2064,128]{1,0:T(8,128)(2,1)S(1)} %collective-permute-done.early, ...), custom_call_target="tpu_custom_call" | custom-call | flops 1 | bytes 1 | tf_op jit(solution)/shard_map/windows/pallas_call | solution.py:298
  33.2 8.1 %collective-permute-done.2.mate = bf16[2,256,256]{2,1,0:T(8,128)(2,1)S(1)} collective-permute-done((bf16[2,256,256]{2,1,0:T(8,128)(2,1)S(1)}, bf16[2,256,256]{2,1,0:T(8,128)(2,1)S(1)}, u32[]{:S(2)}, u32[]{:S(2)}) %collective-permute-start.2) | collective-permute-done | bytes 262176 | tf_op jit(solution)/shard_map/ppermute | solution.py:317
  41.4 4.8 %solo0.1 = (bf16[2,2,128,256]{3,2,1,0:T(8,128)(2,1)S(1)}, f32[2,256,256]{2,1,0:T(8,128)S(1)}, bf16[2,128,256]{2,1,0:T(8,128)(2,1)S(1)}) custom-call(s32[4]{0:T(128)S(1)} %get-tuple-element.28.rows, s32[4]{0:T(128)S(1)} %copy-done.4, bf16[2,256,256]{2,1,0:T(8,128)(2,1)S(1)} %get-tuple-element.37.own, bf16[2,256,256]{2,1,0:T(8,128)(2,1)S(1)} %collective-permute-done.2.mate, ...), custom_call_target="tpu_custom_call" | custom-call | flops 1 | bytes 1 | tf_op jit(solution)/shard_map/solo0/pallas_call | solution.py:298
  46.2 6.0 %collective-permute-start.4 = (bf16[2,2,128,256]{3,2,1,0:T(8,128)(2,1)S(1)}, bf16[2,2,128,256]{3,2,1,0:T(8,128)(2,1)S(1)}, u32[]{:S(2)}, u32[]{:S(2)}) collective-permute-start(bf16[2,2,128,256]{3,2,1,0:T(8,128)(2,1)S(1)} %get-tuple-element.45), channel_id=1, source_target_pairs={{0,128},{1,129},{2,130},{3,131},{4,132},{5,133},{6,134},{7,135},{8... | collective-permute-start | bytes 786440 | tf_op jit(solution)/shard_map/ppermute | solution.py:317
  52.3 4.9 %solo1.1 = (bf16[2,128,256]{2,1,0:T(8,128)(2,1)S(1)}, bf16[2,192,256]{2,1,0:T(8,128)(2,1)S(1)}, f32[2,256,256]{2,1,0:T(8,128)S(1)}, bf16[2,2,128,256]{3,2,1,0:T(8,128)(2,1)S(1)}) custom-call(s32[4]{0:T(128)S(1)} %get-tuple-element.28.rows, s32[4]{0:T(128)S(1)} %copy-done.4, bf16[2,256,256]{2,1,0:T(8,128)(2,1)S(1)} %get-tuple-element.40.own, ...), custom_call_target="tpu_custom_call" | custom-call | flops 99999997952 | bytes 1 | tf_op jit(solution)/shard_map/solo1/pallas_call | solution.py:298
  57.1 4.7 %collective-permute-start.5 = (bf16[2,192,256]{2,1,0:T(8,128)(2,1)S(1)}, bf16[2,192,256]{2,1,0:T(8,128)(2,1)S(1)}, u32[]{:S(2)}, u32[]{:S(2)}) collective-permute-start(bf16[2,192,256]{2,1,0:T(8,128)(2,1)S(1)} %get-tuple-element.47), channel_id=1, source_target_pairs={{0,128},{1,129},{2,130},{3,131},{4,132},{5,133},{6,134},{7,135},{8... | collective-permute-start | bytes 589832 | tf_op jit(solution)/shard_map/ppermute | solution.py:317
  61.9 1.8 %collective-permute-start.6 = (bf16[2,2,128,256]{3,2,1,0:T(8,128)(2,1)S(1)}, bf16[2,2,128,256]{3,2,1,0:T(8,128)(2,1)S(1)}, u32[]{:S(2)}, u32[]{:S(2)}) collective-permute-start(bf16[2,2,128,256]{3,2,1,0:T(8,128)(2,1)S(1)} %get-tuple-element.48), channel_id=1, source_target_pairs={{0,127},{1,0},{2,1},{3,2},{4,3},{5,4},{6,5},{7,6},{8,7},{9,8},{10,... | collective-permute-start | bytes 786440 | tf_op jit(solution)/shard_map/ppermute | solution.py:317
  63.7 5.5 %collective-permute-done.4.back = bf16[2,2,128,256]{3,2,1,0:T(8,128)(2,1)S(1)} collective-permute-done((bf16[2,2,128,256]{3,2,1,0:T(8,128)(2,1)S(1)}, bf16[2,2,128,256]{3,2,1,0:T(8,128)(2,1)S(1)}, u32[]{:S(2)}, u32[]{:S(2)}) %collective-permute-start.4) | collective-permute-done | bytes 262176 | tf_op jit(solution)/shard_map/ppermute | solution.py:317
  69.2 0.1 collective-permute-start.7
  69.3 2.2 %collective-permute-start.8 = (bf16[2,128,256]{2,1,0:T(8,128)(2,1)S(1)}, bf16[2,128,256]{2,1,0:T(8,128)(2,1)S(1)}, u32[]{:S(2)}, u32[]{:S(2)}) collective-permute-start(bf16[2,128,256]{2,1,0:T(8,128)(2,1)S(1)} %get-tuple-element.49), channel_id=1, source_target_pairs={{0,255},{1,128},{2,129},{3,130},{4,131},{5,132},{6,133},{7,134},{8... | collective-permute-start | bytes 393224 | tf_op jit(solution)/shard_map/ppermute | solution.py:317
  71.5 2.3 %own.1.given = f32[2,512,1024]{2,1,0:T(8,128)S(1)} custom-call(s32[4]{0:T(128)S(1)} %get-tuple-element.28.rows, s32[4]{0:T(128)S(1)} %get-tuple-element.29.cols, f32[2,256,256]{2,1,0:T(8,128)S(1)} %get-tuple-element.39.kept0, f32[2,256,256]{2,1,0:T(8,128)S(1)} %get-tuple-element.43.kept1, bf16[2,2,128,256]{3,2,1,0:T(8,128)(2,1)S(1)} %collective-permute-done.4.back), custom_call_target="tpu_custom_call" | custom-call | flops 99999997952 | bytes 1 | tf_op jit(solution)/shard_map/own/pallas_call | solution.py:298
  73.8 7.1 %collective-permute-done.7.relay0 = bf16[2,128,256]{2,1,0:T(8,128)(2,1)S(1)} collective-permute-done((bf16[2,128,256]{2,1,0:T(8,128)(2,1)S(1)}, bf16[2,128,256]{2,1,0:T(8,128)(2,1)S(1)}, u32[]{:S(2)}, u32[]{:S(2)}) %collective-permute-start.7) | collective-permute-done | bytes 131104 | tf_op jit(solution)/shard_map/ppermute | solution.py:317
  81.0 2.8 %rest.1 = (f32[2,512,1024]{2,1,0:T(8,128)S(1)}, f32[1,2,256,1024]{3,2,1,0:T(8,128)}) custom-call(s32[4]{0:T(128)S(1)} %get-tuple-element.28.rows, s32[4]{0:T(128)S(1)} %get-tuple-element.29.cols, s32[8]{0:T(128)S(1)} %get-tuple-element.36.spots, f32[2,512,1024]{2,1,0:T(8,128)S(1)} %own.1.given, ...), custom_call_target="tpu_custom_call", output_to_operand_aliasing={{0}: (3, {})} | custom-call | flops 1 | bytes 1 | tf_op jit(solution)/shard_map/rest/pallas_call | solution.py:298
  (16 shorter events, 0.1 us)
Async XLA Ops:
  0.0 29.9 %copy-start.5 = (f32[256,256]{1,0:T(8,128)S(1)}, f32[256,256]{1,0:T(8,128)}, u32[]{:S(2)}) copy-start(f32[256,256]{1,0:T(8,128)} %param.12) | copy-start | bytes 786436
  2.2 14.0 %collective-permute-start = (bf16[2064,128]{1,0:T(8,128)(2,1)S(1)}, bf16[2064,128]{1,0:T(8,128)(2,1)S(1)}, u32[]{:S(2)}, u32[]{:S(2)}) collective-permute-start(bf16[2064,128]{1,0:T(8,128)(2,1)S(1)} %get-tuple-element.31), channel_id=1, source_target_pairs={{0,127},{1,0},{2,1},{3,2},{4,3},{5,4},{6,5},{7,6},{8,7},{9,8},{10,... | collective-permute-start | bytes 1585160 | tf_op jit(solution)/shard_map/ppermute | solution.py:317
  8.5 13.5 %collective-permute-start.1 = (bf16[2064,128]{1,0:T(8,128)(2,1)S(1)}, bf16[2064,128]{1,0:T(8,128)(2,1)S(1)}, u32[]{:S(2)}, u32[]{:S(2)}) collective-permute-start(bf16[2064,128]{1,0:T(8,128)(2,1)S(1)} %get-tuple-element.34), channel_id=1, source_target_pairs={{0,1},{1,2},{2,3},{3,4},{4,5},{5,6},{6,7},{7,8},{8,9},{9,10},{10,1... | collective-permute-start | bytes 1585160 | tf_op jit(solution)/shard_map/ppermute | solution.py:317
  21.9 19.4 %collective-permute-start.2 = (bf16[2,256,256]{2,1,0:T(8,128)(2,1)S(1)}, bf16[2,256,256]{2,1,0:T(8,128)(2,1)S(1)}, u32[]{:S(2)}, u32[]{:S(2)}) collective-permute-start(bf16[2,256,256]{2,1,0:T(8,128)(2,1)S(1)} %get-tuple-element.38), channel_id=1, source_target_pairs={{0,128},{1,129},{2,130},{3,131},{4,132},{5,133},{6,134},{7,135},{8... | collective-permute-start | bytes 786440 | tf_op jit(solution)/shard_map/ppermute | solution.py:317
  29.8 22.4 %collective-permute-start.3 = (bf16[2,256,256]{2,1,0:T(8,128)(2,1)S(1)}, bf16[2,256,256]{2,1,0:T(8,128)(2,1)S(1)}, u32[]{:S(2)}, u32[]{:S(2)}) collective-permute-start(bf16[2,256,256]{2,1,0:T(8,128)(2,1)S(1)} %get-tuple-element.41), channel_id=1, source_target_pairs={{0,128},{1,129},{2,130},{3,131},{4,132},{5,133},{6,134},{7,135},{8... | collective-permute-start | bytes 786440 | tf_op jit(solution)/shard_map/ppermute | solution.py:317
  30.9 10.5 %copy-start = (bf16[4,2,256,256]{3,2,1,0:T(8,128)(2,1)S(1)}, bf16[4,2,256,256]{3,2,1,0:T(8,128)(2,1)}, u32[]{:S(2)}) copy-start(bf16[4,2,256,256]{3,2,1,0:T(8,128)(2,1)} %probes.3) | copy-start | bytes 3145732
  30.9 10.5 %copy-start.1 = (f32[4,256,256]{2,1,0:T(8,128)S(1)}, f32[4,256,256]{2,1,0:T(8,128)}, u32[]{:S(2)}) copy-start(f32[4,256,256]{2,1,0:T(8,128)} %amplitudes.3) | copy-start | bytes 3145732
  30.9 10.4 %copy-start.2 = (bf16[512,512]{1,0:T(8,128)(2,1)S(1)}, bf16[512,512]{1,0:T(8,128)(2,1)}, u32[]{:S(2)}) copy-start(bf16[512,512]{1,0:T(8,128)(2,1)} %constant.5.clone.second) | copy-start | bytes 1572868
  30.9 10.4 %copy-start.3 = (bf16[512,512]{1,0:T(8,128)(2,1)S(1)}, bf16[512,512]{1,0:T(8,128)(2,1)}, u32[]{:S(2)}) copy-start(bf16[512,512]{1,0:T(8,128)(2,1)} %constant.4.clone.first) | copy-start | bytes 1572868
  30.9 10.4 %copy-start.4 = (s32[4]{0:T(128)S(1)}, s32[4]{0:T(128)}, u32[]{:S(2)}) copy-start(s32[4]{0:T(128)} %picks.3) | copy-start | bytes 52
  46.2 23.0 %collective-permute-start.4 = (bf16[2,2,128,256]{3,2,1,0:T(8,128)(2,1)S(1)}, bf16[2,2,128,256]{3,2,1,0:T(8,128)(2,1)S(1)}, u32[]{:S(2)}, u32[]{:S(2)}) collective-permute-start(bf16[2,2,128,256]{3,2,1,0:T(8,128)(2,1)S(1)} %get-tuple-element.45), channel_id=1, source_target_pairs={{0,128},{1,129},{2,130},{3,131},{4,132},{5,133},{6,134},{7,135},{8... | collective-permute-start | bytes 786440 | tf_op jit(solution)/shard_map/ppermute | solution.py:317
  57.1 16.7 %collective-permute-start.5 = (bf16[2,192,256]{2,1,0:T(8,128)(2,1)S(1)}, bf16[2,192,256]{2,1,0:T(8,128)(2,1)S(1)}, u32[]{:S(2)}, u32[]{:S(2)}) collective-permute-start(bf16[2,192,256]{2,1,0:T(8,128)(2,1)S(1)} %get-tuple-element.47), channel_id=1, source_target_pairs={{0,128},{1,129},{2,130},{3,131},{4,132},{5,133},{6,134},{7,135},{8... | collective-permute-start | bytes 589832 | tf_op jit(solution)/shard_map/ppermute | solution.py:317
  61.9 12.0 %collective-permute-start.6 = (bf16[2,2,128,256]{3,2,1,0:T(8,128)(2,1)S(1)}, bf16[2,2,128,256]{3,2,1,0:T(8,128)(2,1)S(1)}, u32[]{:S(2)}, u32[]{:S(2)}) collective-permute-start(bf16[2,2,128,256]{3,2,1,0:T(8,128)(2,1)S(1)} %get-tuple-element.48), channel_id=1, source_target_pairs={{0,127},{1,0},{2,1},{3,2},{4,3},{5,4},{6,5},{7,6},{8,7},{9,8},{10,... | collective-permute-start | bytes 786440 | tf_op jit(solution)/shard_map/ppermute | solution.py:317
  69.2 11.8 %collective-permute-start.7 = (bf16[2,128,256]{2,1,0:T(8,128)(2,1)S(1)}, bf16[2,128,256]{2,1,0:T(8,128)(2,1)S(1)}, u32[]{:S(2)}, u32[]{:S(2)}) collective-permute-start(bf16[2,128,256]{2,1,0:T(8,128)(2,1)S(1)} %slice_bitcast_fusion), channel_id=1, source_target_pairs={{0,1},{1,2},{2,3},{3,4},{4,5},{5,6},{6,7},{7,8},{8,9},{9,10},{10,1... | collective-permute-start | bytes 393224 | tf_op jit(solution)/shard_map/ppermute | solution.py:317
  69.3 11.7 %collective-permute-start.8 = (bf16[2,128,256]{2,1,0:T(8,128)(2,1)S(1)}, bf16[2,128,256]{2,1,0:T(8,128)(2,1)S(1)}, u32[]{:S(2)}, u32[]{:S(2)}) collective-permute-start(bf16[2,128,256]{2,1,0:T(8,128)(2,1)S(1)} %get-tuple-element.49), channel_id=1, source_target_pairs={{0,255},{1,128},{2,129},{3,130},{4,131},{5,132},{6,133},{7,134},{8... | collective-permute-start | bytes 393224 | tf_op jit(solution)/shard_map/ppermute | solution.py:317

commit v7 on v6

--- a/solution.py
+++ b/solution.py
@@ -332,19 +332,20 @@
     early = move(early, "early")
     late = move(late, "late")
     sent = call(mate_kernel, "mate", [rows, cols, band, early], [full, full], [near])
-    sent0, sent1, late = lax.optimization_barrier((*sent, late))
+    sent0, late = lax.optimization_barrier((sent[0], late))
     mate0 = move(sent0, "mate")
-    mate1 = move(sent1, "mate")
     own0, own1, spots = call(
         own_windows_kernel, "windows", [rows, cols, band, early, late],
         [full, full, arr(8, dtype=jnp.int32)], [near], out_specs=[VM, VM, SM],
     )
+    sent1, own1 = lax.optimization_barrier((sent[1], own1))
+    mate1 = move(sent1, "mate")
     optics = [probes, amplitudes, wave, first, second]
     work = [pltpu.VMEM((2, 2, SIDE, SIDE), BF), pltpu.VMEM((2, 2, SIDE, SIDE), F32)]
     wide_full = arr(2, SIDE, SIDE, dtype=F32)
     back0, kept0, edge0 = call(
         functools.partial(solo_kernel, 0), "solo0", [rows, probe_choice, own0, mate0] + optics,
-        [arr(2, 2, HALF, SIDE), wide_full, half], work,
+        [arr(2, 2, HALF, SIDE), wide_full, half], work, flops=10**11,
     )
     back0 = move(back0, "mate")
     outer1, inband1, kept1, edges = call(

time: 84 us -> 85.9 us (1.023)
  waiting for transfers between devices: 32.6 us -> 40.8 us
  starting transfers between devices: 29.1 us -> 22.8 us
    ppermute x9, waiting for transfers between devices: 32.6 us -> 40.8 us  [shards(): move = lambda x, way: lax.ppermute(x, AXES, route[way])]
    ppermute x9, starting transfers between devices: 29.1 us -> 22.8 us  [shards(): move = lambda x, way: lax.ppermute(x, AXES, route[way])]
  transfers between devices with their start and end apart: 9 -> 9, of which waited for: 5 -> 6; matrix products, arithmetic and copies ran while one was open for 1% -> 1% of each run, Pallas kernels for 19% -> 19%
where the time goes in v7:
time: 85.9 us; the launch traced here: 85.8 us
  waiting for transfers between devices  40.8 us (47%)
  starting transfers between devices  22.8 us (27%)
  Pallas kernels  20.9 us (24%)
  local copies, waits for them, and re-layouts  0.99 us (1%)
    ppermute x9, waiting for transfers between devices, shards(): move = lambda x, way: lax.ppermute(x, AXES, route[way])  40.8 us
    ppermute x9, starting transfers between devices, shards(): move = lambda x, way: lax.ppermute(x, AXES, route[way])  22.8 us
    pallas_call x7, Pallas kernels, call(): pl.pallas_call(kernel, name=name, out_shape=outputs, in_specs=in_specs or...  20.9 us
  transfers between devices with their start and end apart: 9, of which 6 were waited for; matrix products, arithmetic and copies ran while one was open for 1% of the time, Pallas kernels for 19%

profile of v7, /device:TPU:8, one launch (start us, length us, event | category | flops | bytes accessed | tf_op | source)
XLA Modules:
  0.0 85.8 jit_solution(13532035686387350203)
XLA Ops:
  0.0 2.2 %edge.1 = (bf16[2064,128]{1,0:T(8,128)(2,1)S(1)}, bf16[2064,128]{1,0:T(8,128)(2,1)S(1)}, f32[2,256,1024]{2,1,0:T(8,128)S(1)}, s32[4]{0:T(128)S(1)}, s32[4]{0:T(128)S(1)}) custom-call(s32[4]{0:T(128)} %rows_in.1, s32[4]{0:T(128)} %cols_in.1, f32[1,2,256,1024]{3,2,1,0:T(8,128)} %objects_in.1), custom_call_target="tpu_custom_call" | custom-call | flops 1 | bytes 1 | tf_op jit(solution)/shard_map/edge/pallas_call | solution.py:298
  2.2 6.2 %collective-permute-start = (bf16[2064,128]{1,0:T(8,128)(2,1)S(1)}, bf16[2064,128]{1,0:T(8,128)(2,1)S(1)}, u32[]{:S(2)}, u32[]{:S(2)}) collective-permute-start(bf16[2064,128]{1,0:T(8,128)(2,1)S(1)} %get-tuple-element.32), channel_id=1, source_target_pairs={{0,127},{1,0},{2,1},{3,2},{4,3},{5,4},{6,5},{7,6},{8,7},{9,8},{10,... | collective-permute-start | bytes 1585160 | tf_op jit(solution)/shard_map/ppermute | solution.py:317
  8.5 7.7 %collective-permute-done.early = bf16[2064,128]{1,0:T(8,128)(2,1)S(1)} collective-permute-done((bf16[2064,128]{1,0:T(8,128)(2,1)S(1)}, bf16[2064,128]{1,0:T(8,128)(2,1)S(1)}, u32[]{:S(2)}, u32[]{:S(2)}) %collective-permute-start) | collective-permute-done | bytes 528416 | tf_op jit(solution)/shard_map/ppermute | solution.py:317
  16.2 1.6 %mate.1 = (bf16[2,256,256]{2,1,0:T(8,128)(2,1)S(1)}, bf16[2,256,256]{2,1,0:T(8,128)(2,1)S(1)}) custom-call(s32[4]{0:T(128)S(1)} %get-tuple-element.29.rows, s32[4]{0:T(128)S(1)} %get-tuple-element.30.cols, f32[2,256,1024]{2,1,0:T(8,128)S(1)} %get-tuple-element.31.objects, bf16[2064,128]{1,0:T(8,128)(2,1)S(1)} %collective-permute-done.early), custom_call_target="tpu_custom_call" | custom-call | flops 1 | bytes 1 | tf_op jit(solution)/shard_map/mate/pallas_call | solution.py:298
  17.8 4.1 %collective-permute-done.1.late = bf16[2064,128]{1,0:T(8,128)(2,1)S(1)} collective-permute-done((bf16[2064,128]{1,0:T(8,128)(2,1)S(1)}, bf16[2064,128]{1,0:T(8,128)(2,1)S(1)}, u32[]{:S(2)}, u32[]{:S(2)}) %collective-permute-start.1) | collective-permute-done | bytes 528416 | tf_op jit(solution)/shard_map/ppermute | solution.py:317
  21.9 7.9 %collective-permute-start.2 = (bf16[2,256,256]{2,1,0:T(8,128)(2,1)S(1)}, bf16[2,256,256]{2,1,0:T(8,128)(2,1)S(1)}, u32[]{:S(2)}, u32[]{:S(2)}) collective-permute-start(bf16[2,256,256]{2,1,0:T(8,128)(2,1)S(1)} %get-tuple-element.38), channel_id=1, source_target_pairs={{0,128},{1,129},{2,130},{3,131},{4,132},{5,133},{6,134},{7,135},{8... | collective-permute-start | bytes 786440 | tf_op jit(solution)/shard_map/ppermute | solution.py:317
  29.8 0.9 %cosine_bitcast_fusion = (f32[1,256,256]{2,1,0:T(8,128)S(1)}, f32[1,256,256]{2,1,0:T(8,128)S(1)}) fusion(f32[256,256]{1,0:T(8,128)S(1)} %copy-done.5), kind=kLoop, calls=%fused_computation.2 | loop fusion | bytes 786432 | tf_op jit(solution)/shard_map/stack | solution.py:319
  30.8 0.0 copy-start.3
  30.9 0.0 copy-start.4
  30.9 2.2 %windows.1 = (bf16[2,256,256]{2,1,0:T(8,128)(2,1)S(1)}, bf16[2,256,256]{2,1,0:T(8,128)(2,1)S(1)}, s32[8]{0:T(128)S(1)}) custom-call(s32[4]{0:T(128)S(1)} %get-tuple-element.29.rows, s32[4]{0:T(128)S(1)} %get-tuple-element.30.cols, f32[2,256,1024]{2,1,0:T(8,128)S(1)} %get-tuple-element.31.objects, bf16[2064,128]{1,0:T(8,128)(2,1)S(1)} %collective-permute-done.early, ...), custom_call_target="tpu_custom_call" | custom-call | flops 1 | bytes 1 | tf_op jit(solution)/shard_map/windows/pallas_call | solution.py:298
  33.1 0.1 collective-permute-start.3
  33.3 10.5 %collective-permute-done.2.mate = bf16[2,256,256]{2,1,0:T(8,128)(2,1)S(1)} collective-permute-done((bf16[2,256,256]{2,1,0:T(8,128)(2,1)S(1)}, bf16[2,256,256]{2,1,0:T(8,128)(2,1)S(1)}, u32[]{:S(2)}, u32[]{:S(2)}) %collective-permute-start.2) | collective-permute-done | bytes 262176 | tf_op jit(solution)/shard_map/ppermute | solution.py:317
  43.8 4.8 %solo0.1 = (bf16[2,2,128,256]{3,2,1,0:T(8,128)(2,1)S(1)}, f32[2,256,256]{2,1,0:T(8,128)S(1)}, bf16[2,128,256]{2,1,0:T(8,128)(2,1)S(1)}) custom-call(s32[4]{0:T(128)S(1)} %get-tuple-element.29.rows, s32[4]{0:T(128)S(1)} %copy-done.2, bf16[2,256,256]{2,1,0:T(8,128)(2,1)S(1)} %get-tuple-element.37.own, bf16[2,256,256]{2,1,0:T(8,128)(2,1)S(1)} %collective-permute-done.2.mate, ...), custom_call_target="tpu_custom_call" | custom-call | flops 99999997952 | bytes 1 | tf_op jit(solution)/shard_map/solo0/pallas_call | solution.py:298
  48.6 6.8 %collective-permute-start.4 = (bf16[2,2,128,256]{3,2,1,0:T(8,128)(2,1)S(1)}, bf16[2,2,128,256]{3,2,1,0:T(8,128)(2,1)S(1)}, u32[]{:S(2)}, u32[]{:S(2)}) collective-permute-start(bf16[2,2,128,256]{3,2,1,0:T(8,128)(2,1)S(1)} %get-tuple-element.47), channel_id=1, source_target_pairs={{0,128},{1,129},{2,130},{3,131},{4,132},{5,133},{6,134},{7,135},{8... | collective-permute-start | bytes 786440 | tf_op jit(solution)/shard_map/ppermute | solution.py:317
  55.4 4.9 %solo1.1 = (bf16[2,128,256]{2,1,0:T(8,128)(2,1)S(1)}, bf16[2,192,256]{2,1,0:T(8,128)(2,1)S(1)}, f32[2,256,256]{2,1,0:T(8,128)S(1)}, bf16[2,2,128,256]{3,2,1,0:T(8,128)(2,1)S(1)}) custom-call(s32[4]{0:T(128)S(1)} %get-tuple-element.29.rows, s32[4]{0:T(128)S(1)} %copy-done.2, bf16[2,256,256]{2,1,0:T(8,128)(2,1)S(1)} %get-tuple-element.42.own, ...), custom_call_target="tpu_custom_call" | custom-call | flops 99999997952 | bytes 1 | tf_op jit(solution)/shard_map/solo1/pallas_call | solution.py:298
  60.3 0.3 collective-permute-start.5
  60.6 1.2 %collective-permute-start.6 = (bf16[2,2,128,256]{3,2,1,0:T(8,128)(2,1)S(1)}, bf16[2,2,128,256]{3,2,1,0:T(8,128)(2,1)S(1)}, u32[]{:S(2)}, u32[]{:S(2)}) collective-permute-start(bf16[2,2,128,256]{3,2,1,0:T(8,128)(2,1)S(1)} %get-tuple-element.50), channel_id=1, source_target_pairs={{0,127},{1,0},{2,1},{3,2},{4,3},{5,4},{6,5},{7,6},{8,7},{9,8},{10,... | collective-permute-start | bytes 786440 | tf_op jit(solution)/shard_map/ppermute | solution.py:317
  61.8 10.0 %collective-permute-done.4.back = bf16[2,2,128,256]{3,2,1,0:T(8,128)(2,1)S(1)} collective-permute-done((bf16[2,2,128,256]{3,2,1,0:T(8,128)(2,1)S(1)}, bf16[2,2,128,256]{3,2,1,0:T(8,128)(2,1)S(1)}, u32[]{:S(2)}, u32[]{:S(2)}) %collective-permute-start.4) | collective-permute-done | bytes 262176 | tf_op jit(solution)/shard_map/ppermute | solution.py:317
  71.8 0.1 collective-permute-start.7
  71.9 0.1 collective-permute-start.8
  72.0 2.3 %own.1.given = f32[2,512,1024]{2,1,0:T(8,128)S(1)} custom-call(s32[4]{0:T(128)S(1)} %get-tuple-element.29.rows, s32[4]{0:T(128)S(1)} %get-tuple-element.30.cols, f32[2,256,256]{2,1,0:T(8,128)S(1)} %get-tuple-element.39.kept0, f32[2,256,256]{2,1,0:T(8,128)S(1)} %get-tuple-element.45.kept1, bf16[2,2,128,256]{3,2,1,0:T(8,128)(2,1)S(1)} %collective-permute-done.4.back), custom_call_target="tpu_custom_call" | custom-call | flops 99999997952 | bytes 1 | tf_op jit(solution)/shard_map/own/pallas_call | solution.py:298
  74.4 4.3 %collective-permute-done.5.inband = bf16[2,192,256]{2,1,0:T(8,128)(2,1)S(1)} collective-permute-done((bf16[2,192,256]{2,1,0:T(8,128)(2,1)S(1)}, bf16[2,192,256]{2,1,0:T(8,128)(2,1)S(1)}, u32[]{:S(2)}, u32[]{:S(2)}) %collective-permute-start.5) | collective-permute-done | bytes 196640 | tf_op jit(solution)/shard_map/ppermute | solution.py:317
  78.7 4.2 %collective-permute-done.7.relay0 = bf16[2,128,256]{2,1,0:T(8,128)(2,1)S(1)} collective-permute-done((bf16[2,128,256]{2,1,0:T(8,128)(2,1)S(1)}, bf16[2,128,256]{2,1,0:T(8,128)(2,1)S(1)}, u32[]{:S(2)}, u32[]{:S(2)}) %collective-permute-start.7) | collective-permute-done | bytes 131104 | tf_op jit(solution)/shard_map/ppermute | solution.py:317
  82.9 2.8 %rest.1 = (f32[2,512,1024]{2,1,0:T(8,128)S(1)}, f32[1,2,256,1024]{3,2,1,0:T(8,128)}) custom-call(s32[4]{0:T(128)S(1)} %get-tuple-element.29.rows, s32[4]{0:T(128)S(1)} %get-tuple-element.30.cols, s32[8]{0:T(128)S(1)} %get-tuple-element.36.spots, f32[2,512,1024]{2,1,0:T(8,128)S(1)} %own.1.given, ...), custom_call_target="tpu_custom_call", output_to_operand_aliasing={{0}: (3, {})} | custom-call | flops 1 | bytes 1 | tf_op jit(solution)/shard_map/rest/pallas_call | solution.py:298
  (16 shorter events, 0.1 us)
Async XLA Ops:
  0.0 29.8 %copy-start.5 = (f32[256,256]{1,0:T(8,128)S(1)}, f32[256,256]{1,0:T(8,128)}, u32[]{:S(2)}) copy-start(f32[256,256]{1,0:T(8,128)} %param.12) | copy-start | bytes 786436
  2.2 14.0 %collective-permute-start = (bf16[2064,128]{1,0:T(8,128)(2,1)S(1)}, bf16[2064,128]{1,0:T(8,128)(2,1)S(1)}, u32[]{:S(2)}, u32[]{:S(2)}) collective-permute-start(bf16[2064,128]{1,0:T(8,128)(2,1)S(1)} %get-tuple-element.32), channel_id=1, source_target_pairs={{0,127},{1,0},{2,1},{3,2},{4,3},{5,4},{6,5},{7,6},{8,7},{9,8},{10,... | collective-permute-start | bytes 1585160 | tf_op jit(solution)/shard_map/ppermute | solution.py:317
  8.5 13.5 %collective-permute-start.1 = (bf16[2064,128]{1,0:T(8,128)(2,1)S(1)}, bf16[2064,128]{1,0:T(8,128)(2,1)S(1)}, u32[]{:S(2)}, u32[]{:S(2)}) collective-permute-start(bf16[2064,128]{1,0:T(8,128)(2,1)S(1)} %get-tuple-element.34), channel_id=1, source_target_pairs={{0,1},{1,2},{2,3},{3,4},{4,5},{5,6},{6,7},{7,8},{8,9},{9,10},{10,1... | collective-permute-start | bytes 1585160 | tf_op jit(solution)/shard_map/ppermute | solution.py:317
  21.9 21.8 %collective-permute-start.2 = (bf16[2,256,256]{2,1,0:T(8,128)(2,1)S(1)}, bf16[2,256,256]{2,1,0:T(8,128)(2,1)S(1)}, u32[]{:S(2)}, u32[]{:S(2)}) collective-permute-start(bf16[2,256,256]{2,1,0:T(8,128)(2,1)S(1)} %get-tuple-element.38), channel_id=1, source_target_pairs={{0,128},{1,129},{2,130},{3,131},{4,132},{5,133},{6,134},{7,135},{8... | collective-permute-start | bytes 786440 | tf_op jit(solution)/shard_map/ppermute | solution.py:317
  30.8 13.0 %copy-start = (bf16[4,2,256,256]{3,2,1,0:T(8,128)(2,1)S(1)}, bf16[4,2,256,256]{3,2,1,0:T(8,128)(2,1)}, u32[]{:S(2)}) copy-start(bf16[4,2,256,256]{3,2,1,0:T(8,128)(2,1)} %probes.3) | copy-start | bytes 3145732
  30.8 12.9 %copy-start.1 = (f32[4,256,256]{2,1,0:T(8,128)S(1)}, f32[4,256,256]{2,1,0:T(8,128)}, u32[]{:S(2)}) copy-start(f32[4,256,256]{2,1,0:T(8,128)} %amplitudes.3) | copy-start | bytes 3145732
  30.8 12.9 %copy-start.2 = (s32[4]{0:T(128)S(1)}, s32[4]{0:T(128)}, u32[]{:S(2)}) copy-start(s32[4]{0:T(128)} %picks.3) | copy-start | bytes 52
  30.8 12.9 %copy-start.3 = (bf16[512,512]{1,0:T(8,128)(2,1)S(1)}, bf16[512,512]{1,0:T(8,128)(2,1)}, u32[]{:S(2)}) copy-start(bf16[512,512]{1,0:T(8,128)(2,1)} %constant.5.clone.second) | copy-start | bytes 1572868
  30.9 12.9 %copy-start.4 = (bf16[512,512]{1,0:T(8,128)(2,1)S(1)}, bf16[512,512]{1,0:T(8,128)(2,1)}, u32[]{:S(2)}) copy-start(bf16[512,512]{1,0:T(8,128)(2,1)} %constant.4.clone.first) | copy-start | bytes 1572868
  33.1 22.3 %collective-permute-start.3 = (bf16[2,256,256]{2,1,0:T(8,128)(2,1)S(1)}, bf16[2,256,256]{2,1,0:T(8,128)(2,1)S(1)}, u32[]{:S(2)}, u32[]{:S(2)}) collective-permute-start(bf16[2,256,256]{2,1,0:T(8,128)(2,1)S(1)} %get-tuple-element.43), channel_id=1, source_target_pairs={{0,128},{1,129},{2,130},{3,131},{4,132},{5,133},{6,134},{7,135},{8... | collective-permute-start | bytes 786440 | tf_op jit(solution)/shard_map/ppermute | solution.py:317
  48.6 23.2 %collective-permute-start.4 = (bf16[2,2,128,256]{3,2,1,0:T(8,128)(2,1)S(1)}, bf16[2,2,128,256]{3,2,1,0:T(8,128)(2,1)S(1)}, u32[]{:S(2)}, u32[]{:S(2)}) collective-permute-start(bf16[2,2,128,256]{3,2,1,0:T(8,128)(2,1)S(1)} %get-tuple-element.47), channel_id=1, source_target_pairs={{0,128},{1,129},{2,130},{3,131},{4,132},{5,133},{6,134},{7,135},{8... | collective-permute-start | bytes 786440 | tf_op jit(solution)/shard_map/ppermute | solution.py:317
  60.3 18.4 %collective-permute-start.5 = (bf16[2,192,256]{2,1,0:T(8,128)(2,1)S(1)}, bf16[2,192,256]{2,1,0:T(8,128)(2,1)S(1)}, u32[]{:S(2)}, u32[]{:S(2)}) collective-permute-start(bf16[2,192,256]{2,1,0:T(8,128)(2,1)S(1)} %get-tuple-element.49), channel_id=1, source_target_pairs={{0,128},{1,129},{2,130},{3,131},{4,132},{5,133},{6,134},{7,135},{8... | collective-permute-start | bytes 589832 | tf_op jit(solution)/shard_map/ppermute | solution.py:317
  60.6 18.0 %collective-permute-start.6 = (bf16[2,2,128,256]{3,2,1,0:T(8,128)(2,1)S(1)}, bf16[2,2,128,256]{3,2,1,0:T(8,128)(2,1)S(1)}, u32[]{:S(2)}, u32[]{:S(2)}) collective-permute-start(bf16[2,2,128,256]{3,2,1,0:T(8,128)(2,1)S(1)} %get-tuple-element.50), channel_id=1, source_target_pairs={{0,127},{1,0},{2,1},{3,2},{4,3},{5,4},{6,5},{7,6},{8,7},{9,8},{10,... | collective-permute-start | bytes 786440 | tf_op jit(solution)/shard_map/ppermute | solution.py:317
  71.8 11.0 %collective-permute-start.7 = (bf16[2,128,256]{2,1,0:T(8,128)(2,1)S(1)}, bf16[2,128,256]{2,1,0:T(8,128)(2,1)S(1)}, u32[]{:S(2)}, u32[]{:S(2)}) collective-permute-start(bf16[2,128,256]{2,1,0:T(8,128)(2,1)S(1)} %slice_bitcast_fusion), channel_id=1, source_target_pairs={{0,1},{1,2},{2,3},{3,4},{4,5},{5,6},{6,7},{7,8},{8,9},{9,10},{10,1... | collective-permute-start | bytes 393224 | tf_op jit(solution)/shard_map/ppermute | solution.py:317
  71.9 10.9 %collective-permute-start.8 = (bf16[2,128,256]{2,1,0:T(8,128)(2,1)S(1)}, bf16[2,128,256]{2,1,0:T(8,128)(2,1)S(1)}, u32[]{:S(2)}, u32[]{:S(2)}) collective-permute-start(bf16[2,128,256]{2,1,0:T(8,128)(2,1)S(1)} %get-tuple-element.51), channel_id=1, source_target_pairs={{0,255},{1,128},{2,129},{3,130},{4,131},{5,132},{6,133},{7,134},{8... | collective-permute-start | bytes 393224 | tf_op jit(solution)/shard_map/ppermute | solution.py:317

commit v8 on v5

--- a/solution.py
+++ b/solution.py
@@ -82,6 +82,19 @@
     block = pltpu.roll(block, row_shift, 0)
     where = (channel, pl.ds(row_base, count + 8), pl.ds(col_base, WIDE))
     total_ref[where] = total_ref[where] + block
+
+
+def put_near(total_ref, channel, top, left, block, near):
+    row = pl.multiple_of(HALF + near, HALF)
+    col_base, col_shift = column_split(left)
+    shift = top - row
+    block = jnp.concatenate([block, jnp.zeros((HALF, WIDE - SIDE), F32)], axis=1)
+    block = pltpu.roll(block, col_shift, 1)
+    block = pltpu.roll(block, lax.rem(shift + 2 * HALF, HALF), 0)
+    line = lax.broadcasted_iota(jnp.int32, block.shape, 0)
+    kept = jnp.where((line >= shift) & (line < shift + HALF), block, 0.0)
+    where = (channel, pl.ds(row, HALF), pl.ds(col_base, WIDE))
+    total_ref[where] = total_ref[where] + kept
 
 
 def tagged(rows, cols, spots):
@@ -216,13 +229,7 @@
 def solo_kernel(
     number, rows, picks, own, mate, probes, amplitudes, wave, first, second, *refs
 ):
-    if number == 0:
-        sent_outer, sent_inband, kept, edge, held, made = refs
-        edges = edge
-    else:
-        before, sent_outer, sent_inband, kept, both, held, made = refs
-        both[0] = before[...]
-        edges = both.at[1]
+    sent_outer, sent_inband, kept, edges, held, made = refs
     cut = lax.axis_index("cuts")
     spots = places(rows)
     place = jnp.where(cut == 0, spots[number], spots[2 + number])
@@ -270,27 +277,39 @@
         put(top, left, outer[channel].astype(F32))
 
 
-def rest_kernel(
-    rows, cols, spots, given, inband, edges, relay0, relay1, total, output, sems
-):
+def more_kernel(rows, cols, spots, given, inband, edge0, edge1, relay0, total):
     cut = lax.axis_index("cuts")
     shift = jnp.where(cut == 0, BAND, -HALF)
-    copies = []
     for channel in range(2):
         put = functools.partial(put_window, total, channel)
         put_inband(put, rows, cols, 1, inband, channel)
-        for number, relay in enumerate((relay0, relay1)):
-            k = 2 * number
-            put(spots[k] + shift, spots[k + 1], edges[number, channel].astype(F32))
-            put(spots[4 + k] + BAND - HALF - shift, spots[5 + k], relay[channel].astype(F32))
-        copies.append(
-            pltpu.make_async_copy(
-                total.at[channel, pl.ds(HALF, BAND)], output.at[0, channel], sems.at[channel]
-            )
+        put(spots[0] + shift, spots[1], edge0[channel].astype(F32))
+        put(spots[2] + shift, spots[3], edge1[channel].astype(F32))
+        put(spots[4] + BAND - HALF - shift, spots[5], relay0[channel].astype(F32))
+
+
+def last_kernel(spots, given, relay1, total, output, sems):
+    cut = lax.axis_index("cuts")
+    near = pl.multiple_of(jnp.where(cut == 0, 0, HALF), HALF)
+    far = HALF - near
+
+    def copy(channel, start, sem):
+        return pltpu.make_async_copy(
+            total.at[channel, pl.ds(pl.multiple_of(HALF + start, HALF), HALF)],
+            output.at[0, channel, pl.ds(start, HALF)],
+            sem,
         )
+
+    copies = [copy(channel, far, sems.at[channel]) for channel in range(2)]
+    for channel in range(2):
         copies[channel].start()
-    for copy in copies:
-        copy.wait()
+    top = spots[6] + jnp.where(cut == 0, -HALF, BAND)
+    for channel in range(2):
+        put_near(total, channel, top, spots[7], relay1[channel].astype(F32), near)
+        copies.append(copy(channel, near, sems.at[2 + channel]))
+        copies[2 + channel].start()
+    for item in copies:
+        item.wait()
 
 
 def call(kernel, name, inputs, outputs, scratch=(), in_specs=None, out_specs=None, aliases={}, vmem=40, flops=1):
@@ -332,41 +351,49 @@
     early = move(early, "early")
     late = move(late, "late")
     sent = call(mate_kernel, "mate", [rows, cols, band, early], [full, full], [near])
-    *sent, late = lax.optimization_barrier((*sent, late))
-    mates = [move(x, "mate") for x in sent]
+    sent0, late = lax.optimization_barrier((sent[0], late))
+    mate0 = move(sent0, "mate")
     own0, own1, spots = call(
         own_windows_kernel, "windows", [rows, cols, band, early, late],
         [full, full, arr(8, dtype=jnp.int32)], [near], out_specs=[VM, VM, SM],
     )
+    sent1, own1 = lax.optimization_barrier((sent[1], own1))
+    mate1 = move(sent1, "mate")
     optics = [probes, amplitudes, wave, first, second]
     work = [pltpu.VMEM((2, 2, SIDE, SIDE), BF), pltpu.VMEM((2, 2, SIDE, SIDE), F32)]
     wide_full = arr(2, SIDE, SIDE, dtype=F32)
     outer0, inband0, kept0, edge0 = call(
-        functools.partial(solo_kernel, 0), "solo0", [rows, probe_choice, own0, mates[0]] + optics,
-        [half, half, wide_full, half], work,
+        functools.partial(solo_kernel, 0), "solo0", [rows, probe_choice, own0, mate0] + optics,
+        [half, half, wide_full, half], work, flops=10**11,
     )
     outer0 = move(outer0, "mate")
     inband0 = move(inband0, "mate")
-    outer1, inband1, kept1, edges = call(
+    edge0 = move(edge0, "early")
+    outer1, inband1, kept1, edge1 = call(
         functools.partial(solo_kernel, 1), "solo1",
-        [rows, probe_choice, own1, mates[1]] + optics + [edge0],
-        [half, arr(2, HALF + 64, SIDE), wide_full, arr(2, 2, HALF, SIDE)], work, flops=10**11,
-    )
+        [rows, probe_choice, own1, mate1] + optics,
+        [half, arr(2, HALF + 64, SIDE), wide_full, half], work, flops=10**11,
+    )
+    inband1 = move(inband1, "mate")
+    outer1, edge1, outer0 = lax.optimization_barrier((outer1, edge1, outer0))
     relay1 = move(outer1, "direct")
-    inband1 = move(inband1, "mate")
-    edges = move(edges, "early")
+    edge1 = move(edge1, "early")
     relay0 = move(outer0, "late")
     (total,) = call(
         own_kernel, "own", [rows, cols, kept0, kept1, outer0, inband0],
         [arr(2, EXT, COLS, dtype=F32)], flops=10**11,
     )
+    (total,) = call(
+        more_kernel, "more",
+        [rows, cols, spots, total, inband1, edge0, edge1, relay0],
+        [arr(2, EXT, COLS, dtype=F32)], aliases={3: 0}, flops=10**11,
+    )
     _, gradient = call(
-        rest_kernel, "rest",
-        [rows, cols, spots, total, inband1, edges, relay0, relay1],
+        last_kernel, "last", [spots, total, relay1],
         [arr(2, EXT, COLS, dtype=F32), arr(1, 2, BAND, COLS, dtype=F32)],
-        [pltpu.SemaphoreType.DMA((2,))],
+        [pltpu.SemaphoreType.DMA((4,))],
         out_specs=[VM, HB],
-        aliases={3: 0},
+        aliases={1: 0},
     )
     return gradient
 

time: 83.5 us -> 88.9 us (1.065)
  starting transfers between devices: 29.4 us -> 33 us
  Pallas kernels: 20.9 us -> 23.6 us
    ppermute x10 -> x11, starting transfers between devices: 29.4 us -> 33 us  [shards(): move = lambda x, way: lax.ppermute(x, AXES, route[way])]
    pallas_call x7 -> x8, Pallas kernels: 20.9 us -> 23.6 us  [call(): pl.pallas_call(kernel, name=name, out_shape=outputs, in_specs=in_specs or...]
    ppermute x10 -> x11, waiting for transfers between devices: 30.3 us -> 30.3 us  [shards(): move = lambda x, way: lax.ppermute(x, AXES, route[way])]
  transfers between devices with their start and end apart: 10 -> 11, of which waited for: 6 -> 5; matrix products, arithmetic and copies ran while one was open for 1% -> 1% of each run, Pallas kernels for 19% -> 22%
where the time goes in v8:
time: 88.9 us; the launch traced here: 88.2 us
  starting transfers between devices  33 us (37%)
  waiting for transfers between devices  30.3 us (34%)
  Pallas kernels  23.6 us (27%)
  local copies, waits for them, and re-layouts  0.98 us (1%)
    ppermute x11, starting transfers between devices, shards(): move = lambda x, way: lax.ppermute(x, AXES, route[way])  33 us
    ppermute x11, waiting for transfers between devices, shards(): move = lambda x, way: lax.ppermute(x, AXES, route[way])  30.3 us
    pallas_call x8, Pallas kernels, call(): pl.pallas_call(kernel, name=name, out_shape=outputs, in_specs=in_specs or...  23.6 us
  transfers between devices with their start and end apart: 11, of which 5 were waited for; matrix products, arithmetic and copies ran while one was open for 1% of the time, Pallas kernels for 22%

profile of v8, /device:TPU:8, one launch (start us, length us, event | category | flops | bytes accessed | tf_op | source)
XLA Modules:
  0.0 88.2 jit_solution(3542118007171481411)
XLA Ops:
  0.0 2.2 %edge.1 = (bf16[2064,128]{1,0:T(8,128)(2,1)S(1)}, bf16[2064,128]{1,0:T(8,128)(2,1)S(1)}, f32[2,256,1024]{2,1,0:T(8,128)S(1)}, s32[4]{0:T(128)S(1)}, s32[4]{0:T(128)S(1)}) custom-call(s32[4]{0:T(128)} %rows_in.1, s32[4]{0:T(128)} %cols_in.1, f32[1,2,256,1024]{3,2,1,0:T(8,128)} %objects_in.1), custom_call_target="tpu_custom_call" | custom-call | flops 1 | bytes 1 | tf_op jit(solution)/shard_map/edge/pallas_call | solution.py:317
  2.3 0.0 copy-start.3
  2.3 0.0 copy-start.4
  2.3 6.2 %collective-permute-start = (bf16[2064,128]{1,0:T(8,128)(2,1)S(1)}, bf16[2064,128]{1,0:T(8,128)(2,1)S(1)}, u32[]{:S(2)}, u32[]{:S(2)}) collective-permute-start(bf16[2064,128]{1,0:T(8,128)(2,1)S(1)} %get-tuple-element.34), channel_id=1, source_target_pairs={{0,127},{1,0},{2,1},{3,2},{4,3},{5,4},{6,5},{7,6},{8,7},{9,8},{10,... | collective-permute-start | bytes 1585160 | tf_op jit(solution)/shard_map/ppermute | solution.py:336
  8.5 7.7 %collective-permute-done.early = bf16[2064,128]{1,0:T(8,128)(2,1)S(1)} collective-permute-done((bf16[2064,128]{1,0:T(8,128)(2,1)S(1)}, bf16[2064,128]{1,0:T(8,128)(2,1)S(1)}, u32[]{:S(2)}, u32[]{:S(2)}) %collective-permute-start) | collective-permute-done | bytes 528416 | tf_op jit(solution)/shard_map/ppermute | solution.py:336
  16.3 1.6 %mate.1 = (bf16[2,256,256]{2,1,0:T(8,128)(2,1)S(1)}, bf16[2,256,256]{2,1,0:T(8,128)(2,1)S(1)}) custom-call(s32[4]{0:T(128)S(1)} %get-tuple-element.31.rows, s32[4]{0:T(128)S(1)} %get-tuple-element.32.cols, f32[2,256,1024]{2,1,0:T(8,128)S(1)} %get-tuple-element.33.objects, bf16[2064,128]{1,0:T(8,128)(2,1)S(1)} %collective-permute-done.early), custom_call_target="tpu_custom_call" | custom-call | flops 1 | bytes 1 | tf_op jit(solution)/shard_map/mate/pallas_call | solution.py:317
  17.9 4.1 %collective-permute-done.1.late = bf16[2064,128]{1,0:T(8,128)(2,1)S(1)} collective-permute-done((bf16[2064,128]{1,0:T(8,128)(2,1)S(1)}, bf16[2064,128]{1,0:T(8,128)(2,1)S(1)}, u32[]{:S(2)}, u32[]{:S(2)}) %collective-permute-start.1) | collective-permute-done | bytes 528416 | tf_op jit(solution)/shard_map/ppermute | solution.py:336
  22.0 7.9 %collective-permute-start.2 = (bf16[2,256,256]{2,1,0:T(8,128)(2,1)S(1)}, bf16[2,256,256]{2,1,0:T(8,128)(2,1)S(1)}, u32[]{:S(2)}, u32[]{:S(2)}) collective-permute-start(bf16[2,256,256]{2,1,0:T(8,128)(2,1)S(1)} %get-tuple-element.40), channel_id=1, source_target_pairs={{0,128},{1,129},{2,130},{3,131},{4,132},{5,133},{6,134},{7,135},{8... | collective-permute-start | bytes 786440 | tf_op jit(solution)/shard_map/ppermute | solution.py:336
  29.9 0.9 %cosine_bitcast_fusion = (f32[1,256,256]{2,1,0:T(8,128)S(1)}, f32[1,256,256]{2,1,0:T(8,128)S(1)}) fusion(f32[256,256]{1,0:T(8,128)S(1)} %copy-done.5), kind=kLoop, calls=%fused_computation.2 | loop fusion | bytes 786432 | tf_op jit(solution)/shard_map/stack | solution.py:338
  30.9 2.2 %windows.1 = (bf16[2,256,256]{2,1,0:T(8,128)(2,1)S(1)}, bf16[2,256,256]{2,1,0:T(8,128)(2,1)S(1)}, s32[8]{0:T(128)S(1)}) custom-call(s32[4]{0:T(128)S(1)} %get-tuple-element.31.rows, s32[4]{0:T(128)S(1)} %get-tuple-element.32.cols, f32[2,256,1024]{2,1,0:T(8,128)S(1)} %get-tuple-element.33.objects, bf16[2064,128]{1,0:T(8,128)(2,1)S(1)} %collective-permute-done.early, ...), custom_call_target="tpu_custom_call" | custom-call | flops 1 | bytes 1 | tf_op jit(solution)/shard_map/windows/pallas_call | solution.py:317
  33.1 0.1 collective-permute-start.3
  33.3 10.6 %collective-permute-done.2.mate = bf16[2,256,256]{2,1,0:T(8,128)(2,1)S(1)} collective-permute-done((bf16[2,256,256]{2,1,0:T(8,128)(2,1)S(1)}, bf16[2,256,256]{2,1,0:T(8,128)(2,1)S(1)}, u32[]{:S(2)}, u32[]{:S(2)}) %collective-permute-start.2) | collective-permute-done | bytes 262176 | tf_op jit(solution)/shard_map/ppermute | solution.py:336
  43.8 5.5 %solo0.1 = (bf16[2,128,256]{2,1,0:T(8,128)(2,1)S(1)}, bf16[2,128,256]{2,1,0:T(8,128)(2,1)S(1)}, f32[2,256,256]{2,1,0:T(8,128)S(1)}, bf16[2,128,256]{2,1,0:T(8,128)(2,1)}) custom-call(s32[4]{0:T(128)S(1)} %get-tuple-element.31.rows, s32[4]{0:T(128)S(1)} %copy-done.2, bf16[2,256,256]{2,1,0:T(8,128)(2,1)S(1)} %get-tuple-element.39.own, ...), custom_call_target="tpu_custom_call" | custom-call | flops 99999997952 | bytes 1 | tf_op jit(solution)/shard_map/solo0/pallas_call | solution.py:317
  49.3 6.5 %collective-permute-start.4 = (bf16[2,128,256]{2,1,0:T(8,128)(2,1)S(1)}, bf16[2,128,256]{2,1,0:T(8,128)(2,1)S(1)}, u32[]{:S(2)}, u32[]{:S(2)}) collective-permute-start(bf16[2,128,256]{2,1,0:T(8,128)(2,1)S(1)} %get-tuple-element.49), channel_id=1, source_target_pairs={{0,128},{1,129},{2,130},{3,131},{4,132},{5,133},{6,134},{7,135},{8... | collective-permute-start | bytes 393224 | tf_op jit(solution)/shard_map/ppermute | solution.py:336
  55.8 0.0 collective-permute-start.5
  55.9 0.8 collective-permute-start.7
  56.6 5.5 %solo1.1 = (bf16[2,128,256]{2,1,0:T(8,128)(2,1)}, bf16[2,192,256]{2,1,0:T(8,128)(2,1)S(1)}, f32[2,256,256]{2,1,0:T(8,128)S(1)}, bf16[2,128,256]{2,1,0:T(8,128)(2,1)S(1)}) custom-call(s32[4]{0:T(128)S(1)} %get-tuple-element.31.rows, s32[4]{0:T(128)S(1)} %copy-done.2, bf16[2,256,256]{2,1,0:T(8,128)(2,1)S(1)} %get-tuple-element.44.own, ...), custom_call_target="tpu_custom_call" | custom-call | flops 99999997952 | bytes 1 | tf_op jit(solution)/shard_map/solo1/pallas_call | solution.py:317
  62.1 5.1 %collective-permute-start.6 = (bf16[2,192,256]{2,1,0:T(8,128)(2,1)S(1)}, bf16[2,192,256]{2,1,0:T(8,128)(2,1)S(1)}, u32[]{:S(2)}, u32[]{:S(2)}) collective-permute-start(bf16[2,192,256]{2,1,0:T(8,128)(2,1)S(1)} %get-tuple-element.52), channel_id=1, source_target_pairs={{0,128},{1,129},{2,130},{3,131},{4,132},{5,133},{6,134},{7,135},{8... | collective-permute-start | bytes 589832 | tf_op jit(solution)/shard_map/ppermute | solution.py:336
  67.3 6.3 %collective-permute-start.8 = (bf16[2,128,256]{2,1,0:T(8,128)(2,1)S(1)}, bf16[2,128,256]{2,1,0:T(8,128)(2,1)S(1)}, u32[]{:S(2)}, u32[]{:S(2)}) collective-permute-start(bf16[2,128,256]{2,1,0:T(8,128)(2,1)S(1)} %get-tuple-element.54), channel_id=1, source_target_pairs={{0,127},{1,0},{2,1},{3,2},{4,3},{5,4},{6,5},{7,6},{8,7},{9,8},{10,... | collective-permute-start | bytes 393224 | tf_op jit(solution)/shard_map/ppermute | solution.py:336
  73.5 2.3 %own.1.given = f32[2,512,1024]{2,1,0:T(8,128)S(1)} custom-call(s32[4]{0:T(128)S(1)} %get-tuple-element.31.rows, s32[4]{0:T(128)S(1)} %get-tuple-element.32.cols, f32[2,256,256]{2,1,0:T(8,128)S(1)} %get-tuple-element.41.kept0, f32[2,256,256]{2,1,0:T(8,128)S(1)} %get-tuple-element.46.kept1, bf16[2,128,256]{2,1,0:T(8,128)(2,1)S(1)} %collective-permute-done.4.outer, ...), custom_call_target="tpu_custom_call" | custom-call | flops 99999997952 | bytes 1 | tf_op jit(solution)/shard_map/own/pallas_call | solution.py:317
  75.9 1.9 %collective-permute-done.6.inband = bf16[2,192,256]{2,1,0:T(8,128)(2,1)S(1)} collective-permute-done((bf16[2,192,256]{2,1,0:T(8,128)(2,1)S(1)}, bf16[2,192,256]{2,1,0:T(8,128)(2,1)S(1)}, u32[]{:S(2)}, u32[]{:S(2)}) %collective-permute-start.6) | collective-permute-done | bytes 196640 | tf_op jit(solution)/shard_map/ppermute | solution.py:336
  77.8 5.9 %collective-permute-done.9.relay0 = bf16[2,128,256]{2,1,0:T(8,128)(2,1)S(1)} collective-permute-done((bf16[2,128,256]{2,1,0:T(8,128)(2,1)S(1)}, bf16[2,128,256]{2,1,0:T(8,128)(2,1)S(1)}, u32[]{:S(2)}, u32[]{:S(2)}) %collective-permute-start.9) | collective-permute-done | bytes 131104 | tf_op jit(solution)/shard_map/ppermute | solution.py:336
  83.8 1.9 %more.1.given = f32[2,512,1024]{2,1,0:T(8,128)S(1)} custom-call(s32[4]{0:T(128)S(1)} %get-tuple-element.31.rows, s32[4]{0:T(128)S(1)} %get-tuple-element.32.cols, s32[8]{0:T(128)S(1)} %get-tuple-element.38.spots, f32[2,512,1024]{2,1,0:T(8,128)S(1)} %own.1.given, ...), custom_call_target="tpu_custom_call", output_to_operand_aliasing={{}: (3, {})} | custom-call | flops 99999997952 | bytes 1 | tf_op jit(solution)/shard_map/more/pallas_call | solution.py:317
  85.7 2.3 %last.1 = (f32[2,512,1024]{2,1,0:T(8,128)S(1)}, f32[1,2,256,1024]{3,2,1,0:T(8,128)}) custom-call(s32[8]{0:T(128)S(1)} %get-tuple-element.38.spots, f32[2,512,1024]{2,1,0:T(8,128)S(1)} %more.1.given, bf16[2,128,256]{2,1,0:T(8,128)(2,1)} %collective-permute-done.10.relay1), custom_call_target="tpu_custom_call", output_to_operand_aliasing={{0}: (1, {})} | custom-call | flops 1 | bytes 1 | tf_op jit(solution)/shard_map/last/pallas_call | solution.py:317
  (20 shorter events, 0.1 us)
Async XLA Ops:
  0.0 29.9 %copy-start.5 = (f32[256,256]{1,0:T(8,128)S(1)}, f32[256,256]{1,0:T(8,128)}, u32[]{:S(2)}) copy-start(f32[256,256]{1,0:T(8,128)} %param.12) | copy-start | bytes 786436
  2.2 41.6 %copy-start = (bf16[4,2,256,256]{3,2,1,0:T(8,128)(2,1)S(1)}, bf16[4,2,256,256]{3,2,1,0:T(8,128)(2,1)}, u32[]{:S(2)}) copy-start(bf16[4,2,256,256]{3,2,1,0:T(8,128)(2,1)} %probes.3) | copy-start | bytes 3145732
  2.2 41.6 %copy-start.1 = (f32[4,256,256]{2,1,0:T(8,128)S(1)}, f32[4,256,256]{2,1,0:T(8,128)}, u32[]{:S(2)}) copy-start(f32[4,256,256]{2,1,0:T(8,128)} %amplitudes.3) | copy-start | bytes 3145732
  2.3 41.6 %copy-start.2 = (s32[4]{0:T(128)S(1)}, s32[4]{0:T(128)}, u32[]{:S(2)}) copy-start(s32[4]{0:T(128)} %picks.3) | copy-start | bytes 52
  2.3 41.6 %copy-start.3 = (bf16[512,512]{1,0:T(8,128)(2,1)S(1)}, bf16[512,512]{1,0:T(8,128)(2,1)}, u32[]{:S(2)}) copy-start(bf16[512,512]{1,0:T(8,128)(2,1)} %constant.5.clone.second) | copy-start | bytes 1572868
  2.3 41.5 %copy-start.4 = (bf16[512,512]{1,0:T(8,128)(2,1)S(1)}, bf16[512,512]{1,0:T(8,128)(2,1)}, u32[]{:S(2)}) copy-start(bf16[512,512]{1,0:T(8,128)(2,1)} %constant.4.clone.first) | copy-start | bytes 1572868
  2.3 14.0 %collective-permute-start = (bf16[2064,128]{1,0:T(8,128)(2,1)S(1)}, bf16[2064,128]{1,0:T(8,128)(2,1)S(1)}, u32[]{:S(2)}, u32[]{:S(2)}) collective-permute-start(bf16[2064,128]{1,0:T(8,128)(2,1)S(1)} %get-tuple-element.34), channel_id=1, source_target_pairs={{0,127},{1,0},{2,1},{3,2},{4,3},{5,4},{6,5},{7,6},{8,7},{9,8},{10,... | collective-permute-start | bytes 1585160 | tf_op jit(solution)/shard_map/ppermute | solution.py:336
  8.5 13.5 %collective-permute-start.1 = (bf16[2064,128]{1,0:T(8,128)(2,1)S(1)}, bf16[2064,128]{1,0:T(8,128)(2,1)S(1)}, u32[]{:S(2)}, u32[]{:S(2)}) collective-permute-start(bf16[2064,128]{1,0:T(8,128)(2,1)S(1)} %get-tuple-element.36), channel_id=1, source_target_pairs={{0,1},{1,2},{2,3},{3,4},{4,5},{5,6},{6,7},{7,8},{8,9},{9,10},{10,1... | collective-permute-start | bytes 1585160 | tf_op jit(solution)/shard_map/ppermute | solution.py:336
  22.0 21.8 %collective-permute-start.2 = (bf16[2,256,256]{2,1,0:T(8,128)(2,1)S(1)}, bf16[2,256,256]{2,1,0:T(8,128)(2,1)S(1)}, u32[]{:S(2)}, u32[]{:S(2)}) collective-permute-start(bf16[2,256,256]{2,1,0:T(8,128)(2,1)S(1)} %get-tuple-element.40), channel_id=1, source_target_pairs={{0,128},{1,129},{2,130},{3,131},{4,132},{5,133},{6,134},{7,135},{8... | collective-permute-start | bytes 786440 | tf_op jit(solution)/shard_map/ppermute | solution.py:336
  33.1 23.5 %collective-permute-start.3 = (bf16[2,256,256]{2,1,0:T(8,128)(2,1)S(1)}, bf16[2,256,256]{2,1,0:T(8,128)(2,1)S(1)}, u32[]{:S(2)}, u32[]{:S(2)}) collective-permute-start(bf16[2,256,256]{2,1,0:T(8,128)(2,1)S(1)} %get-tuple-element.45), channel_id=1, source_target_pairs={{0,128},{1,129},{2,130},{3,131},{4,132},{5,133},{6,134},{7,135},{8... | collective-permute-start | bytes 786440 | tf_op jit(solution)/shard_map/ppermute | solution.py:336
  49.3 17.9 %collective-permute-start.4 = (bf16[2,128,256]{2,1,0:T(8,128)(2,1)S(1)}, bf16[2,128,256]{2,1,0:T(8,128)(2,1)S(1)}, u32[]{:S(2)}, u32[]{:S(2)}) collective-permute-start(bf16[2,128,256]{2,1,0:T(8,128)(2,1)S(1)} %get-tuple-element.49), channel_id=1, source_target_pairs={{0,128},{1,129},{2,130},{3,131},{4,132},{5,133},{6,134},{7,135},{8... | collective-permute-start | bytes 393224 | tf_op jit(solution)/shard_map/ppermute | solution.py:336
  55.8 17.7 %collective-permute-start.5 = (bf16[2,128,256]{2,1,0:T(8,128)(2,1)S(1)}, bf16[2,128,256]{2,1,0:T(8,128)(2,1)S(1)}, u32[]{:S(2)}, u32[]{:S(2)}) collective-permute-start(bf16[2,128,256]{2,1,0:T(8,128)(2,1)S(1)} %get-tuple-element.51), channel_id=1, source_target_pairs={{0,128},{1,129},{2,130},{3,131},{4,132},{5,133},{6,134},{7,135},{8... | collective-permute-start | bytes 393224 | tf_op jit(solution)/shard_map/ppermute | solution.py:336
  55.9 20.0 %collective-permute-start.7 = (bf16[2,128,256]{2,1,0:T(8,128)(2,1)}, bf16[2,128,256]{2,1,0:T(8,128)(2,1)}, u32[]{:S(2)}, u32[]{:S(2)}) collective-permute-start(bf16[2,128,256]{2,1,0:T(8,128)(2,1)} %get-tuple-element.53), channel_id=1, source_target_pairs={{0,127},{1,0},{2,1},{3,2},{4,3},{5,4},{6,5},{7,6},{8,7},{9,8},{10,... | collective-permute-start | bytes 393224 | tf_op jit(solution)/shard_map/ppermute | solution.py:336
  62.1 15.7 %collective-permute-start.6 = (bf16[2,192,256]{2,1,0:T(8,128)(2,1)S(1)}, bf16[2,192,256]{2,1,0:T(8,128)(2,1)S(1)}, u32[]{:S(2)}, u32[]{:S(2)}) collective-permute-start(bf16[2,192,256]{2,1,0:T(8,128)(2,1)S(1)} %get-tuple-element.52), channel_id=1, source_target_pairs={{0,128},{1,129},{2,130},{3,131},{4,132},{5,133},{6,134},{7,135},{8... | collective-permute-start | bytes 589832 | tf_op jit(solution)/shard_map/ppermute | solution.py:336
  67.3 10.6 %collective-permute-start.8 = (bf16[2,128,256]{2,1,0:T(8,128)(2,1)S(1)}, bf16[2,128,256]{2,1,0:T(8,128)(2,1)S(1)}, u32[]{:S(2)}, u32[]{:S(2)}) collective-permute-start(bf16[2,128,256]{2,1,0:T(8,128)(2,1)S(1)} %get-tuple-element.54), channel_id=1, source_target_pairs={{0,127},{1,0},{2,1},{3,2},{4,3},{5,4},{6,5},{7,6},{8,7},{9,8},{10,... | collective-permute-start | bytes 393224 | tf_op jit(solution)/shard_map/ppermute | solution.py:336
  73.5 12.2 %collective-permute-start.10 = (bf16[2,128,256]{2,1,0:T(8,128)(2,1)}, bf16[2,128,256]{2,1,0:T(8,128)(2,1)}, u32[]{:S(2)}, u32[]{:S(2)}) collective-permute-start(bf16[2,128,256]{2,1,0:T(8,128)(2,1)} %get-tuple-element.55), channel_id=1, source_target_pairs={{0,255},{1,128},{2,129},{3,130},{4,131},{5,132},{6,133},{7,134},{8... | collective-permute-start | bytes 393224 | tf_op jit(solution)/shard_map/ppermute | solution.py:336
  73.5 10.2 %collective-permute-start.9 = (bf16[2,128,256]{2,1,0:T(8,128)(2,1)S(1)}, bf16[2,128,256]{2,1,0:T(8,128)(2,1)S(1)}, u32[]{:S(2)}, u32[]{:S(2)}) collective-permute-start(bf16[2,128,256]{2,1,0:T(8,128)(2,1)S(1)} %collective-permute-done.4.outer), channel_id=1, source_target_pairs={{0,1},{1,2},{2,3},{3,4},{4,5},{5,6},{6,7},{7,8},{8,9},{9,10},{10,1... | collective-permute-start | bytes 393224 | tf_op jit(solution)/shard_map/ppermute | solution.py:336

commit v9 on v6

--- a/solution.py
+++ b/solution.py
@@ -332,9 +332,7 @@
     early = move(early, "early")
     late = move(late, "late")
     sent = call(mate_kernel, "mate", [rows, cols, band, early], [full, full], [near])
-    sent0, sent1, late = lax.optimization_barrier((*sent, late))
-    mate0 = move(sent0, "mate")
-    mate1 = move(sent1, "mate")
+    mate0, mate1 = (move(x, "mate") for x in sent)
     own0, own1, spots = call(
         own_windows_kernel, "windows", [rows, cols, band, early, late],
         [full, full, arr(8, dtype=jnp.int32)], [near], out_specs=[VM, VM, SM],

time: 84 us -> 85.8 us (1.021)
  the two profiles are of different devices: /device:TPU:8 before, /device:TPU:0 now
where the time goes in v9:
time: 85.8 us; the launch traced here: 85.7 us
  waiting for transfers between devices  38.5 us (45%)
  starting transfers between devices  24.9 us (29%)
  Pallas kernels  20.8 us (24%)
  local copies, waits for them, and re-layouts  0.99 us (1%)
    ppermute x9, waiting for transfers between devices, shards(): move = lambda x, way: lax.ppermute(x, AXES, route[way])  38.5 us
    ppermute x9, starting transfers between devices, shards(): move = lambda x, way: lax.ppermute(x, AXES, route[way])  24.9 us
    pallas_call x7, Pallas kernels, call(): pl.pallas_call(kernel, name=name, out_shape=outputs, in_specs=in_specs or...  20.8 us
  transfers between devices with their start and end apart: 9, of which 5 were waited for; matrix products, arithmetic and copies ran while one was open for 1% of the time, Pallas kernels for 19%

profile of v9, /device:TPU:0, one launch (start us, length us, event | category | flops | bytes accessed | tf_op | source)
XLA Modules:
  0.0 85.7 jit_solution(5351524238558574469)
XLA Ops:
  0.0 2.2 %edge.1 = (bf16[2064,128]{1,0:T(8,128)(2,1)S(1)}, bf16[2064,128]{1,0:T(8,128)(2,1)S(1)}, f32[2,256,1024]{2,1,0:T(8,128)S(1)}, s32[4]{0:T(128)S(1)}, s32[4]{0:T(128)S(1)}) custom-call(s32[4]{0:T(128)} %rows_in.1, s32[4]{0:T(128)} %cols_in.1, f32[1,2,256,1024]{3,2,1,0:T(8,128)} %objects_in.1), custom_call_target="tpu_custom_call" | custom-call | flops 1 | bytes 1 | tf_op jit(solution)/shard_map/edge/pallas_call | solution.py:298
  2.2 7.0 %collective-permute-start = (bf16[2064,128]{1,0:T(8,128)(2,1)S(1)}, bf16[2064,128]{1,0:T(8,128)(2,1)S(1)}, u32[]{:S(2)}, u32[]{:S(2)}) collective-permute-start(bf16[2064,128]{1,0:T(8,128)(2,1)S(1)} %get-tuple-element.28), channel_id=1, source_target_pairs={{0,127},{1,0},{2,1},{3,2},{4,3},{5,4},{6,5},{7,6},{8,7},{9,8},{10,... | collective-permute-start | bytes 1585160 | tf_op jit(solution)/shard_map/ppermute | solution.py:317
  9.3 6.7 %collective-permute-done.early = bf16[2064,128]{1,0:T(8,128)(2,1)S(1)} collective-permute-done((bf16[2064,128]{1,0:T(8,128)(2,1)S(1)}, bf16[2064,128]{1,0:T(8,128)(2,1)S(1)}, u32[]{:S(2)}, u32[]{:S(2)}) %collective-permute-start) | collective-permute-done | bytes 528416 | tf_op jit(solution)/shard_map/ppermute | solution.py:317
  16.0 1.6 %mate.1 = (bf16[2,256,256]{2,1,0:T(8,128)(2,1)S(1)}, bf16[2,256,256]{2,1,0:T(8,128)(2,1)S(1)}) custom-call(s32[4]{0:T(128)S(1)} %get-tuple-element.25.rows, s32[4]{0:T(128)S(1)} %get-tuple-element.26.cols, f32[2,256,1024]{2,1,0:T(8,128)S(1)} %get-tuple-element.27.objects, bf16[2064,128]{1,0:T(8,128)(2,1)S(1)} %collective-permute-done.early), custom_call_target="tpu_custom_call" | custom-call | flops 1 | bytes 1 | tf_op jit(solution)/shard_map/mate/pallas_call | solution.py:298
  17.7 11.3 %collective-permute-start.2 = (bf16[2,256,256]{2,1,0:T(8,128)(2,1)S(1)}, bf16[2,256,256]{2,1,0:T(8,128)(2,1)S(1)}, u32[]{:S(2)}, u32[]{:S(2)}) collective-permute-start(bf16[2,256,256]{2,1,0:T(8,128)(2,1)S(1)} %get-tuple-element.32), channel_id=1, source_target_pairs={{0,128},{1,129},{2,130},{3,131},{4,132},{5,133},{6,134},{7,135},{8... | collective-permute-start | bytes 786440 | tf_op jit(solution)/shard_map/ppermute | solution.py:317
  29.0 0.1 collective-permute-start.3
  29.1 0.9 %cosine_bitcast_fusion = (f32[1,256,256]{2,1,0:T(8,128)S(1)}, f32[1,256,256]{2,1,0:T(8,128)S(1)}) fusion(f32[256,256]{1,0:T(8,128)S(1)} %copy-done.5), kind=kLoop, calls=%fused_computation.2 | loop fusion | bytes 786432 | tf_op jit(solution)/shard_map/stack | solution.py:319
  30.0 0.0 copy-start
  30.1 0.0 copy-start.2
  30.1 0.0 copy-start.3
  30.2 2.2 %windows.1 = (bf16[2,256,256]{2,1,0:T(8,128)(2,1)S(1)}, bf16[2,256,256]{2,1,0:T(8,128)(2,1)S(1)}, s32[8]{0:T(128)S(1)}) custom-call(s32[4]{0:T(128)S(1)} %get-tuple-element.25.rows, s32[4]{0:T(128)S(1)} %get-tuple-element.26.cols, f32[2,256,1024]{2,1,0:T(8,128)S(1)} %get-tuple-element.27.objects, bf16[2064,128]{1,0:T(8,128)(2,1)S(1)} %collective-permute-done.early, ...), custom_call_target="tpu_custom_call" | custom-call | flops 1 | bytes 1 | tf_op jit(solution)/shard_map/windows/pallas_call | solution.py:298
  32.4 12.3 %collective-permute-done.2.mate = bf16[2,256,256]{2,1,0:T(8,128)(2,1)S(1)} collective-permute-done((bf16[2,256,256]{2,1,0:T(8,128)(2,1)S(1)}, bf16[2,256,256]{2,1,0:T(8,128)(2,1)S(1)}, u32[]{:S(2)}, u32[]{:S(2)}) %collective-permute-start.2) | collective-permute-done | bytes 262176 | tf_op jit(solution)/shard_map/ppermute | solution.py:317
  44.7 4.8 %solo0.1 = (bf16[2,2,128,256]{3,2,1,0:T(8,128)(2,1)S(1)}, f32[2,256,256]{2,1,0:T(8,128)S(1)}, bf16[2,128,256]{2,1,0:T(8,128)(2,1)S(1)}) custom-call(s32[4]{0:T(128)S(1)} %get-tuple-element.25.rows, s32[4]{0:T(128)S(1)} %copy-done.4, bf16[2,256,256]{2,1,0:T(8,128)(2,1)S(1)} %get-tuple-element.31.own, bf16[2,256,256]{2,1,0:T(8,128)(2,1)S(1)} %collective-permute-done.2.mate, ...), custom_call_target="tpu_custom_call" | custom-call | flops 1 | bytes 1 | tf_op jit(solution)/shard_map/solo0/pallas_call | solution.py:298
  49.6 5.3 %collective-permute-start.4 = (bf16[2,2,128,256]{3,2,1,0:T(8,128)(2,1)S(1)}, bf16[2,2,128,256]{3,2,1,0:T(8,128)(2,1)S(1)}, u32[]{:S(2)}, u32[]{:S(2)}) collective-permute-start(bf16[2,2,128,256]{3,2,1,0:T(8,128)(2,1)S(1)} %get-tuple-element.39), channel_id=1, source_target_pairs={{0,128},{1,129},{2,130},{3,131},{4,132},{5,133},{6,134},{7,135},{8... | collective-permute-start | bytes 786440 | tf_op jit(solution)/shard_map/ppermute | solution.py:317
  54.9 4.9 %solo1.1 = (bf16[2,128,256]{2,1,0:T(8,128)(2,1)S(1)}, bf16[2,192,256]{2,1,0:T(8,128)(2,1)S(1)}, f32[2,256,256]{2,1,0:T(8,128)S(1)}, bf16[2,2,128,256]{3,2,1,0:T(8,128)(2,1)S(1)}) custom-call(s32[4]{0:T(128)S(1)} %get-tuple-element.25.rows, s32[4]{0:T(128)S(1)} %copy-done.4, bf16[2,256,256]{2,1,0:T(8,128)(2,1)S(1)} %get-tuple-element.34.own, ...), custom_call_target="tpu_custom_call" | custom-call | flops 99999997952 | bytes 1 | tf_op jit(solution)/shard_map/solo1/pallas_call | solution.py:298
  59.8 1.0 %collective-permute-start.5 = (bf16[2,192,256]{2,1,0:T(8,128)(2,1)S(1)}, bf16[2,192,256]{2,1,0:T(8,128)(2,1)S(1)}, u32[]{:S(2)}, u32[]{:S(2)}) collective-permute-start(bf16[2,192,256]{2,1,0:T(8,128)(2,1)S(1)} %get-tuple-element.41), channel_id=1, source_target_pairs={{0,128},{1,129},{2,130},{3,131},{4,132},{5,133},{6,134},{7,135},{8... | collective-permute-start | bytes 589832 | tf_op jit(solution)/shard_map/ppermute | solution.py:317
  60.7 10.1 %collective-permute-done.4.back = bf16[2,2,128,256]{3,2,1,0:T(8,128)(2,1)S(1)} collective-permute-done((bf16[2,2,128,256]{3,2,1,0:T(8,128)(2,1)S(1)}, bf16[2,2,128,256]{3,2,1,0:T(8,128)(2,1)S(1)}, u32[]{:S(2)}, u32[]{:S(2)}) %collective-permute-start.4) | collective-permute-done | bytes 262176 | tf_op jit(solution)/shard_map/ppermute | solution.py:317
  70.9 0.1 collective-permute-start.7
  71.0 0.1 collective-permute-start.8
  71.1 2.3 %own.1.given = f32[2,512,1024]{2,1,0:T(8,128)S(1)} custom-call(s32[4]{0:T(128)S(1)} %get-tuple-element.25.rows, s32[4]{0:T(128)S(1)} %get-tuple-element.26.cols, f32[2,256,256]{2,1,0:T(8,128)S(1)} %get-tuple-element.33.kept0, f32[2,256,256]{2,1,0:T(8,128)S(1)} %get-tuple-element.37.kept1, bf16[2,2,128,256]{3,2,1,0:T(8,128)(2,1)S(1)} %collective-permute-done.4.back), custom_call_target="tpu_custom_call" | custom-call | flops 99999997952 | bytes 1 | tf_op jit(solution)/shard_map/own/pallas_call | solution.py:298
  73.4 0.7 collective-permute-done.5.inband
  74.1 8.6 %collective-permute-done.7.relay0 = bf16[2,128,256]{2,1,0:T(8,128)(2,1)S(1)} collective-permute-done((bf16[2,128,256]{2,1,0:T(8,128)(2,1)S(1)}, bf16[2,128,256]{2,1,0:T(8,128)(2,1)S(1)}, u32[]{:S(2)}, u32[]{:S(2)}) %collective-permute-start.7) | collective-permute-done | bytes 131104 | tf_op jit(solution)/shard_map/ppermute | solution.py:317
  82.7 0.0 collective-permute-done.8.relay1
  82.7 2.8 %rest.1 = (f32[2,512,1024]{2,1,0:T(8,128)S(1)}, f32[1,2,256,1024]{3,2,1,0:T(8,128)}) custom-call(s32[4]{0:T(128)S(1)} %get-tuple-element.25.rows, s32[4]{0:T(128)S(1)} %get-tuple-element.26.cols, s32[8]{0:T(128)S(1)} %get-tuple-element.30.spots, f32[2,512,1024]{2,1,0:T(8,128)S(1)} %own.1.given, ...), custom_call_target="tpu_custom_call", output_to_operand_aliasing={{0}: (3, {})} | custom-call | flops 1 | bytes 1 | tf_op jit(solution)/shard_map/rest/pallas_call | solution.py:298
  (16 shorter events, 0.1 us)
Async XLA Ops:
  0.0 29.1 %copy-start.5 = (f32[256,256]{1,0:T(8,128)S(1)}, f32[256,256]{1,0:T(8,128)}, u32[]{:S(2)}) copy-start(f32[256,256]{1,0:T(8,128)} %param.12) | copy-start | bytes 786436
  2.2 13.8 %collective-permute-start = (bf16[2064,128]{1,0:T(8,128)(2,1)S(1)}, bf16[2064,128]{1,0:T(8,128)(2,1)S(1)}, u32[]{:S(2)}, u32[]{:S(2)}) collective-permute-start(bf16[2064,128]{1,0:T(8,128)(2,1)S(1)} %get-tuple-element.28), channel_id=1, source_target_pairs={{0,127},{1,0},{2,1},{3,2},{4,3},{5,4},{6,5},{7,6},{8,7},{9,8},{10,... | collective-permute-start | bytes 1585160 | tf_op jit(solution)/shard_map/ppermute | solution.py:317
  9.3 20.9 %collective-permute-start.1 = (bf16[2064,128]{1,0:T(8,128)(2,1)S(1)}, bf16[2064,128]{1,0:T(8,128)(2,1)S(1)}, u32[]{:S(2)}, u32[]{:S(2)}) collective-permute-start(bf16[2064,128]{1,0:T(8,128)(2,1)S(1)} %get-tuple-element.29), channel_id=1, source_target_pairs={{0,1},{1,2},{2,3},{3,4},{4,5},{5,6},{6,7},{7,8},{8,9},{9,10},{10,1... | collective-permute-start | bytes 1585160 | tf_op jit(solution)/shard_map/ppermute | solution.py:317
  17.7 27.0 %collective-permute-start.2 = (bf16[2,256,256]{2,1,0:T(8,128)(2,1)S(1)}, bf16[2,256,256]{2,1,0:T(8,128)(2,1)S(1)}, u32[]{:S(2)}, u32[]{:S(2)}) collective-permute-start(bf16[2,256,256]{2,1,0:T(8,128)(2,1)S(1)} %get-tuple-element.32), channel_id=1, source_target_pairs={{0,128},{1,129},{2,130},{3,131},{4,132},{5,133},{6,134},{7,135},{8... | collective-permute-start | bytes 786440 | tf_op jit(solution)/shard_map/ppermute | solution.py:317
  29.0 25.9 %collective-permute-start.3 = (bf16[2,256,256]{2,1,0:T(8,128)(2,1)S(1)}, bf16[2,256,256]{2,1,0:T(8,128)(2,1)S(1)}, u32[]{:S(2)}, u32[]{:S(2)}) collective-permute-start(bf16[2,256,256]{2,1,0:T(8,128)(2,1)S(1)} %get-tuple-element.35), channel_id=1, source_target_pairs={{0,128},{1,129},{2,130},{3,131},{4,132},{5,133},{6,134},{7,135},{8... | collective-permute-start | bytes 786440 | tf_op jit(solution)/shard_map/ppermute | solution.py:317
  30.0 14.7 %copy-start = (bf16[4,2,256,256]{3,2,1,0:T(8,128)(2,1)S(1)}, bf16[4,2,256,256]{3,2,1,0:T(8,128)(2,1)}, u32[]{:S(2)}) copy-start(bf16[4,2,256,256]{3,2,1,0:T(8,128)(2,1)} %probes.3) | copy-start | bytes 3145732
  30.1 14.6 %copy-start.1 = (f32[4,256,256]{2,1,0:T(8,128)S(1)}, f32[4,256,256]{2,1,0:T(8,128)}, u32[]{:S(2)}) copy-start(f32[4,256,256]{2,1,0:T(8,128)} %amplitudes.3) | copy-start | bytes 3145732
  30.1 14.6 %copy-start.2 = (bf16[512,512]{1,0:T(8,128)(2,1)S(1)}, bf16[512,512]{1,0:T(8,128)(2,1)}, u32[]{:S(2)}) copy-start(bf16[512,512]{1,0:T(8,128)(2,1)} %constant.5.clone.second) | copy-start | bytes 1572868
  30.1 14.6 %copy-start.3 = (bf16[512,512]{1,0:T(8,128)(2,1)S(1)}, bf16[512,512]{1,0:T(8,128)(2,1)}, u32[]{:S(2)}) copy-start(bf16[512,512]{1,0:T(8,128)(2,1)} %constant.4.clone.first) | copy-start | bytes 1572868
  30.1 14.6 %copy-start.4 = (s32[4]{0:T(128)S(1)}, s32[4]{0:T(128)}, u32[]{:S(2)}) copy-start(s32[4]{0:T(128)} %picks.3) | copy-start | bytes 52
  49.6 21.3 %collective-permute-start.4 = (bf16[2,2,128,256]{3,2,1,0:T(8,128)(2,1)S(1)}, bf16[2,2,128,256]{3,2,1,0:T(8,128)(2,1)S(1)}, u32[]{:S(2)}, u32[]{:S(2)}) collective-permute-start(bf16[2,2,128,256]{3,2,1,0:T(8,128)(2,1)S(1)} %get-tuple-element.39), channel_id=1, source_target_pairs={{0,128},{1,129},{2,130},{3,131},{4,132},{5,133},{6,134},{7,135},{8... | collective-permute-start | bytes 786440 | tf_op jit(solution)/shard_map/ppermute | solution.py:317
  59.8 14.3 %collective-permute-start.5 = (bf16[2,192,256]{2,1,0:T(8,128)(2,1)S(1)}, bf16[2,192,256]{2,1,0:T(8,128)(2,1)S(1)}, u32[]{:S(2)}, u32[]{:S(2)}) collective-permute-start(bf16[2,192,256]{2,1,0:T(8,128)(2,1)S(1)} %get-tuple-element.41), channel_id=1, source_target_pairs={{0,128},{1,129},{2,130},{3,131},{4,132},{5,133},{6,134},{7,135},{8... | collective-permute-start | bytes 589832 | tf_op jit(solution)/shard_map/ppermute | solution.py:317
  60.7 13.4 %collective-permute-start.6 = (bf16[2,2,128,256]{3,2,1,0:T(8,128)(2,1)S(1)}, bf16[2,2,128,256]{3,2,1,0:T(8,128)(2,1)S(1)}, u32[]{:S(2)}, u32[]{:S(2)}) collective-permute-start(bf16[2,2,128,256]{3,2,1,0:T(8,128)(2,1)S(1)} %get-tuple-element.42), channel_id=1, source_target_pairs={{0,127},{1,0},{2,1},{3,2},{4,3},{5,4},{6,5},{7,6},{8,7},{9,8},{10,... | collective-permute-start | bytes 786440 | tf_op jit(solution)/shard_map/ppermute | solution.py:317
  70.9 11.8 %collective-permute-start.7 = (bf16[2,128,256]{2,1,0:T(8,128)(2,1)S(1)}, bf16[2,128,256]{2,1,0:T(8,128)(2,1)S(1)}, u32[]{:S(2)}, u32[]{:S(2)}) collective-permute-start(bf16[2,128,256]{2,1,0:T(8,128)(2,1)S(1)} %slice_bitcast_fusion), channel_id=1, source_target_pairs={{0,1},{1,2},{2,3},{3,4},{4,5},{5,6},{6,7},{7,8},{8,9},{9,10},{10,1... | collective-permute-start | bytes 393224 | tf_op jit(solution)/shard_map/ppermute | solution.py:317
  71.0 11.8 %collective-permute-start.8 = (bf16[2,128,256]{2,1,0:T(8,128)(2,1)S(1)}, bf16[2,128,256]{2,1,0:T(8,128)(2,1)S(1)}, u32[]{:S(2)}, u32[]{:S(2)}) collective-permute-start(bf16[2,128,256]{2,1,0:T(8,128)(2,1)S(1)} %get-tuple-element.43), channel_id=1, source_target_pairs={{0,255},{1,128},{2,129},{3,130},{4,131},{5,132},{6,133},{7,134},{8... | collective-permute-start | bytes 393224 | tf_op jit(solution)/shard_map/ppermute | solution.py:317

commit v10 on v7

--- a/solution.py
+++ b/solution.py
@@ -332,8 +332,7 @@
     early = move(early, "early")
     late = move(late, "late")
     sent = call(mate_kernel, "mate", [rows, cols, band, early], [full, full], [near])
-    sent0, late = lax.optimization_barrier((sent[0], late))
-    mate0 = move(sent0, "mate")
+    mate0 = move(sent[0], "mate")
     own0, own1, spots = call(
         own_windows_kernel, "windows", [rows, cols, band, early, late],
         [full, full, arr(8, dtype=jnp.int32)], [near], out_specs=[VM, VM, SM],

time: 85.9 us -> 84.7 us (0.986); the launches traced: 85.8 us -> 83.3 us
  waiting for transfers between devices: 40.8 us -> 34.5 us
  starting transfers between devices: 22.8 us -> 26.7 us
    ppermute x9, waiting for transfers between devices: 40.8 us -> 34.5 us  [shards(): move = lambda x, way: lax.ppermute(x, AXES, route[way])]
    ppermute x9, starting transfers between devices: 22.8 us -> 26.7 us  [shards(): move = lambda x, way: lax.ppermute(x, AXES, route[way])]
where the time goes in v10:
time: 84.7 us; the launch traced here: 83.3 us
  waiting for transfers between devices  34.5 us (41%)
  starting transfers between devices  26.7 us (32%)
  Pallas kernels  20.8 us (25%)
  local copies, waits for them, and re-layouts  0.99 us (1%)
    ppermute x9, waiting for transfers between devices, shards(): move = lambda x, way: lax.ppermute(x, AXES, route[way])  34.5 us
    ppermute x9, starting transfers between devices, shards(): move = lambda x, way: lax.ppermute(x, AXES, route[way])  26.7 us
    pallas_call x7, Pallas kernels, call(): pl.pallas_call(kernel, name=name, out_shape=outputs, in_specs=in_specs or...  20.8 us
  transfers between devices with their start and end apart: 9, of which 6 were waited for; matrix products, arithmetic and copies ran while one was open for 1% of the time, Pallas kernels for 19%

profile of v10, /device:TPU:8, one launch (start us, length us, event | category | flops | bytes accessed | tf_op | source)
XLA Modules:
  0.0 83.3 jit_solution(18397239244602075984)
XLA Ops:
  0.0 2.2 %edge.1 = (bf16[2064,128]{1,0:T(8,128)(2,1)S(1)}, bf16[2064,128]{1,0:T(8,128)(2,1)S(1)}, f32[2,256,1024]{2,1,0:T(8,128)S(1)}, s32[4]{0:T(128)S(1)}, s32[4]{0:T(128)S(1)}) custom-call(s32[4]{0:T(128)} %rows_in.1, s32[4]{0:T(128)} %cols_in.1, f32[1,2,256,1024]{3,2,1,0:T(8,128)} %objects_in.1), custom_call_target="tpu_custom_call" | custom-call | flops 1 | bytes 1 | tf_op jit(solution)/shard_map/edge/pallas_call | solution.py:298
  2.2 6.2 %collective-permute-start = (bf16[2064,128]{1,0:T(8,128)(2,1)S(1)}, bf16[2064,128]{1,0:T(8,128)(2,1)S(1)}, u32[]{:S(2)}, u32[]{:S(2)}) collective-permute-start(bf16[2064,128]{1,0:T(8,128)(2,1)S(1)} %get-tuple-element.30), channel_id=1, source_target_pairs={{0,127},{1,0},{2,1},{3,2},{4,3},{5,4},{6,5},{7,6},{8,7},{9,8},{10,... | collective-permute-start | bytes 1585160 | tf_op jit(solution)/shard_map/ppermute | solution.py:317
  8.5 7.7 %collective-permute-done.early = bf16[2064,128]{1,0:T(8,128)(2,1)S(1)} collective-permute-done((bf16[2064,128]{1,0:T(8,128)(2,1)S(1)}, bf16[2064,128]{1,0:T(8,128)(2,1)S(1)}, u32[]{:S(2)}, u32[]{:S(2)}) %collective-permute-start) | collective-permute-done | bytes 528416 | tf_op jit(solution)/shard_map/ppermute | solution.py:317
  16.2 1.6 %mate.1 = (bf16[2,256,256]{2,1,0:T(8,128)(2,1)S(1)}, bf16[2,256,256]{2,1,0:T(8,128)(2,1)S(1)}) custom-call(s32[4]{0:T(128)S(1)} %get-tuple-element.27.rows, s32[4]{0:T(128)S(1)} %get-tuple-element.28.cols, f32[2,256,1024]{2,1,0:T(8,128)S(1)} %get-tuple-element.29.objects, bf16[2064,128]{1,0:T(8,128)(2,1)S(1)} %collective-permute-done.early), custom_call_target="tpu_custom_call" | custom-call | flops 1 | bytes 1 | tf_op jit(solution)/shard_map/mate/pallas_call | solution.py:298
  17.8 12.4 %collective-permute-start.2 = (bf16[2,256,256]{2,1,0:T(8,128)(2,1)S(1)}, bf16[2,256,256]{2,1,0:T(8,128)(2,1)S(1)}, u32[]{:S(2)}, u32[]{:S(2)}) collective-permute-start(bf16[2,256,256]{2,1,0:T(8,128)(2,1)S(1)} %get-tuple-element.34), channel_id=1, source_target_pairs={{0,128},{1,129},{2,130},{3,131},{4,132},{5,133},{6,134},{7,135},{8... | collective-permute-start | bytes 786440 | tf_op jit(solution)/shard_map/ppermute | solution.py:317
  30.3 0.9 %cosine_bitcast_fusion = (f32[1,256,256]{2,1,0:T(8,128)S(1)}, f32[1,256,256]{2,1,0:T(8,128)S(1)}) fusion(f32[256,256]{1,0:T(8,128)S(1)} %copy-done.5), kind=kLoop, calls=%fused_computation.2 | loop fusion | bytes 786432 | tf_op jit(solution)/shard_map/stack | solution.py:319
  31.3 0.0 copy-start.3
  31.3 0.0 copy-start.4
  31.3 2.2 %windows.1 = (bf16[2,256,256]{2,1,0:T(8,128)(2,1)S(1)}, bf16[2,256,256]{2,1,0:T(8,128)(2,1)S(1)}, s32[8]{0:T(128)S(1)}) custom-call(s32[4]{0:T(128)S(1)} %get-tuple-element.27.rows, s32[4]{0:T(128)S(1)} %get-tuple-element.28.cols, f32[2,256,1024]{2,1,0:T(8,128)S(1)} %get-tuple-element.29.objects, bf16[2064,128]{1,0:T(8,128)(2,1)S(1)} %collective-permute-done.early, ...), custom_call_target="tpu_custom_call" | custom-call | flops 1 | bytes 1 | tf_op jit(solution)/shard_map/windows/pallas_call | solution.py:298
  33.6 0.1 collective-permute-start.3
  33.7 9.6 %collective-permute-done.2.mate = bf16[2,256,256]{2,1,0:T(8,128)(2,1)S(1)} collective-permute-done((bf16[2,256,256]{2,1,0:T(8,128)(2,1)S(1)}, bf16[2,256,256]{2,1,0:T(8,128)(2,1)S(1)}, u32[]{:S(2)}, u32[]{:S(2)}) %collective-permute-start.2) | collective-permute-done | bytes 262176 | tf_op jit(solution)/shard_map/ppermute | solution.py:317
  43.4 4.8 %solo0.1 = (bf16[2,2,128,256]{3,2,1,0:T(8,128)(2,1)S(1)}, f32[2,256,256]{2,1,0:T(8,128)S(1)}, bf16[2,128,256]{2,1,0:T(8,128)(2,1)S(1)}) custom-call(s32[4]{0:T(128)S(1)} %get-tuple-element.27.rows, s32[4]{0:T(128)S(1)} %copy-done.2, bf16[2,256,256]{2,1,0:T(8,128)(2,1)S(1)} %get-tuple-element.33.own, bf16[2,256,256]{2,1,0:T(8,128)(2,1)S(1)} %collective-permute-done.2.mate, ...), custom_call_target="tpu_custom_call" | custom-call | flops 99999997952 | bytes 1 | tf_op jit(solution)/shard_map/solo0/pallas_call | solution.py:298
  48.2 5.4 %collective-permute-start.4 = (bf16[2,2,128,256]{3,2,1,0:T(8,128)(2,1)S(1)}, bf16[2,2,128,256]{3,2,1,0:T(8,128)(2,1)S(1)}, u32[]{:S(2)}, u32[]{:S(2)}) collective-permute-start(bf16[2,2,128,256]{3,2,1,0:T(8,128)(2,1)S(1)} %get-tuple-element.43), channel_id=1, source_target_pairs={{0,128},{1,129},{2,130},{3,131},{4,132},{5,133},{6,134},{7,135},{8... | collective-permute-start | bytes 786440 | tf_op jit(solution)/shard_map/ppermute | solution.py:317
  53.6 4.9 %solo1.1 = (bf16[2,128,256]{2,1,0:T(8,128)(2,1)S(1)}, bf16[2,192,256]{2,1,0:T(8,128)(2,1)S(1)}, f32[2,256,256]{2,1,0:T(8,128)S(1)}, bf16[2,2,128,256]{3,2,1,0:T(8,128)(2,1)S(1)}) custom-call(s32[4]{0:T(128)S(1)} %get-tuple-element.27.rows, s32[4]{0:T(128)S(1)} %copy-done.2, bf16[2,256,256]{2,1,0:T(8,128)(2,1)S(1)} %get-tuple-element.38.own, ...), custom_call_target="tpu_custom_call" | custom-call | flops 99999997952 | bytes 1 | tf_op jit(solution)/shard_map/solo1/pallas_call | solution.py:298
  58.5 0.8 %collective-permute-start.5 = (bf16[2,192,256]{2,1,0:T(8,128)(2,1)S(1)}, bf16[2,192,256]{2,1,0:T(8,128)(2,1)S(1)}, u32[]{:S(2)}, u32[]{:S(2)}) collective-permute-start(bf16[2,192,256]{2,1,0:T(8,128)(2,1)S(1)} %get-tuple-element.45), channel_id=1, source_target_pairs={{0,128},{1,129},{2,130},{3,131},{4,132},{5,133},{6,134},{7,135},{8... | collective-permute-start | bytes 589832 | tf_op jit(solution)/shard_map/ppermute | solution.py:317
  59.4 1.5 %collective-permute-start.6 = (bf16[2,2,128,256]{3,2,1,0:T(8,128)(2,1)S(1)}, bf16[2,2,128,256]{3,2,1,0:T(8,128)(2,1)S(1)}, u32[]{:S(2)}, u32[]{:S(2)}) collective-permute-start(bf16[2,2,128,256]{3,2,1,0:T(8,128)(2,1)S(1)} %get-tuple-element.46), channel_id=1, source_target_pairs={{0,127},{1,0},{2,1},{3,2},{4,3},{5,4},{6,5},{7,6},{8,7},{9,8},{10,... | collective-permute-start | bytes 786440 | tf_op jit(solution)/shard_map/ppermute | solution.py:317
  60.8 9.4 %collective-permute-done.4.back = bf16[2,2,128,256]{3,2,1,0:T(8,128)(2,1)S(1)} collective-permute-done((bf16[2,2,128,256]{3,2,1,0:T(8,128)(2,1)S(1)}, bf16[2,2,128,256]{3,2,1,0:T(8,128)(2,1)S(1)}, u32[]{:S(2)}, u32[]{:S(2)}) %collective-permute-start.4) | collective-permute-done | bytes 262176 | tf_op jit(solution)/shard_map/ppermute | solution.py:317
  70.2 0.1 collective-permute-start.7
  70.3 0.1 collective-permute-start.8
  70.4 2.3 %own.1.given = f32[2,512,1024]{2,1,0:T(8,128)S(1)} custom-call(s32[4]{0:T(128)S(1)} %get-tuple-element.27.rows, s32[4]{0:T(128)S(1)} %get-tuple-element.28.cols, f32[2,256,256]{2,1,0:T(8,128)S(1)} %get-tuple-element.35.kept0, f32[2,256,256]{2,1,0:T(8,128)S(1)} %get-tuple-element.41.kept1, bf16[2,2,128,256]{3,2,1,0:T(8,128)(2,1)S(1)} %collective-permute-done.4.back), custom_call_target="tpu_custom_call" | custom-call | flops 99999997952 | bytes 1 | tf_op jit(solution)/shard_map/own/pallas_call | solution.py:298
  72.7 3.4 %collective-permute-done.5.inband = bf16[2,192,256]{2,1,0:T(8,128)(2,1)S(1)} collective-permute-done((bf16[2,192,256]{2,1,0:T(8,128)(2,1)S(1)}, bf16[2,192,256]{2,1,0:T(8,128)(2,1)S(1)}, u32[]{:S(2)}, u32[]{:S(2)}) %collective-permute-start.5) | collective-permute-done | bytes 196640 | tf_op jit(solution)/shard_map/ppermute | solution.py:317
  76.1 4.2 %collective-permute-done.7.relay0 = bf16[2,128,256]{2,1,0:T(8,128)(2,1)S(1)} collective-permute-done((bf16[2,128,256]{2,1,0:T(8,128)(2,1)S(1)}, bf16[2,128,256]{2,1,0:T(8,128)(2,1)S(1)}, u32[]{:S(2)}, u32[]{:S(2)}) %collective-permute-start.7) | collective-permute-done | bytes 131104 | tf_op jit(solution)/shard_map/ppermute | solution.py:317
  80.4 0.1 collective-permute-done.8.relay1
  80.4 2.8 %rest.1 = (f32[2,512,1024]{2,1,0:T(8,128)S(1)}, f32[1,2,256,1024]{3,2,1,0:T(8,128)}) custom-call(s32[4]{0:T(128)S(1)} %get-tuple-element.27.rows, s32[4]{0:T(128)S(1)} %get-tuple-element.28.cols, s32[8]{0:T(128)S(1)} %get-tuple-element.32.spots, f32[2,512,1024]{2,1,0:T(8,128)S(1)} %own.1.given, ...), custom_call_target="tpu_custom_call", output_to_operand_aliasing={{0}: (3, {})} | custom-call | flops 1 | bytes 1 | tf_op jit(solution)/shard_map/rest/pallas_call | solution.py:298
  (16 shorter events, 0.1 us)
Async XLA Ops:
  0.0 30.3 %copy-start.5 = (f32[256,256]{1,0:T(8,128)S(1)}, f32[256,256]{1,0:T(8,128)}, u32[]{:S(2)}) copy-start(f32[256,256]{1,0:T(8,128)} %param.12) | copy-start | bytes 786436
  2.2 14.0 %collective-permute-start = (bf16[2064,128]{1,0:T(8,128)(2,1)S(1)}, bf16[2064,128]{1,0:T(8,128)(2,1)S(1)}, u32[]{:S(2)}, u32[]{:S(2)}) collective-permute-start(bf16[2064,128]{1,0:T(8,128)(2,1)S(1)} %get-tuple-element.30), channel_id=1, source_target_pairs={{0,127},{1,0},{2,1},{3,2},{4,3},{5,4},{6,5},{7,6},{8,7},{9,8},{10,... | collective-permute-start | bytes 1585160 | tf_op jit(solution)/shard_map/ppermute | solution.py:317
  8.5 22.9 %collective-permute-start.1 = (bf16[2064,128]{1,0:T(8,128)(2,1)S(1)}, bf16[2064,128]{1,0:T(8,128)(2,1)S(1)}, u32[]{:S(2)}, u32[]{:S(2)}) collective-permute-start(bf16[2064,128]{1,0:T(8,128)(2,1)S(1)} %get-tuple-element.31), channel_id=1, source_target_pairs={{0,1},{1,2},{2,3},{3,4},{4,5},{5,6},{6,7},{7,8},{8,9},{9,10},{10,1... | collective-permute-start | bytes 1585160 | tf_op jit(solution)/shard_map/ppermute | solution.py:317
  17.8 25.5 %collective-permute-start.2 = (bf16[2,256,256]{2,1,0:T(8,128)(2,1)S(1)}, bf16[2,256,256]{2,1,0:T(8,128)(2,1)S(1)}, u32[]{:S(2)}, u32[]{:S(2)}) collective-permute-start(bf16[2,256,256]{2,1,0:T(8,128)(2,1)S(1)} %get-tuple-element.34), channel_id=1, source_target_pairs={{0,128},{1,129},{2,130},{3,131},{4,132},{5,133},{6,134},{7,135},{8... | collective-permute-start | bytes 786440 | tf_op jit(solution)/shard_map/ppermute | solution.py:317
  31.2 12.1 %copy-start = (bf16[4,2,256,256]{3,2,1,0:T(8,128)(2,1)S(1)}, bf16[4,2,256,256]{3,2,1,0:T(8,128)(2,1)}, u32[]{:S(2)}) copy-start(bf16[4,2,256,256]{3,2,1,0:T(8,128)(2,1)} %probes.3) | copy-start | bytes 3145732
  31.2 12.1 %copy-start.1 = (f32[4,256,256]{2,1,0:T(8,128)S(1)}, f32[4,256,256]{2,1,0:T(8,128)}, u32[]{:S(2)}) copy-start(f32[4,256,256]{2,1,0:T(8,128)} %amplitudes.3) | copy-start | bytes 3145732
  31.2 12.1 %copy-start.2 = (s32[4]{0:T(128)S(1)}, s32[4]{0:T(128)}, u32[]{:S(2)}) copy-start(s32[4]{0:T(128)} %picks.3) | copy-start | bytes 52
  31.3 12.1 %copy-start.3 = (bf16[512,512]{1,0:T(8,128)(2,1)S(1)}, bf16[512,512]{1,0:T(8,128)(2,1)}, u32[]{:S(2)}) copy-start(bf16[512,512]{1,0:T(8,128)(2,1)} %constant.5.clone.second) | copy-start | bytes 1572868
  31.3 12.1 %copy-start.4 = (bf16[512,512]{1,0:T(8,128)(2,1)S(1)}, bf16[512,512]{1,0:T(8,128)(2,1)}, u32[]{:S(2)}) copy-start(bf16[512,512]{1,0:T(8,128)(2,1)} %constant.4.clone.first) | copy-start | bytes 1572868
  33.6 20.1 %collective-permute-start.3 = (bf16[2,256,256]{2,1,0:T(8,128)(2,1)S(1)}, bf16[2,256,256]{2,1,0:T(8,128)(2,1)S(1)}, u32[]{:S(2)}, u32[]{:S(2)}) collective-permute-start(bf16[2,256,256]{2,1,0:T(8,128)(2,1)S(1)} %get-tuple-element.39), channel_id=1, source_target_pairs={{0,128},{1,129},{2,130},{3,131},{4,132},{5,133},{6,134},{7,135},{8... | collective-permute-start | bytes 786440 | tf_op jit(solution)/shard_map/ppermute | solution.py:317
  48.2 22.0 %collective-permute-start.4 = (bf16[2,2,128,256]{3,2,1,0:T(8,128)(2,1)S(1)}, bf16[2,2,128,256]{3,2,1,0:T(8,128)(2,1)S(1)}, u32[]{:S(2)}, u32[]{:S(2)}) collective-permute-start(bf16[2,2,128,256]{3,2,1,0:T(8,128)(2,1)S(1)} %get-tuple-element.43), channel_id=1, source_target_pairs={{0,128},{1,129},{2,130},{3,131},{4,132},{5,133},{6,134},{7,135},{8... | collective-permute-start | bytes 786440 | tf_op jit(solution)/shard_map/ppermute | solution.py:317
  58.5 17.6 %collective-permute-start.5 = (bf16[2,192,256]{2,1,0:T(8,128)(2,1)S(1)}, bf16[2,192,256]{2,1,0:T(8,128)(2,1)S(1)}, u32[]{:S(2)}, u32[]{:S(2)}) collective-permute-start(bf16[2,192,256]{2,1,0:T(8,128)(2,1)S(1)} %get-tuple-element.45), channel_id=1, source_target_pairs={{0,128},{1,129},{2,130},{3,131},{4,132},{5,133},{6,134},{7,135},{8... | collective-permute-start | bytes 589832 | tf_op jit(solution)/shard_map/ppermute | solution.py:317
  59.4 16.8 %collective-permute-start.6 = (bf16[2,2,128,256]{3,2,1,0:T(8,128)(2,1)S(1)}, bf16[2,2,128,256]{3,2,1,0:T(8,128)(2,1)S(1)}, u32[]{:S(2)}, u32[]{:S(2)}) collective-permute-start(bf16[2,2,128,256]{3,2,1,0:T(8,128)(2,1)S(1)} %get-tuple-element.46), channel_id=1, source_target_pairs={{0,127},{1,0},{2,1},{3,2},{4,3},{5,4},{6,5},{7,6},{8,7},{9,8},{10,... | collective-permute-start | bytes 786440 | tf_op jit(solution)/shard_map/ppermute | solution.py:317
  70.2 10.1 %collective-permute-start.7 = (bf16[2,128,256]{2,1,0:T(8,128)(2,1)S(1)}, bf16[2,128,256]{2,1,0:T(8,128)(2,1)S(1)}, u32[]{:S(2)}, u32[]{:S(2)}) collective-permute-start(bf16[2,128,256]{2,1,0:T(8,128)(2,1)S(1)} %slice_bitcast_fusion), channel_id=1, source_target_pairs={{0,1},{1,2},{2,3},{3,4},{4,5},{5,6},{6,7},{7,8},{8,9},{9,10},{10,1... | collective-permute-start | bytes 393224 | tf_op jit(solution)/shard_map/ppermute | solution.py:317
  70.3 10.1 %collective-permute-start.8 = (bf16[2,128,256]{2,1,0:T(8,128)(2,1)S(1)}, bf16[2,128,256]{2,1,0:T(8,128)(2,1)S(1)}, u32[]{:S(2)}, u32[]{:S(2)}) collective-permute-start(bf16[2,128,256]{2,1,0:T(8,128)(2,1)S(1)} %get-tuple-element.47), channel_id=1, source_target_pairs={{0,255},{1,128},{2,129},{3,130},{4,131},{5,132},{6,133},{7,134},{8... | collective-permute-start | bytes 393224 | tf_op jit(solution)/shard_map/ppermute | solution.py:317

commit v11 on v10

--- a/solution.py
+++ b/solution.py
@@ -217,12 +217,12 @@
     number, rows, picks, own, mate, probes, amplitudes, wave, first, second, *refs
 ):
     if number == 0:
-        sent, kept, edges, held, made = refs
-        sent_outer, sent_inband = sent.at[0], sent.at[1]
+        sent_outer, sent_inband, kept, edges, held, made = refs
     else:
-        before, sent_outer, sent_inband, kept, both, held, made = refs
-        both[0] = before[...]
-        edges = both.at[1]
+        outer_before, edge_before, outers, sent_inband, kept, both, held, made = refs
+        outers[0] = outer_before[...]
+        both[0] = edge_before[...]
+        sent_outer, edges = outers.at[1], both.at[1]
     cut = lax.axis_index("cuts")
     spots = places(rows)
     place = jnp.where(cut == 0, spots[number], spots[2 + number])
@@ -254,10 +254,9 @@
     spot = jnp.where(upper, spots[number], spots[2 + number])
     skip = jnp.where(upper, SIDE - inband.shape[1], 0)
     put(rows[spot] + HALF + skip, cols[spot], inband[channel].astype(F32))
-    return rows[spot] + HALF + jnp.where(upper, 0, HALF), cols[spot]
-
-
-def own_kernel(rows, cols, kept0, kept1, back, total):
+
+
+def own_kernel(rows, cols, kept0, kept1, inband, total):
     cut = lax.axis_index("cuts")
     places_here = places(rows)
     total[...] = jnp.zeros_like(total)
@@ -266,12 +265,11 @@
         for number, kept in enumerate((kept0, kept1)):
             spot = jnp.where(cut == 0, places_here[number], places_here[2 + number])
             put(rows[spot] + HALF, cols[spot], kept[channel])
-        top, left = put_inband(put, rows, cols, 0, back.at[1], channel)
-        put(top, left, back[0, channel].astype(F32))
+        put_inband(put, rows, cols, 0, inband, channel)
 
 
 def rest_kernel(
-    rows, cols, spots, given, inband, edges, relay0, relay1, total, output, sems
+    rows, cols, spots, given, inband, outers, edges, total, output, sems
 ):
     cut = lax.axis_index("cuts")
     shift = jnp.where(cut == 0, BAND, -HALF)
@@ -279,10 +277,11 @@
     for channel in range(2):
         put = functools.partial(put_window, total, channel)
         put_inband(put, rows, cols, 1, inband, channel)
-        for number, relay in enumerate((relay0, relay1)):
+        for number in range(2):
             k = 2 * number
             put(spots[k] + shift, spots[k + 1], edges[number, channel].astype(F32))
-            put(spots[4 + k] + BAND - HALF - shift, spots[5 + k], relay[channel].astype(F32))
+            top = spots[4 + k] + BAND - HALF - shift
+            put(top, spots[5 + k], outers[number, channel].astype(F32))
         copies.append(
             pltpu.make_async_copy(
                 total.at[channel, pl.ds(HALF, BAND)], output.at[0, channel], sems.at[channel]
@@ -342,28 +341,27 @@
     optics = [probes, amplitudes, wave, first, second]
     work = [pltpu.VMEM((2, 2, SIDE, SIDE), BF), pltpu.VMEM((2, 2, SIDE, SIDE), F32)]
     wide_full = arr(2, SIDE, SIDE, dtype=F32)
-    back0, kept0, edge0 = call(
+    inner = arr(2, HALF + 64, SIDE)
+    pair = arr(2, 2, HALF, SIDE)
+    outer0, inband0, kept0, edge0 = call(
         functools.partial(solo_kernel, 0), "solo0", [rows, probe_choice, own0, mate0] + optics,
-        [arr(2, 2, HALF, SIDE), wide_full, half], work, flops=10**11,
-    )
-    back0 = move(back0, "mate")
-    outer1, inband1, kept1, edges = call(
+        [half, inner, wide_full, half], work, flops=10**11,
+    )
+    inband0 = move(inband0, "mate")
+    outers, inband1, kept1, edges = call(
         functools.partial(solo_kernel, 1), "solo1",
-        [rows, probe_choice, own1, mate1] + optics + [edge0],
-        [half, arr(2, HALF + 64, SIDE), wide_full, arr(2, 2, HALF, SIDE)], work, flops=10**11,
+        [rows, probe_choice, own1, mate1] + optics + [outer0, edge0],
+        [pair, inner, wide_full, pair], work, flops=10**11,
     )
     inband1 = move(inband1, "mate")
-    outer1, back0 = lax.optimization_barrier((outer1, back0))
-    relay1 = move(outer1, "direct")
+    outers = move(outers, "direct")
     edges = move(edges, "early")
-    relay0 = move(back0[0], "late")
     (total,) = call(
-        own_kernel, "own", [rows, cols, kept0, kept1, back0],
+        own_kernel, "own", [rows, cols, kept0, kept1, inband0],
         [arr(2, EXT, COLS, dtype=F32)], flops=10**11,
     )
     _, gradient = call(
-        rest_kernel, "rest",
-        [rows, cols, spots, total, inband1, edges, relay0, relay1],
+        rest_kernel, "rest", [rows, cols, spots, total, inband1, outers, edges],
         [arr(2, EXT, COLS, dtype=F32), arr(1, 2, BAND, COLS, dtype=F32)],
         [pltpu.SemaphoreType.DMA((2,))],
         out_specs=[VM, HB],

time: 84.7 us -> 83.8 us (0.989)
  the two profiles are of different devices: /device:TPU:8 before, /device:TPU:1 now
where the time goes in v11:
time: 83.8 us; the launch traced here: 83.7 us
  starting transfers between devices  32.1 us (38%)
  waiting for transfers between devices  29.4 us (35%)
  Pallas kernels  20.8 us (25%)
  local copies, waits for them, and re-layouts  0.98 us (1%)
    ppermute x8, starting transfers between devices, shards(): move = lambda x, way: lax.ppermute(x, AXES, route[way])  32.1 us
    ppermute x8, waiting for transfers between devices, shards(): move = lambda x, way: lax.ppermute(x, AXES, route[way])  29.4 us
    pallas_call x7, Pallas kernels, call(): pl.pallas_call(kernel, name=name, out_shape=outputs, in_specs=in_specs or...  20.8 us
  transfers between devices with their start and end apart: 8, of which 4 were waited for; matrix products, arithmetic and copies ran while one was open for 1% of the time, Pallas kernels for 19%

profile of v11, /device:TPU:1, one launch (start us, length us, event | category | flops | bytes accessed | tf_op | source)
XLA Modules:
  0.0 83.7 jit_solution(6796196016131411868)
XLA Ops:
  0.0 2.2 %edge.1 = (bf16[2064,128]{1,0:T(8,128)(2,1)S(1)}, bf16[2064,128]{1,0:T(8,128)(2,1)S(1)}, f32[2,256,1024]{2,1,0:T(8,128)S(1)}, s32[4]{0:T(128)S(1)}, s32[4]{0:T(128)S(1)}) custom-call(s32[4]{0:T(128)} %rows_in.1, s32[4]{0:T(128)} %cols_in.1, f32[1,2,256,1024]{3,2,1,0:T(8,128)} %objects_in.1), custom_call_target="tpu_custom_call" | custom-call | flops 1 | bytes 1 | tf_op jit(solution)/shard_map/edge/pallas_call | solution.py:297
  2.2 3.3 %collective-permute-start = (bf16[2064,128]{1,0:T(8,128)(2,1)S(1)}, bf16[2064,128]{1,0:T(8,128)(2,1)S(1)}, u32[]{:S(2)}, u32[]{:S(2)}) collective-permute-start(bf16[2064,128]{1,0:T(8,128)(2,1)S(1)} %get-tuple-element.29), channel_id=1, source_target_pairs={{0,127},{1,0},{2,1},{3,2},{4,3},{5,4},{6,5},{7,6},{8,7},{9,8},{10,... | collective-permute-start | bytes 1585160 | tf_op jit(solution)/shard_map/ppermute | solution.py:316
  5.6 6.7 %collective-permute-done.early = bf16[2064,128]{1,0:T(8,128)(2,1)S(1)} collective-permute-done((bf16[2064,128]{1,0:T(8,128)(2,1)S(1)}, bf16[2064,128]{1,0:T(8,128)(2,1)S(1)}, u32[]{:S(2)}, u32[]{:S(2)}) %collective-permute-start) | collective-permute-done | bytes 528416 | tf_op jit(solution)/shard_map/ppermute | solution.py:316
  12.2 1.6 %mate.1 = (bf16[2,256,256]{2,1,0:T(8,128)(2,1)S(1)}, bf16[2,256,256]{2,1,0:T(8,128)(2,1)S(1)}) custom-call(s32[4]{0:T(128)S(1)} %get-tuple-element.26.rows, s32[4]{0:T(128)S(1)} %get-tuple-element.27.cols, f32[2,256,1024]{2,1,0:T(8,128)S(1)} %get-tuple-element.28.objects, bf16[2064,128]{1,0:T(8,128)(2,1)S(1)} %collective-permute-done.early), custom_call_target="tpu_custom_call" | custom-call | flops 1 | bytes 1 | tf_op jit(solution)/shard_map/mate/pallas_call | solution.py:297
  13.9 5.4 %collective-permute-start.2 = (bf16[2,256,256]{2,1,0:T(8,128)(2,1)S(1)}, bf16[2,256,256]{2,1,0:T(8,128)(2,1)S(1)}, u32[]{:S(2)}, u32[]{:S(2)}) collective-permute-start(bf16[2,256,256]{2,1,0:T(8,128)(2,1)S(1)} %get-tuple-element.33), channel_id=1, source_target_pairs={{0,128},{1,129},{2,130},{3,131},{4,132},{5,133},{6,134},{7,135},{8... | collective-permute-start | bytes 786440 | tf_op jit(solution)/shard_map/ppermute | solution.py:316
  19.2 0.9 %cosine_bitcast_fusion = (f32[1,256,256]{2,1,0:T(8,128)S(1)}, f32[1,256,256]{2,1,0:T(8,128)S(1)}) fusion(f32[256,256]{1,0:T(8,128)S(1)} %copy-done.5), kind=kLoop, calls=%fused_computation.2 | loop fusion | bytes 786432 | tf_op jit(solution)/shard_map/stack | solution.py:318
  20.2 0.0 copy-start
  20.2 0.0 copy-start.1
  20.2 0.0 copy-start.2
  20.2 0.0 copy-start.3
  20.2 0.0 copy-start.4
  20.3 2.2 %windows.1 = (bf16[2,256,256]{2,1,0:T(8,128)(2,1)S(1)}, bf16[2,256,256]{2,1,0:T(8,128)(2,1)S(1)}, s32[8]{0:T(128)S(1)}) custom-call(s32[4]{0:T(128)S(1)} %get-tuple-element.26.rows, s32[4]{0:T(128)S(1)} %get-tuple-element.27.cols, f32[2,256,1024]{2,1,0:T(8,128)S(1)} %get-tuple-element.28.objects, bf16[2064,128]{1,0:T(8,128)(2,1)S(1)} %collective-permute-done.early, ...), custom_call_target="tpu_custom_call" | custom-call | flops 1 | bytes 1 | tf_op jit(solution)/shard_map/windows/pallas_call | solution.py:297
  22.5 6.0 %collective-permute-start.3 = (bf16[2,256,256]{2,1,0:T(8,128)(2,1)S(1)}, bf16[2,256,256]{2,1,0:T(8,128)(2,1)S(1)}, u32[]{:S(2)}, u32[]{:S(2)}) collective-permute-start(bf16[2,256,256]{2,1,0:T(8,128)(2,1)S(1)} %get-tuple-element.38), channel_id=1, source_target_pairs={{0,128},{1,129},{2,130},{3,131},{4,132},{5,133},{6,134},{7,135},{8... | collective-permute-start | bytes 786440 | tf_op jit(solution)/shard_map/ppermute | solution.py:316
  28.6 4.8 %solo0.1 = (bf16[2,128,256]{2,1,0:T(8,128)(2,1)S(1)}, bf16[2,192,256]{2,1,0:T(8,128)(2,1)S(1)}, f32[2,256,256]{2,1,0:T(8,128)S(1)}, bf16[2,128,256]{2,1,0:T(8,128)(2,1)S(1)}) custom-call(s32[4]{0:T(128)S(1)} %get-tuple-element.26.rows, s32[4]{0:T(128)S(1)} %copy-done.2, bf16[2,256,256]{2,1,0:T(8,128)(2,1)S(1)} %get-tuple-element.32.own, ...), custom_call_target="tpu_custom_call" | custom-call | flops 99999997952 | bytes 1 | tf_op jit(solution)/shard_map/solo0/pallas_call | solution.py:297
  33.4 0.5 collective-permute-start.4
  33.9 10.6 %collective-permute-done.3.mate = bf16[2,256,256]{2,1,0:T(8,128)(2,1)S(1)} collective-permute-done((bf16[2,256,256]{2,1,0:T(8,128)(2,1)S(1)}, bf16[2,256,256]{2,1,0:T(8,128)(2,1)S(1)}, u32[]{:S(2)}, u32[]{:S(2)}) %collective-permute-start.3) | collective-permute-done | bytes 262176 | tf_op jit(solution)/shard_map/ppermute | solution.py:316
  44.5 4.9 %solo1.1 = (bf16[2,2,128,256]{3,2,1,0:T(8,128)(2,1)S(1)}, bf16[2,192,256]{2,1,0:T(8,128)(2,1)S(1)}, f32[2,256,256]{2,1,0:T(8,128)S(1)}, bf16[2,2,128,256]{3,2,1,0:T(8,128)(2,1)S(1)}) custom-call(s32[4]{0:T(128)S(1)} %get-tuple-element.26.rows, s32[4]{0:T(128)S(1)} %copy-done.2, bf16[2,256,256]{2,1,0:T(8,128)(2,1)S(1)} %get-tuple-element.37.own, ...), custom_call_target="tpu_custom_call" | custom-call | flops 99999997952 | bytes 1 | tf_op jit(solution)/shard_map/solo1/pallas_call | solution.py:297
  49.4 5.0 %collective-permute-start.5 = (bf16[2,192,256]{2,1,0:T(8,128)(2,1)S(1)}, bf16[2,192,256]{2,1,0:T(8,128)(2,1)S(1)}, u32[]{:S(2)}, u32[]{:S(2)}) collective-permute-start(bf16[2,192,256]{2,1,0:T(8,128)(2,1)S(1)} %get-tuple-element.43), channel_id=1, source_target_pairs={{0,128},{1,129},{2,130},{3,131},{4,132},{5,133},{6,134},{7,135},{8... | collective-permute-start | bytes 589832 | tf_op jit(solution)/shard_map/ppermute | solution.py:316
  54.4 11.7 %collective-permute-start.6 = (bf16[2,2,128,256]{3,2,1,0:T(8,128)(2,1)S(1)}, bf16[2,2,128,256]{3,2,1,0:T(8,128)(2,1)S(1)}, u32[]{:S(2)}, u32[]{:S(2)}) collective-permute-start(bf16[2,2,128,256]{3,2,1,0:T(8,128)(2,1)S(1)} %get-tuple-element.44), channel_id=1, source_target_pairs={{0,255},{1,128},{2,129},{3,130},{4,131},{5,132},{6,133},{7,134},{8... | collective-permute-start | bytes 786440 | tf_op jit(solution)/shard_map/ppermute | solution.py:316
  66.0 0.3 collective-permute-start.7
  66.3 2.3 %own.1.given = f32[2,512,1024]{2,1,0:T(8,128)S(1)} custom-call(s32[4]{0:T(128)S(1)} %get-tuple-element.26.rows, s32[4]{0:T(128)S(1)} %get-tuple-element.27.cols, f32[2,256,256]{2,1,0:T(8,128)S(1)} %get-tuple-element.34.kept0, f32[2,256,256]{2,1,0:T(8,128)S(1)} %get-tuple-element.41.kept1, bf16[2,192,256]{2,1,0:T(8,128)(2,1)S(1)} %collective-permute-done.4.inband), custom_call_target="tpu_custom_call" | custom-call | flops 99999997952 | bytes 1 | tf_op jit(solution)/shard_map/own/pallas_call | solution.py:297
  68.7 1.8 %collective-permute-done.5.inband = bf16[2,192,256]{2,1,0:T(8,128)(2,1)S(1)} collective-permute-done((bf16[2,192,256]{2,1,0:T(8,128)(2,1)S(1)}, bf16[2,192,256]{2,1,0:T(8,128)(2,1)S(1)}, u32[]{:S(2)}, u32[]{:S(2)}) %collective-permute-start.5) | collective-permute-done | bytes 196640 | tf_op jit(solution)/shard_map/ppermute | solution.py:316
  70.4 10.3 %collective-permute-done.6.outers = bf16[2,2,128,256]{3,2,1,0:T(8,128)(2,1)S(1)} collective-permute-done((bf16[2,2,128,256]{3,2,1,0:T(8,128)(2,1)S(1)}, bf16[2,2,128,256]{3,2,1,0:T(8,128)(2,1)S(1)}, u32[]{:S(2)}, u32[]{:S(2)}) %collective-permute-start.6) | collective-permute-done | bytes 262176 | tf_op jit(solution)/shard_map/ppermute | solution.py:316
  80.7 2.8 %rest.1 = (f32[2,512,1024]{2,1,0:T(8,128)S(1)}, f32[1,2,256,1024]{3,2,1,0:T(8,128)}) custom-call(s32[4]{0:T(128)S(1)} %get-tuple-element.26.rows, s32[4]{0:T(128)S(1)} %get-tuple-element.27.cols, s32[8]{0:T(128)S(1)} %get-tuple-element.31.spots, f32[2,512,1024]{2,1,0:T(8,128)S(1)} %own.1.given, ...), custom_call_target="tpu_custom_call", output_to_operand_aliasing={{0}: (3, {})} | custom-call | flops 1 | bytes 1 | tf_op jit(solution)/shard_map/rest/pallas_call | solution.py:297
  (13 shorter events, 0.1 us)
Async XLA Ops:
  0.0 19.2 %copy-start.5 = (f32[256,256]{1,0:T(8,128)S(1)}, f32[256,256]{1,0:T(8,128)}, u32[]{:S(2)}) copy-start(f32[256,256]{1,0:T(8,128)} %param.12) | copy-start | bytes 786436
  2.2 10.0 %collective-permute-start = (bf16[2064,128]{1,0:T(8,128)(2,1)S(1)}, bf16[2064,128]{1,0:T(8,128)(2,1)S(1)}, u32[]{:S(2)}, u32[]{:S(2)}) collective-permute-start(bf16[2064,128]{1,0:T(8,128)(2,1)S(1)} %get-tuple-element.29), channel_id=1, source_target_pairs={{0,127},{1,0},{2,1},{3,2},{4,3},{5,4},{6,5},{7,6},{8,7},{9,8},{10,... | collective-permute-start | bytes 1585160 | tf_op jit(solution)/shard_map/ppermute | solution.py:316
  5.5 14.7 %collective-permute-start.1 = (bf16[2064,128]{1,0:T(8,128)(2,1)S(1)}, bf16[2064,128]{1,0:T(8,128)(2,1)S(1)}, u32[]{:S(2)}, u32[]{:S(2)}) collective-permute-start(bf16[2064,128]{1,0:T(8,128)(2,1)S(1)} %get-tuple-element.30), channel_id=1, source_target_pairs={{0,1},{1,2},{2,3},{3,4},{4,5},{5,6},{6,7},{7,8},{8,9},{9,10},{10,1... | collective-permute-start | bytes 1585160 | tf_op jit(solution)/shard_map/ppermute | solution.py:316
  13.9 14.6 %collective-permute-start.2 = (bf16[2,256,256]{2,1,0:T(8,128)(2,1)S(1)}, bf16[2,256,256]{2,1,0:T(8,128)(2,1)S(1)}, u32[]{:S(2)}, u32[]{:S(2)}) collective-permute-start(bf16[2,256,256]{2,1,0:T(8,128)(2,1)S(1)} %get-tuple-element.33), channel_id=1, source_target_pairs={{0,128},{1,129},{2,130},{3,131},{4,132},{5,133},{6,134},{7,135},{8... | collective-permute-start | bytes 786440 | tf_op jit(solution)/shard_map/ppermute | solution.py:316
  20.2 8.3 %copy-start = (bf16[4,2,256,256]{3,2,1,0:T(8,128)(2,1)S(1)}, bf16[4,2,256,256]{3,2,1,0:T(8,128)(2,1)}, u32[]{:S(2)}) copy-start(bf16[4,2,256,256]{3,2,1,0:T(8,128)(2,1)} %probes.3) | copy-start | bytes 3145732
  20.2 8.3 %copy-start.1 = (f32[4,256,256]{2,1,0:T(8,128)S(1)}, f32[4,256,256]{2,1,0:T(8,128)}, u32[]{:S(2)}) copy-start(f32[4,256,256]{2,1,0:T(8,128)} %amplitudes.3) | copy-start | bytes 3145732
  20.2 8.3 %copy-start.2 = (s32[4]{0:T(128)S(1)}, s32[4]{0:T(128)}, u32[]{:S(2)}) copy-start(s32[4]{0:T(128)} %picks.3) | copy-start | bytes 52
  20.2 8.3 %copy-start.3 = (bf16[512,512]{1,0:T(8,128)(2,1)S(1)}, bf16[512,512]{1,0:T(8,128)(2,1)}, u32[]{:S(2)}) copy-start(bf16[512,512]{1,0:T(8,128)(2,1)} %constant.5.clone.second) | copy-start | bytes 1572868
  20.2 8.3 %copy-start.4 = (bf16[512,512]{1,0:T(8,128)(2,1)S(1)}, bf16[512,512]{1,0:T(8,128)(2,1)}, u32[]{:S(2)}) copy-start(bf16[512,512]{1,0:T(8,128)(2,1)} %constant.4.clone.first) | copy-start | bytes 1572868
  22.5 22.0 %collective-permute-start.3 = (bf16[2,256,256]{2,1,0:T(8,128)(2,1)S(1)}, bf16[2,256,256]{2,1,0:T(8,128)(2,1)S(1)}, u32[]{:S(2)}, u32[]{:S(2)}) collective-permute-start(bf16[2,256,256]{2,1,0:T(8,128)(2,1)S(1)} %get-tuple-element.38), channel_id=1, source_target_pairs={{0,128},{1,129},{2,130},{3,131},{4,132},{5,133},{6,134},{7,135},{8... | collective-permute-start | bytes 786440 | tf_op jit(solution)/shard_map/ppermute | solution.py:316
  33.4 32.9 %collective-permute-start.4 = (bf16[2,192,256]{2,1,0:T(8,128)(2,1)S(1)}, bf16[2,192,256]{2,1,0:T(8,128)(2,1)S(1)}, u32[]{:S(2)}, u32[]{:S(2)}) collective-permute-start(bf16[2,192,256]{2,1,0:T(8,128)(2,1)S(1)} %get-tuple-element.42), channel_id=1, source_target_pairs={{0,128},{1,129},{2,130},{3,131},{4,132},{5,133},{6,134},{7,135},{8... | collective-permute-start | bytes 589832 | tf_op jit(solution)/shard_map/ppermute | solution.py:316
  49.4 21.1 %collective-permute-start.5 = (bf16[2,192,256]{2,1,0:T(8,128)(2,1)S(1)}, bf16[2,192,256]{2,1,0:T(8,128)(2,1)S(1)}, u32[]{:S(2)}, u32[]{:S(2)}) collective-permute-start(bf16[2,192,256]{2,1,0:T(8,128)(2,1)S(1)} %get-tuple-element.43), channel_id=1, source_target_pairs={{0,128},{1,129},{2,130},{3,131},{4,132},{5,133},{6,134},{7,135},{8... | collective-permute-start | bytes 589832 | tf_op jit(solution)/shard_map/ppermute | solution.py:316
  54.4 26.4 %collective-permute-start.6 = (bf16[2,2,128,256]{3,2,1,0:T(8,128)(2,1)S(1)}, bf16[2,2,128,256]{3,2,1,0:T(8,128)(2,1)S(1)}, u32[]{:S(2)}, u32[]{:S(2)}) collective-permute-start(bf16[2,2,128,256]{3,2,1,0:T(8,128)(2,1)S(1)} %get-tuple-element.44), channel_id=1, source_target_pairs={{0,255},{1,128},{2,129},{3,130},{4,131},{5,132},{6,133},{7,134},{8... | collective-permute-start | bytes 786440 | tf_op jit(solution)/shard_map/ppermute | solution.py:316
  66.0 14.7 %collective-permute-start.7 = (bf16[2,2,128,256]{3,2,1,0:T(8,128)(2,1)S(1)}, bf16[2,2,128,256]{3,2,1,0:T(8,128)(2,1)S(1)}, u32[]{:S(2)}, u32[]{:S(2)}) collective-permute-start(bf16[2,2,128,256]{3,2,1,0:T(8,128)(2,1)S(1)} %get-tuple-element.45), channel_id=1, source_target_pairs={{0,127},{1,0},{2,1},{3,2},{4,3},{5,4},{6,5},{7,6},{8,7},{9,8},{10,... | collective-permute-start | bytes 786440 | tf_op jit(solution)/shard_map/ppermute | solution.py:316

commit v12 on v11

--- a/solution.py
+++ b/solution.py
@@ -82,6 +82,19 @@
     block = pltpu.roll(block, row_shift, 0)
     where = (channel, pl.ds(row_base, count + 8), pl.ds(col_base, WIDE))
     total_ref[where] = total_ref[where] + block
+
+
+def put_near(total_ref, channel, top, left, block, near):
+    row = pl.multiple_of(HALF + near, HALF)
+    col_base, col_shift = column_split(left)
+    shift = top - row
+    block = jnp.concatenate([block, jnp.zeros((HALF, WIDE - SIDE), F32)], axis=1)
+    block = pltpu.roll(block, col_shift, 1)
+    block = pltpu.roll(block, lax.rem(shift + 2 * HALF, HALF), 0)
+    line = lax.broadcasted_iota(jnp.int32, block.shape, 0)
+    kept = jnp.where((line >= shift) & (line < shift + HALF), block, 0.0)
+    where = (channel, pl.ds(row, HALF), pl.ds(col_base, WIDE))
+    total_ref[where] = total_ref[where] + kept
 
 
 def tagged(rows, cols, spots):
@@ -122,33 +135,39 @@
             late[where] = objects[channel, pl.ds(HALF - start, HALF), lanes].astype(BF)
 
 
-def cut_pair(rows, cols, objects, edge, lower, spots, outputs, near):
+def strip_window(rows, cols, objects, edge, lower, spot, output, near):
     start = pl.multiple_of(jnp.where(lower, BAND, 0), HALF)
     own = pl.multiple_of(jnp.where(lower, 0, HALF), HALF)
-    for channel in range(2):
-        for k in range(COLS // 128):
+    col_base, col_shift = column_split(cols[spot])
+    row_base, row_shift = row_split(rows[spot] + own, HALF + BAND - SIDE - 8)
+    count = SIDE + 8
+    for channel in range(2):
+        first = channel * COLS + col_base
+        for k in range(WIDE // 128):
             near[channel, pl.ds(start, HALF), 128 * k : 128 * (k + 1)] = edge[
-                pl.ds((channel * (COLS // 128) + k) * HALF, HALF)
+                pl.ds(pl.multiple_of(first + HALF * k, HALF), HALF)
             ].astype(F32)
-        near[channel, pl.ds(own, BAND)] = objects[channel]
-        for spot, output in zip(spots, outputs):
-            output[channel] = cut_window(
-                lambda r, c: near[channel, r, c], rows[spot] + own, cols[spot], SIDE, BAND + HALF
-            ).astype(BF)
-
-
-def mate_kernel(rows, cols, objects, early, window0, window1, near):
+        near[channel, pl.ds(own, BAND)] = objects[channel, :, pl.ds(col_base, WIDE)]
+        block = near[channel, pl.ds(row_base, count)]
+        block = pltpu.roll(block, lax.rem(count - row_shift, count), 0)[:SIDE]
+        block = pltpu.roll(block, lax.rem(WIDE - col_shift, WIDE), 1)[:, :SIDE]
+        output[channel] = block.astype(BF)
+
+
+def mate_kernel(rows, cols, objects, early, window, near):
     lower = lax.axis_index("cuts") == 0
     u0, u1, l0, l1 = places(rows)
-    spots = jnp.where(lower, l0, u0), jnp.where(lower, l1, u1)
-    cut_pair(rows, cols, objects, early, lower, spots, (window0, window1), near)
-
-
-def own_windows_kernel(rows, cols, objects, early, late, window0, window1, spots, near):
+    spot = jnp.where(lower, l0, u0)
+    strip_window(rows, cols, objects, early, lower, spot, window, near)
+
+
+def windows_kernel(rows, cols, objects, early, late, sent, own0, own1, spots, near):
     lower = lax.axis_index("cuts") == 1
     u0, u1, l0, l1 = places(rows)
-    mine = jnp.where(lower, l0, u0), jnp.where(lower, l1, u1)
-    cut_pair(rows, cols, objects, late, lower, mine, (window0, window1), near)
+    other = jnp.where(lower, u1, l1)
+    strip_window(rows, cols, objects, early, jnp.logical_not(lower), other, sent, near)
+    for spot, output in ((jnp.where(lower, l0, u0), own0), (jnp.where(lower, l1, u1), own1)):
+        strip_window(rows, cols, objects, late, lower, spot, output, near)
     decode(early, late, spots)
 
 
@@ -268,25 +287,40 @@
         put_inband(put, rows, cols, 0, inband, channel)
 
 
-def rest_kernel(
-    rows, cols, spots, given, inband, outers, edges, total, output, sems
-):
+def half_copy(total, output, channel, start, sem):
+    return pltpu.make_async_copy(
+        total.at[channel, pl.ds(pl.multiple_of(HALF + start, HALF), HALF)],
+        output.at[0, channel, pl.ds(pl.multiple_of(start, HALF), HALF)],
+        sem,
+    )
+
+
+def more_kernel(rows, cols, spots, given, inband, edges, total, output, sems):
     cut = lax.axis_index("cuts")
     shift = jnp.where(cut == 0, BAND, -HALF)
+    far = jnp.where(cut == 0, HALF, 0)
     copies = []
     for channel in range(2):
         put = functools.partial(put_window, total, channel)
         put_inband(put, rows, cols, 1, inband, channel)
-        for number in range(2):
-            k = 2 * number
-            put(spots[k] + shift, spots[k + 1], edges[number, channel].astype(F32))
-            top = spots[4 + k] + BAND - HALF - shift
-            put(top, spots[5 + k], outers[number, channel].astype(F32))
-        copies.append(
-            pltpu.make_async_copy(
-                total.at[channel, pl.ds(HALF, BAND)], output.at[0, channel], sems.at[channel]
-            )
-        )
+        for k in range(2):
+            put(spots[2 * k] + shift, spots[2 * k + 1], edges[k, channel].astype(F32))
+        copies.append(half_copy(total, output, channel, far, sems.at[channel]))
+        copies[channel].start()
+    for copy in copies:
+        copy.wait()
+
+
+def last_kernel(spots, given, outers, written, total, output, sems):
+    cut = lax.axis_index("cuts")
+    near = jnp.where(cut == 0, 0, HALF)
+    shift = jnp.where(cut == 0, -HALF, BAND)
+    copies = []
+    for channel in range(2):
+        for k in range(2):
+            top, left = spots[4 + 2 * k] + shift, spots[5 + 2 * k]
+            put_near(total, channel, top, left, outers[k, channel].astype(F32), near)
+        copies.append(half_copy(total, output, channel, near, sems.at[channel]))
         copies[channel].start()
     for copy in copies:
         copy.wait()
@@ -319,7 +353,7 @@
     half = arr(2, HALF, SIDE)
 
     full = arr(2, SIDE, SIDE)
-    near = pltpu.VMEM((2, BAND + HALF, COLS), F32)
+    near = pltpu.VMEM((2, BAND + HALF, WIDE), F32)
     early, late, band, rows, cols = call(
         edge_kernel, "edge",
         [pltpu.with_memory_space_constraint(x, pltpu.HBM) for x in (scan_rows, scan_cols, objects)],
@@ -330,13 +364,12 @@
     )
     early = move(early, "early")
     late = move(late, "late")
-    sent = call(mate_kernel, "mate", [rows, cols, band, early], [full, full], [near])
-    mate0 = move(sent[0], "mate")
-    own0, own1, spots = call(
-        own_windows_kernel, "windows", [rows, cols, band, early, late],
-        [full, full, arr(8, dtype=jnp.int32)], [near], out_specs=[VM, VM, SM],
-    )
-    sent1, own1 = lax.optimization_barrier((sent[1], own1))
+    (sent0,) = call(mate_kernel, "mate", [rows, cols, band, early], [full], [near])
+    mate0 = move(sent0, "mate")
+    sent1, own0, own1, spots = call(
+        windows_kernel, "windows", [rows, cols, band, early, late],
+        [full, full, full, arr(8, dtype=jnp.int32)], [near], out_specs=[VM, VM, VM, SM],
+    )
     mate1 = move(sent1, "mate")
     optics = [probes, amplitudes, wave, first, second]
     work = [pltpu.VMEM((2, 2, SIDE, SIDE), BF), pltpu.VMEM((2, 2, SIDE, SIDE), F32)]
@@ -360,12 +393,15 @@
         own_kernel, "own", [rows, cols, kept0, kept1, inband0],
         [arr(2, EXT, COLS, dtype=F32)], flops=10**11,
     )
+    results = [arr(2, EXT, COLS, dtype=F32), arr(1, 2, BAND, COLS, dtype=F32)]
+    total, written = call(
+        more_kernel, "more", [rows, cols, spots, total, inband1, edges], results,
+        [pltpu.SemaphoreType.DMA((2,))], out_specs=[VM, HB], aliases={3: 0}, flops=10**11,
+    )
     _, gradient = call(
-        rest_kernel, "rest", [rows, cols, spots, total, inband1, outers, edges],
-        [arr(2, EXT, COLS, dtype=F32), arr(1, 2, BAND, COLS, dtype=F32)],
+        last_kernel, "last", [spots, total, outers, written], results,
         [pltpu.SemaphoreType.DMA((2,))],
-        out_specs=[VM, HB],
-        aliases={3: 0},
+        in_specs=[SM, VM, VM, HB], out_specs=[VM, HB], aliases={1: 0, 3: 1},
     )
     return gradient
 

time: 83.8 us -> 83.5 us (level)
  waiting for transfers between devices: 29.4 us -> 27.1 us
  Pallas kernels: 20.8 us -> 22.9 us
    ppermute x8, waiting for transfers between devices: 29.4 us -> 27.1 us  [shards(): move = lambda x, way: lax.ppermute(x, AXES, route[way])]
    pallas_call x7 -> x8, Pallas kernels: 20.8 us -> 22.9 us  [call(): pl.pallas_call(kernel, name=name, out_shape=outputs, in_specs=in_specs or...]
  transfers between devices with their start and end apart: 8 -> 8, of which waited for: 4 -> 4; matrix products, arithmetic and copies ran while one was open for 1% -> 1% of each run, Pallas kernels for 19% -> 22%
where the time goes in v12:
time: 83.5 us; the launch traced here: 83.4 us
  starting transfers between devices  32.1 us (38%)
  waiting for transfers between devices  27.1 us (32%)
  Pallas kernels  22.9 us (27%)
  local copies, waits for them, and re-layouts  0.98 us (1%)
    ppermute x8, starting transfers between devices, shards(): move = lambda x, way: lax.ppermute(x, AXES, route[way])  32.1 us
    ppermute x8, waiting for transfers between devices, shards(): move = lambda x, way: lax.ppermute(x, AXES, route[way])  27.1 us
    pallas_call x8, Pallas kernels, call(): pl.pallas_call(kernel, name=name, out_shape=outputs, in_specs=in_specs or...  22.9 us
  transfers between devices with their start and end apart: 8, of which 4 were waited for; matrix products, arithmetic and copies ran while one was open for 1% of the time, Pallas kernels for 22%

profile of v12, /device:TPU:1, one launch (start us, length us, event | category | flops | bytes accessed | tf_op | source)
XLA Modules:
  0.0 83.4 jit_solution(18439964779352337101)
XLA Ops:
  0.0 2.2 %edge.1 = (bf16[2064,128]{1,0:T(8,128)(2,1)S(1)}, bf16[2064,128]{1,0:T(8,128)(2,1)S(1)}, f32[2,256,1024]{2,1,0:T(8,128)S(1)}, s32[4]{0:T(128)S(1)}, s32[4]{0:T(128)S(1)}) custom-call(s32[4]{0:T(128)} %rows_in.1, s32[4]{0:T(128)} %cols_in.1, f32[1,2,256,1024]{3,2,1,0:T(8,128)} %objects_in.1), custom_call_target="tpu_custom_call" | custom-call | flops 1 | bytes 1 | tf_op jit(solution)/shard_map/edge/pallas_call | solution.py:331
  2.2 3.3 %collective-permute-start = (bf16[2064,128]{1,0:T(8,128)(2,1)S(1)}, bf16[2064,128]{1,0:T(8,128)(2,1)S(1)}, u32[]{:S(2)}, u32[]{:S(2)}) collective-permute-start(bf16[2064,128]{1,0:T(8,128)(2,1)S(1)} %get-tuple-element.28), channel_id=1, source_target_pairs={{0,127},{1,0},{2,1},{3,2},{4,3},{5,4},{6,5},{7,6},{8,7},{9,8},{10,... | collective-permute-start | bytes 1585160 | tf_op jit(solution)/shard_map/ppermute | solution.py:350
  5.6 6.7 %collective-permute-done.early = bf16[2064,128]{1,0:T(8,128)(2,1)S(1)} collective-permute-done((bf16[2064,128]{1,0:T(8,128)(2,1)S(1)}, bf16[2064,128]{1,0:T(8,128)(2,1)S(1)}, u32[]{:S(2)}, u32[]{:S(2)}) %collective-permute-start) | collective-permute-done | bytes 528416 | tf_op jit(solution)/shard_map/ppermute | solution.py:350
  12.2 1.0 %mate.1 = bf16[2,256,256]{2,1,0:T(8,128)(2,1)S(1)} custom-call(s32[4]{0:T(128)S(1)} %get-tuple-element.25.rows, s32[4]{0:T(128)S(1)} %get-tuple-element.26.cols, f32[2,256,1024]{2,1,0:T(8,128)S(1)} %get-tuple-element.27.objects, bf16[2064,128]{1,0:T(8,128)(2,1)S(1)} %collective-permute-done.early), custom_call_target="tpu_custom_call" | custom-call | flops 1 | bytes 1 | tf_op jit(solution)/shard_map/mate/pallas_call | solution.py:331
  13.2 5.4 %collective-permute-start.2 = (bf16[2,256,256]{2,1,0:T(8,128)(2,1)S(1)}, bf16[2,256,256]{2,1,0:T(8,128)(2,1)S(1)}, u32[]{:S(2)}, u32[]{:S(2)}) collective-permute-start(bf16[2,256,256]{2,1,0:T(8,128)(2,1)S(1)} %mate.1), channel_id=1, source_target_pairs={{0,128},{1,129},{2,130},{3,131},{4,132},{5,133},{6,134},{7,135},{8... | collective-permute-start | bytes 786440 | tf_op jit(solution)/shard_map/ppermute | solution.py:350
  18.6 0.9 %cosine_bitcast_fusion = (f32[1,256,256]{2,1,0:T(8,128)S(1)}, f32[1,256,256]{2,1,0:T(8,128)S(1)}) fusion(f32[256,256]{1,0:T(8,128)S(1)} %copy-done.5), kind=kLoop, calls=%fused_computation.2 | loop fusion | bytes 786432 | tf_op jit(solution)/shard_map/stack | solution.py:352
  19.6 0.0 copy-start.1
  19.6 0.0 copy-start.2
  19.6 0.0 copy-start.3
  19.6 0.0 copy-start.4
  19.7 2.5 %windows.1 = (bf16[2,256,256]{2,1,0:T(8,128)(2,1)S(1)}, bf16[2,256,256]{2,1,0:T(8,128)(2,1)S(1)}, bf16[2,256,256]{2,1,0:T(8,128)(2,1)S(1)}, s32[8]{0:T(128)S(1)}) custom-call(s32[4]{0:T(128)S(1)} %get-tuple-element.25.rows, s32[4]{0:T(128)S(1)} %get-tuple-element.26.cols, f32[2,256,1024]{2,1,0:T(8,128)S(1)} %get-tuple-element.27.objects, ...), custom_call_target="tpu_custom_call" | custom-call | flops 1 | bytes 1 | tf_op jit(solution)/shard_map/windows/pallas_call | solution.py:331
  22.2 6.9 %collective-permute-start.3 = (bf16[2,256,256]{2,1,0:T(8,128)(2,1)S(1)}, bf16[2,256,256]{2,1,0:T(8,128)(2,1)S(1)}, u32[]{:S(2)}, u32[]{:S(2)}) collective-permute-start(bf16[2,256,256]{2,1,0:T(8,128)(2,1)S(1)} %get-tuple-element.34), channel_id=1, source_target_pairs={{0,128},{1,129},{2,130},{3,131},{4,132},{5,133},{6,134},{7,135},{8... | collective-permute-start | bytes 786440 | tf_op jit(solution)/shard_map/ppermute | solution.py:350
  29.1 4.8 %solo0.1 = (bf16[2,128,256]{2,1,0:T(8,128)(2,1)S(1)}, bf16[2,192,256]{2,1,0:T(8,128)(2,1)S(1)}, f32[2,256,256]{2,1,0:T(8,128)S(1)}, bf16[2,128,256]{2,1,0:T(8,128)(2,1)S(1)}) custom-call(s32[4]{0:T(128)S(1)} %get-tuple-element.25.rows, s32[4]{0:T(128)S(1)} %copy-done.2, bf16[2,256,256]{2,1,0:T(8,128)(2,1)S(1)} %get-tuple-element.31.own, ...), custom_call_target="tpu_custom_call" | custom-call | flops 99999997952 | bytes 1 | tf_op jit(solution)/shard_map/solo0/pallas_call | solution.py:331
  33.9 0.1 collective-permute-start.4
  34.0 10.5 %collective-permute-done.3.mate = bf16[2,256,256]{2,1,0:T(8,128)(2,1)S(1)} collective-permute-done((bf16[2,256,256]{2,1,0:T(8,128)(2,1)S(1)}, bf16[2,256,256]{2,1,0:T(8,128)(2,1)S(1)}, u32[]{:S(2)}, u32[]{:S(2)}) %collective-permute-start.3) | collective-permute-done | bytes 262176 | tf_op jit(solution)/shard_map/ppermute | solution.py:350
  44.5 5.6 %solo1.1 = (bf16[2,2,128,256]{3,2,1,0:T(8,128)(2,1)}, bf16[2,192,256]{2,1,0:T(8,128)(2,1)S(1)}, f32[2,256,256]{2,1,0:T(8,128)S(1)}, bf16[2,2,128,256]{3,2,1,0:T(8,128)(2,1)S(1)}) custom-call(s32[4]{0:T(128)S(1)} %get-tuple-element.25.rows, s32[4]{0:T(128)S(1)} %copy-done.2, bf16[2,256,256]{2,1,0:T(8,128)(2,1)S(1)} %get-tuple-element.33.own, ...), custom_call_target="tpu_custom_call" | custom-call | flops 99999997952 | bytes 1 | tf_op jit(solution)/shard_map/solo1/pallas_call | solution.py:331
  50.1 4.9 %collective-permute-start.5 = (bf16[2,192,256]{2,1,0:T(8,128)(2,1)S(1)}, bf16[2,192,256]{2,1,0:T(8,128)(2,1)S(1)}, u32[]{:S(2)}, u32[]{:S(2)}) collective-permute-start(bf16[2,192,256]{2,1,0:T(8,128)(2,1)S(1)} %get-tuple-element.39), channel_id=1, source_target_pairs={{0,128},{1,129},{2,130},{3,131},{4,132},{5,133},{6,134},{7,135},{8... | collective-permute-start | bytes 589832 | tf_op jit(solution)/shard_map/ppermute | solution.py:350
  55.0 8.0 %collective-permute-start.6 = (bf16[2,2,128,256]{3,2,1,0:T(8,128)(2,1)S(1)}, bf16[2,2,128,256]{3,2,1,0:T(8,128)(2,1)S(1)}, u32[]{:S(2)}, u32[]{:S(2)}) collective-permute-start(bf16[2,2,128,256]{3,2,1,0:T(8,128)(2,1)S(1)} %get-tuple-element.40), channel_id=1, source_target_pairs={{0,127},{1,0},{2,1},{3,2},{4,3},{5,4},{6,5},{7,6},{8,7},{9,8},{10,... | collective-permute-start | bytes 786440 | tf_op jit(solution)/shard_map/ppermute | solution.py:350
  63.0 3.5 %collective-permute-start.7 = (bf16[2,2,128,256]{3,2,1,0:T(8,128)(2,1)}, bf16[2,2,128,256]{3,2,1,0:T(8,128)(2,1)}, u32[]{:S(2)}, u32[]{:S(2)}) collective-permute-start(bf16[2,2,128,256]{3,2,1,0:T(8,128)(2,1)} %get-tuple-element.42), channel_id=1, source_target_pairs={{0,255},{1,128},{2,129},{3,130},{4,131},{5,132},{6,133},{7,134},{8... | collective-permute-start | bytes 786440 | tf_op jit(solution)/shard_map/ppermute | solution.py:350
  66.5 2.3 %own.1.given = f32[2,512,1024]{2,1,0:T(8,128)S(1)} custom-call(s32[4]{0:T(128)S(1)} %get-tuple-element.25.rows, s32[4]{0:T(128)S(1)} %get-tuple-element.26.cols, f32[2,256,256]{2,1,0:T(8,128)S(1)} %get-tuple-element.32.kept0, f32[2,256,256]{2,1,0:T(8,128)S(1)} %get-tuple-element.37.kept1, bf16[2,192,256]{2,1,0:T(8,128)(2,1)S(1)} %collective-permute-done.4.inband), custom_call_target="tpu_custom_call" | custom-call | flops 99999997952 | bytes 1 | tf_op jit(solution)/shard_map/own/pallas_call | solution.py:331
  68.8 1.8 %collective-permute-done.5.inband = bf16[2,192,256]{2,1,0:T(8,128)(2,1)S(1)} collective-permute-done((bf16[2,192,256]{2,1,0:T(8,128)(2,1)S(1)}, bf16[2,192,256]{2,1,0:T(8,128)(2,1)S(1)}, u32[]{:S(2)}, u32[]{:S(2)}) %collective-permute-start.5) | collective-permute-done | bytes 196640 | tf_op jit(solution)/shard_map/ppermute | solution.py:350
  70.6 2.2 %more.1 = (f32[2,512,1024]{2,1,0:T(8,128)S(1)}, f32[1,2,256,1024]{3,2,1,0:T(8,128)}) custom-call(s32[4]{0:T(128)S(1)} %get-tuple-element.25.rows, s32[4]{0:T(128)S(1)} %get-tuple-element.26.cols, s32[8]{0:T(128)S(1)} %get-tuple-element.30.spots, f32[2,512,1024]{2,1,0:T(8,128)S(1)} %own.1.given, ...), custom_call_target="tpu_custom_call", output_to_operand_aliasing={{0}: (3, {})} | custom-call | flops 99999997952 | bytes 1 | tf_op jit(solution)/shard_map/more/pallas_call | solution.py:331
  72.8 8.1 %collective-permute-done.7.outers = bf16[2,2,128,256]{3,2,1,0:T(8,128)(2,1)} collective-permute-done((bf16[2,2,128,256]{3,2,1,0:T(8,128)(2,1)}, bf16[2,2,128,256]{3,2,1,0:T(8,128)(2,1)}, u32[]{:S(2)}, u32[]{:S(2)}) %collective-permute-start.7) | collective-permute-done | bytes 262176 | tf_op jit(solution)/shard_map/ppermute | solution.py:350
  80.9 2.3 %last.1 = (f32[2,512,1024]{2,1,0:T(8,128)S(1)}, f32[1,2,256,1024]{3,2,1,0:T(8,128)}) custom-call(s32[8]{0:T(128)S(1)} %get-tuple-element.30.spots, f32[2,512,1024]{2,1,0:T(8,128)S(1)} %get-tuple-element.41.given, bf16[2,2,128,256]{3,2,1,0:T(8,128)(2,1)} %collective-permute-done.7.outers, ...), custom_call_target="tpu_custom_call", output_to_operand_aliasing={{0}: (1, {}), {1}: (3, {})} | custom-call | flops 1 | bytes 1 | tf_op jit(solution)/shard_map/last/pallas_call | solution.py:331
  (14 shorter events, 0.1 us)
Async XLA Ops:
  0.0 18.6 %copy-start.5 = (f32[256,256]{1,0:T(8,128)S(1)}, f32[256,256]{1,0:T(8,128)}, u32[]{:S(2)}) copy-start(f32[256,256]{1,0:T(8,128)} %param.12) | copy-start | bytes 786436
  2.2 10.0 %collective-permute-start = (bf16[2064,128]{1,0:T(8,128)(2,1)S(1)}, bf16[2064,128]{1,0:T(8,128)(2,1)S(1)}, u32[]{:S(2)}, u32[]{:S(2)}) collective-permute-start(bf16[2064,128]{1,0:T(8,128)(2,1)S(1)} %get-tuple-element.28), channel_id=1, source_target_pairs={{0,127},{1,0},{2,1},{3,2},{4,3},{5,4},{6,5},{7,6},{8,7},{9,8},{10,... | collective-permute-start | bytes 1585160 | tf_op jit(solution)/shard_map/ppermute | solution.py:350
  5.5 14.1 %collective-permute-start.1 = (bf16[2064,128]{1,0:T(8,128)(2,1)S(1)}, bf16[2064,128]{1,0:T(8,128)(2,1)S(1)}, u32[]{:S(2)}, u32[]{:S(2)}) collective-permute-start(bf16[2064,128]{1,0:T(8,128)(2,1)S(1)} %get-tuple-element.29), channel_id=1, source_target_pairs={{0,1},{1,2},{2,3},{3,4},{4,5},{5,6},{6,7},{7,8},{8,9},{9,10},{10,1... | collective-permute-start | bytes 1585160 | tf_op jit(solution)/shard_map/ppermute | solution.py:350
  13.2 15.8 %collective-permute-start.2 = (bf16[2,256,256]{2,1,0:T(8,128)(2,1)S(1)}, bf16[2,256,256]{2,1,0:T(8,128)(2,1)S(1)}, u32[]{:S(2)}, u32[]{:S(2)}) collective-permute-start(bf16[2,256,256]{2,1,0:T(8,128)(2,1)S(1)} %mate.1), channel_id=1, source_target_pairs={{0,128},{1,129},{2,130},{3,131},{4,132},{5,133},{6,134},{7,135},{8... | collective-permute-start | bytes 786440 | tf_op jit(solution)/shard_map/ppermute | solution.py:350
  19.6 9.5 %copy-start = (bf16[4,2,256,256]{3,2,1,0:T(8,128)(2,1)S(1)}, bf16[4,2,256,256]{3,2,1,0:T(8,128)(2,1)}, u32[]{:S(2)}) copy-start(bf16[4,2,256,256]{3,2,1,0:T(8,128)(2,1)} %probes.3) | copy-start | bytes 3145732
  19.6 9.5 %copy-start.1 = (f32[4,256,256]{2,1,0:T(8,128)S(1)}, f32[4,256,256]{2,1,0:T(8,128)}, u32[]{:S(2)}) copy-start(f32[4,256,256]{2,1,0:T(8,128)} %amplitudes.3) | copy-start | bytes 3145732
  19.6 9.5 %copy-start.2 = (s32[4]{0:T(128)S(1)}, s32[4]{0:T(128)}, u32[]{:S(2)}) copy-start(s32[4]{0:T(128)} %picks.3) | copy-start | bytes 52
  19.6 9.5 %copy-start.3 = (bf16[512,512]{1,0:T(8,128)(2,1)S(1)}, bf16[512,512]{1,0:T(8,128)(2,1)}, u32[]{:S(2)}) copy-start(bf16[512,512]{1,0:T(8,128)(2,1)} %constant.5.clone.second) | copy-start | bytes 1572868
  19.6 9.5 %copy-start.4 = (bf16[512,512]{1,0:T(8,128)(2,1)S(1)}, bf16[512,512]{1,0:T(8,128)(2,1)}, u32[]{:S(2)}) copy-start(bf16[512,512]{1,0:T(8,128)(2,1)} %constant.4.clone.first) | copy-start | bytes 1572868
  22.2 22.4 %collective-permute-start.3 = (bf16[2,256,256]{2,1,0:T(8,128)(2,1)S(1)}, bf16[2,256,256]{2,1,0:T(8,128)(2,1)S(1)}, u32[]{:S(2)}, u32[]{:S(2)}) collective-permute-start(bf16[2,256,256]{2,1,0:T(8,128)(2,1)S(1)} %get-tuple-element.34), channel_id=1, source_target_pairs={{0,128},{1,129},{2,130},{3,131},{4,132},{5,133},{6,134},{7,135},{8... | collective-permute-start | bytes 786440 | tf_op jit(solution)/shard_map/ppermute | solution.py:350
  33.9 32.6 %collective-permute-start.4 = (bf16[2,192,256]{2,1,0:T(8,128)(2,1)S(1)}, bf16[2,192,256]{2,1,0:T(8,128)(2,1)S(1)}, u32[]{:S(2)}, u32[]{:S(2)}) collective-permute-start(bf16[2,192,256]{2,1,0:T(8,128)(2,1)S(1)} %get-tuple-element.38), channel_id=1, source_target_pairs={{0,128},{1,129},{2,130},{3,131},{4,132},{5,133},{6,134},{7,135},{8... | collective-permute-start | bytes 589832 | tf_op jit(solution)/shard_map/ppermute | solution.py:350
  50.1 20.5 %collective-permute-start.5 = (bf16[2,192,256]{2,1,0:T(8,128)(2,1)S(1)}, bf16[2,192,256]{2,1,0:T(8,128)(2,1)S(1)}, u32[]{:S(2)}, u32[]{:S(2)}) collective-permute-start(bf16[2,192,256]{2,1,0:T(8,128)(2,1)S(1)} %get-tuple-element.39), channel_id=1, source_target_pairs={{0,128},{1,129},{2,130},{3,131},{4,132},{5,133},{6,134},{7,135},{8... | collective-permute-start | bytes 589832 | tf_op jit(solution)/shard_map/ppermute | solution.py:350
  55.0 15.6 %collective-permute-start.6 = (bf16[2,2,128,256]{3,2,1,0:T(8,128)(2,1)S(1)}, bf16[2,2,128,256]{3,2,1,0:T(8,128)(2,1)S(1)}, u32[]{:S(2)}, u32[]{:S(2)}) collective-permute-start(bf16[2,2,128,256]{3,2,1,0:T(8,128)(2,1)S(1)} %get-tuple-element.40), channel_id=1, source_target_pairs={{0,127},{1,0},{2,1},{3,2},{4,3},{5,4},{6,5},{7,6},{8,7},{9,8},{10,... | collective-permute-start | bytes 786440 | tf_op jit(solution)/shard_map/ppermute | solution.py:350
  63.0 17.9 %collective-permute-start.7 = (bf16[2,2,128,256]{3,2,1,0:T(8,128)(2,1)}, bf16[2,2,128,256]{3,2,1,0:T(8,128)(2,1)}, u32[]{:S(2)}, u32[]{:S(2)}) collective-permute-start(bf16[2,2,128,256]{3,2,1,0:T(8,128)(2,1)} %get-tuple-element.42), channel_id=1, source_target_pairs={{0,255},{1,128},{2,129},{3,130},{4,131},{5,132},{6,133},{7,134},{8... | collective-permute-start | bytes 786440 | tf_op jit(solution)/shard_map/ppermute | solution.py:350

commit v13 on v12

--- a/solution.py
+++ b/solution.py
@@ -238,10 +238,9 @@
     if number == 0:
         sent_outer, sent_inband, kept, edges, held, made = refs
     else:
-        outer_before, edge_before, outers, sent_inband, kept, both, held, made = refs
-        outers[0] = outer_before[...]
+        edge_before, sent_outer, sent_inband, kept, both, held, made = refs
         both[0] = edge_before[...]
-        sent_outer, edges = outers.at[1], both.at[1]
+        edges = both.at[1]
     cut = lax.axis_index("cuts")
     spots = places(rows)
     place = jnp.where(cut == 0, spots[number], spots[2 + number])
@@ -275,7 +274,7 @@
     put(rows[spot] + HALF + skip, cols[spot], inband[channel].astype(F32))
 
 
-def own_kernel(rows, cols, kept0, kept1, inband, total):
+def own_kernel(rows, cols, spots, kept0, kept1, inband, outer, total):
     cut = lax.axis_index("cuts")
     places_here = places(rows)
     total[...] = jnp.zeros_like(total)
@@ -285,6 +284,8 @@
             spot = jnp.where(cut == 0, places_here[number], places_here[2 + number])
             put(rows[spot] + HALF, cols[spot], kept[channel])
         put_inband(put, rows, cols, 0, inband, channel)
+        shift = jnp.where(cut == 0, -HALF, BAND)
+        put(spots[4] + shift, spots[5], outer[channel].astype(F32))
 
 
 def half_copy(total, output, channel, start, sem):
@@ -311,15 +312,13 @@
         copy.wait()
 
 
-def last_kernel(spots, given, outers, written, total, output, sems):
+def last_kernel(spots, given, outer, written, total, output, sems):
     cut = lax.axis_index("cuts")
     near = jnp.where(cut == 0, 0, HALF)
     shift = jnp.where(cut == 0, -HALF, BAND)
     copies = []
     for channel in range(2):
-        for k in range(2):
-            top, left = spots[4 + 2 * k] + shift, spots[5 + 2 * k]
-            put_near(total, channel, top, left, outers[k, channel].astype(F32), near)
+        put_near(total, channel, spots[6] + shift, spots[7], outer[channel].astype(F32), near)
         copies.append(half_copy(total, output, channel, near, sems.at[channel]))
         copies[channel].start()
     for copy in copies:
@@ -381,16 +380,17 @@
         [half, inner, wide_full, half], work, flops=10**11,
     )
     inband0 = move(inband0, "mate")
-    outers, inband1, kept1, edges = call(
+    outer0 = move(outer0, "direct")
+    outer1, inband1, kept1, edges = call(
         functools.partial(solo_kernel, 1), "solo1",
-        [rows, probe_choice, own1, mate1] + optics + [outer0, edge0],
-        [pair, inner, wide_full, pair], work, flops=10**11,
+        [rows, probe_choice, own1, mate1] + optics + [edge0],
+        [half, inner, wide_full, pair], work, flops=10**11,
     )
     inband1 = move(inband1, "mate")
-    outers = move(outers, "direct")
+    outer1 = move(outer1, "direct")
     edges = move(edges, "early")
     (total,) = call(
-        own_kernel, "own", [rows, cols, kept0, kept1, inband0],
+        own_kernel, "own", [rows, cols, spots, kept0, kept1, inband0, outer0],
         [arr(2, EXT, COLS, dtype=F32)], flops=10**11,
     )
     results = [arr(2, EXT, COLS, dtype=F32), arr(1, 2, BAND, COLS, dtype=F32)]
@@ -399,7 +399,7 @@
         [pltpu.SemaphoreType.DMA((2,))], out_specs=[VM, HB], aliases={3: 0}, flops=10**11,
     )
     _, gradient = call(
-        last_kernel, "last", [spots, total, outers, written], results,
+        last_kernel, "last", [spots, total, outer1, written], results,
         [pltpu.SemaphoreType.DMA((2,))],
         in_specs=[SM, VM, VM, HB], out_specs=[VM, HB], aliases={1: 0, 3: 1},
     )

time: 83.5 us -> 85.7 us (1.026)
  the two profiles are of different devices: /device:TPU:1 before, /device:TPU:8 now
where the time goes in v13:
time: 85.7 us; the launch traced here: 85.5 us
  starting transfers between devices  36.7 us (43%)
  waiting for transfers between devices  24.7 us (29%)
  Pallas kernels  22.8 us (27%)
  local copies, waits for them, and re-layouts  0.98 us (1%)
    ppermute x9, starting transfers between devices, shards(): move = lambda x, way: lax.ppermute(x, AXES, route[way])  36.7 us
    ppermute x9, waiting for transfers between devices, shards(): move = lambda x, way: lax.ppermute(x, AXES, route[way])  24.7 us
    pallas_call x8, Pallas kernels, call(): pl.pallas_call(kernel, name=name, out_shape=outputs, in_specs=in_specs or...  22.8 us
  transfers between devices with their start and end apart: 9, of which 3 were waited for; matrix products, arithmetic and copies ran while one was open for 1% of the time, Pallas kernels for 22%

profile of v13, /device:TPU:8, one launch (start us, length us, event | category | flops | bytes accessed | tf_op | source)
XLA Modules:
  0.0 85.5 jit_solution(3341909169235191916)
XLA Ops:
  0.0 2.2 %edge.1 = (bf16[2064,128]{1,0:T(8,128)(2,1)S(1)}, bf16[2064,128]{1,0:T(8,128)(2,1)S(1)}, f32[2,256,1024]{2,1,0:T(8,128)S(1)}, s32[4]{0:T(128)S(1)}, s32[4]{0:T(128)S(1)}) custom-call(s32[4]{0:T(128)} %rows_in.1, s32[4]{0:T(128)} %cols_in.1, f32[1,2,256,1024]{3,2,1,0:T(8,128)} %objects_in.1), custom_call_target="tpu_custom_call" | custom-call | flops 1 | bytes 1 | tf_op jit(solution)/shard_map/edge/pallas_call | solution.py:330
  2.2 6.2 %collective-permute-start = (bf16[2064,128]{1,0:T(8,128)(2,1)S(1)}, bf16[2064,128]{1,0:T(8,128)(2,1)S(1)}, u32[]{:S(2)}, u32[]{:S(2)}) collective-permute-start(bf16[2064,128]{1,0:T(8,128)(2,1)S(1)} %get-tuple-element.28), channel_id=1, source_target_pairs={{0,127},{1,0},{2,1},{3,2},{4,3},{5,4},{6,5},{7,6},{8,7},{9,8},{10,... | collective-permute-start | bytes 1585160 | tf_op jit(solution)/shard_map/ppermute | solution.py:349
  8.5 7.7 %collective-permute-done.early = bf16[2064,128]{1,0:T(8,128)(2,1)S(1)} collective-permute-done((bf16[2064,128]{1,0:T(8,128)(2,1)S(1)}, bf16[2064,128]{1,0:T(8,128)(2,1)S(1)}, u32[]{:S(2)}, u32[]{:S(2)}) %collective-permute-start) | collective-permute-done | bytes 528416 | tf_op jit(solution)/shard_map/ppermute | solution.py:349
  16.2 1.0 %mate.1 = bf16[2,256,256]{2,1,0:T(8,128)(2,1)S(1)} custom-call(s32[4]{0:T(128)S(1)} %get-tuple-element.25.rows, s32[4]{0:T(128)S(1)} %get-tuple-element.26.cols, f32[2,256,1024]{2,1,0:T(8,128)S(1)} %get-tuple-element.27.objects, bf16[2064,128]{1,0:T(8,128)(2,1)S(1)} %collective-permute-done.early), custom_call_target="tpu_custom_call" | custom-call | flops 1 | bytes 1 | tf_op jit(solution)/shard_map/mate/pallas_call | solution.py:330
  17.2 15.5 %collective-permute-start.2 = (bf16[2,256,256]{2,1,0:T(8,128)(2,1)S(1)}, bf16[2,256,256]{2,1,0:T(8,128)(2,1)S(1)}, u32[]{:S(2)}, u32[]{:S(2)}) collective-permute-start(bf16[2,256,256]{2,1,0:T(8,128)(2,1)S(1)} %mate.1), channel_id=1, source_target_pairs={{0,128},{1,129},{2,130},{3,131},{4,132},{5,133},{6,134},{7,135},{8... | collective-permute-start | bytes 786440 | tf_op jit(solution)/shard_map/ppermute | solution.py:349
  32.7 0.9 %cosine_bitcast_fusion = (f32[1,256,256]{2,1,0:T(8,128)S(1)}, f32[1,256,256]{2,1,0:T(8,128)S(1)}) fusion(f32[256,256]{1,0:T(8,128)S(1)} %copy-done.5), kind=kLoop, calls=%fused_computation.2 | loop fusion | bytes 786432 | tf_op jit(solution)/shard_map/stack | solution.py:351
  33.6 0.0 copy-start.1
  33.6 0.0 copy-start.2
  33.6 0.0 copy-start.3
  33.7 0.0 copy-start.4
  33.7 2.5 %windows.1 = (bf16[2,256,256]{2,1,0:T(8,128)(2,1)S(1)}, bf16[2,256,256]{2,1,0:T(8,128)(2,1)S(1)}, bf16[2,256,256]{2,1,0:T(8,128)(2,1)S(1)}, s32[8]{0:T(128)S(1)}) custom-call(s32[4]{0:T(128)S(1)} %get-tuple-element.25.rows, s32[4]{0:T(128)S(1)} %get-tuple-element.26.cols, f32[2,256,1024]{2,1,0:T(8,128)S(1)} %get-tuple-element.27.objects, ...), custom_call_target="tpu_custom_call" | custom-call | flops 1 | bytes 1 | tf_op jit(solution)/shard_map/windows/pallas_call | solution.py:330
  36.2 0.5 collective-permute-start.3
  36.7 6.3 %collective-permute-done.2.mate = bf16[2,256,256]{2,1,0:T(8,128)(2,1)S(1)} collective-permute-done((bf16[2,256,256]{2,1,0:T(8,128)(2,1)S(1)}, bf16[2,256,256]{2,1,0:T(8,128)(2,1)S(1)}, u32[]{:S(2)}, u32[]{:S(2)}) %collective-permute-start.2) | collective-permute-done | bytes 262176 | tf_op jit(solution)/shard_map/ppermute | solution.py:349
  43.0 4.8 %solo0.1 = (bf16[2,128,256]{2,1,0:T(8,128)(2,1)S(1)}, bf16[2,192,256]{2,1,0:T(8,128)(2,1)S(1)}, f32[2,256,256]{2,1,0:T(8,128)S(1)}, bf16[2,128,256]{2,1,0:T(8,128)(2,1)S(1)}) custom-call(s32[4]{0:T(128)S(1)} %get-tuple-element.25.rows, s32[4]{0:T(128)S(1)} %copy-done.2, bf16[2,256,256]{2,1,0:T(8,128)(2,1)S(1)} %get-tuple-element.31.own, ...), custom_call_target="tpu_custom_call" | custom-call | flops 99999997952 | bytes 1 | tf_op jit(solution)/shard_map/solo0/pallas_call | solution.py:330
  47.9 3.7 %collective-permute-start.5 = (bf16[2,128,256]{2,1,0:T(8,128)(2,1)S(1)}, bf16[2,128,256]{2,1,0:T(8,128)(2,1)S(1)}, u32[]{:S(2)}, u32[]{:S(2)}) collective-permute-start(bf16[2,128,256]{2,1,0:T(8,128)(2,1)S(1)} %get-tuple-element.38), channel_id=1, source_target_pairs={{0,255},{1,128},{2,129},{3,130},{4,131},{5,132},{6,133},{7,134},{8... | collective-permute-start | bytes 393224 | tf_op jit(solution)/shard_map/ppermute | solution.py:349
  51.6 1.9 %collective-permute-start.4 = (bf16[2,192,256]{2,1,0:T(8,128)(2,1)S(1)}, bf16[2,192,256]{2,1,0:T(8,128)(2,1)S(1)}, u32[]{:S(2)}, u32[]{:S(2)}) collective-permute-start(bf16[2,192,256]{2,1,0:T(8,128)(2,1)S(1)} %get-tuple-element.37), channel_id=1, source_target_pairs={{0,128},{1,129},{2,130},{3,131},{4,132},{5,133},{6,134},{7,135},{8... | collective-permute-start | bytes 589832 | tf_op jit(solution)/shard_map/ppermute | solution.py:349
  53.5 5.5 %solo1.1 = (bf16[2,128,256]{2,1,0:T(8,128)(2,1)}, bf16[2,192,256]{2,1,0:T(8,128)(2,1)S(1)}, f32[2,256,256]{2,1,0:T(8,128)S(1)}, bf16[2,2,128,256]{3,2,1,0:T(8,128)(2,1)S(1)}) custom-call(s32[4]{0:T(128)S(1)} %get-tuple-element.25.rows, s32[4]{0:T(128)S(1)} %copy-done.2, bf16[2,256,256]{2,1,0:T(8,128)(2,1)S(1)} %get-tuple-element.33.own, ...), custom_call_target="tpu_custom_call" | custom-call | flops 99999997952 | bytes 1 | tf_op jit(solution)/shard_map/solo1/pallas_call | solution.py:330
  59.0 0.4 collective-permute-start.8
  59.4 4.9 %collective-permute-start.6 = (bf16[2,192,256]{2,1,0:T(8,128)(2,1)S(1)}, bf16[2,192,256]{2,1,0:T(8,128)(2,1)S(1)}, u32[]{:S(2)}, u32[]{:S(2)}) collective-permute-start(bf16[2,192,256]{2,1,0:T(8,128)(2,1)S(1)} %get-tuple-element.39), channel_id=1, source_target_pairs={{0,128},{1,129},{2,130},{3,131},{4,132},{5,133},{6,134},{7,135},{8... | collective-permute-start | bytes 589832 | tf_op jit(solution)/shard_map/ppermute | solution.py:349
  64.4 3.6 %collective-permute-start.7 = (bf16[2,2,128,256]{3,2,1,0:T(8,128)(2,1)S(1)}, bf16[2,2,128,256]{3,2,1,0:T(8,128)(2,1)S(1)}, u32[]{:S(2)}, u32[]{:S(2)}) collective-permute-start(bf16[2,2,128,256]{3,2,1,0:T(8,128)(2,1)S(1)} %get-tuple-element.40), channel_id=1, source_target_pairs={{0,127},{1,0},{2,1},{3,2},{4,3},{5,4},{6,5},{7,6},{8,7},{9,8},{10,... | collective-permute-start | bytes 786440 | tf_op jit(solution)/shard_map/ppermute | solution.py:349
  68.0 2.5 %own.1.given = f32[2,512,1024]{2,1,0:T(8,128)S(1)} custom-call(s32[4]{0:T(128)S(1)} %get-tuple-element.25.rows, s32[4]{0:T(128)S(1)} %get-tuple-element.26.cols, s32[8]{0:T(128)S(1)} %get-tuple-element.30.spots, f32[2,256,256]{2,1,0:T(8,128)S(1)} %get-tuple-element.32.kept0, f32[2,256,256]{2,1,0:T(8,128)S(1)} %get-tuple-element.36.kept1, ...), custom_call_target="tpu_custom_call" | custom-call | flops 99999997952 | bytes 1 | tf_op jit(solution)/shard_map/own/pallas_call | solution.py:330
  70.4 10.6 %collective-permute-done.6.inband = bf16[2,192,256]{2,1,0:T(8,128)(2,1)S(1)} collective-permute-done((bf16[2,192,256]{2,1,0:T(8,128)(2,1)S(1)}, bf16[2,192,256]{2,1,0:T(8,128)(2,1)S(1)}, u32[]{:S(2)}, u32[]{:S(2)}) %collective-permute-start.6) | collective-permute-done | bytes 196640 | tf_op jit(solution)/shard_map/ppermute | solution.py:349
  81.1 2.2 %more.1 = (f32[2,512,1024]{2,1,0:T(8,128)S(1)}, f32[1,2,256,1024]{3,2,1,0:T(8,128)}) custom-call(s32[4]{0:T(128)S(1)} %get-tuple-element.25.rows, s32[4]{0:T(128)S(1)} %get-tuple-element.26.cols, s32[8]{0:T(128)S(1)} %get-tuple-element.30.spots, f32[2,512,1024]{2,1,0:T(8,128)S(1)} %own.1.given, ...), custom_call_target="tpu_custom_call", output_to_operand_aliasing={{0}: (3, {})} | custom-call | flops 99999997952 | bytes 1 | tf_op jit(solution)/shard_map/more/pallas_call | solution.py:330
  83.3 2.1 %last.1 = (f32[2,512,1024]{2,1,0:T(8,128)S(1)}, f32[1,2,256,1024]{3,2,1,0:T(8,128)}) custom-call(s32[8]{0:T(128)S(1)} %get-tuple-element.30.spots, f32[2,512,1024]{2,1,0:T(8,128)S(1)} %get-tuple-element.41.given, bf16[2,128,256]{2,1,0:T(8,128)(2,1)} %collective-permute-done.8.outer, ...), custom_call_target="tpu_custom_call", output_to_operand_aliasing={{0}: (1, {}), {1}: (3, {})} | custom-call | flops 1 | bytes 1 | tf_op jit(solution)/shard_map/last/pallas_call | solution.py:330
  (16 shorter events, 0.1 us)
Async XLA Ops:
  0.0 32.7 %copy-start.5 = (f32[256,256]{1,0:T(8,128)S(1)}, f32[256,256]{1,0:T(8,128)}, u32[]{:S(2)}) copy-start(f32[256,256]{1,0:T(8,128)} %param.12) | copy-start | bytes 786436
  2.2 14.0 %collective-permute-start = (bf16[2064,128]{1,0:T(8,128)(2,1)S(1)}, bf16[2064,128]{1,0:T(8,128)(2,1)S(1)}, u32[]{:S(2)}, u32[]{:S(2)}) collective-permute-start(bf16[2064,128]{1,0:T(8,128)(2,1)S(1)} %get-tuple-element.28), channel_id=1, source_target_pairs={{0,127},{1,0},{2,1},{3,2},{4,3},{5,4},{6,5},{7,6},{8,7},{9,8},{10,... | collective-permute-start | bytes 1585160 | tf_op jit(solution)/shard_map/ppermute | solution.py:349
  8.5 25.3 %collective-permute-start.1 = (bf16[2064,128]{1,0:T(8,128)(2,1)S(1)}, bf16[2064,128]{1,0:T(8,128)(2,1)S(1)}, u32[]{:S(2)}, u32[]{:S(2)}) collective-permute-start(bf16[2064,128]{1,0:T(8,128)(2,1)S(1)} %get-tuple-element.29), channel_id=1, source_target_pairs={{0,1},{1,2},{2,3},{3,4},{4,5},{5,6},{6,7},{7,8},{8,9},{9,10},{10,1... | collective-permute-start | bytes 1585160 | tf_op jit(solution)/shard_map/ppermute | solution.py:349
  17.2 25.8 %collective-permute-start.2 = (bf16[2,256,256]{2,1,0:T(8,128)(2,1)S(1)}, bf16[2,256,256]{2,1,0:T(8,128)(2,1)S(1)}, u32[]{:S(2)}, u32[]{:S(2)}) collective-permute-start(bf16[2,256,256]{2,1,0:T(8,128)(2,1)S(1)} %mate.1), channel_id=1, source_target_pairs={{0,128},{1,129},{2,130},{3,131},{4,132},{5,133},{6,134},{7,135},{8... | collective-permute-start | bytes 786440 | tf_op jit(solution)/shard_map/ppermute | solution.py:349
  33.6 9.4 %copy-start = (bf16[4,2,256,256]{3,2,1,0:T(8,128)(2,1)S(1)}, bf16[4,2,256,256]{3,2,1,0:T(8,128)(2,1)}, u32[]{:S(2)}) copy-start(bf16[4,2,256,256]{3,2,1,0:T(8,128)(2,1)} %probes.3) | copy-start | bytes 3145732
  33.6 9.4 %copy-start.1 = (f32[4,256,256]{2,1,0:T(8,128)S(1)}, f32[4,256,256]{2,1,0:T(8,128)}, u32[]{:S(2)}) copy-start(f32[4,256,256]{2,1,0:T(8,128)} %amplitudes.3) | copy-start | bytes 3145732
  33.6 9.4 %copy-start.2 = (s32[4]{0:T(128)S(1)}, s32[4]{0:T(128)}, u32[]{:S(2)}) copy-start(s32[4]{0:T(128)} %picks.3) | copy-start | bytes 52
  33.6 9.4 %copy-start.3 = (bf16[512,512]{1,0:T(8,128)(2,1)S(1)}, bf16[512,512]{1,0:T(8,128)(2,1)}, u32[]{:S(2)}) copy-start(bf16[512,512]{1,0:T(8,128)(2,1)} %constant.5.clone.second) | copy-start | bytes 1572868
  33.7 9.4 %copy-start.4 = (bf16[512,512]{1,0:T(8,128)(2,1)S(1)}, bf16[512,512]{1,0:T(8,128)(2,1)}, u32[]{:S(2)}) copy-start(bf16[512,512]{1,0:T(8,128)(2,1)} %constant.4.clone.first) | copy-start | bytes 1572868
  36.2 17.3 %collective-permute-start.3 = (bf16[2,256,256]{2,1,0:T(8,128)(2,1)S(1)}, bf16[2,256,256]{2,1,0:T(8,128)(2,1)S(1)}, u32[]{:S(2)}, u32[]{:S(2)}) collective-permute-start(bf16[2,256,256]{2,1,0:T(8,128)(2,1)S(1)} %get-tuple-element.34), channel_id=1, source_target_pairs={{0,128},{1,129},{2,130},{3,131},{4,132},{5,133},{6,134},{7,135},{8... | collective-permute-start | bytes 786440 | tf_op jit(solution)/shard_map/ppermute | solution.py:349
  47.9 20.1 %collective-permute-start.5 = (bf16[2,128,256]{2,1,0:T(8,128)(2,1)S(1)}, bf16[2,128,256]{2,1,0:T(8,128)(2,1)S(1)}, u32[]{:S(2)}, u32[]{:S(2)}) collective-permute-start(bf16[2,128,256]{2,1,0:T(8,128)(2,1)S(1)} %get-tuple-element.38), channel_id=1, source_target_pairs={{0,255},{1,128},{2,129},{3,130},{4,131},{5,132},{6,133},{7,134},{8... | collective-permute-start | bytes 393224 | tf_op jit(solution)/shard_map/ppermute | solution.py:349
  51.6 16.3 %collective-permute-start.4 = (bf16[2,192,256]{2,1,0:T(8,128)(2,1)S(1)}, bf16[2,192,256]{2,1,0:T(8,128)(2,1)S(1)}, u32[]{:S(2)}, u32[]{:S(2)}) collective-permute-start(bf16[2,192,256]{2,1,0:T(8,128)(2,1)S(1)} %get-tuple-element.37), channel_id=1, source_target_pairs={{0,128},{1,129},{2,130},{3,131},{4,132},{5,133},{6,134},{7,135},{8... | collective-permute-start | bytes 589832 | tf_op jit(solution)/shard_map/ppermute | solution.py:349
  59.0 24.3 %collective-permute-start.8 = (bf16[2,128,256]{2,1,0:T(8,128)(2,1)}, bf16[2,128,256]{2,1,0:T(8,128)(2,1)}, u32[]{:S(2)}, u32[]{:S(2)}) collective-permute-start(bf16[2,128,256]{2,1,0:T(8,128)(2,1)} %get-tuple-element.42), channel_id=1, source_target_pairs={{0,255},{1,128},{2,129},{3,130},{4,131},{5,132},{6,133},{7,134},{8... | collective-permute-start | bytes 393224 | tf_op jit(solution)/shard_map/ppermute | solution.py:349
  59.4 21.6 %collective-permute-start.6 = (bf16[2,192,256]{2,1,0:T(8,128)(2,1)S(1)}, bf16[2,192,256]{2,1,0:T(8,128)(2,1)S(1)}, u32[]{:S(2)}, u32[]{:S(2)}) collective-permute-start(bf16[2,192,256]{2,1,0:T(8,128)(2,1)S(1)} %get-tuple-element.39), channel_id=1, source_target_pairs={{0,128},{1,129},{2,130},{3,131},{4,132},{5,133},{6,134},{7,135},{8... | collective-permute-start | bytes 589832 | tf_op jit(solution)/shard_map/ppermute | solution.py:349
  64.4 16.7 %collective-permute-start.7 = (bf16[2,2,128,256]{3,2,1,0:T(8,128)(2,1)S(1)}, bf16[2,2,128,256]{3,2,1,0:T(8,128)(2,1)S(1)}, u32[]{:S(2)}, u32[]{:S(2)}) collective-permute-start(bf16[2,2,128,256]{3,2,1,0:T(8,128)(2,1)S(1)} %get-tuple-element.40), channel_id=1, source_target_pairs={{0,127},{1,0},{2,1},{3,2},{4,3},{5,4},{6,5},{7,6},{8,7},{9,8},{10,... | collective-permute-start | bytes 786440 | tf_op jit(solution)/shard_map/ppermute | solution.py:349

commit v14 on v12

--- a/solution.py
+++ b/solution.py
@@ -365,6 +365,7 @@
     early = move(early, "early")
     late = move(late, "late")
     (sent0,) = call(mate_kernel, "mate", [rows, cols, band, early], [full], [near])
+    sent0, late = lax.optimization_barrier((sent0, late))
     mate0 = move(sent0, "mate")
     sent1, own0, own1, spots = call(
         windows_kernel, "windows", [rows, cols, band, early, late],

time: 83.5 us -> 86.3 us (1.034)
  starting transfers between devices: 32.1 us -> 42.6 us
  waiting for transfers between devices: 27.1 us -> 19.4 us
    ppermute x8, starting transfers between devices: 32.1 us -> 42.6 us  [shards(): move = lambda x, way: lax.ppermute(x, AXES, route[way])]
    ppermute x8, waiting for transfers between devices: 27.1 us -> 19.4 us  [shards(): move = lambda x, way: lax.ppermute(x, AXES, route[way])]
  transfers between devices with their start and end apart: 8 -> 8, of which waited for: 4 -> 5; matrix products, arithmetic and copies ran while one was open for 1% -> 1% of each run, Pallas kernels for 22% -> 21%
where the time goes in v14:
time: 86.3 us; the launch traced here: 86.2 us
  starting transfers between devices  42.6 us (49%)
  Pallas kernels  22.9 us (27%)
  waiting for transfers between devices  19.4 us (22%)
  local copies, waits for them, and re-layouts  0.98 us (1%)
    ppermute x8, starting transfers between devices, shards(): move = lambda x, way: lax.ppermute(x, AXES, route[way])  42.6 us
    pallas_call x8, Pallas kernels, call(): pl.pallas_call(kernel, name=name, out_shape=outputs, in_specs=in_specs or...  22.9 us
    ppermute x8, waiting for transfers between devices, shards(): move = lambda x, way: lax.ppermute(x, AXES, route[way])  19.4 us
  transfers between devices with their start and end apart: 8, of which 5 were waited for; matrix products, arithmetic and copies ran while one was open for 1% of the time, Pallas kernels for 21%

profile of v14, /device:TPU:1, one launch (start us, length us, event | category | flops | bytes accessed | tf_op | source)
XLA Modules:
  0.0 86.2 jit_solution(6959940946794471757)
XLA Ops:
  0.0 2.2 %edge.1 = (bf16[2064,128]{1,0:T(8,128)(2,1)S(1)}, bf16[2064,128]{1,0:T(8,128)(2,1)S(1)}, f32[2,256,1024]{2,1,0:T(8,128)S(1)}, s32[4]{0:T(128)S(1)}, s32[4]{0:T(128)S(1)}) custom-call(s32[4]{0:T(128)} %rows_in.1, s32[4]{0:T(128)} %cols_in.1, f32[1,2,256,1024]{3,2,1,0:T(8,128)} %objects_in.1), custom_call_target="tpu_custom_call" | custom-call | flops 1 | bytes 1 | tf_op jit(solution)/shard_map/edge/pallas_call | solution.py:331
  2.2 3.3 %collective-permute-start = (bf16[2064,128]{1,0:T(8,128)(2,1)S(1)}, bf16[2064,128]{1,0:T(8,128)(2,1)S(1)}, u32[]{:S(2)}, u32[]{:S(2)}) collective-permute-start(bf16[2064,128]{1,0:T(8,128)(2,1)S(1)} %get-tuple-element.30), channel_id=1, source_target_pairs={{0,127},{1,0},{2,1},{3,2},{4,3},{5,4},{6,5},{7,6},{8,7},{9,8},{10,... | collective-permute-start | bytes 1585160 | tf_op jit(solution)/shard_map/ppermute | solution.py:350
  5.6 6.7 %collective-permute-done.early = bf16[2064,128]{1,0:T(8,128)(2,1)S(1)} collective-permute-done((bf16[2064,128]{1,0:T(8,128)(2,1)S(1)}, bf16[2064,128]{1,0:T(8,128)(2,1)S(1)}, u32[]{:S(2)}, u32[]{:S(2)}) %collective-permute-start) | collective-permute-done | bytes 528416 | tf_op jit(solution)/shard_map/ppermute | solution.py:350
  12.2 1.0 %mate.1 = bf16[2,256,256]{2,1,0:T(8,128)(2,1)S(1)} custom-call(s32[4]{0:T(128)S(1)} %get-tuple-element.27.rows, s32[4]{0:T(128)S(1)} %get-tuple-element.28.cols, f32[2,256,1024]{2,1,0:T(8,128)S(1)} %get-tuple-element.29.objects, bf16[2064,128]{1,0:T(8,128)(2,1)S(1)} %collective-permute-done.early), custom_call_target="tpu_custom_call" | custom-call | flops 1 | bytes 1 | tf_op jit(solution)/shard_map/mate/pallas_call | solution.py:331
  13.2 0.7 collective-permute-done.1.late
  13.9 10.7 %collective-permute-start.2 = (bf16[2,256,256]{2,1,0:T(8,128)(2,1)S(1)}, bf16[2,256,256]{2,1,0:T(8,128)(2,1)S(1)}, u32[]{:S(2)}, u32[]{:S(2)}) collective-permute-start(bf16[2,256,256]{2,1,0:T(8,128)(2,1)S(1)} %mate.1), channel_id=1, source_target_pairs={{0,128},{1,129},{2,130},{3,131},{4,132},{5,133},{6,134},{7,135},{8... | collective-permute-start | bytes 786440 | tf_op jit(solution)/shard_map/ppermute | solution.py:350
  24.6 0.9 %cosine_bitcast_fusion = (f32[1,256,256]{2,1,0:T(8,128)S(1)}, f32[1,256,256]{2,1,0:T(8,128)S(1)}) fusion(f32[256,256]{1,0:T(8,128)S(1)} %copy-done.5), kind=kLoop, calls=%fused_computation.2 | loop fusion | bytes 786432 | tf_op jit(solution)/shard_map/stack | solution.py:352
  25.6 0.0 copy-start
  25.6 0.0 copy-start.3
  25.6 0.0 copy-start.4
  25.7 2.5 %windows.1 = (bf16[2,256,256]{2,1,0:T(8,128)(2,1)S(1)}, bf16[2,256,256]{2,1,0:T(8,128)(2,1)S(1)}, bf16[2,256,256]{2,1,0:T(8,128)(2,1)S(1)}, s32[8]{0:T(128)S(1)}) custom-call(s32[4]{0:T(128)S(1)} %get-tuple-element.27.rows, s32[4]{0:T(128)S(1)} %get-tuple-element.28.cols, f32[2,256,1024]{2,1,0:T(8,128)S(1)} %get-tuple-element.29.objects, ...), custom_call_target="tpu_custom_call" | custom-call | flops 1 | bytes 1 | tf_op jit(solution)/shard_map/windows/pallas_call | solution.py:331
  28.2 0.1 collective-permute-start.3
  28.3 0.1 collective-permute-done.2.mate
  28.4 4.8 %solo0.1 = (bf16[2,128,256]{2,1,0:T(8,128)(2,1)S(1)}, bf16[2,192,256]{2,1,0:T(8,128)(2,1)S(1)}, f32[2,256,256]{2,1,0:T(8,128)S(1)}, bf16[2,128,256]{2,1,0:T(8,128)(2,1)S(1)}) custom-call(s32[4]{0:T(128)S(1)} %get-tuple-element.27.rows, s32[4]{0:T(128)S(1)} %copy-done.2, bf16[2,256,256]{2,1,0:T(8,128)(2,1)S(1)} %get-tuple-element.34.own, ...), custom_call_target="tpu_custom_call" | custom-call | flops 99999997952 | bytes 1 | tf_op jit(solution)/shard_map/solo0/pallas_call | solution.py:331
  33.3 16.8 %collective-permute-start.4 = (bf16[2,192,256]{2,1,0:T(8,128)(2,1)S(1)}, bf16[2,192,256]{2,1,0:T(8,128)(2,1)S(1)}, u32[]{:S(2)}, u32[]{:S(2)}) collective-permute-start(bf16[2,192,256]{2,1,0:T(8,128)(2,1)S(1)} %get-tuple-element.42), channel_id=1, source_target_pairs={{0,128},{1,129},{2,130},{3,131},{4,132},{5,133},{6,134},{7,135},{8... | collective-permute-start | bytes 589832 | tf_op jit(solution)/shard_map/ppermute | solution.py:350
  50.1 5.6 %solo1.1 = (bf16[2,2,128,256]{3,2,1,0:T(8,128)(2,1)}, bf16[2,192,256]{2,1,0:T(8,128)(2,1)S(1)}, f32[2,256,256]{2,1,0:T(8,128)S(1)}, bf16[2,2,128,256]{3,2,1,0:T(8,128)(2,1)S(1)}) custom-call(s32[4]{0:T(128)S(1)} %get-tuple-element.27.rows, s32[4]{0:T(128)S(1)} %copy-done.2, bf16[2,256,256]{2,1,0:T(8,128)(2,1)S(1)} %get-tuple-element.37.own, ...), custom_call_target="tpu_custom_call" | custom-call | flops 99999997952 | bytes 1 | tf_op jit(solution)/shard_map/solo1/pallas_call | solution.py:331
  55.6 0.7 collective-permute-start.5
  56.3 9.9 %collective-permute-start.6 = (bf16[2,2,128,256]{3,2,1,0:T(8,128)(2,1)S(1)}, bf16[2,2,128,256]{3,2,1,0:T(8,128)(2,1)S(1)}, u32[]{:S(2)}, u32[]{:S(2)}) collective-permute-start(bf16[2,2,128,256]{3,2,1,0:T(8,128)(2,1)S(1)} %get-tuple-element.44), channel_id=1, source_target_pairs={{0,127},{1,0},{2,1},{3,2},{4,3},{5,4},{6,5},{7,6},{8,7},{9,8},{10,... | collective-permute-start | bytes 786440 | tf_op jit(solution)/shard_map/ppermute | solution.py:350
  66.1 1.2 %collective-permute-start.7 = (bf16[2,2,128,256]{3,2,1,0:T(8,128)(2,1)}, bf16[2,2,128,256]{3,2,1,0:T(8,128)(2,1)}, u32[]{:S(2)}, u32[]{:S(2)}) collective-permute-start(bf16[2,2,128,256]{3,2,1,0:T(8,128)(2,1)} %get-tuple-element.46), channel_id=1, source_target_pairs={{0,255},{1,128},{2,129},{3,130},{4,131},{5,132},{6,133},{7,134},{8... | collective-permute-start | bytes 786440 | tf_op jit(solution)/shard_map/ppermute | solution.py:350
  67.4 2.3 %own.1.given = f32[2,512,1024]{2,1,0:T(8,128)S(1)} custom-call(s32[4]{0:T(128)S(1)} %get-tuple-element.27.rows, s32[4]{0:T(128)S(1)} %get-tuple-element.28.cols, f32[2,256,256]{2,1,0:T(8,128)S(1)} %get-tuple-element.36.kept0, f32[2,256,256]{2,1,0:T(8,128)S(1)} %get-tuple-element.41.kept1, bf16[2,192,256]{2,1,0:T(8,128)(2,1)S(1)} %collective-permute-done.4.inband), custom_call_target="tpu_custom_call" | custom-call | flops 99999997952 | bytes 1 | tf_op jit(solution)/shard_map/own/pallas_call | solution.py:331
  69.7 4.7 %collective-permute-done.5.inband = bf16[2,192,256]{2,1,0:T(8,128)(2,1)S(1)} collective-permute-done((bf16[2,192,256]{2,1,0:T(8,128)(2,1)S(1)}, bf16[2,192,256]{2,1,0:T(8,128)(2,1)S(1)}, u32[]{:S(2)}, u32[]{:S(2)}) %collective-permute-start.5) | collective-permute-done | bytes 196640 | tf_op jit(solution)/shard_map/ppermute | solution.py:350
  74.4 2.2 %more.1 = (f32[2,512,1024]{2,1,0:T(8,128)S(1)}, f32[1,2,256,1024]{3,2,1,0:T(8,128)}) custom-call(s32[4]{0:T(128)S(1)} %get-tuple-element.27.rows, s32[4]{0:T(128)S(1)} %get-tuple-element.28.cols, s32[8]{0:T(128)S(1)} %get-tuple-element.33.spots, f32[2,512,1024]{2,1,0:T(8,128)S(1)} %own.1.given, ...), custom_call_target="tpu_custom_call", output_to_operand_aliasing={{0}: (3, {})} | custom-call | flops 99999997952 | bytes 1 | tf_op jit(solution)/shard_map/more/pallas_call | solution.py:331
  76.6 7.2 %collective-permute-done.7.outers = bf16[2,2,128,256]{3,2,1,0:T(8,128)(2,1)} collective-permute-done((bf16[2,2,128,256]{3,2,1,0:T(8,128)(2,1)}, bf16[2,2,128,256]{3,2,1,0:T(8,128)(2,1)}, u32[]{:S(2)}, u32[]{:S(2)}) %collective-permute-start.7) | collective-permute-done | bytes 262176 | tf_op jit(solution)/shard_map/ppermute | solution.py:350
  83.7 2.3 %last.1 = (f32[2,512,1024]{2,1,0:T(8,128)S(1)}, f32[1,2,256,1024]{3,2,1,0:T(8,128)}) custom-call(s32[8]{0:T(128)S(1)} %get-tuple-element.33.spots, f32[2,512,1024]{2,1,0:T(8,128)S(1)} %get-tuple-element.45.given, bf16[2,2,128,256]{3,2,1,0:T(8,128)(2,1)} %collective-permute-done.7.outers, ...), custom_call_target="tpu_custom_call", output_to_operand_aliasing={{0}: (1, {}), {1}: (3, {})} | custom-call | flops 1 | bytes 1 | tf_op jit(solution)/shard_map/last/pallas_call | solution.py:331
  (14 shorter events, 0.1 us)
Async XLA Ops:
  0.0 24.6 %copy-start.5 = (f32[256,256]{1,0:T(8,128)S(1)}, f32[256,256]{1,0:T(8,128)}, u32[]{:S(2)}) copy-start(f32[256,256]{1,0:T(8,128)} %param.12) | copy-start | bytes 786436
  2.2 10.0 %collective-permute-start = (bf16[2064,128]{1,0:T(8,128)(2,1)S(1)}, bf16[2064,128]{1,0:T(8,128)(2,1)S(1)}, u32[]{:S(2)}, u32[]{:S(2)}) collective-permute-start(bf16[2064,128]{1,0:T(8,128)(2,1)S(1)} %get-tuple-element.30), channel_id=1, source_target_pairs={{0,127},{1,0},{2,1},{3,2},{4,3},{5,4},{6,5},{7,6},{8,7},{9,8},{10,... | collective-permute-start | bytes 1585160 | tf_op jit(solution)/shard_map/ppermute | solution.py:350
  5.5 8.4 %collective-permute-start.1 = (bf16[2064,128]{1,0:T(8,128)(2,1)S(1)}, bf16[2064,128]{1,0:T(8,128)(2,1)S(1)}, u32[]{:S(2)}, u32[]{:S(2)}) collective-permute-start(bf16[2064,128]{1,0:T(8,128)(2,1)S(1)} %get-tuple-element.31), channel_id=1, source_target_pairs={{0,1},{1,2},{2,3},{3,4},{4,5},{5,6},{6,7},{7,8},{8,9},{9,10},{10,1... | collective-permute-start | bytes 1585160 | tf_op jit(solution)/shard_map/ppermute | solution.py:350
  13.9 14.4 %collective-permute-start.2 = (bf16[2,256,256]{2,1,0:T(8,128)(2,1)S(1)}, bf16[2,256,256]{2,1,0:T(8,128)(2,1)S(1)}, u32[]{:S(2)}, u32[]{:S(2)}) collective-permute-start(bf16[2,256,256]{2,1,0:T(8,128)(2,1)S(1)} %mate.1), channel_id=1, source_target_pairs={{0,128},{1,129},{2,130},{3,131},{4,132},{5,133},{6,134},{7,135},{8... | collective-permute-start | bytes 786440 | tf_op jit(solution)/shard_map/ppermute | solution.py:350
  25.6 2.8 %copy-start = (bf16[4,2,256,256]{3,2,1,0:T(8,128)(2,1)S(1)}, bf16[4,2,256,256]{3,2,1,0:T(8,128)(2,1)}, u32[]{:S(2)}) copy-start(bf16[4,2,256,256]{3,2,1,0:T(8,128)(2,1)} %probes.3) | copy-start | bytes 3145732
  25.6 2.8 %copy-start.1 = (f32[4,256,256]{2,1,0:T(8,128)S(1)}, f32[4,256,256]{2,1,0:T(8,128)}, u32[]{:S(2)}) copy-start(f32[4,256,256]{2,1,0:T(8,128)} %amplitudes.3) | copy-start | bytes 3145732
  25.6 2.8 %copy-start.2 = (s32[4]{0:T(128)S(1)}, s32[4]{0:T(128)}, u32[]{:S(2)}) copy-start(s32[4]{0:T(128)} %picks.3) | copy-start | bytes 52
  25.6 2.8 %copy-start.3 = (bf16[512,512]{1,0:T(8,128)(2,1)S(1)}, bf16[512,512]{1,0:T(8,128)(2,1)}, u32[]{:S(2)}) copy-start(bf16[512,512]{1,0:T(8,128)(2,1)} %constant.5.clone.second) | copy-start | bytes 1572868
  25.6 2.8 %copy-start.4 = (bf16[512,512]{1,0:T(8,128)(2,1)S(1)}, bf16[512,512]{1,0:T(8,128)(2,1)}, u32[]{:S(2)}) copy-start(bf16[512,512]{1,0:T(8,128)(2,1)} %constant.4.clone.first) | copy-start | bytes 1572868
  28.2 21.9 %collective-permute-start.3 = (bf16[2,256,256]{2,1,0:T(8,128)(2,1)S(1)}, bf16[2,256,256]{2,1,0:T(8,128)(2,1)S(1)}, u32[]{:S(2)}, u32[]{:S(2)}) collective-permute-start(bf16[2,256,256]{2,1,0:T(8,128)(2,1)S(1)} %get-tuple-element.38), channel_id=1, source_target_pairs={{0,128},{1,129},{2,130},{3,131},{4,132},{5,133},{6,134},{7,135},{8... | collective-permute-start | bytes 786440 | tf_op jit(solution)/shard_map/ppermute | solution.py:350
  33.3 34.1 %collective-permute-start.4 = (bf16[2,192,256]{2,1,0:T(8,128)(2,1)S(1)}, bf16[2,192,256]{2,1,0:T(8,128)(2,1)S(1)}, u32[]{:S(2)}, u32[]{:S(2)}) collective-permute-start(bf16[2,192,256]{2,1,0:T(8,128)(2,1)S(1)} %get-tuple-element.42), channel_id=1, source_target_pairs={{0,128},{1,129},{2,130},{3,131},{4,132},{5,133},{6,134},{7,135},{8... | collective-permute-start | bytes 589832 | tf_op jit(solution)/shard_map/ppermute | solution.py:350
  55.6 18.7 %collective-permute-start.5 = (bf16[2,192,256]{2,1,0:T(8,128)(2,1)S(1)}, bf16[2,192,256]{2,1,0:T(8,128)(2,1)S(1)}, u32[]{:S(2)}, u32[]{:S(2)}) collective-permute-start(bf16[2,192,256]{2,1,0:T(8,128)(2,1)S(1)} %get-tuple-element.43), channel_id=1, source_target_pairs={{0,128},{1,129},{2,130},{3,131},{4,132},{5,133},{6,134},{7,135},{8... | collective-permute-start | bytes 589832 | tf_op jit(solution)/shard_map/ppermute | solution.py:350
  56.3 18.1 %collective-permute-start.6 = (bf16[2,2,128,256]{3,2,1,0:T(8,128)(2,1)S(1)}, bf16[2,2,128,256]{3,2,1,0:T(8,128)(2,1)S(1)}, u32[]{:S(2)}, u32[]{:S(2)}) collective-permute-start(bf16[2,2,128,256]{3,2,1,0:T(8,128)(2,1)S(1)} %get-tuple-element.44), channel_id=1, source_target_pairs={{0,127},{1,0},{2,1},{3,2},{4,3},{5,4},{6,5},{7,6},{8,7},{9,8},{10,... | collective-permute-start | bytes 786440 | tf_op jit(solution)/shard_map/ppermute | solution.py:350
  66.1 17.6 %collective-permute-start.7 = (bf16[2,2,128,256]{3,2,1,0:T(8,128)(2,1)}, bf16[2,2,128,256]{3,2,1,0:T(8,128)(2,1)}, u32[]{:S(2)}, u32[]{:S(2)}) collective-permute-start(bf16[2,2,128,256]{3,2,1,0:T(8,128)(2,1)} %get-tuple-element.46), channel_id=1, source_target_pairs={{0,255},{1,128},{2,129},{3,130},{4,131},{5,132},{6,133},{7,134},{8... | collective-permute-start | bytes 786440 | tf_op jit(solution)/shard_map/ppermute | solution.py:350

commit v15 on v12

--- a/solution.py
+++ b/solution.py
@@ -364,6 +364,7 @@
     )
     early = move(early, "early")
     late = move(late, "late")
+    early, wave = lax.optimization_barrier((early, wave))
     (sent0,) = call(mate_kernel, "mate", [rows, cols, band, early], [full], [near])
     mate0 = move(sent0, "mate")
     sent1, own0, own1, spots = call(

time: 83.5 us -> 83.5 us (level)
  starting transfers between devices: 32.1 us -> 33.1 us
  waiting for transfers between devices: 27.1 us -> 26.1 us
    ppermute x8, starting transfers between devices: 32.1 us -> 33.1 us  [shards(): move = lambda x, way: lax.ppermute(x, AXES, route[way])]
    ppermute x8, waiting for transfers between devices: 27.1 us -> 26.1 us  [shards(): move = lambda x, way: lax.ppermute(x, AXES, route[way])]
where the time goes in v15:
time: 83.5 us; the launch traced here: 83.4 us
  starting transfers between devices  33.1 us (40%)
  waiting for transfers between devices  26.1 us (31%)
  Pallas kernels  22.9 us (27%)
  local copies, waits for them, and re-layouts  0.98 us (1%)
    ppermute x8, starting transfers between devices, shards(): move = lambda x, way: lax.ppermute(x, AXES, route[way])  33.1 us
    ppermute x8, waiting for transfers between devices, shards(): move = lambda x, way: lax.ppermute(x, AXES, route[way])  26.1 us
    pallas_call x8, Pallas kernels, call(): pl.pallas_call(kernel, name=name, out_shape=outputs, in_specs=in_specs or...  22.9 us
  transfers between devices with their start and end apart: 8, of which 4 were waited for; matrix products, arithmetic and copies ran while one was open for 1% of the time, Pallas kernels for 22%

profile of v15, /device:TPU:1, one launch (start us, length us, event | category | flops | bytes accessed | tf_op | source)
XLA Modules:
  0.0 83.4 jit_solution(9774463660102841931)
XLA Ops:
  0.0 2.2 %edge.1 = (bf16[2064,128]{1,0:T(8,128)(2,1)S(1)}, bf16[2064,128]{1,0:T(8,128)(2,1)S(1)}, f32[2,256,1024]{2,1,0:T(8,128)S(1)}, s32[4]{0:T(128)S(1)}, s32[4]{0:T(128)S(1)}) custom-call(s32[4]{0:T(128)} %rows_in.1, s32[4]{0:T(128)} %cols_in.1, f32[1,2,256,1024]{3,2,1,0:T(8,128)} %objects_in.1), custom_call_target="tpu_custom_call" | custom-call | flops 1 | bytes 1 | tf_op jit(solution)/shard_map/edge/pallas_call | solution.py:331
  2.2 3.3 %collective-permute-start = (bf16[2064,128]{1,0:T(8,128)(2,1)S(1)}, bf16[2064,128]{1,0:T(8,128)(2,1)S(1)}, u32[]{:S(2)}, u32[]{:S(2)}) collective-permute-start(bf16[2064,128]{1,0:T(8,128)(2,1)S(1)} %get-tuple-element.30), channel_id=1, source_target_pairs={{0,127},{1,0},{2,1},{3,2},{4,3},{5,4},{6,5},{7,6},{8,7},{9,8},{10,... | collective-permute-start | bytes 1585160 | tf_op jit(solution)/shard_map/ppermute | solution.py:350
  5.6 0.9 %cosine_bitcast_fusion = (f32[1,256,256]{2,1,0:T(8,128)S(1)}, f32[1,256,256]{2,1,0:T(8,128)S(1)}) fusion(f32[256,256]{1,0:T(8,128)S(1)} %copy-done.5), kind=kLoop, calls=%fused_computation.2 | loop fusion | bytes 786432 | tf_op jit(solution)/shard_map/stack | solution.py:352
  6.6 5.7 %collective-permute-done.early = bf16[2064,128]{1,0:T(8,128)(2,1)S(1)} collective-permute-done((bf16[2064,128]{1,0:T(8,128)(2,1)S(1)}, bf16[2064,128]{1,0:T(8,128)(2,1)S(1)}, u32[]{:S(2)}, u32[]{:S(2)}) %collective-permute-start) | collective-permute-done | bytes 528416 | tf_op jit(solution)/shard_map/ppermute | solution.py:350
  12.2 1.0 %mate.1 = bf16[2,256,256]{2,1,0:T(8,128)(2,1)S(1)} custom-call(s32[4]{0:T(128)S(1)} %get-tuple-element.27.rows, s32[4]{0:T(128)S(1)} %get-tuple-element.28.cols, f32[2,256,1024]{2,1,0:T(8,128)S(1)} %get-tuple-element.29.objects, bf16[2064,128]{1,0:T(8,128)(2,1)S(1)} %collective-permute-done.early), custom_call_target="tpu_custom_call" | custom-call | flops 1 | bytes 1 | tf_op jit(solution)/shard_map/mate/pallas_call | solution.py:331
  13.3 0.0 copy-start.1
  13.3 0.0 copy-start.2
  13.3 0.0 copy-start.3
  13.3 0.0 copy-start.4
  13.3 5.4 %collective-permute-start.2 = (bf16[2,256,256]{2,1,0:T(8,128)(2,1)S(1)}, bf16[2,256,256]{2,1,0:T(8,128)(2,1)S(1)}, u32[]{:S(2)}, u32[]{:S(2)}) collective-permute-start(bf16[2,256,256]{2,1,0:T(8,128)(2,1)S(1)} %mate.1), channel_id=1, source_target_pairs={{0,128},{1,129},{2,130},{3,131},{4,132},{5,133},{6,134},{7,135},{8... | collective-permute-start | bytes 786440 | tf_op jit(solution)/shard_map/ppermute | solution.py:350
  18.7 2.5 %windows.1 = (bf16[2,256,256]{2,1,0:T(8,128)(2,1)S(1)}, bf16[2,256,256]{2,1,0:T(8,128)(2,1)S(1)}, bf16[2,256,256]{2,1,0:T(8,128)(2,1)S(1)}, s32[8]{0:T(128)S(1)}) custom-call(s32[4]{0:T(128)S(1)} %get-tuple-element.27.rows, s32[4]{0:T(128)S(1)} %get-tuple-element.28.cols, f32[2,256,1024]{2,1,0:T(8,128)S(1)} %get-tuple-element.29.objects, ...), custom_call_target="tpu_custom_call" | custom-call | flops 1 | bytes 1 | tf_op jit(solution)/shard_map/windows/pallas_call | solution.py:331
  21.1 7.9 %collective-permute-start.3 = (bf16[2,256,256]{2,1,0:T(8,128)(2,1)S(1)}, bf16[2,256,256]{2,1,0:T(8,128)(2,1)S(1)}, u32[]{:S(2)}, u32[]{:S(2)}) collective-permute-start(bf16[2,256,256]{2,1,0:T(8,128)(2,1)S(1)} %get-tuple-element.38), channel_id=1, source_target_pairs={{0,128},{1,129},{2,130},{3,131},{4,132},{5,133},{6,134},{7,135},{8... | collective-permute-start | bytes 786440 | tf_op jit(solution)/shard_map/ppermute | solution.py:350
  29.0 4.8 %solo0.1 = (bf16[2,128,256]{2,1,0:T(8,128)(2,1)S(1)}, bf16[2,192,256]{2,1,0:T(8,128)(2,1)S(1)}, f32[2,256,256]{2,1,0:T(8,128)S(1)}, bf16[2,128,256]{2,1,0:T(8,128)(2,1)S(1)}) custom-call(s32[4]{0:T(128)S(1)} %get-tuple-element.27.rows, s32[4]{0:T(128)S(1)} %copy-done.2, bf16[2,256,256]{2,1,0:T(8,128)(2,1)S(1)} %get-tuple-element.34.own, ...), custom_call_target="tpu_custom_call" | custom-call | flops 99999997952 | bytes 1 | tf_op jit(solution)/shard_map/solo0/pallas_call | solution.py:331
  33.9 0.1 collective-permute-start.4
  34.0 10.5 %collective-permute-done.3.mate = bf16[2,256,256]{2,1,0:T(8,128)(2,1)S(1)} collective-permute-done((bf16[2,256,256]{2,1,0:T(8,128)(2,1)S(1)}, bf16[2,256,256]{2,1,0:T(8,128)(2,1)S(1)}, u32[]{:S(2)}, u32[]{:S(2)}) %collective-permute-start.3) | collective-permute-done | bytes 262176 | tf_op jit(solution)/shard_map/ppermute | solution.py:350
  44.5 5.6 %solo1.1 = (bf16[2,2,128,256]{3,2,1,0:T(8,128)(2,1)}, bf16[2,192,256]{2,1,0:T(8,128)(2,1)S(1)}, f32[2,256,256]{2,1,0:T(8,128)S(1)}, bf16[2,2,128,256]{3,2,1,0:T(8,128)(2,1)S(1)}) custom-call(s32[4]{0:T(128)S(1)} %get-tuple-element.27.rows, s32[4]{0:T(128)S(1)} %copy-done.2, bf16[2,256,256]{2,1,0:T(8,128)(2,1)S(1)} %get-tuple-element.37.own, ...), custom_call_target="tpu_custom_call" | custom-call | flops 99999997952 | bytes 1 | tf_op jit(solution)/shard_map/solo1/pallas_call | solution.py:331
  50.1 4.9 %collective-permute-start.5 = (bf16[2,192,256]{2,1,0:T(8,128)(2,1)S(1)}, bf16[2,192,256]{2,1,0:T(8,128)(2,1)S(1)}, u32[]{:S(2)}, u32[]{:S(2)}) collective-permute-start(bf16[2,192,256]{2,1,0:T(8,128)(2,1)S(1)} %get-tuple-element.43), channel_id=1, source_target_pairs={{0,128},{1,129},{2,130},{3,131},{4,132},{5,133},{6,134},{7,135},{8... | collective-permute-start | bytes 589832 | tf_op jit(solution)/shard_map/ppermute | solution.py:350
  55.0 8.0 %collective-permute-start.6 = (bf16[2,2,128,256]{3,2,1,0:T(8,128)(2,1)S(1)}, bf16[2,2,128,256]{3,2,1,0:T(8,128)(2,1)S(1)}, u32[]{:S(2)}, u32[]{:S(2)}) collective-permute-start(bf16[2,2,128,256]{3,2,1,0:T(8,128)(2,1)S(1)} %get-tuple-element.44), channel_id=1, source_target_pairs={{0,127},{1,0},{2,1},{3,2},{4,3},{5,4},{6,5},{7,6},{8,7},{9,8},{10,... | collective-permute-start | bytes 786440 | tf_op jit(solution)/shard_map/ppermute | solution.py:350
  63.0 3.5 %collective-permute-start.7 = (bf16[2,2,128,256]{3,2,1,0:T(8,128)(2,1)}, bf16[2,2,128,256]{3,2,1,0:T(8,128)(2,1)}, u32[]{:S(2)}, u32[]{:S(2)}) collective-permute-start(bf16[2,2,128,256]{3,2,1,0:T(8,128)(2,1)} %get-tuple-element.46), channel_id=1, source_target_pairs={{0,255},{1,128},{2,129},{3,130},{4,131},{5,132},{6,133},{7,134},{8... | collective-permute-start | bytes 786440 | tf_op jit(solution)/shard_map/ppermute | solution.py:350
  66.5 2.3 %own.1.given = f32[2,512,1024]{2,1,0:T(8,128)S(1)} custom-call(s32[4]{0:T(128)S(1)} %get-tuple-element.27.rows, s32[4]{0:T(128)S(1)} %get-tuple-element.28.cols, f32[2,256,256]{2,1,0:T(8,128)S(1)} %get-tuple-element.36.kept0, f32[2,256,256]{2,1,0:T(8,128)S(1)} %get-tuple-element.41.kept1, bf16[2,192,256]{2,1,0:T(8,128)(2,1)S(1)} %collective-permute-done.4.inband), custom_call_target="tpu_custom_call" | custom-call | flops 99999997952 | bytes 1 | tf_op jit(solution)/shard_map/own/pallas_call | solution.py:331
  68.8 1.8 %collective-permute-done.5.inband = bf16[2,192,256]{2,1,0:T(8,128)(2,1)S(1)} collective-permute-done((bf16[2,192,256]{2,1,0:T(8,128)(2,1)S(1)}, bf16[2,192,256]{2,1,0:T(8,128)(2,1)S(1)}, u32[]{:S(2)}, u32[]{:S(2)}) %collective-permute-start.5) | collective-permute-done | bytes 196640 | tf_op jit(solution)/shard_map/ppermute | solution.py:350
  70.6 2.2 %more.1 = (f32[2,512,1024]{2,1,0:T(8,128)S(1)}, f32[1,2,256,1024]{3,2,1,0:T(8,128)}) custom-call(s32[4]{0:T(128)S(1)} %get-tuple-element.27.rows, s32[4]{0:T(128)S(1)} %get-tuple-element.28.cols, s32[8]{0:T(128)S(1)} %get-tuple-element.33.spots, f32[2,512,1024]{2,1,0:T(8,128)S(1)} %own.1.given, ...), custom_call_target="tpu_custom_call", output_to_operand_aliasing={{0}: (3, {})} | custom-call | flops 99999997952 | bytes 1 | tf_op jit(solution)/shard_map/more/pallas_call | solution.py:331
  72.8 8.1 %collective-permute-done.7.outers = bf16[2,2,128,256]{3,2,1,0:T(8,128)(2,1)} collective-permute-done((bf16[2,2,128,256]{3,2,1,0:T(8,128)(2,1)}, bf16[2,2,128,256]{3,2,1,0:T(8,128)(2,1)}, u32[]{:S(2)}, u32[]{:S(2)}) %collective-permute-start.7) | collective-permute-done | bytes 262176 | tf_op jit(solution)/shard_map/ppermute | solution.py:350
  80.9 2.3 %last.1 = (f32[2,512,1024]{2,1,0:T(8,128)S(1)}, f32[1,2,256,1024]{3,2,1,0:T(8,128)}) custom-call(s32[8]{0:T(128)S(1)} %get-tuple-element.33.spots, f32[2,512,1024]{2,1,0:T(8,128)S(1)} %get-tuple-element.45.given, bf16[2,2,128,256]{3,2,1,0:T(8,128)(2,1)} %collective-permute-done.7.outers, ...), custom_call_target="tpu_custom_call", output_to_operand_aliasing={{0}: (1, {}), {1}: (3, {})} | custom-call | flops 1 | bytes 1 | tf_op jit(solution)/shard_map/last/pallas_call | solution.py:331
  (14 shorter events, 0.1 us)
Async XLA Ops:
  0.0 5.6 %copy-start.5 = (f32[256,256]{1,0:T(8,128)S(1)}, f32[256,256]{1,0:T(8,128)}, u32[]{:S(2)}) copy-start(f32[256,256]{1,0:T(8,128)} %param.12) | copy-start | bytes 786436
  2.2 10.0 %collective-permute-start = (bf16[2064,128]{1,0:T(8,128)(2,1)S(1)}, bf16[2064,128]{1,0:T(8,128)(2,1)S(1)}, u32[]{:S(2)}, u32[]{:S(2)}) collective-permute-start(bf16[2064,128]{1,0:T(8,128)(2,1)S(1)} %get-tuple-element.30), channel_id=1, source_target_pairs={{0,127},{1,0},{2,1},{3,2},{4,3},{5,4},{6,5},{7,6},{8,7},{9,8},{10,... | collective-permute-start | bytes 1585160 | tf_op jit(solution)/shard_map/ppermute | solution.py:350
  5.5 13.1 %collective-permute-start.1 = (bf16[2064,128]{1,0:T(8,128)(2,1)S(1)}, bf16[2064,128]{1,0:T(8,128)(2,1)S(1)}, u32[]{:S(2)}, u32[]{:S(2)}) collective-permute-start(bf16[2064,128]{1,0:T(8,128)(2,1)S(1)} %get-tuple-element.32), channel_id=1, source_target_pairs={{0,1},{1,2},{2,3},{3,4},{4,5},{5,6},{6,7},{7,8},{8,9},{9,10},{10,1... | collective-permute-start | bytes 1585160 | tf_op jit(solution)/shard_map/ppermute | solution.py:350
  13.3 15.8 %copy-start = (bf16[4,2,256,256]{3,2,1,0:T(8,128)(2,1)S(1)}, bf16[4,2,256,256]{3,2,1,0:T(8,128)(2,1)}, u32[]{:S(2)}) copy-start(bf16[4,2,256,256]{3,2,1,0:T(8,128)(2,1)} %probes.3) | copy-start | bytes 3145732
  13.3 15.7 %copy-start.1 = (f32[4,256,256]{2,1,0:T(8,128)S(1)}, f32[4,256,256]{2,1,0:T(8,128)}, u32[]{:S(2)}) copy-start(f32[4,256,256]{2,1,0:T(8,128)} %amplitudes.3) | copy-start | bytes 3145732
  13.3 15.7 %copy-start.2 = (s32[4]{0:T(128)S(1)}, s32[4]{0:T(128)}, u32[]{:S(2)}) copy-start(s32[4]{0:T(128)} %picks.3) | copy-start | bytes 52
  13.3 15.7 %copy-start.3 = (bf16[512,512]{1,0:T(8,128)(2,1)S(1)}, bf16[512,512]{1,0:T(8,128)(2,1)}, u32[]{:S(2)}) copy-start(bf16[512,512]{1,0:T(8,128)(2,1)} %constant.5.clone.second) | copy-start | bytes 1572868
  13.3 15.7 %copy-start.4 = (bf16[512,512]{1,0:T(8,128)(2,1)S(1)}, bf16[512,512]{1,0:T(8,128)(2,1)}, u32[]{:S(2)}) copy-start(bf16[512,512]{1,0:T(8,128)(2,1)} %constant.4.clone.first) | copy-start | bytes 1572868
  13.3 15.7 %collective-permute-start.2 = (bf16[2,256,256]{2,1,0:T(8,128)(2,1)S(1)}, bf16[2,256,256]{2,1,0:T(8,128)(2,1)S(1)}, u32[]{:S(2)}, u32[]{:S(2)}) collective-permute-start(bf16[2,256,256]{2,1,0:T(8,128)(2,1)S(1)} %mate.1), channel_id=1, source_target_pairs={{0,128},{1,129},{2,130},{3,131},{4,132},{5,133},{6,134},{7,135},{8... | collective-permute-start | bytes 786440 | tf_op jit(solution)/shard_map/ppermute | solution.py:350
  21.1 23.4 %collective-permute-start.3 = (bf16[2,256,256]{2,1,0:T(8,128)(2,1)S(1)}, bf16[2,256,256]{2,1,0:T(8,128)(2,1)S(1)}, u32[]{:S(2)}, u32[]{:S(2)}) collective-permute-start(bf16[2,256,256]{2,1,0:T(8,128)(2,1)S(1)} %get-tuple-element.38), channel_id=1, source_target_pairs={{0,128},{1,129},{2,130},{3,131},{4,132},{5,133},{6,134},{7,135},{8... | collective-permute-start | bytes 786440 | tf_op jit(solution)/shard_map/ppermute | solution.py:350
  33.9 32.6 %collective-permute-start.4 = (bf16[2,192,256]{2,1,0:T(8,128)(2,1)S(1)}, bf16[2,192,256]{2,1,0:T(8,128)(2,1)S(1)}, u32[]{:S(2)}, u32[]{:S(2)}) collective-permute-start(bf16[2,192,256]{2,1,0:T(8,128)(2,1)S(1)} %get-tuple-element.42), channel_id=1, source_target_pairs={{0,128},{1,129},{2,130},{3,131},{4,132},{5,133},{6,134},{7,135},{8... | collective-permute-start | bytes 589832 | tf_op jit(solution)/shard_map/ppermute | solution.py:350
  50.1 20.5 %collective-permute-start.5 = (bf16[2,192,256]{2,1,0:T(8,128)(2,1)S(1)}, bf16[2,192,256]{2,1,0:T(8,128)(2,1)S(1)}, u32[]{:S(2)}, u32[]{:S(2)}) collective-permute-start(bf16[2,192,256]{2,1,0:T(8,128)(2,1)S(1)} %get-tuple-element.43), channel_id=1, source_target_pairs={{0,128},{1,129},{2,130},{3,131},{4,132},{5,133},{6,134},{7,135},{8... | collective-permute-start | bytes 589832 | tf_op jit(solution)/shard_map/ppermute | solution.py:350
  55.0 15.6 %collective-permute-start.6 = (bf16[2,2,128,256]{3,2,1,0:T(8,128)(2,1)S(1)}, bf16[2,2,128,256]{3,2,1,0:T(8,128)(2,1)S(1)}, u32[]{:S(2)}, u32[]{:S(2)}) collective-permute-start(bf16[2,2,128,256]{3,2,1,0:T(8,128)(2,1)S(1)} %get-tuple-element.44), channel_id=1, source_target_pairs={{0,127},{1,0},{2,1},{3,2},{4,3},{5,4},{6,5},{7,6},{8,7},{9,8},{10,... | collective-permute-start | bytes 786440 | tf_op jit(solution)/shard_map/ppermute | solution.py:350
  63.0 17.9 %collective-permute-start.7 = (bf16[2,2,128,256]{3,2,1,0:T(8,128)(2,1)}, bf16[2,2,128,256]{3,2,1,0:T(8,128)(2,1)}, u32[]{:S(2)}, u32[]{:S(2)}) collective-permute-start(bf16[2,2,128,256]{3,2,1,0:T(8,128)(2,1)} %get-tuple-element.46), channel_id=1, source_target_pairs={{0,255},{1,128},{2,129},{3,130},{4,131},{5,132},{6,133},{7,134},{8... | collective-permute-start | bytes 786440 | tf_op jit(solution)/shard_map/ppermute | solution.py:350
